TPU v7x, 32 devices: a whole 2x2x4 slice. The times are simulated.
32 devices in a mesh: fsdp: 8 (over y, x, core), seq: 4 (over z).
Axes of the slice: x: 2, y: 2, z: 4, core: 2. Of those that a mesh axis runs over, the one named last changes fastest.
Arguments:
- layer_input: bfloat16 [16, 1024, 512], P('fsdp', 'seq'), may hold values from -6 to 6
- lengths: int32 [16], P('fsdp'), may hold values from 512 to 1024, as said below
- ln1_gain: bfloat16 [512], P('fsdp'), may hold values from 0.099609375 to 1.8984375
- ln1_bias: bfloat16 [512], P('fsdp'), may hold values from -1.5 to 1.5
- w_qkv: bfloat16 [512, 1536], P('fsdp'), may hold values from -0.25 to 0.25
- w_rel: bfloat16 [512, 512], P('fsdp'), may hold values from -0.25 to 0.25
- bias_u: bfloat16 [512], P('fsdp'), may hold values from -2.5 to 2.5
- bias_v: bfloat16 [512], P('fsdp'), may hold values from -2.5 to 2.5
- w_out: bfloat16 [512, 512], P('fsdp'), may hold values from -3 to 3
- ln2_gain: bfloat16 [512], P('fsdp'), may hold values from 0.099609375 to 1.8984375
- ln2_bias: bfloat16 [512], P('fsdp'), may hold values from -1.5 to 1.5
- w_up: bfloat16 [512, 2048], P('fsdp'), may hold values from -0.25 to 0.25
- up_bias: bfloat16 [2048], P('fsdp'), may hold values from -2.5 to 2.5
- w_down: bfloat16 [2048, 512], P('fsdp'), may hold values from -0.125 to 0.125
- down_bias: bfloat16 [512], P('fsdp'), may hold values from -1.5 to 1.5
- grad_out: bfloat16 [16, 1024, 512], P('fsdp', 'seq'), may hold values from -6 to 6
Outputs:
- layer_output: bfloat16 [16, 1024, 512], P('fsdp', 'seq')
- grad_x: float32 [16, 1024, 512], P('fsdp', 'seq')
- grad_ln1_gain: float32 [512], P('fsdp')
- grad_ln1_bias: float32 [512], P('fsdp')
- grad_w_qkv: float32 [512, 1536], P('fsdp')
- grad_w_rel: float32 [512, 512], P('fsdp')
- grad_bias_u: float32 [512], P('fsdp')
- grad_bias_v: float32 [512], P('fsdp')
- grad_w_out: float32 [512, 512], P('fsdp')
- grad_ln2_gain: float32 [512], P('fsdp')
- grad_ln2_bias: float32 [512], P('fsdp')
- grad_w_up: float32 [512, 2048], P('fsdp')
- grad_up_bias: float32 [2048], P('fsdp')
- grad_w_down: float32 [2048, 512], P('fsdp')
- grad_down_bias: float32 [512], P('fsdp')
Inputs may be any that keep to these rules, and one draw needn't show every extreme that they name: `lengths`: in every draw some slot has exactly 1024 live positions and some exactly 512.
All inputs are finite; a program needn't handle non-finite values.
Results may differ from a plain program's by a relative error of at most 0.017.
Values may be sent and summed in bfloat16 or wider, within the bound.
No kernel may reach another device: no remote copies, remote signals or barrier semaphores. Data moves between devices by JAX's collectives and lax.ppermute only.
A program may use at most 192 MiB of HBM per device.

v0:
```python
import math

import jax
import jax.numpy as jnp
from jax import lax
from jax.sharding import PartitionSpec as P

H = 8
HEAD_DIM = 64


NEG_FILL = -1e30
NORM_EPS = 1e-05


def norm_parts(values):
    mean_val = jnp.mean(values, axis=-1, keepdims=True)
    centered = values - mean_val
    inv_std = lax.rsqrt(jnp.mean(centered * centered, axis=-1, keepdims=True) + NORM_EPS)
    return (centered * inv_std, inv_std)


def norm_back(grad_norm, x_hat, inv_std):
    first_mean = jnp.mean(grad_norm, axis=-1, keepdims=True)
    second_mean = jnp.mean(grad_norm * x_hat, axis=-1, keepdims=True)
    return inv_std * (grad_norm - first_mean - x_hat * second_mean)


def position_table(count_rows, feature_count):
    steps = lax.iota(jnp.float32, count_rows)
    half_count = feature_count // 2
    inv_freq = jnp.exp(
        lax.iota(jnp.float32, half_count) * (-2.0 * math.log(10000.0) / feature_count)
    )
    angles = steps[:, None] * inv_freq[None, :]
    return jnp.concatenate([jnp.sin(angles), jnp.cos(angles)], axis=1)


def skew_rows(matrix):
    leading = matrix.shape[:-2]
    row_count, col_count = matrix.shape[-2:]
    flattened = matrix.reshape(leading + (row_count * col_count,))
    picked = flattened[..., row_count - 1 : row_count - 1 + row_count * (col_count - 1)]
    return picked.reshape(leading + (row_count, col_count - 1))[..., : col_count - row_count]


def unskew_rows(matrix):
    leading = matrix.shape[:-2]
    row_count, key_count = matrix.shape[-2:]
    axis_pos = len(leading)
    widened = jnp.pad(matrix, [(0, 0)] * axis_pos + [(0, 0), (0, row_count - 1)])
    flattened = widened.reshape(leading + (row_count * (key_count + row_count - 1),))
    flattened = jnp.pad(flattened, [(0, 0)] * axis_pos + [(row_count - 1, 1)])
    return flattened.reshape(leading + (row_count, key_count + row_count))


def per_device(
    layer_input,
    lengths,
    ln1_gain,
    ln1_bias,
    w_qkv,
    w_rel,
    bias_u,
    bias_v,
    w_out,
    ln2_gain,
    ln2_bias,
    w_up,
    up_bias,
    w_down,
    down_bias,
    grad_out,
):
    weights = (
        lax.all_gather(ln1_gain, "fsdp", axis=0, tiled=True),
        lax.all_gather(ln1_bias, "fsdp", axis=0, tiled=True),
        lax.all_gather(w_qkv, "fsdp", axis=0, tiled=True),
        lax.all_gather(w_rel, "fsdp", axis=0, tiled=True),
        lax.all_gather(bias_u, "fsdp", axis=0, tiled=True),
        lax.all_gather(bias_v, "fsdp", axis=0, tiled=True),
        lax.all_gather(w_out, "fsdp", axis=0, tiled=True),
        lax.all_gather(ln2_gain, "fsdp", axis=0, tiled=True),
        lax.all_gather(ln2_bias, "fsdp", axis=0, tiled=True),
        lax.all_gather(w_up, "fsdp", axis=0, tiled=True),
        lax.all_gather(up_bias, "fsdp", axis=0, tiled=True),
        lax.all_gather(w_down, "fsdp", axis=0, tiled=True),
        lax.all_gather(down_bias, "fsdp", axis=0, tiled=True),
    )
    (
        gain_one,
        shift_one,
        query_key_value_matrix,
        rel_weight,
        first_bias,
        second_bias,
        output_matrix,
        gain_two,
        shift_two,
        up_matrix,
        up_shift,
        down_matrix,
        down_shift,
    ) = weights
    gain_one = gain_one.astype(jnp.float32)
    shift_one = shift_one.astype(jnp.float32)
    gain_two = gain_two.astype(jnp.float32)
    shift_two = shift_two.astype(jnp.float32)
    up_shift = up_shift.astype(jnp.float32)
    down_shift = down_shift.astype(jnp.float32)
    slots, block_len, width = layer_input.shape
    seq_count = lax.axis_size("seq")
    seq_rank = lax.axis_index("seq")
    head_dim = HEAD_DIM
    group = H // seq_count
    full_len = block_len * seq_count
    score_scale = 1.0 / math.sqrt(head_dim)
    q_block = 512
    num_blocks = full_len // q_block
    win_len = full_len + q_block
    x_float = layer_input.astype(jnp.float32)
    x_hat_one, inv_std_one = norm_parts(x_float)
    first_normalized = (x_hat_one * gain_one + shift_one).astype(jnp.bfloat16)
    qkv_local = jnp.einsum(
        "mcr,rk->mck", first_normalized, query_key_value_matrix, preferred_element_type=jnp.float32
    ).astype(jnp.bfloat16)
    qkv_heads = lax.all_to_all(qkv_local, "seq", split_axis=2, concat_axis=1, tiled=True)
    qkv_heads = qkv_heads.reshape(slots, full_len, group, 3, head_dim)
    queries = qkv_heads[:, :, :, 0]
    keys = qkv_heads[:, :, :, 1]
    values = qkv_heads[:, :, :, 2]
    head_start = seq_rank * group
    head_bias_u = lax.dynamic_slice_in_dim(
        first_bias.astype(jnp.float32).reshape(H, head_dim), head_start, group, 0
    )
    head_bias_v = lax.dynamic_slice_in_dim(
        second_bias.astype(jnp.float32).reshape(H, head_dim), head_start, group, 0
    )
    query_u = (queries.astype(jnp.float32) + head_bias_u).astype(jnp.bfloat16)
    query_v = (queries.astype(jnp.float32) + head_bias_v).astype(jnp.bfloat16)
    table_rev = position_table(full_len, width).astype(jnp.bfloat16)[::-1]
    rel_cols = lax.dynamic_slice_in_dim(rel_weight, head_start * head_dim, group * head_dim, 1)
    rel_rev = jnp.dot(table_rev, rel_cols, preferred_element_type=jnp.float32).astype(jnp.bfloat16)
    rel_ext = jnp.concatenate([rel_rev, jnp.zeros_like(rel_rev)], axis=0).reshape(
        2 * full_len, group, head_dim
    )
    col_ids = lax.iota(jnp.int32, full_len)

    def scores_block(first_row):
        qu_part = lax.dynamic_slice_in_dim(query_u, first_row, q_block, 1)
        qv_part = lax.dynamic_slice_in_dim(query_v, first_row, q_block, 1)
        window_start = full_len - q_block - first_row
        rel_win = lax.dynamic_slice_in_dim(rel_ext, window_start, win_len, 0)
        content = jnp.einsum("sqhe,skhe->shqk", qu_part, keys, preferred_element_type=jnp.float32)
        rel_raw = jnp.einsum("sqhe,the->shqt", qv_part, rel_win, preferred_element_type=jnp.float32)
        rel_part = skew_rows(rel_raw)
        row_ids = first_row + lax.iota(jnp.int32, q_block)
        causal = col_ids[None, :] <= row_ids[:, None]
        inside = col_ids[None, :] < lengths[:, None]
        allowed = causal[None, None, :, :] & inside[:, None, None, :]
        scores = jnp.where(allowed, (content + rel_part) * score_scale, NEG_FILL)
        return (scores, qu_part, qv_part, rel_win, window_start)

    def forward_block(block_index):
        first_row = block_index * q_block
        scores, qu_part, qv_part, rel_win, window_start = scores_block(first_row)
        top = jnp.max(scores, axis=-1, keepdims=True)
        expo = jnp.exp(scores - top)
        total = jnp.sum(expo, axis=-1, keepdims=True)
        probs = (expo / total).astype(jnp.bfloat16)
        out_part = jnp.einsum(
            "shqk,skhe->sqhe", probs, values, preferred_element_type=jnp.float32
        ).astype(jnp.bfloat16)
        return (out_part, top[..., 0] + jnp.log(total[..., 0]))

    block_outs, block_lse = lax.map(forward_block, jnp.arange(num_blocks, dtype=jnp.int32))
    attn_heads = jnp.moveaxis(block_outs, 0, 1).reshape(slots, full_len, group * head_dim)
    attention_sequence = lax.all_to_all(attn_heads, "seq", split_axis=1, concat_axis=2, tiled=True)
    attention_projected = jnp.einsum(
        "mcr,rk->mck", attention_sequence, output_matrix, preferred_element_type=jnp.float32
    )
    resid = x_float + attention_projected
    x_hat_two, inv_std_two = norm_parts(resid)
    second_normalized = (x_hat_two * gain_two + shift_two).astype(jnp.bfloat16)
    pre_act = (
        jnp.einsum("oka,ac->okc", second_normalized, up_matrix, preferred_element_type=jnp.float32)
        + up_shift
    )
    normal_cdf = 0.5 * (1.0 + lax.erf(pre_act * (1.0 / math.sqrt(2.0))))
    hidden_state = (pre_act * normal_cdf).astype(jnp.bfloat16)
    down_proj = (
        jnp.einsum("zcp,pr->zcr", hidden_state, down_matrix, preferred_element_type=jnp.float32)
        + down_shift
    )
    output = (resid + down_proj).astype(jnp.bfloat16)
    positions = seq_rank * block_len + lax.iota(jnp.int32, block_len)
    live = (positions[None, :] < lengths[:, None]).astype(jnp.bfloat16)
    result_gradient = grad_out * live[:, :, None]
    grad_y_float = result_gradient.astype(jnp.float32)
    g_down_shift = jnp.sum(grad_y_float, axis=(0, 1))
    down_gradient = jnp.einsum(
        "hki,hku->iu", hidden_state, result_gradient, preferred_element_type=jnp.float32
    )
    hidden_gradient = jnp.einsum(
        "gvu,ju->gvj", result_gradient, down_matrix, preferred_element_type=jnp.float32
    )
    deriv = normal_cdf + pre_act * jnp.exp(-0.5 * pre_act * pre_act) * (
        1.0 / math.sqrt(2.0 * math.pi)
    )
    preactivation_gradient = (hidden_gradient * deriv).astype(jnp.bfloat16)
    g_up_shift = jnp.sum(preactivation_gradient.astype(jnp.float32), axis=(0, 1))
    up_gradient = jnp.einsum(
        "oiz,oix->zx", second_normalized, preactivation_gradient, preferred_element_type=jnp.float32
    )
    second_norm_gradient = jnp.einsum(
        "rau,ku->rak", preactivation_gradient, up_matrix, preferred_element_type=jnp.float32
    )
    g_gain_two = jnp.sum(second_norm_gradient * x_hat_two, axis=(0, 1))
    g_shift_two = jnp.sum(second_norm_gradient, axis=(0, 1))
    g_resid = grad_y_float + norm_back(second_norm_gradient * gain_two, x_hat_two, inv_std_two)
    attention_gradient = g_resid.astype(jnp.bfloat16)
    output_gradient = jnp.einsum(
        "zau,zam->um", attention_sequence, attention_gradient, preferred_element_type=jnp.float32
    )
    g_attn_seq = jnp.einsum(
        "urz,jz->urj", attention_gradient, output_matrix, preferred_element_type=jnp.float32
    ).astype(jnp.bfloat16)
    g_attn_heads = lax.all_to_all(
        g_attn_seq, "seq", split_axis=2, concat_axis=1, tiled=True
    ).reshape(slots, full_len, group, head_dim)

    def backward_block(carry, block_index):
        g_keys, g_vals, g_ext = carry
        first_row = block_index * q_block
        scores, qu_part, qv_part, rel_win, window_start = scores_block(first_row)
        probs = jnp.exp(scores - block_lse[block_index][..., None])
        d_out = lax.dynamic_slice_in_dim(g_attn_heads, first_row, q_block, 1)
        g_vals = g_vals + jnp.einsum(
            "shqk,sqhe->skhe", probs.astype(jnp.bfloat16), d_out, preferred_element_type=jnp.float32
        )
        g_probs = jnp.einsum("sqhe,skhe->shqk", d_out, values, preferred_element_type=jnp.float32)
        inner = jnp.sum(probs * g_probs, axis=-1, keepdims=True)
        g_scores = (probs * (g_probs - inner)).astype(jnp.bfloat16)
        g_qu = (
            jnp.einsum("shqk,skhe->sqhe", g_scores, keys, preferred_element_type=jnp.float32)
            * score_scale
        )
        g_keys = (
            g_keys
            + jnp.einsum("shqk,sqhe->skhe", g_scores, qu_part, preferred_element_type=jnp.float32)
            * score_scale
        )
        g_wide = unskew_rows(g_scores)
        g_qv = (
            jnp.einsum("shqt,the->sqhe", g_wide, rel_win, preferred_element_type=jnp.float32)
            * score_scale
        )
        g_win = (
            jnp.einsum("shqt,sqhe->sthe", g_wide, qv_part, preferred_element_type=jnp.float32)
            * score_scale
        )
        g_old = lax.dynamic_slice_in_dim(g_ext, window_start, win_len, 1)
        g_ext = lax.dynamic_update_slice_in_dim(g_ext, g_old + g_win, window_start, 1)
        return ((g_keys, g_vals, g_ext), (g_qu, g_qv))

    zero_heads = jnp.zeros((slots, full_len, group, head_dim), jnp.float32)
    zero_ext = jnp.zeros((slots, 2 * full_len, group, head_dim), jnp.float32)
    (g_keys, g_vals, g_ext), (g_qu_blocks, g_qv_blocks) = lax.scan(
        backward_block, (zero_heads, zero_heads, zero_ext), jnp.arange(num_blocks, dtype=jnp.int32)
    )
    g_qu = jnp.moveaxis(g_qu_blocks, 0, 1).reshape(slots, full_len, group, head_dim)
    g_qv = jnp.moveaxis(g_qv_blocks, 0, 1).reshape(slots, full_len, group, head_dim)
    g_queries = g_qu + g_qv
    g_bias_u_heads = jnp.sum(g_qu, axis=(0, 1))
    g_bias_v_heads = jnp.sum(g_qv, axis=(0, 1))
    g_qkv_heads = (
        jnp.stack([g_queries, g_keys, g_vals], axis=3)
        .astype(jnp.bfloat16)
        .reshape(slots, full_len, group * 3 * head_dim)
    )
    query_key_value_gradient = lax.all_to_all(
        g_qkv_heads, "seq", split_axis=1, concat_axis=2, tiled=True
    )
    g_rel_low = g_ext[:, :full_len].astype(jnp.bfloat16)
    g_rel_heads = jnp.einsum(
        "td,sthe->dhe", table_rev, g_rel_low, preferred_element_type=jnp.float32
    ).reshape(width, group * head_dim)
    g_rel_weight = lax.dynamic_update_slice_in_dim(
        jnp.zeros((width, width), jnp.float32), g_rel_heads, head_start * head_dim, 1
    )
    g_bias_u = lax.dynamic_update_slice_in_dim(
        jnp.zeros((H, head_dim), jnp.float32), g_bias_u_heads, head_start, 0
    ).reshape(width)
    g_bias_v = lax.dynamic_update_slice_in_dim(
        jnp.zeros((H, head_dim), jnp.float32), g_bias_v_heads, head_start, 0
    ).reshape(width)
    query_key_value_weight_gradient = jnp.einsum(
        "zau,zam->um",
        first_normalized,
        query_key_value_gradient,
        preferred_element_type=jnp.float32,
    )
    first_norm_gradient = jnp.einsum(
        "urz,jz->urj",
        query_key_value_gradient,
        query_key_value_matrix,
        preferred_element_type=jnp.float32,
    )
    g_gain_one = jnp.sum(first_norm_gradient * x_hat_one, axis=(0, 1))
    g_shift_one = jnp.sum(first_norm_gradient, axis=(0, 1))
    g_input = g_resid + norm_back(first_norm_gradient * gain_one, x_hat_one, inv_std_one)
    partial_shards = (
        lax.psum_scatter(g_gain_one, "fsdp", scatter_dimension=0, tiled=True),
        lax.psum_scatter(g_shift_one, "fsdp", scatter_dimension=0, tiled=True),
        lax.psum_scatter(query_key_value_weight_gradient, "fsdp", scatter_dimension=0, tiled=True),
        lax.psum_scatter(g_rel_weight, "fsdp", scatter_dimension=0, tiled=True),
        lax.psum_scatter(g_bias_u, "fsdp", scatter_dimension=0, tiled=True),
        lax.psum_scatter(g_bias_v, "fsdp", scatter_dimension=0, tiled=True),
        lax.psum_scatter(output_gradient, "fsdp", scatter_dimension=0, tiled=True),
        lax.psum_scatter(g_gain_two, "fsdp", scatter_dimension=0, tiled=True),
        lax.psum_scatter(g_shift_two, "fsdp", scatter_dimension=0, tiled=True),
        lax.psum_scatter(up_gradient, "fsdp", scatter_dimension=0, tiled=True),
        lax.psum_scatter(g_up_shift, "fsdp", scatter_dimension=0, tiled=True),
        lax.psum_scatter(down_gradient, "fsdp", scatter_dimension=0, tiled=True),
        lax.psum_scatter(g_down_shift, "fsdp", scatter_dimension=0, tiled=True),
    )
    shards = lax.psum(
        (
            partial_shards[0],
            partial_shards[1],
            partial_shards[2],
            partial_shards[3],
            partial_shards[4],
            partial_shards[5],
            partial_shards[6],
            partial_shards[7],
            partial_shards[8],
            partial_shards[9],
            partial_shards[10],
            partial_shards[11],
            partial_shards[12],
        ),
        "seq",
    )
    return (
        output,
        g_input,
        shards[0],
        shards[1],
        shards[2],
        shards[3],
        shards[4],
        shards[5],
        shards[6],
        shards[7],
        shards[8],
        shards[9],
        shards[10],
        shards[11],
        shards[12],
    )


def solution(mesh):
    placed = (
        P("fsdp", "seq", None),
        P("fsdp"),
        P("fsdp"),
        P("fsdp"),
        P("fsdp", None),
        P("fsdp", None),
        P("fsdp"),
        P("fsdp"),
        P("fsdp", None),
        P("fsdp"),
        P("fsdp"),
        P("fsdp", None),
        P("fsdp"),
        P("fsdp", None),
        P("fsdp"),
        P("fsdp", "seq", None),
    )
    return jax.shard_map(
        per_device,
        mesh=mesh,
        in_specs=placed,
        out_specs=(
            P("fsdp", "seq", None),
            P("fsdp", "seq", None),
            P("fsdp"),
            P("fsdp"),
            P("fsdp", None),
            P("fsdp", None),
            P("fsdp"),
            P("fsdp"),
            P("fsdp", None),
            P("fsdp"),
            P("fsdp"),
            P("fsdp", None),
            P("fsdp"),
            P("fsdp", None),
            P("fsdp"),
        ),
        check_vma=False,
    )
```

profile of v0, /device:TPU:0, one launch (start us, length us, event | category | flops | bytes accessed | tf_op | source)
XLA Modules:
  0.0 1018.0 jit_solution(2045283806885661960)
XLA Ops:
  16.6 16.1 %all-reduce.21 = (bf16[512]{0:T(512)(128)(2,1)S(1)}, bf16[512]{0:T(512)(128)(2,1)S(1)}, bf16[512]{0:T(512)(128)(2,1)S(1)}, bf16[512]{0:T(512)(128)(2,1)S(1)}, bf...) all-reduce(bf16[512]{0:T(512)(128)(2,1)S(1)} %dynamic-update-slice., ...), channel_id=1, replica_groups=mesh['fsdp'=8,'seq'=4] {'fsdp'}, use_global_device_ids=true, to_apply=%add.5 | all-reduce | flops 3584 | bytes 14336
  54.7 12.6 %rev.3 = bf16[1024,512]{1,0:T(8,128)(2,1)S(1)} reverse(bf16[1024,512]{1,0:T(8,128)(2,1)} %pad_maximum_fusion.1), dimensions={0} | reverse | bytes 2097152 | tf_op jit(solution)/shard_map/rev | solution.py:141
  67.3 9.8 all_gather.43
  77.7 8.4 all-to-all-done
  94.9 201.7 %while.38 = (s32[]{:T(128)}, bf16[2,2,512,2,64]{2,4,3,1,0:T(8,128)(2,1)}, f32[2,2,2,512]{3,2,1,0:T(2,128)S(1)}, s32[2]{0:T(128)S(1)}, s32[2]{0:T(128)S(1)}, /*in...) while((s32[]{:T(128)}, ...), condition=%wide.region_5.6_spmd.clone.clone, body=%wide.region_2.5_spmd.clone.clone.sunk | while | flops 960102912 | bytes 152216352 | solution.py:176
  109.8 6.4 convolution_bitcast_fusion.8
  116.1 12.6 %copy.145 = f32[2,2,512,1536]{3,2,1,0:T(8,128)} copy(f32[2,2,512,1536]{2,3,0,1:T(8,128)} %convolution_bitcast_fusion.8) | data formatting | bytes 25165824 | tf_op jit(solution)/shard_map/while/body/eval_jaxpr/sqhe,the->shqt/transpose | solution.py:155
  128.7 21.6 %reshape.454 = f32[2,2,786432]{2,1,0:T(2,128)} reshape(f32[2,2,512,1536]{3,2,1,0:T(8,128)} %copy.145) | data formatting | bytes 25165824 | tf_op jit(solution)/shard_map/while/body/eval_jaxpr/reshape | solution.py:42
  150.3 16.2 %slice.83 = f32[2,2,785920]{2,1,0:T(2,128)} slice(f32[2,2,786432]{2,1,0:T(2,128)} %reshape.454), slice={[0:2], [0:2], [511:786431]} | slice | bytes 25149440 | tf_op jit(solution)/shard_map/while/body/eval_jaxpr/slice | solution.py:43
  166.5 25.8 %reshape.455 = f32[2,2,512,1535]{3,2,1,0:T(8,128)} reshape(f32[2,2,785920]{2,1,0:T(2,128)} %slice.83) | data formatting | bytes 25149440 | tf_op jit(solution)/shard_map/while/body/eval_jaxpr/reshape | solution.py:44
  203.7 6.4 convolution_bitcast_fusion.8
  210.0 12.6 %copy.145 = f32[2,2,512,1536]{3,2,1,0:T(8,128)} copy(f32[2,2,512,1536]{2,3,0,1:T(8,128)} %convolution_bitcast_fusion.8) | data formatting | bytes 25165824 | tf_op jit(solution)/shard_map/while/body/eval_jaxpr/sqhe,the->shqt/transpose | solution.py:155
  222.6 21.6 %reshape.454 = f32[2,2,786432]{2,1,0:T(2,128)} reshape(f32[2,2,512,1536]{3,2,1,0:T(8,128)} %copy.145) | data formatting | bytes 25165824 | tf_op jit(solution)/shard_map/while/body/eval_jaxpr/reshape | solution.py:42
  244.2 16.2 %slice.83 = f32[2,2,785920]{2,1,0:T(2,128)} slice(f32[2,2,786432]{2,1,0:T(2,128)} %reshape.454), slice={[0:2], [0:2], [511:786431]} | slice | bytes 25149440 | tf_op jit(solution)/shard_map/while/body/eval_jaxpr/slice | solution.py:43
  260.4 25.8 %reshape.455 = f32[2,2,512,1535]{3,2,1,0:T(8,128)} reshape(f32[2,2,785920]{2,1,0:T(2,128)} %slice.83) | data formatting | bytes 25149440 | tf_op jit(solution)/shard_map/while/body/eval_jaxpr/reshape | solution.py:44
  308.7 9.0 all-gather
  317.8 9.9 all_gather.45
  332.0 6.2 multiply_convert_fusion.1
  338.3 5.6 convert_reduce_fusion
  355.2 13.4 %all-to-all-done.2 = bf16[2,256,512]{1,0,2:T(2,128)(2,1)S(1)} async-done(((bf16[2,256,512]{1,0,2:T(2,128)(2,1)}), bf16[2,256,512]{1,0,2:T(2,128)(2,1)S(1)}, u32[]{:S(2)}, u32[]{:S(2)}) %all-to-all-start.2) | async-done | bytes 524320 | tf_op jit(solution)/shard_map/all_to_all | solution.py:228
  370.4 357.3 %while.39 = (s32[]{:T(128)}, f32[2,1024,2,64]{1,3,2,0:T(8,128)}, f32[2,1024,2,64]{1,3,2,0:T(8,128)}, f32[2,2048,2,64]{1,3,2,0:T(8,128)S(1)}, f32[2,2,512,2,64]{2...) while((s32[]{:T(128)}, f32[2,1024,2,64]{1,3,2,0:T(8,128)}, ...), condition=%wide.region_12.13_spmd.clone.clone, body=%wide.region_10.12_spmd.clone.clone.sunk | while | flops 2575041024 | bytes 391906432 | solution.py:268
  394.1 7.4 convolution_bitcast_fusion.9
  401.5 12.6 %copy.149 = f32[2,2,512,1536]{3,2,1,0:T(8,128)} copy(f32[2,2,512,1536]{2,3,0,1:T(8,128)} %convolution_bitcast_fusion.9) | data formatting | bytes 25165824 | tf_op jit(solution)/shard_map/while/body/eval_jaxpr/sqhe,the->shqt/transpose | solution.py:155
  414.1 21.6 %reshape.456 = f32[2,2,786432]{2,1,0:T(2,128)} reshape(f32[2,2,512,1536]{3,2,1,0:T(8,128)} %copy.149) | data formatting | bytes 25165824 | tf_op jit(solution)/shard_map/while/body/eval_jaxpr/reshape | solution.py:42
  435.7 16.2 %slice.84 = f32[2,2,785920]{2,1,0:T(2,128)} slice(f32[2,2,786432]{2,1,0:T(2,128)} %reshape.456), slice={[0:2], [0:2], [511:786431]} | slice | bytes 25149440 | tf_op jit(solution)/shard_map/while/body/eval_jaxpr/slice | solution.py:43
  451.9 25.8 %reshape.457 = f32[2,2,512,1535]{3,2,1,0:T(8,128)} reshape(f32[2,2,785920]{2,1,0:T(2,128)} %slice.84) | data formatting | bytes 25149440 | tf_op jit(solution)/shard_map/while/body/eval_jaxpr/reshape | solution.py:44
  477.7 5.6 fusion.191
  486.2 7.8 multiply_reduce_fusion.7
  503.4 14.0 %reshape.458 = bf16[2,2,785920]{2,1,0:T(2,128)(2,1)} reshape(bf16[2,2,512,1535]{3,2,1,0:T(8,128)(2,1)} %pad.31) | data formatting | bytes 12574720 | tf_op jit(solution)/shard_map/while/body/eval_jaxpr/reshape | solution.py:52
  517.4 10.7 %pad.32 = bf16[2,2,786432]{2,1,0:T(2,128)(2,1)} pad(bf16[2,2,785920]{2,1,0:T(2,128)(2,1)} %reshape.458, bf16[]{:T(256)} %constant.153.clone.1..sunk), padding=0_0x0_0x511_1 | pad | bytes 12578818 | tf_op jit(solution)/shard_map/while/body/eval_jaxpr/jit(_pad)/pad | solution.py:53
  528.2 9.6 reshape.459
  557.6 7.4 convolution_bitcast_fusion.9
  565.1 12.6 %copy.149 = f32[2,2,512,1536]{3,2,1,0:T(8,128)} copy(f32[2,2,512,1536]{2,3,0,1:T(8,128)} %convolution_bitcast_fusion.9) | data formatting | bytes 25165824 | tf_op jit(solution)/shard_map/while/body/eval_jaxpr/sqhe,the->shqt/transpose | solution.py:155
  577.7 21.6 %reshape.456 = f32[2,2,786432]{2,1,0:T(2,128)} reshape(f32[2,2,512,1536]{3,2,1,0:T(8,128)} %copy.149) | data formatting | bytes 25165824 | tf_op jit(solution)/shard_map/while/body/eval_jaxpr/reshape | solution.py:42
  599.3 16.2 %slice.84 = f32[2,2,785920]{2,1,0:T(2,128)} slice(f32[2,2,786432]{2,1,0:T(2,128)} %reshape.456), slice={[0:2], [0:2], [511:786431]} | slice | bytes 25149440 | tf_op jit(solution)/shard_map/while/body/eval_jaxpr/slice | solution.py:43
  615.5 25.8 %reshape.457 = f32[2,2,512,1535]{3,2,1,0:T(8,128)} reshape(f32[2,2,785920]{2,1,0:T(2,128)} %slice.84) | data formatting | bytes 25149440 | tf_op jit(solution)/shard_map/while/body/eval_jaxpr/reshape | solution.py:44
  641.3 5.6 fusion.191
  649.8 7.8 multiply_reduce_fusion.7
  667.0 14.0 %reshape.458 = bf16[2,2,785920]{2,1,0:T(2,128)(2,1)} reshape(bf16[2,2,512,1535]{3,2,1,0:T(8,128)(2,1)} %pad.31) | data formatting | bytes 12574720 | tf_op jit(solution)/shard_map/while/body/eval_jaxpr/reshape | solution.py:52
  681.0 10.7 %pad.32 = bf16[2,2,786432]{2,1,0:T(2,128)(2,1)} pad(bf16[2,2,785920]{2,1,0:T(2,128)(2,1)} %reshape.458, bf16[]{:T(256)} %constant.153.clone.1..sunk), padding=0_0x0_0x511_1 | pad | bytes 12578818 | tf_op jit(solution)/shard_map/while/body/eval_jaxpr/jit(_pad)/pad | solution.py:53
  691.7 9.6 reshape.459
  748.0 39.3 %all_to_all.66 = bf16[2,1024,384]{2,0,1:T(2,128)(2,1)S(1)} all-to-all(bf16[2,1024,384]{2,0,1:T(2,128)(2,1)S(1)} %copy.81), channel_id=1, replica_groups=mesh['fsdp'=8,'seq'=4] {'seq'}, dimensions={1} | all-to-all | bytes 3145728 | tf_op jit(solution)/shard_map/all_to_all | solution.py:281
  792.0 27.6 %reduce-scatter.12.cloned.1.call-done = f32[64,2048]{1,0:T(8,128)} async-done(((f32[512,2048]{1,0:T(8,128)}), f32[64,2048]{1,0:T(8,128)}) %reduce-scatter.12.cloned.1.call-update) | async-done | bytes 524304 | tf_op jit(solution)/shard_map/reduce_scatter | solution.py:322
  819.6 55.1 %reduce-scatter.14.cloned.1.call-done = f32[256,512]{1,0:T(8,128)} async-done(((f32[2048,512]{1,0:T(8,128)}), f32[256,512]{1,0:T(8,128)}) %reduce-scatter.14.cloned.1.call-update) | async-done | bytes 524304 | tf_op jit(solution)/shard_map/reduce_scatter | solution.py:324
  874.7 49.6 %reduce-scatter.6.cloned.1.call-done = f32[64,1536]{1,0:T(8,128)} async-done(((f32[512,1536]{1,0:T(8,128)}), f32[64,1536]{1,0:T(8,128)}) %reduce-scatter.6.cloned.1.call-update) | async-done | bytes 393232 | tf_op jit(solution)/shard_map/reduce_scatter | solution.py:315
  932.5 24.7 %all-reduce.18 = (f32[512]{0:T(512)S(1)}, f32[512]{0:T(512)S(1)}, f32[512]{0:T(512)S(1)}, f32[512]{0:T(512)S(1)}, f32[512]{0:T(512)S(1)}, /*index=5*/f32[512]{0:T(512)S(1)}, f32[2048]{0:T(1024)S(1)}, f32[512]{0:T(512)S(1)}) all-reduce(f32[512]{0:T(512)S(1)} %get-tuple-element.579, ...), channel_id=2, replica_groups=mesh['fsdp'=8,'seq'=4] {'fsdp'}, use_global_device_ids=true, to_apply=%region_16.17.clone | all-reduce | flops 5632 | bytes 45056
  957.8 12.4 %all-reduce.19 = (f32[64]{0:T(128)}, f32[64]{0:T(128)}, f32[64]{0:T(128)}, f32[64]{0:T(128)}, f32[64]{0:T(128)}, /*index=5*/f32[64]{0:T(128)}, f32[256]{0:T(256)}, f32[64]{0:T(128)}) all-reduce(f32[64]{0:T(128)S(1)} %dynamic-slice.8, f32[64]{0:T(128)S(1)} %dynamic-slice.10, ...), channel_id=1, replica_groups=mesh['fsdp'=8,'seq'=4] {'seq'}, use_global_device_ids=true, to_apply=%region_17.18 | all-reduce | flops 704 | bytes 5632 | tf_op jit(solution)/shard_map/psum | solution.py:327
  972.8 29.8 %all-reduce.24.cloned.1.call-done = (f32[64,1536]{1,0:T(8,128)}, f32[64,512]{1,0:T(8,128)}, f32[64,512]{1,0:T(8,128)}, f32[64,2048]{1,0:T(8,128)}, f32[256,512]{1,0:T(8,128)}) async-done(((f32[64,1536]{1,0:T(8,128)}, f32[64,512]{1,0:T(8,128)}, f32[64,512]{1,0:T(8,128)}, f32[64,2048]{1,0:T(8,128)}, f32[256,512]{1,0:T(8,128)}), (f32[64,1536]{1,0:T(8,128)}, f32[64,512]{1,0:T(8,128)}, f32[64,512]{1,0:T(8,128)}, ...) | async-done | bytes 1703952 | tf_op jit(solution)/shard_map/psum | solution.py:327
  (327 shorter events, 193.2 us)
Async XLA Ops:
  7.2 31.3 %all-gather.5.cloned.1.call-start = ((), (), s32[]{:S(2)}) async-start(), calls=%async_computation.9 | async-start | bytes 1769472 | tf_op jit(solution)/shard_map/all_gather | solution.py:78
  7.9 324.1 %all-gather.7.cloned.1.call-start = ((), (), s32[]{:S(2)}) async-start(), calls=%async_computation.10 | async-start | bytes 2359296 | tf_op jit(solution)/shard_map/all_gather | solution.py:85
  32.7 11.3 %copy-start.44 = (f32[512]{0:T(512)}, f32[512]{0:T(512)S(1)}, u32[]{:S(2)}) copy-start(f32[512]{0:T(512)S(1)} %convert_element_type.120) | copy-start | bytes 6148
  32.7 11.3 %copy-start.51 = (f32[512]{0:T(512)}, f32[512]{0:T(512)S(1)}, u32[]{:S(2)}) copy-start(f32[512]{0:T(512)S(1)} %convert_element_type.121) | copy-start | bytes 6148
  33.9 10.0 copy-start.41
  35.3 8.7 copy-start.46
  44.0 23.4 %copy-start.32 = (bf16[64,512]{1,0:T(8,128)(2,1)S(1)}, bf16[64,512]{1,0:T(8,128)(2,1)}, u32[]{:S(2)}) copy-start(bf16[64,512]{1,0:T(8,128)(2,1)} %param.25) | copy-start | bytes 196612
  44.0 42.1 %all-to-all-start = ((bf16[2,256,1536]{1,0,2:T(2,128)(2,1)}), bf16[2,256,1536]{1,0,2:T(2,128)(2,1)S(1)}, u32[]{:S(2)}, u32[]{:S(2)}) async-start(bf16[2,256,1536]{1,0,2:T(2,128)(2,1)} %copy.67), calls=%async_computation | async-start | bytes 3145728 | tf_op jit(solution)/shard_map/all_to_all | solution.py:127
  48.7 289.5 %all-gather.9.cloned.1.call-start = ((), (), s32[]{:S(2)}) async-start(), calls=%async_computation.11 | async-start | bytes 2359296 | tf_op jit(solution)/shard_map/all_gather | solution.py:87
  67.3 21.1 %copy-start.17 = (bf16[1024,512]{1,0:T(8,128)(2,1)}, bf16[1024,512]{1,0:T(8,128)(2,1)S(1)}, u32[]{:S(2)}) copy-start(bf16[1024,512]{1,0:T(8,128)(2,1)S(1)} %rev.3) | copy-start | bytes 3145732
  88.5 6.5 copy-start.34
  296.6 34.1 %copy-start.4 = (bf16[2,1024,2,64]{1,3,2,0:T(8,128)(2,1)}, bf16[2,1024,2,64]{1,3,2,0:T(8,128)(2,1)S(1)}, u32[]{:S(2)}) copy-start(bf16[2,1024,2,64]{1,3,2,0:T(8,128)(2,1)S(1)} %get-tuple-element.998) | copy-start | bytes 1572868
  296.6 34.0 %copy-start.6 = (bf16[2048,2,64]{0,2,1:T(8,128)(2,1)}, bf16[2048,2,64]{0,2,1:T(8,128)(2,1)S(1)}, u32[]{:S(2)}) copy-start(bf16[2048,2,64]{0,2,1:T(8,128)(2,1)S(1)} %get-tuple-element.999) | copy-start | bytes 1572868
  296.6 34.0 %copy-start.8 = (bf16[2,1024,2,64]{1,3,0,2:T(8,128)(2,1)}, bf16[2,1024,2,64]{1,3,0,2:T(8,128)(2,1)S(1)}, u32[]{:S(2)}) copy-start(bf16[2,1024,2,64]{1,3,0,2:T(8,128)(2,1)S(1)} %get-tuple-element.1000) | copy-start | bytes 1572868
  296.7 34.0 %copy-start.11 = (bf16[2,1024,2,64]{1,3,2,0:T(8,128)(2,1)}, bf16[2,1024,2,64]{1,3,2,0:T(8,128)(2,1)S(1)}, u32[]{:S(2)}) copy-start(bf16[2,1024,2,64]{1,3,2,0:T(8,128)(2,1)S(1)} %get-tuple-element.1001) | copy-start | bytes 1572868
  296.7 12.0 %copy-start.57 = (bf16[512]{0:T(512)(128)(2,1)S(1)}, bf16[512]{0:T(512)(128)(2,1)}, u32[]{:S(2)}) copy-start(bf16[512]{0:T(512)(128)(2,1)} %get-tuple-element.661) | copy-start | bytes 3076
  296.7 12.0 %copy-start.56 = (bf16[512]{0:T(512)(128)(2,1)S(1)}, bf16[512]{0:T(512)(128)(2,1)}, u32[]{:S(2)}) copy-start(bf16[512]{0:T(512)(128)(2,1)} %get-tuple-element.660) | copy-start | bytes 3076
  296.7 12.0 %copy-start.59 = (bf16[256]{0:T(256)(128)(2,1)S(1)}, bf16[256]{0:T(256)(128)(2,1)}, u32[]{:S(2)}) copy-start(bf16[256]{0:T(256)(128)(2,1)} %param.32) | copy-start | bytes 1540
  296.7 21.1 %copy-start.33 = (bf16[64,512]{1,0:T(8,128)(2,1)S(1)}, bf16[64,512]{1,0:T(8,128)(2,1)}, u32[]{:S(2)}) copy-start(bf16[64,512]{1,0:T(8,128)(2,1)} %param.28) | copy-start | bytes 196612
  296.7 32.2 %copy-start.18 = (bf16[2,256,512]{2,1,0:T(8,128)(2,1)S(1)}, bf16[2,256,512]{2,1,0:T(8,128)(2,1)}, u32[]{:S(2)}) copy-start(bf16[2,256,512]{2,1,0:T(8,128)(2,1)} %param.20) | copy-start | bytes 1572868
  304.5 23.3 %all-to-all-start.1 = ((bf16[2,1024,128]{2,0,1:T(2,128)(2,1)}), bf16[2,1024,128]{2,0,1:T(2,128)(2,1)}, u32[]{:S(2)}, u32[]{:S(2)}) async-start(bf16[2,1024,128]{2,0,1:T(2,128)(2,1)} %reshape.439), calls=%async_computation.1 | async-start | bytes 1048576 | tf_op jit(solution)/shard_map/all_to_all | solution.py:178
  308.7 37.3 %copy-start.30 = (f32[512]{0:T(512)}, f32[512]{0:T(512)S(1)}, u32[]{:S(2)}) copy-start(f32[512]{0:T(512)S(1)} %convert_element_type.129) | copy-start | bytes 6148
  308.7 29.5 %copy-start.37 = (f32[512]{0:T(512)}, f32[512]{0:T(512)S(1)}, u32[]{:S(2)}) copy-start(f32[512]{0:T(512)S(1)} %convert_element_type.130) | copy-start | bytes 6148
  327.8 18.2 %copy-start.49 = (bf16[2,256]{1,0:T(2,128)(2,1)}, bf16[2,256]{1,0:T(2,128)(2,1)S(1)}, u32[]{:S(2)}) copy-start(bf16[2,256]{1,0:T(2,128)(2,1)S(1)} %compare_convert_fusion) | copy-start | bytes 3076
  330.7 15.2 %copy-start.35 = (f32[2,256]{1,0:T(2,128)}, f32[2,256]{1,0:T(2,128)S(1)}, u32[]{:S(2)}) copy-start(f32[2,256]{1,0:T(2,128)S(1)} %broadcast_multiply_fusion.4) | copy-start | bytes 6148
  332.0 14.0 %copy-start.39 = (f32[2,256]{1,0:T(2,128)}, f32[2,256]{1,0:T(2,128)S(1)}, u32[]{:S(2)}) copy-start(f32[2,256]{1,0:T(2,128)S(1)} %add_rsqrt_fusion) | copy-start | bytes 6148
  332.0 6.2 copy-start.28
  345.9 7.7 copy-start.21
  347.0 22.0 %copy-start.12 = (f32[2,256,512]{2,1,0:T(8,128)}, f32[2,256,512]{2,1,0:T(8,128)S(1)}, u32[]{:S(2)}) copy-start(f32[2,256,512]{2,1,0:T(8,128)S(1)} %get-tuple-element.675) | copy-start | bytes 3145732
  348.6 20.0 %all-to-all-start.2 = ((bf16[2,256,512]{1,0,2:T(2,128)(2,1)}), bf16[2,256,512]{1,0,2:T(2,128)(2,1)S(1)}, u32[]{:S(2)}, u32[]{:S(2)}) async-start(bf16[2,256,512]{1,0,2:T(2,128)(2,1)} %copy.74), calls=%async_computation.2 | async-start | bytes 1048576 | tf_op jit(solution)/shard_map/all_to_all | solution.py:228
  353.6 16.8 %copy-start.5 = (bf16[2,1024,2,64]{1,3,2,0:T(8,128)(2,1)S(1)}, bf16[2,1024,2,64]{1,3,2,0:T(8,128)(2,1)}, u32[]{:S(2)}) copy-start(bf16[2,1024,2,64]{1,3,2,0:T(8,128)(2,1)} %copy-done.4) | copy-start | bytes 1572868
  353.6 438.4 %reduce-scatter.10.cloned.1.call-start = ((), (), s32[]{:S(2)}) async-start(), calls=%async_computation.14 | async-start | bytes 1179648 | tf_op jit(solution)/shard_map/reduce_scatter | solution.py:319
  355.1 436.9 %reduce-scatter.8.cloned.1.call-start = ((), (), s32[]{:S(2)}) async-start(), calls=%async_computation.13 | async-start | bytes 1179648 | tf_op jit(solution)/shard_map/reduce_scatter | solution.py:316
  486.2 11.1 %slice-start = ((s8[8388608]{0:T(1024)(128)(4,1)}), s8[4194304]{0:T(1024)(128)(4,1)S(1)}, s32[]{:S(2)}) async-start(s8[8388608]{0:T(1024)(128)(4,1)} %bitcast.231), calls=%async_computation.18 | async-start | bytes 8388608 | tf_op jit(solution)/shard_map/while
  486.2 11.1 %slice-start.1 = ((s8[8388608]{0:T(1024)(128)(4,1)}), s8[4194304]{0:T(1024)(128)(4,1)S(1)}, s32[]{:S(2)}) async-start(s8[8388608]{0:T(1024)(128)(4,1)} %bitcast.231), calls=%async_computation.19 | async-start | bytes 8388608 | tf_op jit(solution)/shard_map/while
  649.8 11.1 %slice-start = ((s8[8388608]{0:T(1024)(128)(4,1)}), s8[4194304]{0:T(1024)(128)(4,1)S(1)}, s32[]{:S(2)}) async-start(s8[8388608]{0:T(1024)(128)(4,1)} %bitcast.231), calls=%async_computation.18 | async-start | bytes 8388608 | tf_op jit(solution)/shard_map/while
  649.8 11.1 %slice-start.1 = ((s8[8388608]{0:T(1024)(128)(4,1)}), s8[4194304]{0:T(1024)(128)(4,1)S(1)}, s32[]{:S(2)}) async-start(s8[8388608]{0:T(1024)(128)(4,1)} %bitcast.231), calls=%async_computation.19 | async-start | bytes 8388608 | tf_op jit(solution)/shard_map/while
  730.8 88.8 %reduce-scatter.12.cloned.1.call-start = ((), (), s32[]{:S(2)}) async-start(), calls=%async_computation.15 | async-start | bytes 4718592 | tf_op jit(solution)/shard_map/reduce_scatter | solution.py:322
  736.2 138.5 %reduce-scatter.14.cloned.1.call-start = ((), (), s32[]{:S(2)}) async-start(), calls=%async_computation.16 | async-start | bytes 4718592 | tf_op jit(solution)/shard_map/reduce_scatter | solution.py:324
  741.4 182.9 %reduce-scatter.6.cloned.1.call-start = ((), (), s32[]{:S(2)}) async-start(), calls=%async_computation.12 | async-start | bytes 3538944 | tf_op jit(solution)/shard_map/reduce_scatter | solution.py:315
  747.9 39.7 %copy-start.19 = (bf16[2,256,512]{2,1,0:T(8,128)(2,1)S(1)}, bf16[2,256,512]{2,1,0:T(8,128)(2,1)}, u32[]{:S(2)}) copy-start(bf16[2,256,512]{2,1,0:T(8,128)(2,1)} %param.20) | copy-start | bytes 1572868
  747.9 39.7 %copy-start.42 = (f32[2,256]{1,0:T(2,128)S(1)}, f32[2,256]{1,0:T(2,128)}, u32[]{:S(2)}) copy-start(f32[2,256]{1,0:T(2,128)} %copy-done.41) | copy-start | bytes 6148
  747.9 39.7 %copy-start.45 = (f32[512]{0:T(512)S(1)}, f32[512]{0:T(512)}, u32[]{:S(2)}) copy-start(f32[512]{0:T(512)} %copy-done.44) | copy-start | bytes 6148
  747.9 39.7 %copy-start.47 = (f32[2,256]{1,0:T(2,128)S(1)}, f32[2,256]{1,0:T(2,128)}, u32[]{:S(2)}) copy-start(f32[2,256]{1,0:T(2,128)} %copy-done.46) | copy-start | bytes 6148
  747.9 39.7 %copy-start.52 = (f32[512]{0:T(512)S(1)}, f32[512]{0:T(512)}, u32[]{:S(2)}) copy-start(f32[512]{0:T(512)} %copy-done.51) | copy-start | bytes 6148
  790.5 133.9 %copy-start.16 = (f32[2,256,512]{2,1,0:T(8,128)S(1)}, f32[2,256,512]{2,1,0:T(8,128)}, u32[]{:S(2)}) copy-start(f32[2,256,512]{2,1,0:T(8,128)} %copy-done.14) | copy-start | bytes 3145732
  790.5 212.1 %all-reduce.24.cloned.1.call-start = ((), (), s32[]{:S(2)}) async-start(), calls=%async_computation.17 | async-start | bytes 3407872 | tf_op jit(solution)/shard_map/psum | solution.py:327
  928.6 41.5 %copy-start.13 = (f32[2,256,512]{2,1,0:T(8,128)S(1)}, f32[2,256,512]{2,1,0:T(8,128)}, u32[]{:S(2)}) copy-start(f32[2,256,512]{2,1,0:T(8,128)} %copy-done.12) | copy-start | bytes 3145732
  (36 other events, 129.5 us)
Sparse Core Ops, SparseCore 0:
  9.9 28.4 all-gather.4
  40.3 27.8 all-gather.6
  70.2 27.8 all-gather.8
  357.3 36.4 reduce-scatter.9
  730.9 34.1 reduce-scatter.7
  768.2 51.3 reduce-scatter.11
  823.3 51.3 reduce-scatter.13
  878.1 46.2 reduce-scatter.5
  927.3 75.2 all-reduce.23
where the time goes:
time: 1030 us; the launch traced here: 1020 us
  local copies, waits for them, and re-layouts  453 us (44%)
  waiting for transfers between devices  189 us (18%)
  matrix products  147 us (14%)
  blocking collectives  121 us (12%)
  loops' own time  50.3 us (5%)
  other arithmetic  25.1 us (2%)
  between operations  17.1 us (2%)
  starting transfers between devices  14.2 us (1%)
    reshape x4, local copies, waits for them, and re-layouts, skew_rows(): picked.reshape(leading + (row_count, col_count - 1))  103 us
    reshape x4, local copies, waits for them, and re-layouts, skew_rows(): flattened = matrix.reshape(leading + (row_count * col_count,))  86.3 us
    slice x4, local copies, waits for them, and re-layouts, skew_rows(): flattened[..., row_count - 1:row_count - 1 + row_count * (col_count - 1)]  64.9 us
    reduce_scatter x1, waiting for transfers between devices, per_device(): lax.psum_scatter(down_gradient, 'fsdp', scatter_dimension=0, tiled=True)  55.1 us
    transpose x4, local copies, waits for them, and re-layouts, scores_block(): jnp.einsum('sqhe,the->shqt', qv_part, rel_win, preferred_element_type=jnp...  50.5 us
    reduce_scatter x1, waiting for transfers between devices, per_device(): lax.psum_scatter(query_key_value_weight_gradient, 'fsdp', scatter_dimensi...  49.6 us
    unnamed x2, blocking collectives  40.8 us
    all_to_all x1, blocking collectives, per_device(): lax.all_to_all(g_qkv_heads, 'seq', split_axis=1, concat_axis=2, tiled=True)  39.3 us
  transfers between devices with their start and end apart: 12, of which 7 were waited for; matrix products, arithmetic and copies ran while one was open for 58% of the time, Pallas kernels for 0%

commit v1 on v0

--- a/solution.py
+++ b/solution.py
@@ -1,8 +1,11 @@
+import functools
 import math
 
 import jax
 import jax.numpy as jnp
 from jax import lax
+from jax.experimental import pallas as pl
+from jax.experimental.pallas import tpu as pltpu
 from jax.sharding import PartitionSpec as P
 
 H = 8
@@ -11,6 +14,176 @@
 
 NEG_FILL = -1e30
 NORM_EPS = 1e-05
+
+
+bf, f32 = jnp.bfloat16, jnp.float32
+NEG = NEG_FILL
+HD = HEAD_DIM
+NT = (((1,), (1,)), ((), ()))
+NN = (((1,), (0,)), ((), ()))
+
+
+def dot(a, b, dims):
+    return lax.dot_general(a, b, dims, preferred_element_type=f32)
+
+
+def masked_tail(s, keep, block):
+    tail = jnp.where(keep, s[:, s.shape[1] - block :], NEG)
+    if s.shape[1] == block:
+        return tail
+    return jnp.concatenate([s[:, : s.shape[1] - block], tail], axis=1)
+
+
+def scores(qu, qv, keys, rel_rev, keep, block):
+    span = keys.shape[0]
+    rel = dot(qv, rel_rev, NT)
+    rel = pltpu.roll(rel, (span - block + 1) % span, 1, stride=1, stride_axis=0)
+    return masked_tail(dot(qu, keys, NT) + rel, keep, block)
+
+
+def attn_fwd_body(len_ref, q_ref, k_ref, v_ref, r_ref, bu_ref, bv_ref, o_ref, lse_ref, *, block):
+    full = q_ref.shape[0]
+    lane = lax.broadcasted_iota(jnp.int32, (block, 2 * HD), 1)
+    sides = (lane < HD, lane >= HD)
+    length = len_ref[0]
+    col = lax.broadcasted_iota(jnp.int32, (1, full), 1)
+    bias = jnp.where(col < length, 0.0, NEG)
+    tri = lax.broadcasted_iota(jnp.int32, (block, block), 1) <= lax.broadcasted_iota(
+        jnp.int32, (block, block), 0
+    )
+    for first in range(0, full, block):
+        span = first + block
+        q = q_ref[first:span, :].astype(f32)
+        qu = (q + bu_ref[...]).astype(bf).astype(f32) * 0.125
+        qv = (q + bv_ref[...]).astype(bf).astype(f32) * 0.125
+        outs = []
+        for head, side in enumerate(sides):
+            s = scores(
+                jnp.where(side, qu, 0.0).astype(bf),
+                jnp.where(side, qv, 0.0).astype(bf),
+                k_ref[:span, :],
+                r_ref[full - span :, :],
+                tri,
+                block,
+            )
+            s = s + bias[:, :span]
+            top = jnp.max(s, axis=1, keepdims=True)
+            e = jnp.exp(s - top)
+            total = jnp.sum(e, axis=1, keepdims=True)
+            outs.append(dot(e.astype(bf), v_ref[:span, :], NN) / total)
+            lse_ref[head, first:span, :] = top + jnp.log(total)
+        o_ref[first:span, :] = jnp.where(sides[0], outs[0], outs[1]).astype(bf)
+
+
+def attn_fwd(length, qkv, rel_rev, bias_u, bias_v, *, block=256):
+    full, cols = rel_rev.shape
+    pairs = cols // (2 * HD)
+    at = lambda part: pl.BlockSpec((full, 2 * HD), lambda pair, _: (0, part * pairs + pair))
+    row = pl.BlockSpec((1, 2 * HD), lambda pair, _: (0, pair))
+    return pl.pallas_call(
+        functools.partial(attn_fwd_body, block=block),
+        out_shape=(
+            jax.ShapeDtypeStruct((full, cols), bf),
+            jax.ShapeDtypeStruct((2 * pairs, full, 1), f32),
+        ),
+        grid_spec=pltpu.PrefetchScalarGridSpec(
+            num_scalar_prefetch=1,
+            grid=(pairs,),
+            in_specs=[at(0), at(1), at(2), at(0), row, row],
+            out_specs=(at(0), pl.BlockSpec((2, full, 1), lambda pair, _: (pair, 0, 0))),
+        ),
+        cost_estimate=pl.CostEstimate(
+            flops=12 * full * full * cols, bytes_accessed=10 * full * cols, transcendentals=0
+        ),
+        compiler_params=pltpu.CompilerParams(vmem_limit_bytes=60 << 20),
+        name="attn_fwd",
+    )(length, qkv, qkv, qkv, rel_rev, bias_u, bias_v)
+
+
+def attn_bwd_body(len_ref, q_ref, k_ref, v_ref, r_ref, bu_ref, bv_ref, lse_ref, do_ref, *refs, block):
+    dq_ref, dk_ref, dv_ref, dr_ref, gu_ref, gv_ref, dk_t, dv_t, dr_t = refs
+    full = q_ref.shape[0]
+    length = len_ref[0]
+    lane = lax.broadcasted_iota(jnp.int32, (block, 2 * HD), 1)
+    sides = (lane < HD, lane >= HD)
+    rows = lax.broadcasted_iota(jnp.int32, (block, block), 0)
+    cols = lax.broadcasted_iota(jnp.int32, (block, block), 1)
+    tri = cols <= rows
+    flip = jnp.where(rows + cols == block - 1, 1.0, 0.0).astype(bf)
+    row = lax.broadcasted_iota(jnp.int32, (block, 1), 0)
+    for ref in (dk_t, dv_t, dr_t, dq_ref, gu_ref, gv_ref):
+        ref[...] = jnp.zeros_like(ref)
+    for first in range(0, full, block):
+        span = first + block
+
+        @pl.when(first < length)
+        def _():
+            q = q_ref[first:span, :].astype(f32)
+            qu = (q + bu_ref[...]).astype(bf).astype(f32) * 0.125
+            qv = (q + bv_ref[...]).astype(bf).astype(f32) * 0.125
+            do = do_ref[first:span, :].astype(f32)
+            qu_t = jnp.transpose(qu).astype(bf)
+            do_t = jnp.transpose(do).astype(bf)
+            qv_t = jnp.transpose(dot(flip, qv.astype(bf), NN)).astype(bf)
+            dqu, dqv = [], []
+            for head, side in enumerate(sides):
+                at = slice(head * HD, (head + 1) * HD)
+                s = scores(
+                    jnp.where(side, qu, 0.0).astype(bf),
+                    jnp.where(side, qv, 0.0).astype(bf),
+                    k_ref[:span, :],
+                    r_ref[full - span :, :],
+                    tri,
+                    block,
+                )
+                lse = jnp.where(first + row < length, lse_ref[head, first:span, :], -NEG)
+                p = jnp.exp(s - lse)
+                dp = dot(jnp.where(side, do, 0.0).astype(bf), v_ref[:span, :], NT)
+                t = p * dp
+                ds = (t - p * jnp.sum(t, axis=1, keepdims=True)).astype(bf)
+                dv_t[at, :span] += dot(do_t[at], p.astype(bf), NN)
+                both = dot(jnp.concatenate([qu_t[at], flip], axis=0), ds, NN)
+                dk_t[at, :span] += both[:HD]
+                dqu.append(dot(ds, k_ref[:span, :], NN))
+                ds_rev = pltpu.roll(both[HD:], 0, 1, stride=1, stride_axis=0).astype(bf)
+                dr_t[at, full - span :] += dot(qv_t[at], ds_rev, NN)
+                dqv.append(dot(ds_rev, r_ref[full - span :, :], NN))
+            dqu = jnp.where(sides[0], dqu[0], dqu[1]) * 0.125
+            dqv = jnp.where(sides[0], dqv[0], dqv[1]) * 0.125
+            gu_ref[...] += jnp.sum(dqu, axis=0, keepdims=True)
+            gv_ref[...] += jnp.sum(dqv, axis=0, keepdims=True)
+            dq_ref[first:span, :] = (dqu + dot(flip, dqv.astype(bf), NN)).astype(bf)
+
+    dk_ref[...] = jnp.transpose(dk_t[...]).astype(bf)
+    dv_ref[...] = jnp.transpose(dv_t[...]).astype(bf)
+    dr_ref[...] = jnp.transpose(dr_t[...]).astype(bf)
+
+
+def attn_bwd(length, qkv, rel_rev, bias_u, bias_v, lse, d_out, *, pair, block=256):
+    full, cols = rel_rev.shape
+    pairs = cols // (2 * HD)
+    at = lambda part: pl.BlockSpec((full, 2 * HD), lambda i, _: (0, part * pairs + pair))
+    row = pl.BlockSpec((1, 2 * HD), lambda i, _: (0, pair))
+    out = pl.BlockSpec((full, 2 * HD), lambda i, _: (0, 0))
+    out_row = pl.BlockSpec((1, 2 * HD), lambda i, _: (0, 0))
+    return pl.pallas_call(
+        functools.partial(attn_bwd_body, block=block),
+        out_shape=(jax.ShapeDtypeStruct((full, 2 * HD), bf),) * 4
+        + (jax.ShapeDtypeStruct((1, 2 * HD), f32),) * 2,
+        grid_spec=pltpu.PrefetchScalarGridSpec(
+            num_scalar_prefetch=1,
+            grid=(1,),
+            in_specs=[at(0), at(1), at(2), at(0), row, row]
+            + [pl.BlockSpec((2, full, 1), lambda i, _: (pair, 0, 0)), at(0)],
+            out_specs=(out,) * 4 + (out_row, out_row),
+            scratch_shapes=[pltpu.VMEM((2 * HD, full), f32)] * 3,
+        ),
+        cost_estimate=pl.CostEstimate(
+            flops=36 * full * full * HD * 4, bytes_accessed=20 * full * HD * 2, transcendentals=0
+        ),
+        compiler_params=pltpu.CompilerParams(vmem_limit_bytes=60 << 20),
+        name="attn_bwd",
+    )(length, qkv, qkv, qkv, rel_rev, bias_u, bias_v, lse, d_out)
 
 
 def norm_parts(values):
@@ -54,7 +227,7 @@
     return flattened.reshape(leading + (row_count, key_count + row_count))
 
 
-def per_device(
+def head_split_device(
     layer_input,
     lengths,
     ln1_gain,
@@ -361,6 +534,702 @@
     )
 
 
+def swap_core(values):
+    size = lax.axis_size("fsdp")
+    return lax.ppermute(values, "fsdp", [(i, i ^ 1) for i in range(size)])
+
+
+def swap_chip(values, mask):
+    size = lax.axis_size("fsdp")
+    return lax.ppermute(values, "fsdp", [(i, i ^ (2 * mask)) for i in range(size)])
+
+
+def swap_seq(values, mask):
+    size = lax.axis_size("seq")
+    return lax.ppermute(values, "seq", [(i, i ^ mask) for i in range(size)])
+
+
+def slot_pairs(turn):
+    seq, pairs = lax.axis_size("seq"), []
+    for f in range(lax.axis_size("fsdp")):
+        for z in range(seq):
+            to_f, to_z = (f & ~1) | (z & 1), 2 * (f & 1) + (turn ^ (z >> 1))
+            pairs.append((f * seq + z, to_f * seq + to_z))
+    return pairs
+
+
+def to_slots(values, seq_rank):
+    return [
+        lax.ppermute(
+            lax.dynamic_index_in_dim(values, turn ^ (seq_rank >> 1), 0, keepdims=False),
+            ("fsdp", "seq"),
+            slot_pairs(turn),
+        )
+        for turn in (0, 1)
+    ]
+
+
+def together(*values):
+    return lax.optimization_barrier(values)
+
+
+def whole(*shape):
+    return pl.BlockSpec(shape, lambda *_: (0,) * len(shape))
+
+
+def kernel_call(body, name, meta, args, outs, *, grid=(1,), in_specs=None, out_specs=None, scratch=(), flops=0):
+    in_specs = in_specs or [whole(*a.shape) for a in args]
+    out_specs = out_specs or [whole(*shape) for shape, _ in outs]
+    moved = sum(a.size * a.dtype.itemsize for a in args)
+    moved += sum(math.prod(shape) * jnp.dtype(kind).itemsize for shape, kind in outs)
+    return pl.pallas_call(
+        body,
+        out_shape=[jax.ShapeDtypeStruct(shape, kind) for shape, kind in outs],
+        grid_spec=pltpu.PrefetchScalarGridSpec(
+            num_scalar_prefetch=1,
+            grid=grid,
+            in_specs=in_specs,
+            out_specs=out_specs,
+            scratch_shapes=scratch,
+        ),
+        compiler_params=pltpu.CompilerParams(vmem_limit_bytes=60 << 20),
+        cost_estimate=pl.CostEstimate(flops=flops, bytes_accessed=moved, transcendentals=0),
+        name=name,
+    )(meta, *args)
+
+
+TN = (((0,), (0,)), ((), ()))
+CORE, CHIP, RANK, LIVE = range(4)
+
+
+def aligned(index, size):
+    return pl.multiple_of(index * size, size)
+
+
+def pack_body(meta, qkv_ref, rel_ref, up_ref, out_ref, down_ref, *refs):
+    small, (attn_ref, feed_ref, send_ref) = refs[:8], refs[8:]
+    core = meta[CORE]
+    shard = qkv_ref.shape[0]
+    qkv, rel, up, out, down = qkv_ref[...], rel_ref[...], up_ref[...], out_ref[...], down_ref[...]
+    heads, hd = rel.shape[1] // HEAD_DIM // 2, HEAD_DIM
+    unit = up.shape[1] // 8
+    packs, ups = [], []
+    row = jnp.concatenate([ref[i : i + 1] for ref in small for i in range(ref.shape[0])], axis=1)
+    row = jnp.concatenate([row, jnp.zeros((1, 4 * heads * hd - row.shape[1]), row.dtype)], axis=1)
+    rows = jnp.broadcast_to(row, (8, row.shape[1]))
+    for side in (0, 1):
+        parts = [
+            qkv[:, ((2 * j + side) * 3 + t) * hd : ((2 * j + side) * 3 + t + 1) * hd]
+            for t in range(3)
+            for j in range(heads)
+        ]
+        parts += [rel[:, (2 * j + side) * hd : (2 * j + side + 1) * hd] for j in range(heads)]
+        packs.append(jnp.concatenate(parts, axis=1))
+        ups.append(
+            jnp.concatenate([up[:, (2 * j + side) * unit : (2 * j + side + 1) * unit] for j in range(4)], axis=1)
+        )
+    first = core == 0
+    folded = jnp.concatenate([out[: shard // 2], out[shard // 2 :]], axis=1)
+    attn_ref[:shard] = jnp.where(first, packs[0], packs[1])
+    attn_ref[shard:] = rows
+    send_ref[:shard] = jnp.where(first, packs[1], packs[0])
+    send_ref[shard : shard + 8] = rows
+    send_ref[shard + 8 : 2 * shard + 8] = jnp.where(first, ups[1], ups[0])
+    send_ref[2 * shard + 8 :] = folded
+    feed_ref[:shard] = jnp.where(first, ups[0], ups[1])
+    feed_ref[shard : shard + shard // 2] = folded
+    feed_ref[shard + shard // 2 :] = jnp.concatenate([down[: 2 * shard], down[2 * shard :]], axis=1)
+
+
+def ordered(meta, own, other):
+    first = meta[CORE] == 0
+    return jnp.concatenate([jnp.where(first, own, other), jnp.where(first, other, own)], axis=0)
+
+
+def slot_block(meta, step, own, other, store):
+    turn = (step >> 1) ^ (meta[RANK] & 1)
+    local = (step & 1) == meta[CORE]
+    for t in (0, 1):
+        pl.when(local & (turn == t))(functools.partial(store, own[t]))
+        pl.when(jnp.logical_not(local) & (turn == t))(functools.partial(store, other[t]))
+
+
+def norm_rows(values):
+    mean_val = jnp.mean(values, axis=1, keepdims=True)
+    centered = values - mean_val
+    inv_std = lax.rsqrt(jnp.mean(centered * centered, axis=1, keepdims=True) + NORM_EPS)
+    return centered * inv_std, inv_std
+
+
+def project_body(meta, *refs):
+    packs, own_x, other_x = refs[0:4], refs[4:6], refs[6:8]
+    table_ref, qkv_ref, h_ref, x_ref, rel_ref, w_ref, vec_ref, up_ref, bias_ref = refs[8:17]
+    step, chip = pl.program_id(0), meta[CHIP]
+    width = w_ref.shape[0]
+    shard = width // 8
+    span = qkv_ref.shape[1]
+    cols = span // 3
+
+    @pl.when(step == 0)
+    def _():
+        first = meta[CORE] == 0
+        vec_ref[...] = jnp.zeros_like(vec_ref)
+        own_rows = []
+        for k in range(4):
+            at = pl.ds(aligned(chip ^ k, 2 * shard), 2 * shard)
+            own, other = packs[k][: shard + 8], packs[k][shard + 8 :]
+            w_ref[at, :] = ordered(meta, own[:shard], other[:shard])
+            own_row, other_row = own[shard : shard + 1].astype(f32), other[shard : shard + 1].astype(f32)
+            own_rows.append(own_row)
+            low, high = jnp.where(first, own_row, other_row), jnp.where(first, other_row, own_row)
+            for row, source in enumerate((0, 1, 4, 5, 6)):
+                piece = slice(source * shard, (source + 1) * shard)
+                vec_ref[row : row + 1, at] = jnp.concatenate([low[:, piece], high[:, piece]], axis=1)
+            unit = up_ref.shape[1] // 4
+            up_ref[:, pl.ds(aligned(chip ^ k, unit), unit)] = own_row[:, 7 * shard : 7 * shard + unit]
+        even = chip & 1 == 0
+        for k in (0, 2):
+            at = pl.ds(aligned((chip ^ k) >> 1, 2 * shard), 2 * shard)
+            low = jnp.where(even, own_rows[k], own_rows[k + 1])
+            high = jnp.where(even, own_rows[k + 1], own_rows[k])
+            for row, source in enumerate((2, 3)):
+                piece = slice(source * shard, (source + 1) * shard)
+                bias_ref[row : row + 1, at] = jnp.concatenate([low[:, piece], high[:, piece]], axis=1)
+
+    def copy(ref):
+        x_ref[...] = ref[...]
+
+    slot_block(meta, step, own_x, other_x, copy)
+    x_hat, _ = norm_rows(x_ref[...].astype(f32))
+    h = (x_hat * vec_ref[0:1, :] + vec_ref[1:2, :]).astype(bf)
+    h_ref[...] = h
+    qkv_ref[...] = dot(h, w_ref[:, :span], NN).astype(bf)
+    rel_ref[...] = dot(table_ref[...], w_ref[:, span:], NN).astype(bf)
+
+
+def feed_body(meta, *refs):
+    packs, own_g, other_g = refs[0:4], refs[4:6], refs[6:8]
+    x_ref, o_own, o_other, vec_ref, bias_ref = refs[8:13]
+    (g_ref, df_ref, h_ref, dy_ref, y1_ref, y_keep, dh_keep, dh_send, y_send, sum_ref, wo_mine) = refs[13:24]
+    up_w, down_w, wo_theirs = refs[24:27]
+    step, chip, core = pl.program_id(0), meta[CHIP], meta[CORE]
+    width = up_w.shape[0]
+    shard, unit, block = width // 8, down_w.shape[0] // 4, x_ref.shape[0]
+    fold = shard // 2
+
+    @pl.when(step == 0)
+    def _():
+        sum_ref[...] = jnp.zeros_like(sum_ref)
+        for k in range(4):
+            pack = packs[k]
+            own, other = pack[:shard], pack[shard + fold + 2 * shard : 2 * shard + fold + 2 * shard]
+            up_w[pl.ds(aligned(chip ^ k, 2 * shard), 2 * shard), :] = ordered(meta, own, other)
+            at = pl.ds(aligned(chip ^ k, shard), shard)
+            rows = pack[shard : shard + fold]
+            wo_mine[at, :] = jnp.concatenate([rows[:, :width], rows[:, width:]], axis=0)
+            rows = pack[4 * shard + fold :]
+            wo_theirs[at, :] = jnp.concatenate([rows[:, :width], rows[:, width:]], axis=0)
+            rows = pack[shard + fold : 3 * shard + fold]
+            down_w[pl.ds(aligned(chip ^ k, unit), unit), :] = jnp.concatenate(
+                [rows[:, :width], rows[:, width:]], axis=0
+            )
+
+    at = step * block + lax.broadcasted_iota(jnp.int32, (block, 1), 0)
+
+    def load(ref):
+        dy_ref[...] = jnp.where(at < meta[LIVE], ref[...].astype(f32), 0.0).astype(bf)
+
+    slot_block(meta, step, own_g, other_g, load)
+    y1 = x_ref[...].astype(f32) + (dot(o_own[...], wo_mine[...], NN) + dot(o_other[...], wo_theirs[...], NN))
+    y1_ref[...] = y1
+    x_hat, _ = norm_rows(y1)
+    h = (x_hat * vec_ref[2:3, :] + vec_ref[3:4, :]).astype(bf)
+    h_ref[...] = h
+    f = dot(h, up_w[...], NN) + bias_ref[...]
+    cdf = 0.5 * (1.0 + lax.erf(f * (1.0 / math.sqrt(2.0))))
+    g = (f * cdf).astype(bf)
+    g_ref[...] = g
+    z = dot(g, down_w[...], NN)
+    dy = dy_ref[...]
+    dg = dot(dy, down_w[...], NT)
+    df = (dg * (cdf + f * jnp.exp(-0.5 * f * f) * (1.0 / math.sqrt(2.0 * math.pi)))).astype(bf)
+    df_ref[...] = df
+    dh = dot(df, up_w[...], NT)
+    dh_keep[...] = dh
+    dh_send[...] = dh.astype(bf)
+    sum_ref[0:1, :width] += jnp.sum(dh * x_hat, axis=0, keepdims=True)
+    sum_ref[1:2, :width] += jnp.sum(dh, axis=0, keepdims=True)
+    sum_ref[3:4, :] += jnp.sum(df.astype(f32), axis=0, keepdims=True)
+    local = (step & 1) == core
+
+    @pl.when(local)
+    def _():
+        y_keep[...] = y1 + z + vec_ref[4:5, :]
+        sum_ref[2:3, :width] += jnp.sum(dy.astype(f32), axis=0, keepdims=True)
+
+    @pl.when(jnp.logical_not(local))
+    def _():
+        y_send[...] = z.astype(bf)
+
+
+def norm_two_body(meta, y1_ref, dh_keep, dh_came, dy_ref, vec_ref, y_keep, y_came, wo_ref, o_ref, *refs):
+    out0, out1, resid_ref, do_ref, go_ref = refs
+    step = pl.program_id(0)
+
+    @pl.when(step == 0)
+    def _():
+        go_ref[...] = jnp.zeros_like(go_ref)
+
+    x_hat, inv_std = norm_rows(y1_ref[...])
+    e = (dh_keep[...] + dh_came[...].astype(f32)) * vec_ref[2:3, :]
+    first = jnp.mean(e, axis=1, keepdims=True)
+    second = jnp.mean(e * x_hat, axis=1, keepdims=True)
+    grad = dy_ref[...].astype(f32) + inv_std * (e - first - x_hat * second)
+    da = grad.astype(bf)
+    do_ref[...] = dot(da, wo_ref[...], NT).astype(bf)
+    go_ref[...] += dot(o_ref[...], da, TN)
+    turn = (step >> 1) ^ (meta[RANK] & 1)
+    local = (step & 1) == meta[CORE]
+
+    @pl.when(local)
+    def _():
+        resid_ref[...] = grad
+        y = (y_keep[...] + y_came[...].astype(f32)).astype(bf)
+
+        @pl.when(turn == 0)
+        def _():
+            out0[...] = y
+
+        @pl.when(turn == 1)
+        def _():
+            out1[...] = y
+
+
+def feed_grad_body(meta, h_ref, df_ref, sum_ref, g_ref, dy_ref, *outs):
+    k = pl.program_id(0)
+    rows = h_ref.shape[1]
+    grad = dot(h_ref[...], df_ref[...], TN)
+    at = pl.ds(aligned(meta[CHIP] ^ k, rows), rows)
+    unit = df_ref.shape[1] // 4
+    tail = jnp.concatenate(
+        [sum_ref[0:1, at], sum_ref[1:2, at], sum_ref[2:3, at]]
+        + [sum_ref[3:4, pl.ds(aligned(meta[CHIP] ^ k, unit), unit)]],
+        axis=1,
+    )
+    tail = jnp.concatenate([tail, jnp.zeros((1, df_ref.shape[1] - tail.shape[1]), f32)], axis=1)
+    tail = jnp.broadcast_to(tail, (16, tail.shape[1]))
+    down = dot(g_ref[...], dy_ref[...], TN)
+    half = unit // 2
+    for index, out in enumerate(outs):
+
+        @pl.when(k == index)
+        def _():
+            out[:rows] = grad.astype(out.dtype)
+            out[rows : rows + 16] = tail.astype(out.dtype)
+            out[rows + 16 :] = jnp.concatenate([down[:half], down[half:]], axis=1).astype(out.dtype)
+
+
+def qkv_back_body(meta, *refs):
+    grads, rels = refs[:6], refs[6:8]
+    w_ref, x_ref, h_ref, table_ref, gu_ref, gv_ref, go_ref = refs[8:15]
+    keep_ref, send_ref = refs[15:17]
+    outs, acc, sums = refs[17:21], refs[21], refs[22]
+    step, chip = pl.program_id(0), meta[CHIP]
+    width = x_ref.shape[1]
+    rows = width // 4
+
+    @pl.when(step == 0)
+    def _():
+        sums[...] = jnp.zeros_like(sums)
+        acc[...] = jnp.zeros_like(acc)
+
+    dqkv = jnp.concatenate([ref[...] for ref in grads], axis=1)
+    drel = jnp.concatenate([ref[...] for ref in rels], axis=1)
+    span = dqkv.shape[1]
+    acc[:, :span] += dot(h_ref[...], dqkv, TN)
+    acc[:, span:] += dot(table_ref[...], drel, TN)
+    dh = dot(dqkv, w_ref[:, :span], NT)
+    x_hat, _ = norm_rows(x_ref[...].astype(f32))
+    sums[0:1, :] += jnp.sum(dh * x_hat, axis=0, keepdims=True)
+    sums[1:2, :] += jnp.sum(dh, axis=0, keepdims=True)
+    local = (step & 1) == meta[CORE]
+
+    @pl.when(local)
+    def _():
+        keep_ref[...] = dh
+
+    @pl.when(jnp.logical_not(local))
+    def _():
+        send_ref[...] = dh.astype(bf)
+
+    @pl.when(step == pl.num_programs(0) - 1)
+    def _():
+        for k, out in enumerate(outs):
+            at = pl.ds(aligned(chip ^ k, rows), rows)
+            pair = pl.ds(aligned((chip ^ k) >> 1, rows), rows)
+            tail = [sums[0:1, at], sums[1:2, at], gu_ref[0:1, pair], gv_ref[0:1, pair]]
+            tail = jnp.concatenate(tail + [jnp.zeros((1, acc.shape[1] - 4 * rows), f32)], axis=1)
+            out[:rows] = acc[at, :].astype(out.dtype)
+            out[rows : rows + 16] = jnp.broadcast_to(tail, (16, tail.shape[1])).astype(out.dtype)
+            shard = rows // 2
+            lines = go_ref[pl.ds(aligned(chip ^ k, shard), shard), :]
+            lines = jnp.concatenate([lines[: shard // 2], lines[shard // 2 :]], axis=1)
+            out[rows + 16 :] = lines.astype(out.dtype)
+
+
+def norm_one_body(meta, x_ref, dh_keep, dh_came, resid_ref, vec_ref, out0, out1):
+    turn = pl.program_id(0) ^ (meta[RANK] & 1)
+    x_hat, inv_std = norm_rows(x_ref[...].astype(f32))
+    e = (dh_keep[...] + dh_came[...].astype(f32)) * vec_ref[0:1, :]
+    first = jnp.mean(e, axis=1, keepdims=True)
+    second = jnp.mean(e * x_hat, axis=1, keepdims=True)
+    grad = (resid_ref[...] + inv_std * (e - first - x_hat * second)).astype(bf)
+
+    @pl.when(turn == 0)
+    def _():
+        out0[...] = grad
+
+    @pl.when(turn == 1)
+    def _():
+        out1[...] = grad
+
+
+def chip_sum_body(meta, own, *refs):
+    *came, keep, send = refs
+    half = keep.shape[1]
+    for out, side in ((keep, meta[RANK] & 1), (send, 1 - (meta[RANK] & 1))):
+        at = pl.ds(aligned(side, half), half)
+        total = own[:, at]
+        for ref in came:
+            total = total + ref[:, at].astype(f32)
+        out[...] = total.astype(out.dtype)
+
+
+def chip_sum(meta, parts, name):
+    rows, size = parts[0].shape
+    return kernel_call(chip_sum_body, name, meta, parts, [((rows, size // 2), f32), ((rows, size // 2), bf)])
+
+
+def halves(meta, mine, other):
+    low = meta[RANK] & 1 == 0
+    return jnp.concatenate([jnp.where(low, mine, other), jnp.where(low, other, mine)], axis=1)
+
+
+def early_out_body(meta, mine, other, up_ref, down_ref):
+    both = halves(meta, mine[...], other[...])
+    rows, width = up_ref.shape[0], down_ref.shape[1]
+    up_ref[...] = both[:rows]
+    down = both[rows:].astype(f32)
+    down_ref[...] = jnp.concatenate([down[:, :width], down[:, width:]], axis=0)
+
+
+def late_pack_body(meta, up_ref, mine, other, late_ref, out_ref, send_ref):
+    both = halves(meta, mine[...], other[...])
+    rows, width = up_ref.shape[0] - 16, out_ref.shape[1]
+    shard = rows // 2
+    late_ref[...] = both[: rows + 16]
+    out = both[rows + 16 :].astype(f32)
+    out_ref[...] = jnp.concatenate([out[:, :width], out[:, width:]], axis=0)
+    up = up_ref[...]
+    for at, part in ((0, up), (up.shape[1], both)):
+        theirs = jnp.where(meta[CORE] == 0, part[shard:rows], part[:shard])
+        send_ref[:shard, at : at + up.shape[1]] = theirs
+        send_ref[shard:, at : at + up.shape[1]] = part[rows : rows + 8]
+
+
+def late_out_body(meta, up_ref, late_ref, came_ref, g_up, g_qkv, g_rel, vec_ref):
+    shard = g_up.shape[0]
+    rows, size = 2 * shard, up_ref.shape[1]
+    unit, hd, heads = size // 4, HEAD_DIM, H // 2
+    first = meta[CORE] == 0
+    came = came_ref[...]
+    pair = []
+    for at, ref in ((0, up_ref), (size, late_ref)):
+        mine = jnp.where(first, ref[:shard], ref[shard:rows])
+        theirs = came[:shard, at : at + size]
+        pair.append([jnp.where(first, mine, theirs), jnp.where(first, theirs, mine)])
+    for j in range(4):
+        for side in (0, 1):
+            at = (2 * j + side) * unit
+            g_up[:, at : at + unit] = pair[0][side][:, j * unit : (j + 1) * unit].astype(f32)
+    cols = heads * hd
+    g_qkv[...] = jnp.concatenate(
+        [
+            pair[1][h & 1][:, t * cols + (h >> 1) * hd : t * cols + ((h >> 1) + 1) * hd]
+            for h in range(2 * heads)
+            for t in range(3)
+        ],
+        axis=1,
+    ).astype(f32)
+    g_rel[...] = jnp.concatenate(
+        [
+            pair[1][h & 1][:, 3 * cols + (h >> 1) * hd : 3 * cols + ((h >> 1) + 1) * hd]
+            for h in range(2 * heads)
+        ],
+        axis=1,
+    ).astype(f32)
+    own = [ref[rows : rows + 1].astype(f32) for ref in (up_ref, late_ref)]
+    both = [own[0] + came[shard : shard + 1, :size].astype(f32), own[1] + came[shard : shard + 1, size:].astype(f32)]
+    odd_chip = meta[CHIP] & 1 == 0
+    vec_ref[...] = jnp.zeros_like(vec_ref)
+    picks = [(both[1], 0, first), (both[1], 1, first), (own[1], 2, odd_chip), (own[1], 3, odd_chip)]
+    picks += [(both[0], 0, first), (both[0], 1, first), (both[0], 2, first)]
+    for row, (source, at, low) in enumerate(picks):
+        piece = source[:, at * rows : (at + 1) * rows]
+        vec_ref[row : row + 1, :shard] = jnp.where(low, piece[:, :shard], piece[:, shard:])
+    vec_ref[7:8, :] = own[0][:, 3 * rows : 3 * rows + unit]
+
+
+def place_body(meta, y0, y1, x0, x1, y_ref, x_ref):
+    high = meta[RANK] >> 1 == 1
+    y_ref[0] = jnp.where(high, y1[...], y0[...])
+    y_ref[1] = jnp.where(high, y0[...], y1[...])
+    x_ref[0] = jnp.where(high, x1[...], x0[...]).astype(f32)
+    x_ref[1] = jnp.where(high, x0[...], x1[...]).astype(f32)
+
+
+def slot_split_device(
+    layer_input,
+    lengths,
+    ln1_gain,
+    ln1_bias,
+    w_qkv,
+    w_rel,
+    bias_u,
+    bias_v,
+    w_out,
+    ln2_gain,
+    ln2_bias,
+    w_up,
+    up_bias,
+    w_down,
+    down_bias,
+    grad_out,
+):
+    slots, block, width = layer_input.shape
+    rank, device = lax.axis_index("seq"), lax.axis_index("fsdp")
+    core, chip = device & 1, device >> 1
+    full, heads = 4 * block, H // 2
+    cols, shard, unit = heads * HEAD_DIM, width // 8, up_bias.shape[0]
+    mine_ff = 4 * unit
+
+    x_own = to_slots(layer_input, rank)
+    where = jnp.stack([core, chip, rank, rank]).astype(jnp.int32)
+    vectors = (ln1_gain, ln1_bias, bias_u, bias_v, ln2_gain, ln2_bias, down_bias, up_bias)
+    attn_rows, fold = shard + 8, shard // 2
+    attn_pack, feed_pack, pack_send = kernel_call(
+        pack_body,
+        "pack",
+        where,
+        [w_qkv, w_rel, w_up, w_out, w_down] + [v.reshape(-1, min(128, v.size)) for v in vectors],
+        [((attn_rows, 4 * cols), bf), ((3 * shard + fold, 4 * cols), bf), ((attn_rows + shard + fold, 4 * cols), bf)],
+    )
+    pack_came = swap_core(pack_send)
+    attn_pack = jnp.concatenate([attn_pack, pack_came[:attn_rows]], axis=0)
+    both = swap_core(lengths)
+    length = jnp.where(core == rank >> 1, lengths, both)
+    length = jnp.where(rank & 1 == 0, length[0], length[1])
+    meta = jnp.stack([core, chip, rank, length]).astype(jnp.int32)
+    length_arr = length.reshape(1)
+
+    steps = (full - 1 - lax.iota(jnp.int32, full)).astype(f32)
+    attn_pack, steps = together(attn_pack, steps)
+    attn_packs = [attn_pack] + [swap_chip(attn_pack, k) for k in (1, 2, 3)]
+    grad_out, *x_own = together(grad_out, *x_own)
+    grad_own = to_slots(grad_out, rank)
+    inv_freq = jnp.exp(lax.iota(f32, width // 2) * (-2.0 * math.log(10000.0) / width))
+    angles = steps[:, None] * inv_freq[None, :]
+    table = jnp.concatenate([jnp.sin(angles), jnp.cos(angles)], axis=1).astype(bf)
+
+    x_other = [swap_core(x) for x in x_own]
+    by_step = lambda width: pl.BlockSpec((block, width), lambda i, _: (i, 0))
+    qkv, h1, x_slot, rel, w_own, vecs, up_b, biases = kernel_call(
+        project_body,
+        "project",
+        where,
+        attn_packs + x_own + x_other + [table],
+        [((full, 3 * cols), bf), ((full, width), bf), ((full, width), bf), ((full, cols), bf)]
+        + [((width, 4 * cols), bf), ((8, width), f32), ((1, mine_ff), f32), ((2, cols), f32)],
+        grid=(4,),
+        in_specs=[whole(2 * attn_rows, 4 * cols)] * 4 + [whole(block, width)] * 4 + [by_step(width)],
+        out_specs=[by_step(3 * cols), by_step(width), by_step(width), by_step(cols)]
+        + [whole(width, 4 * cols), whole(8, width), whole(1, mine_ff), whole(2, cols)],
+        flops=2 * full * width * 4 * cols,
+    )
+    own_u, own_v = biases[0:1], biases[1:2]
+    qkv, *grad_own = together(qkv, *grad_own)
+    attn, lse = attn_fwd(length_arr, qkv, rel, own_u, own_v)
+
+    feed_pack = jnp.concatenate([feed_pack, pack_came[attn_rows:]], axis=0)
+    feed_pack, *_ = together(feed_pack, *attn_packs)
+    feed_packs = [swap_chip(feed_pack, k) for k in (1, 2, 3)]
+    grad_other = [swap_core(g) for g in grad_own]
+    attn, *rest = together(attn, *feed_packs, *grad_other)
+    feed_packs, grad_other = [feed_pack] + rest[:3], rest[3:]
+
+    attn_other = swap_core(attn)
+    kept = lambda width: pl.BlockSpec((block, width), lambda i, _: (i >> 1, 0))
+    half = full // 2
+    g, df, h2, dy, y1, y_keep, dh_keep, dh_send, y_send, early, wo_mine = kernel_call(
+        feed_body,
+        "feed",
+        meta,
+        feed_packs + grad_own + grad_other + [x_slot, attn, attn_other, vecs, up_b],
+        [((full, mine_ff), bf)] * 2 + [((full, width), bf)] * 2
+        + [((full, width), f32), ((half, width), f32), ((full, width), f32), ((full, width), bf)]
+        + [((half, width), bf), ((8, mine_ff), f32), ((cols, width), bf)],
+        grid=(4,),
+        in_specs=[whole(*feed_pack.shape)] * 4 + [whole(block, width)] * 4
+        + [by_step(width), by_step(cols), by_step(cols), whole(8, width), whole(1, mine_ff)],
+        out_specs=[by_step(mine_ff)] * 2 + [by_step(width)] * 3 + [kept(width)] + [by_step(width)] * 2
+        + [kept(width), whole(8, mine_ff), whole(cols, width)],
+        scratch=[
+            pltpu.VMEM((width, mine_ff), bf),
+            pltpu.VMEM((mine_ff, width), bf),
+            pltpu.VMEM((cols, width), bf),
+        ],
+        flops=8 * full * width * mine_ff,
+    )
+    dh_came = swap_core(dh_send)
+    y_came = swap_core(y_send)
+    by_chip = lambda rows, size: pl.BlockSpec((rows, size), lambda k, m: (0, m[CHIP] ^ k))
+    blocks = lambda rows: [((rows, 2 * width), f32)] + [((rows, 2 * width), bf)] * 3
+    early_parts = kernel_call(
+        feed_grad_body,
+        "feed_grad",
+        meta,
+        [h2, df, early, g, dy],
+        blocks(2 * shard + 16 + unit // 2),
+        grid=(4,),
+        in_specs=[by_chip(full, 2 * shard), whole(full, mine_ff), whole(8, mine_ff)]
+        + [by_chip(full, unit), whole(full, width)],
+        flops=4 * full * width * mine_ff,
+    )
+    out0, out1, g_resid, d_attn, g_out = kernel_call(
+        norm_two_body,
+        "norm_two",
+        meta,
+        [y1, dh_keep, dh_came, dy, vecs, y_keep, y_came, wo_mine, attn],
+        [((block, width), bf)] * 2 + [((half, width), f32), ((full, cols), bf), ((cols, width), f32)],
+        grid=(4,),
+        in_specs=[by_step(width)] * 4 + [whole(8, width)] + [kept(width)] * 2 + [whole(cols, width), by_step(cols)],
+        out_specs=[whole(block, width)] * 2 + [kept(width), by_step(cols), whole(cols, width)],
+        flops=4 * full * width * cols,
+    )
+    y_turns = [
+        lax.ppermute(out, ("fsdp", "seq"), [(b, a) for a, b in slot_pairs(turn)])
+        for turn, out in enumerate((out0, out1))
+    ]
+    back = lambda pair: attn_bwd(length_arr, qkv, rel, own_u, own_v, lse, d_attn, pair=pair)
+    early_came = [swap_chip(early_parts[k], k) for k in (1, 2, 3)]
+    *first_pair, y0, y1, e1, e2, e3 = together(*back(0), *y_turns, *early_came)
+    y_turns = [y0, y1]
+    early_keep, early_send = chip_sum(meta, [early_parts[0], e1, e2, e3], "early_chips")
+    d_attn, early_send, lse = together(d_attn, early_send, lse)
+    *second_pair, early_came = together(*back(1), swap_seq(early_send, 1))
+    q0, k0, v0, r0, u0, b0 = first_pair
+    q1, k1, v1, r1, u1, b1 = second_pair
+    early_pair = (early_keep + early_came.astype(f32)).astype(bf)
+    early_pair, q1 = together(early_pair, q1)
+    early_came = swap_seq(early_pair, 2)
+    rows = 2 * shard + 16
+    pair_step = pl.BlockSpec((block, 2 * HEAD_DIM), lambda i, _: (i, 0))
+    dh1_keep, dh1_send, *late_parts = kernel_call(
+        qkv_back_body,
+        "qkv_back",
+        meta,
+        [q0, q1, k0, k1, v0, v1, r0, r1, w_own, x_slot, h1, table]
+        + [jnp.concatenate([u0, u1], axis=1), jnp.concatenate([b0, b1], axis=1), g_out],
+        [((half, width), f32), ((half, width), bf)] + blocks(rows + fold),
+        grid=(4,),
+        in_specs=[pair_step] * 8 + [whole(width, 4 * cols)] + [by_step(width)] * 3
+        + [whole(1, cols), whole(1, cols), whole(cols, width)],
+        out_specs=[kept(width)] * 2 + [whole(rows + fold, 2 * width)] * 4,
+        scratch=[pltpu.VMEM((width, 4 * cols), f32), pltpu.VMEM((8, width), f32)],
+        flops=14 * full * width * cols,
+    )
+    late_came = [swap_chip(late_parts[k], k) for k in (1, 2, 3)]
+    dh1_came = swap_core(dh1_send)
+    dh1_came, early_came = together(dh1_came, early_came)
+    early_mine = (early_pair.astype(f32) + early_came.astype(f32)).astype(bf)
+    early_other = swap_seq(early_mine, 1)
+    by_half = pl.BlockSpec((block, width), lambda i, _: (i, 0))
+    own_rows = pl.BlockSpec((block, width), lambda i, m: (2 * i + m[CORE], 0))
+    x0, x1 = kernel_call(
+        norm_one_body,
+        "norm_one",
+        meta,
+        [x_slot, dh1_keep, dh1_came, g_resid, vecs],
+        [((block, width), bf)] * 2,
+        grid=(2,),
+        in_specs=[own_rows] + [by_half] * 3 + [whole(8, width)],
+        out_specs=[whole(block, width)] * 2,
+    )
+    *late_came, x0, x1, early_other = together(*late_came, x0, x1, early_other)
+    x_turns = [
+        lax.ppermute(out, ("fsdp", "seq"), [(b, a) for a, b in slot_pairs(turn)])
+        for turn, out in enumerate((x0, x1))
+    ]
+    late_keep, late_send = chip_sum(meta, [late_parts[0]] + late_came, "late_chips")
+    g_up_rows, g_down = kernel_call(
+        early_out_body,
+        "early_out",
+        meta,
+        [early_mine, early_other],
+        [((rows, 2 * width), bf), ((unit, width), f32)],
+    )
+    late_pair = (late_keep + swap_seq(late_send, 1).astype(f32)).astype(bf)
+    late_came, g_up_rows, g_down, *x_turns = together(swap_seq(late_pair, 2), g_up_rows, g_down, *x_turns)
+    late_mine = (late_pair.astype(f32) + late_came.astype(f32)).astype(bf)
+    output, grad_x = kernel_call(
+        place_body,
+        "place",
+        meta,
+        y_turns + x_turns,
+        [((2, block, width), bf), ((2, block, width), f32)],
+    )
+    late_other, output, grad_x = together(swap_seq(late_mine, 1), output, grad_x)
+    late, g_w_out, send = kernel_call(
+        late_pack_body,
+        "late_pack",
+        meta,
+        [g_up_rows, late_mine, late_other],
+        [((rows, 2 * width), bf), ((shard, width), f32), ((shard + 8, 4 * width), bf)],
+    )
+    g_up, g_qkv, g_rel, vecs = kernel_call(
+        late_out_body,
+        "late_out",
+        meta,
+        [g_up_rows, late, swap_core(send)],
+        [((shard, 2 * mine_ff), f32), ((shard, 6 * cols), f32), ((shard, 2 * cols), f32), ((8, unit), f32)],
+    )
+    small = lambda row: vecs[row, :shard]
+    return (
+        output,
+        grad_x,
+        small(0),
+        small(1),
+        g_qkv,
+        g_rel,
+        small(2),
+        small(3),
+        g_w_out,
+        small(4),
+        small(5),
+        g_up,
+        vecs[7],
+        g_down,
+        small(6),
+    )
+
+
+def per_device(*args):
+    one_slot_a_chip = lax.axis_size("fsdp") == 8 and lax.axis_size("seq") == 4
+    if one_slot_a_chip and args[0].shape[0] == 2:
+        return slot_split_device(*args)
+    return head_split_device(*args)
+
+
 def solution(mesh):
     placed = (
         P("fsdp", "seq", None),

time: 1030 us -> 222 us (0.22)
  local copies, waits for them, and re-layouts: 453 us -> 11.2 us
  waiting for transfers between devices: 189 us -> 37.2 us
  matrix products: 147 us -> 0 us
  blocking collectives: 121 us -> 0 us
  Pallas kernels: 0 us -> 106 us
  loops' own time: 50.3 us -> 0 us
  starting transfers between devices: 14.2 us -> 52.7 us
  between operations: 17.1 us -> 2.45 us
  other arithmetic: 25.1 us -> 10.7 us
    reshape x20 -> x0, local copies, waits for them, and re-layouts: 250 us -> none  [the longest x4 103 us: skew_rows(): picked.reshape(leading + (row_count, col_count - 1))]
    dot_general x36 -> x0, matrix products: 147 us -> none  [the longest x4 27.6 us: scores_block(): jnp.einsum('sqhe,the->shqt', qv_part, rel_win, preferred_element_type=jnp...]
    reduce_scatter x5 -> x0, waiting for transfers between devices: 132 us -> none  [the longest x1 55.1 us: per_device(): lax.psum_scatter(down_gradient, 'fsdp', scatter_dimension=0, tiled=True)]
    pallas_call x0 -> x16, Pallas kernels: none -> 106 us  [the longest x13 68.7 us: kernel_call(): pl.pallas_call(body, out_shape=[jax.ShapeDtypeStruct(shape, kind) for sha...]
    slice x4 -> x5, local copies, waits for them, and re-layouts: 64.9 us -> 3.2 us  [the longest x1 1.33 us: slot_split_device(): own_u, own_v = (biases[0:1], biases[1:2])]
    ppermute x0 -> x37, starting transfers between devices: none -> 52.7 us  [the longest x12 16.4 us: swap_chip(): lax.ppermute(values, 'fsdp', [(i, i ^ 2 * mask) for i in range(size)])]
    transpose x4 -> x0, local copies, waits for them, and re-layouts: 50.5 us -> none  [scores_block(): jnp.einsum('sqhe,the->shqt', qv_part, rel_win, preferred_element_type=jnp...]
    another operation x2 -> x0, loops' own time: 50.3 us -> none  [the longest x1 35 us: per_device(): lax.scan(backward_block, (zero_heads, zero_heads, zero_ext), jnp.arange(n...]
  transfers between devices with their start and end apart: 12 -> 37, of which waited for: 7 -> 11; matrix products, arithmetic and copies ran while one was open for 58% -> 6% of each run, Pallas kernels for 0% -> 33%
where the time goes in v1:
time: 222 us; the launch traced here: 220 us
  Pallas kernels  106 us (48%)
  starting transfers between devices  52.7 us (24%)
  waiting for transfers between devices  37.2 us (17%)
  local copies, waits for them, and re-layouts  11.2 us (5%)
  other arithmetic  10.7 us (5%)
  between operations  2.45 us (1%)
    pallas_call x13, Pallas kernels, kernel_call(): pl.pallas_call(body, out_shape=[jax.ShapeDtypeStruct(shape, kind) for sha...  68.7 us
    ppermute x6, waiting for transfers between devices, swap_seq(): return lax.ppermute(values, 'seq', [(i, i ^ mask) for i in range(size)])  25.3 us
    pallas_call x2, Pallas kernels, attn_bwd(): pl.pallas_call(functools.partial(attn_bwd_body, block=block), out_shape=(...  25.1 us
    ppermute x12, starting transfers between devices, swap_chip(): lax.ppermute(values, 'fsdp', [(i, i ^ 2 * mask) for i in range(size)])  16.4 us
    pallas_call x1, Pallas kernels, attn_fwd(): pl.pallas_call(functools.partial(attn_fwd_body, block=block), out_shape=(...  11.8 us
    ppermute x4, starting transfers between devices, slot_split_device(): lax.ppermute(out, ('fsdp', 'seq'), [(b, a) for a, b in slot_pairs(turn)])  11.3 us
    ppermute x11, starting transfers between devices, swap_core(): return lax.ppermute(values, 'fsdp', [(i, i ^ 1) for i in range(size)])  11 us
    ppermute x12, waiting for transfers between devices, swap_chip(): lax.ppermute(values, 'fsdp', [(i, i ^ 2 * mask) for i in range(size)])  8.86 us
  transfers between devices with their start and end apart: 37, of which 11 were waited for; matrix products, arithmetic and copies ran while one was open for 6% of the time, Pallas kernels for 33%

profile of v1, /device:TPU:0, one launch (start us, length us, event | category | flops | bytes accessed | tf_op | source)
XLA Modules:
  0.0 220.0 jit_solution(6999955959211571687)
XLA Ops:
  2.2 2.7 %collective-permute-start.6 = (bf16[256,512]{1,0:T(8,128)(2,1)S(1)}, bf16[256,512]{1,0:T(8,128)(2,1)S(1)}, u32[]{:S(2)}, u32[]{:S(2)}) collective-permute-start(bf16[256,512]{1,0:T(8,128)(2,1)S(1)} %get-tuple-element.263), channel_id=1, source_target_pairs={{0,1},{1,5},{2,0},{3,4},{4,3},{5,7},{6,2},{7,6},{8,9},{9,13},{10,8... | collective-permute-start | bytes 786440 | tf_op jit(solution)/shard_map/ppermute | solution.py:563
  6.2 3.0 %pack.1 = (bf16[72,1024]{1,0:T(8,128)(2,1)}, bf16[224,1024]{1,0:T(8,128)(2,1)}, bf16[168,1024]{1,0:T(8,128)(2,1)}) custom-call(s32[4]{0:T(128)} %get-tuple-element.259.meta, bf16[64,1536]{1,0:T(8,128)(2,1)} %qkv_ref.1, bf16[64,512]{1,0:T(8,128)(2,1)} %rel_ref.1, bf16[64,2048]{1,0:T(8,128)(2,1)} %up_ref.1, bf16[64,512]{1,0:T(8,128)(2,1)} %out_ref.1, ...), custom_call_target="tpu_custom_call" | custom-call | bytes 1803648 | tf_op jit(solution)/shard_map/pack/pallas_call | solution.py:585
  9.2 3.4 %collective-permute-start.1 = (bf16[168,1024]{1,0:T(8,128)(2,1)}, bf16[168,1024]{1,0:T(8,128)(2,1)S(1)}, u32[]{:S(2)}, u32[]{:S(2)}) collective-permute-start(bf16[168,1024]{1,0:T(8,128)(2,1)} %get-tuple-element.138), channel_id=1, source_target_pairs={{0,4},{4,0},{8,12},{12,8},{16,20},{20,16},{24,28},{28,24},{1,5},{5... | collective-permute-start | bytes 1032200 | tf_op jit(solution)/shard_map/ppermute | solution.py:539
  16.8 2.8 %collective-permute-start.4 = (bf16[144,1024]{1,0:T(8,128)(2,1)S(1)}, bf16[144,1024]{1,0:T(8,128)(2,1)S(1)}, u32[]{:S(2)}, u32[]{:S(2)}) collective-permute-start(bf16[144,1024]{1,0:T(8,128)(2,1)S(1)} %pad_maximum_fusion.2.refs_0_), channel_id=1, source_target_pairs={{0,24},{4,28},{8,16},{12,20},{16,8},{20,12},{24,0},{28,4},{1,25},{... | collective-permute-start | bytes 884744 | tf_op jit(solution)/shard_map/ppermute | solution.py:544
  20.4 4.2 %fusion = (bf16[1024,256]{1,0:T(8,128)(2,1)S(1)}, bf16[1024,256]{1,0:T(8,128)(2,1)S(1)}) fusion(f32[256]{0:T(256)S(1)} %multiply_exponential_fusion, f32[1024]{0:T(1024)S(1)} %subtract_convert_fusion), kind=kLoop, calls=%fused_computation.2 | loop fusion | flops 786432 | bytes 1053696 | tf_op jit(solution)/shard_map/convert
  24.7 2.9 %collective-permute-done.4.refs_3_ = bf16[144,1024]{1,0:T(8,128)(2,1)S(1)} collective-permute-done((bf16[144,1024]{1,0:T(8,128)(2,1)S(1)}, bf16[144,1024]{1,0:T(8,128)(2,1)S(1)}, u32[]{:S(2)}, u32[]{:S(2)}) %collective-permute-start.4) | collective-permute-done | bytes 294944 | tf_op jit(solution)/shard_map/ppermute | solution.py:544
  27.6 4.1 %collective-permute-start.10 = (bf16[256,512]{1,0:T(8,128)(2,1)S(1)}, bf16[256,512]{1,0:T(8,128)(2,1)S(1)}, u32[]{:S(2)}, u32[]{:S(2)}) collective-permute-start(bf16[256,512]{1,0:T(8,128)(2,1)S(1)} %get-tuple-element.261), channel_id=1, source_target_pairs={{0,1},{1,5},{2,0},{3,4},{4,3},{5,7},{6,2},{7,6},{8,9},{9,13},{10,8... | collective-permute-start | bytes 786440 | tf_op jit(solution)/shard_map/ppermute | solution.py:563
  31.7 1.9 collective-permute-done.3.refs_2_
  33.6 1.3 collective-permute-start.9
  35.0 1.9 collective-permute-start.13
  36.9 1.3 collective-permute-start.12
  40.0 6.9 %project.1 = (bf16[1024,768]{1,0:T(8,128)(2,1)}, bf16[1024,512]{1,0:T(8,128)(2,1)}, bf16[1024,512]{1,0:T(8,128)(2,1)}, bf16[1024,256]{1,0:T(8,128)(2,1)}, bf16[5...) custom-call(s32[4]{0:T(128)} %get-tuple-element.259.meta, ...), custom_call_target="tpu_custom_call" | custom-call | flops 1073741824 | bytes 8542208 | tf_op jit(solution)/shard_map/project/pallas_call | solution.py:585
  46.9 5.4 %collective-permute-start.14 = (bf16[256,512]{1,0:T(8,128)(2,1)}, bf16[256,512]{1,0:T(8,128)(2,1)S(1)}, u32[]{:S(2)}, u32[]{:S(2)}) collective-permute-start(bf16[256,512]{1,0:T(8,128)(2,1)} %collective-permute-done.9.refs_4_), channel_id=1, source_target_pairs={{0,4},{4,0},{8,12},{12,8},{16,20},{20,16},{24,28},{28,24},{1,5},{5... | collective-permute-start | bytes 786440 | tf_op jit(solution)/shard_map/ppermute | solution.py:539
  52.4 1.3 fusion.2
  53.7 11.8 %attn_fwd.1 = (bf16[1024,256]{1,0:T(8,128)(2,1)}, f32[4,1024,1]{2,1,0:T(8,128)}) custom-call(s32[1]{0:T(128)} %bitcast.5.len_ref, bf16[1024,768]{1,0:T(8,128)(2,1)} %get-tuple-element.145.q_ref.k_ref.v_ref, bf16[1024,768]{1,0:T(8,128)(2,1)} %get-tuple-element.145.q_ref.k_ref.v_ref, bf16[1024,768]{1,0:T(8,128)(2,1)} %get-tuple-element.145.q_ref.k_ref.v_ref, ...), custom_call_target="tpu_custom_call" | custom-call | flops 3221225472 | bytes 2621440 | tf_op jit(solution)/shard_map/attn_fwd/pallas_call | solution.py:83
  65.6 2.0 collective-permute-done.12.refs_2_
  68.5 1.2 collective-permute-done.16.refs_10_
  70.5 13.2 %feed.1 = (bf16[1024,1024]{1,0:T(8,128)(2,1)}, bf16[1024,1024]{1,0:T(8,128)(2,1)}, bf16[1024,512]{1,0:T(8,128)(2,1)}, bf16[1024,512]{1,0:T(8,128)(2,1)}, f32[102...) custom-call(s32[4]{0:T(128)} %pad_add_fusion.meta, ...), custom_call_target="tpu_custom_call" | custom-call | flops 4294967296 | bytes 19189760 | tf_op jit(solution)/shard_map/feed/pallas_call | solution.py:585
  84.3 8.0 %feed_grad.1 = (f32[272,1024]{1,0:T(8,128)}, bf16[272,1024]{1,0:T(8,128)(2,1)}, bf16[272,1024]{1,0:T(8,128)(2,1)}, bf16[272,1024]{1,0:T(8,128)(2,1)}) custom-call(s32[4]{0:T(128)} %pad_add_fusion.meta, bf16[1024,512]{1,0:T(8,128)(2,1)} %get-tuple-element.179.h_ref, bf16[1024,1024]{1,0:T(8,128)(2,1)} %get-tuple-element.180.df_ref, ...), custom_call_target="tpu_custom_call" | custom-call | flops 2147483648 | bytes 9109504 | tf_op jit(solution)/shard_map/feed_grad/pallas_call | solution.py:585
  92.3 1.7 collective-permute-start.21
  94.7 1.1 collective-permute-start.23
  97.0 7.9 %norm_two.1 = (bf16[256,512]{1,0:T(8,128)(2,1)}, bf16[256,512]{1,0:T(8,128)(2,1)}, f32[512,512]{1,0:T(8,128)}, bf16[1024,256]{1,0:T(8,128)(2,1)}, f32[256,512]{1,0:T(8,128)}) custom-call(s32[4]{0:T(128)} %pad_add_fusion.meta, f32[1024,512]{1,0:T(8,128)} %get-tuple-element.163.y1_ref, f32[1024,512]{1,0:T(8,128)} %get-tuple-element.164.dh_keep, ...), custom_call_target="tpu_custom_call" | custom-call | flops 536870912 | bytes 11288576 | tf_op jit(solution)/shard_map/norm_two/pallas_call | solution.py:585
  104.9 1.6 collective-permute-start.19
  106.5 5.6 %collective-permute-start.20 = (bf16[256,512]{1,0:T(8,128)(2,1)}, bf16[256,512]{1,0:T(8,128)(2,1)S(1)}, u32[]{:S(2)}, u32[]{:S(2)}) collective-permute-start(bf16[256,512]{1,0:T(8,128)(2,1)} %get-tuple-element.178), channel_id=1, source_target_pairs={{1,0},{5,1},{0,2},{4,3},{3,4},{7,5},{2,6},{6,7},{9,8},{13,9},{8,10... | collective-permute-start | bytes 786440 | tf_op jit(solution)/shard_map/ppermute | solution.py:1120
  112.1 12.5 %attn_bwd.2 = (bf16[1024,128]{1,0:T(8,128)(2,1)}, bf16[1024,128]{1,0:T(8,128)(2,1)}, bf16[1024,128]{1,0:T(8,128)(2,1)}, bf16[1024,128]{1,0:T(8,128)(2,1)}, f32[1,128]{1,0:T(1,128)}, /*index=5*/f32[1,128]{1,0:T(1,128)}) custom-call(s32[1]{0:T(128)} %bitcast.5.len_ref, bf16[1024,768]{1,0:T(8,128)(2,1)} %get-tuple-element.145.q_ref.k_ref.v_ref, ...), custom_call_target="tpu_custom_call" | custom-call | flops 9663676416 | bytes 2621440 | tf_op jit(solution)/shard_map/attn_bwd/pallas_call | solution.py:169
  125.9 3.4 %early_chips.1 = (f32[272,512]{1,0:T(8,128)}, bf16[272,512]{1,0:T(8,128)(2,1)}) custom-call(s32[4]{0:T(128)} %pad_add_fusion.meta, f32[272,1024]{1,0:T(8,128)} %get-tuple-element.187.own, bf16[272,1024]{1,0:T(8,128)(2,1)} %copy-done.4, bf16[272,1024]{1,0:T(8,128)(2,1)} %copy-done.5, bf16[272,1024]{1,0:T(8,128)(2,1)} %copy-done.6), custom_call_target="tpu_custom_call" | custom-call | bytes 3620864 | tf_op jit(solution)/shard_map/early_chips/pallas_call | solution.py:585
  129.9 12.6 %attn_bwd.3 = (bf16[1024,128]{1,0:T(8,128)(2,1)}, bf16[1024,128]{1,0:T(8,128)(2,1)}, bf16[1024,128]{1,0:T(8,128)(2,1)}, bf16[1024,128]{1,0:T(8,128)(2,1)}, f32[1,128]{1,0:T(1,128)}, /*index=5*/f32[1,128]{1,0:T(1,128)}) custom-call(s32[1]{0:T(128)} %bitcast.5.len_ref, bf16[1024,768]{1,0:T(8,128)(2,1)} %get-tuple-element.145.q_ref.k_ref.v_ref, ...), custom_call_target="tpu_custom_call" | custom-call | flops 9663676416 | bytes 2621440 | tf_op jit(solution)/shard_map/attn_bwd/pallas_call | solution.py:169
  142.6 1.2 pad_maximum_fusion.3
  143.8 8.5 %qkv_back.1 = (f32[512,512]{1,0:T(8,128)}, bf16[512,512]{1,0:T(8,128)(2,1)}, f32[176,1024]{1,0:T(8,128)}, bf16[176,1024]{1,0:T(8,128)(2,1)}, bf16[176,1024]{1,0:T(8,128)(2,1)}, /*index=5*/bf16[176,1024]{1,0:T(8,128)(2,1)}) custom-call(s32[4]{0:T(128)} %pad_add_fusion.meta, bf16[1024,128]{1,0:T(8,128)(2,1)} %get-tuple-element.186.refs_0_, ...), custom_call_target="tpu_custom_call" | custom-call | flops 1879048192 | bytes 10192896 | tf_op jit(solution)/shard_map/qkv_back/pallas_call | solution.py:585
  152.6 4.2 %collective-permute-start.25 = (bf16[176,1024]{1,0:T(8,128)(2,1)}, bf16[176,1024]{1,0:T(8,128)(2,1)S(1)}, u32[]{:S(2)}, u32[]{:S(2)}) collective-permute-start(bf16[176,1024]{1,0:T(8,128)(2,1)} %get-tuple-element.219), channel_id=1, source_target_pairs={{0,8},{4,12},{8,0},{12,4},{16,24},{20,28},{24,16},{28,20},{1,9},{5... | collective-permute-start | bytes 1081352 | tf_op jit(solution)/shard_map/ppermute | solution.py:544
  158.2 10.1 %collective-permute-done.29 = bf16[272,512]{1,0:T(8,128)(2,1)S(1)} collective-permute-done((bf16[272,512]{1,0:T(8,128)(2,1)S(1)}, bf16[272,512]{1,0:T(8,128)(2,1)S(1)}, u32[]{:S(2)}, u32[]{:S(2)}) %collective-permute-start.29) | collective-permute-done | bytes 278560 | tf_op jit(solution)/shard_map/ppermute | solution.py:549
  169.1 3.7 %norm_one.1 = (bf16[256,512]{1,0:T(8,128)(2,1)}, bf16[256,512]{1,0:T(8,128)(2,1)}) custom-call(s32[4]{0:T(128)} %pad_add_fusion.meta, bf16[1024,512]{1,0:T(8,128)(2,1)} %get-tuple-element.159.refs_8_.refs_9_.x_ref, f32[512,512]{1,0:T(8,128)} %get-tuple-element.222.dh_keep, bf16[512,512]{1,0:T(8,128)(2,1)} %copy-done.10, ...), custom_call_target="tpu_custom_call" | custom-call | bytes 4210688 | tf_op jit(solution)/shard_map/norm_one/pallas_call | solution.py:585
  172.8 2.1 collective-permute-done.26.refs_1_
  174.9 1.6 collective-permute-done.30.other
  176.5 3.0 %late_chips.1 = (f32[176,512]{1,0:T(8,128)}, bf16[176,512]{1,0:T(8,128)(2,1)}) custom-call(s32[4]{0:T(128)} %pad_add_fusion.meta, f32[176,1024]{1,0:T(8,128)} %get-tuple-element.218.own, bf16[176,1024]{1,0:T(8,128)(2,1)} %copy-done.12, bf16[176,1024]{1,0:T(8,128)(2,1)} %copy-done.13, bf16[176,1024]{1,0:T(8,128)(2,1)} %copy-done.14), custom_call_target="tpu_custom_call" | custom-call | bytes 2342912 | tf_op jit(solution)/shard_map/late_chips/pallas_call | solution.py:585
  179.8 1.6 collective-permute-start.33
  181.4 2.4 %collective-permute-start.34 = (bf16[256,512]{1,0:T(8,128)(2,1)}, bf16[256,512]{1,0:T(8,128)(2,1)S(1)}, u32[]{:S(2)}, u32[]{:S(2)}) collective-permute-start(bf16[256,512]{1,0:T(8,128)(2,1)} %get-tuple-element.239), channel_id=1, source_target_pairs={{1,0},{5,1},{0,2},{4,3},{3,4},{7,5},{2,6},{6,7},{9,8},{13,9},{8,10... | collective-permute-start | bytes 786440 | tf_op jit(solution)/shard_map/ppermute | solution.py:1170
  183.8 1.4 collective-permute-done.31
  186.2 3.4 %collective-permute-start.32 = (bf16[176,512]{1,0:T(8,128)(2,1)S(1)}, bf16[176,512]{1,0:T(8,128)(2,1)S(1)}, u32[]{:S(2)}, u32[]{:S(2)}) collective-permute-start(bf16[176,512]{1,0:T(8,128)(2,1)S(1)} %add_convert_fusion.3), channel_id=1, source_target_pairs={{0,2},{1,3},{2,0},{3,1},{4,6},{5,7},{6,4},{7,5},{8,10},{9,11},{10,... | collective-permute-start | bytes 540680 | tf_op jit(solution)/shard_map/ppermute | solution.py:549
  189.6 2.6 %early_out.1 = (bf16[144,1024]{1,0:T(8,128)(2,1)}, f32[256,512]{1,0:T(8,128)}) custom-call(s32[4]{0:T(128)} %pad_add_fusion.meta, bf16[272,512]{1,0:T(8,128)(2,1)} %copy-done, bf16[272,512]{1,0:T(8,128)(2,1)} %copy-done.17), custom_call_target="tpu_custom_call" | custom-call | bytes 1376256 | tf_op jit(solution)/shard_map/early_out/pallas_call | solution.py:585
  192.3 10.6 %collective-permute-done.32 = bf16[176,512]{1,0:T(8,128)(2,1)S(1)} collective-permute-done((bf16[176,512]{1,0:T(8,128)(2,1)S(1)}, bf16[176,512]{1,0:T(8,128)(2,1)S(1)}, u32[]{:S(2)}, u32[]{:S(2)}) %collective-permute-start.32) | collective-permute-done | bytes 180256 | tf_op jit(solution)/shard_map/ppermute | solution.py:549
  203.8 3.0 %place.1 = (bf16[2,256,512]{2,1,0:T(8,128)(2,1)}, f32[2,256,512]{2,1,0:T(8,128)}) custom-call(s32[4]{0:T(128)} %pad_add_fusion.meta, bf16[256,512]{1,0:T(8,128)(2,1)} %copy-done.18, bf16[256,512]{1,0:T(8,128)(2,1)} %copy-done.19, bf16[256,512]{1,0:T(8,128)(2,1)} %copy-done.20, bf16[256,512]{1,0:T(8,128)(2,1)} %copy-done.21), custom_call_target="tpu_custom_call" | custom-call | bytes 2621440 | tf_op jit(solution)/shard_map/place/pallas_call | solution.py:585
  206.9 1.6 collective-permute-done.35.other
  209.2 2.6 %late_pack.1 = (bf16[144,1024]{1,0:T(8,128)(2,1)}, f32[64,512]{1,0:T(8,128)}, bf16[72,2048]{1,0:T(8,128)(2,1)}) custom-call(s32[4]{0:T(128)} %pad_add_fusion.meta, bf16[144,1024]{1,0:T(8,128)(2,1)} %get-tuple-element.249.up_ref, bf16[176,512]{1,0:T(8,128)(2,1)} %copy-done.2, bf16[176,512]{1,0:T(8,128)(2,1)} %copy-done.22), custom_call_target="tpu_custom_call" | custom-call | bytes 1376256 | tf_op jit(solution)/shard_map/late_pack/pallas_call | solution.py:585
  211.8 1.8 collective-permute-done.36.came_ref
  214.3 2.9 %late_out.1 = (f32[64,2048]{1,0:T(8,128)}, f32[64,1536]{1,0:T(8,128)}, f32[64,512]{1,0:T(8,128)}, f32[8,256]{1,0:T(8,128)}) custom-call(s32[4]{0:T(128)} %pad_add_fusion.meta, bf16[144,1024]{1,0:T(8,128)(2,1)} %get-tuple-element.249.up_ref, bf16[144,1024]{1,0:T(8,128)(2,1)} %get-tuple-element.251.late_ref, bf16[72,2048]{1,0:T(8,128)(2,1)} %copy-done.15), custom_call_target="tpu_custom_call" | custom-call | bytes 1941504 | tf_op jit(solution)/shard_map/late_out/pallas_call | solution.py:585
  217.2 1.3 slice.54
  218.5 1.5 slice_bitcast_fusion
  (138 shorter events, 20.7 us)
Async XLA Ops:
  0.6 19.4 %copy-start.9 = (bf16[2,256,512]{2,1,0:T(8,128)(2,1)S(1)}, bf16[2,256,512]{2,1,0:T(8,128)(2,1)}, u32[]{:S(2)}) copy-start(bf16[2,256,512]{2,1,0:T(8,128)(2,1)} %param.31) | copy-start | bytes 1572868
  0.7 12.0 %collective-permute-start = (s32[2]{0:T(128)}, s32[2]{0:T(128)S(1)}, u32[]{:S(2)}, u32[]{:S(2)}) collective-permute-start(s32[2]{0:T(128)} %param.17), channel_id=1, source_target_pairs={{0,4},{4,0},{8,12},{12,8},{16,20},{20,16},{24,28},{28,24},{1,5},{5... | collective-permute-start | bytes 32 | tf_op jit(solution)/shard_map/ppermute | solution.py:539
  2.2 12.9 %collective-permute-start.6 = (bf16[256,512]{1,0:T(8,128)(2,1)S(1)}, bf16[256,512]{1,0:T(8,128)(2,1)S(1)}, u32[]{:S(2)}, u32[]{:S(2)}) collective-permute-start(bf16[256,512]{1,0:T(8,128)(2,1)S(1)} %get-tuple-element.263), channel_id=1, source_target_pairs={{0,1},{1,5},{2,0},{3,4},{4,3},{5,7},{6,2},{7,6},{8,9},{9,13},{10,8... | collective-permute-start | bytes 786440 | tf_op jit(solution)/shard_map/ppermute | solution.py:563
  5.0 10.3 %collective-permute-start.5 = (bf16[256,512]{1,0:T(8,128)(2,1)S(1)}, bf16[256,512]{1,0:T(8,128)(2,1)S(1)}, u32[]{:S(2)}, u32[]{:S(2)}) collective-permute-start(bf16[256,512]{1,0:T(8,128)(2,1)S(1)} %get-tuple-element.264), channel_id=1, source_target_pairs={{0,0},{1,4},{2,1},{3,5},{4,2},{5,6},{6,3},{7,7},{8,8},{9,12},{10,9... | collective-permute-start | bytes 786440 | tf_op jit(solution)/shard_map/ppermute | solution.py:563
  9.2 25.7 %copy-start.11 = (bf16[224,1024]{1,0:T(8,128)(2,1)S(1)}, bf16[224,1024]{1,0:T(8,128)(2,1)}, u32[]{:S(2)}) copy-start(bf16[224,1024]{1,0:T(8,128)(2,1)} %get-tuple-element.149) | copy-start | bytes 1376260
  9.2 6.6 %collective-permute-start.1 = (bf16[168,1024]{1,0:T(8,128)(2,1)}, bf16[168,1024]{1,0:T(8,128)(2,1)S(1)}, u32[]{:S(2)}, u32[]{:S(2)}) collective-permute-start(bf16[168,1024]{1,0:T(8,128)(2,1)} %get-tuple-element.138), channel_id=1, source_target_pairs={{0,4},{4,0},{8,12},{12,8},{16,20},{20,16},{24,28},{28,24},{1,5},{5... | collective-permute-start | bytes 1032200 | tf_op jit(solution)/shard_map/ppermute | solution.py:539
  15.2 19.8 %copy-start.31 = (bf16[256,512]{1,0:T(8,128)(2,1)}, bf16[256,512]{1,0:T(8,128)(2,1)S(1)}, u32[]{:S(2)}) copy-start(bf16[256,512]{1,0:T(8,128)(2,1)S(1)} %collective-permute-done.6.refs_5_) | copy-start | bytes 786436
  15.2 19.8 %copy-start.32 = (bf16[256,512]{1,0:T(8,128)(2,1)}, bf16[256,512]{1,0:T(8,128)(2,1)S(1)}, u32[]{:S(2)}) copy-start(bf16[256,512]{1,0:T(8,128)(2,1)S(1)} %collective-permute-done.5.refs_4_) | copy-start | bytes 786436
  15.2 21.7 %collective-permute-start.7 = (bf16[256,512]{1,0:T(8,128)(2,1)S(1)}, bf16[256,512]{1,0:T(8,128)(2,1)}, u32[]{:S(2)}, u32[]{:S(2)}) collective-permute-start(bf16[256,512]{1,0:T(8,128)(2,1)S(1)} %collective-permute-done.5.refs_4_), channel_id=1, source_target_pairs={{0,4},{4,0},{8,12},{12,8},{16,20},{20,16},{24,28},{28,24},{1,5},{5... | collective-permute-start | bytes 786440 | tf_op jit(solution)/shard_map/ppermute | solution.py:539
  15.8 22.5 %collective-permute-start.8 = (bf16[256,512]{1,0:T(8,128)(2,1)S(1)}, bf16[256,512]{1,0:T(8,128)(2,1)S(1)}, u32[]{:S(2)}, u32[]{:S(2)}) collective-permute-start(bf16[256,512]{1,0:T(8,128)(2,1)S(1)} %collective-permute-done.6.refs_5_), channel_id=1, source_target_pairs={{0,4},{4,0},{8,12},{12,8},{16,20},{20,16},{24,28},{28,24},{1,5},{5... | collective-permute-start | bytes 786440 | tf_op jit(solution)/shard_map/ppermute | solution.py:539
  16.8 23.2 %copy-start.16 = (bf16[144,1024]{1,0:T(8,128)(2,1)}, bf16[144,1024]{1,0:T(8,128)(2,1)S(1)}, u32[]{:S(2)}) copy-start(bf16[144,1024]{1,0:T(8,128)(2,1)S(1)} %pad_maximum_fusion.2.refs_0_) | copy-start | bytes 884740
  16.8 10.8 %collective-permute-start.4 = (bf16[144,1024]{1,0:T(8,128)(2,1)S(1)}, bf16[144,1024]{1,0:T(8,128)(2,1)S(1)}, u32[]{:S(2)}, u32[]{:S(2)}) collective-permute-start(bf16[144,1024]{1,0:T(8,128)(2,1)S(1)} %pad_maximum_fusion.2.refs_0_), channel_id=1, source_target_pairs={{0,24},{4,28},{8,16},{12,20},{16,8},{20,12},{24,0},{28,4},{1,25},{... | collective-permute-start | bytes 884744 | tf_op jit(solution)/shard_map/ppermute | solution.py:544
  19.6 14.0 %collective-permute-start.3 = (bf16[144,1024]{1,0:T(8,128)(2,1)S(1)}, bf16[144,1024]{1,0:T(8,128)(2,1)S(1)}, u32[]{:S(2)}, u32[]{:S(2)}) collective-permute-start(bf16[144,1024]{1,0:T(8,128)(2,1)S(1)} %pad_maximum_fusion.2.refs_0_), channel_id=1, source_target_pairs={{0,16},{4,20},{8,24},{12,28},{16,0},{20,4},{24,8},{28,12},{1,17},{... | collective-permute-start | bytes 884744 | tf_op jit(solution)/shard_map/ppermute | solution.py:544
  20.1 14.9 %collective-permute-start.2 = (bf16[144,1024]{1,0:T(8,128)(2,1)S(1)}, bf16[144,1024]{1,0:T(8,128)(2,1)}, u32[]{:S(2)}, u32[]{:S(2)}) collective-permute-start(bf16[144,1024]{1,0:T(8,128)(2,1)S(1)} %pad_maximum_fusion.2.refs_0_), channel_id=1, source_target_pairs={{0,8},{4,12},{8,0},{12,4},{16,24},{20,28},{24,16},{28,20},{1,9},{5... | collective-permute-start | bytes 884744 | tf_op jit(solution)/shard_map/ppermute | solution.py:544
  27.6 19.3 %collective-permute-start.10 = (bf16[256,512]{1,0:T(8,128)(2,1)S(1)}, bf16[256,512]{1,0:T(8,128)(2,1)S(1)}, u32[]{:S(2)}, u32[]{:S(2)}) collective-permute-start(bf16[256,512]{1,0:T(8,128)(2,1)S(1)} %get-tuple-element.261), channel_id=1, source_target_pairs={{0,1},{1,5},{2,0},{3,4},{4,3},{5,7},{6,2},{7,6},{8,9},{9,13},{10,8... | collective-permute-start | bytes 786440 | tf_op jit(solution)/shard_map/ppermute | solution.py:563
  33.6 13.3 %collective-permute-start.9 = (bf16[256,512]{1,0:T(8,128)(2,1)S(1)}, bf16[256,512]{1,0:T(8,128)(2,1)}, u32[]{:S(2)}, u32[]{:S(2)}) collective-permute-start(bf16[256,512]{1,0:T(8,128)(2,1)S(1)} %get-tuple-element.262), channel_id=1, source_target_pairs={{0,0},{1,4},{2,1},{3,5},{4,2},{5,6},{6,3},{7,7},{8,8},{9,12},{10,9... | collective-permute-start | bytes 786440 | tf_op jit(solution)/shard_map/ppermute | solution.py:563
  35.0 30.5 %collective-permute-start.13 = (bf16[320,1024]{1,0:T(8,128)(2,1)S(1)}, bf16[320,1024]{1,0:T(8,128)(2,1)S(1)}, u32[]{:S(2)}, u32[]{:S(2)}) collective-permute-start(bf16[320,1024]{1,0:T(8,128)(2,1)S(1)} %pad_maximum_fusion.1.refs_0_), channel_id=1, source_target_pairs={{0,24},{4,28},{8,16},{12,20},{16,8},{20,12},{24,0},{28,4},{1,25},{... | collective-permute-start | bytes 1966088 | tf_op jit(solution)/shard_map/ppermute | solution.py:544
  36.9 30.6 %collective-permute-start.12 = (bf16[320,1024]{1,0:T(8,128)(2,1)S(1)}, bf16[320,1024]{1,0:T(8,128)(2,1)S(1)}, u32[]{:S(2)}, u32[]{:S(2)}) collective-permute-start(bf16[320,1024]{1,0:T(8,128)(2,1)S(1)} %pad_maximum_fusion.1.refs_0_), channel_id=1, source_target_pairs={{0,16},{4,20},{8,24},{12,28},{16,0},{20,4},{24,8},{28,12},{1,17},{... | collective-permute-start | bytes 1966088 | tf_op jit(solution)/shard_map/ppermute | solution.py:544
  38.2 29.3 %collective-permute-start.11 = (bf16[320,1024]{1,0:T(8,128)(2,1)S(1)}, bf16[320,1024]{1,0:T(8,128)(2,1)S(1)}, u32[]{:S(2)}, u32[]{:S(2)}) collective-permute-start(bf16[320,1024]{1,0:T(8,128)(2,1)S(1)} %pad_maximum_fusion.1.refs_0_), channel_id=1, source_target_pairs={{0,8},{4,12},{8,0},{12,4},{16,24},{20,28},{24,16},{28,20},{1,9},{5... | collective-permute-start | bytes 1966088 | tf_op jit(solution)/shard_map/ppermute | solution.py:544
  46.9 18.6 %copy-start.33 = (bf16[256,512]{1,0:T(8,128)(2,1)}, bf16[256,512]{1,0:T(8,128)(2,1)S(1)}, u32[]{:S(2)}) copy-start(bf16[256,512]{1,0:T(8,128)(2,1)S(1)} %collective-permute-done.10.refs_5_) | copy-start | bytes 786436
  46.9 18.6 %collective-permute-start.14 = (bf16[256,512]{1,0:T(8,128)(2,1)}, bf16[256,512]{1,0:T(8,128)(2,1)S(1)}, u32[]{:S(2)}, u32[]{:S(2)}) collective-permute-start(bf16[256,512]{1,0:T(8,128)(2,1)} %collective-permute-done.9.refs_4_), channel_id=1, source_target_pairs={{0,4},{4,0},{8,12},{12,8},{16,20},{20,16},{24,28},{28,24},{1,5},{5... | collective-permute-start | bytes 786440 | tf_op jit(solution)/shard_map/ppermute | solution.py:539
  52.3 13.2 %collective-permute-start.15 = (bf16[256,512]{1,0:T(8,128)(2,1)S(1)}, bf16[256,512]{1,0:T(8,128)(2,1)S(1)}, u32[]{:S(2)}, u32[]{:S(2)}) collective-permute-start(bf16[256,512]{1,0:T(8,128)(2,1)S(1)} %collective-permute-done.10.refs_5_), channel_id=1, source_target_pairs={{0,4},{4,0},{8,12},{12,8},{16,20},{20,16},{24,28},{28,24},{1,5},{5... | collective-permute-start | bytes 786440 | tf_op jit(solution)/shard_map/ppermute | solution.py:539
  67.5 2.2 collective-permute-start.16
  83.7 12.1 %collective-permute-start.17 = (bf16[1024,512]{1,0:T(8,128)(2,1)}, bf16[1024,512]{1,0:T(8,128)(2,1)S(1)}, u32[]{:S(2)}, u32[]{:S(2)}) collective-permute-start(bf16[1024,512]{1,0:T(8,128)(2,1)} %get-tuple-element.165), channel_id=1, source_target_pairs={{0,4},{4,0},{8,12},{12,8},{16,20},{20,16},{24,28},{28,24},{1,5},{5... | collective-permute-start | bytes 3145736 | tf_op jit(solution)/shard_map/ppermute | solution.py:539
  83.9 11.9 %collective-permute-start.18 = (bf16[512,512]{1,0:T(8,128)(2,1)}, bf16[512,512]{1,0:T(8,128)(2,1)S(1)}, u32[]{:S(2)}, u32[]{:S(2)}) collective-permute-start(bf16[512,512]{1,0:T(8,128)(2,1)} %get-tuple-element.168), channel_id=1, source_target_pairs={{0,4},{4,0},{8,12},{12,8},{16,20},{20,16},{24,28},{28,24},{1,5},{5... | collective-permute-start | bytes 1572872 | tf_op jit(solution)/shard_map/ppermute | solution.py:539
  92.3 32.4 %collective-permute-start.21 = (bf16[272,1024]{1,0:T(8,128)(2,1)}, bf16[272,1024]{1,0:T(8,128)(2,1)S(1)}, u32[]{:S(2)}, u32[]{:S(2)}) collective-permute-start(bf16[272,1024]{1,0:T(8,128)(2,1)} %get-tuple-element.183), channel_id=1, source_target_pairs={{0,8},{4,12},{8,0},{12,4},{16,24},{20,28},{24,16},{28,20},{1,9},{5... | collective-permute-start | bytes 1671176 | tf_op jit(solution)/shard_map/ppermute | solution.py:544
  94.0 30.7 %collective-permute-start.22 = (bf16[272,1024]{1,0:T(8,128)(2,1)}, bf16[272,1024]{1,0:T(8,128)(2,1)S(1)}, u32[]{:S(2)}, u32[]{:S(2)}) collective-permute-start(bf16[272,1024]{1,0:T(8,128)(2,1)} %get-tuple-element.184), channel_id=1, source_target_pairs={{0,16},{4,20},{8,24},{12,28},{16,0},{20,4},{24,8},{28,12},{1,17},{... | collective-permute-start | bytes 1671176 | tf_op jit(solution)/shard_map/ppermute | solution.py:544
  94.7 30.0 %collective-permute-start.23 = (bf16[272,1024]{1,0:T(8,128)(2,1)}, bf16[272,1024]{1,0:T(8,128)(2,1)S(1)}, u32[]{:S(2)}, u32[]{:S(2)}) collective-permute-start(bf16[272,1024]{1,0:T(8,128)(2,1)} %get-tuple-element.185), channel_id=1, source_target_pairs={{0,24},{4,28},{8,16},{12,20},{16,8},{20,12},{24,0},{28,4},{1,25},{... | collective-permute-start | bytes 1671176 | tf_op jit(solution)/shard_map/ppermute | solution.py:544
  104.9 19.8 %collective-permute-start.19 = (bf16[256,512]{1,0:T(8,128)(2,1)}, bf16[256,512]{1,0:T(8,128)(2,1)S(1)}, u32[]{:S(2)}, u32[]{:S(2)}) collective-permute-start(bf16[256,512]{1,0:T(8,128)(2,1)} %get-tuple-element.177), channel_id=1, source_target_pairs={{0,0},{4,1},{1,2},{5,3},{2,4},{6,5},{3,6},{7,7},{8,8},{12,9},{9,10... | collective-permute-start | bytes 786440 | tf_op jit(solution)/shard_map/ppermute | solution.py:1120
  106.5 18.2 %collective-permute-start.20 = (bf16[256,512]{1,0:T(8,128)(2,1)}, bf16[256,512]{1,0:T(8,128)(2,1)S(1)}, u32[]{:S(2)}, u32[]{:S(2)}) collective-permute-start(bf16[256,512]{1,0:T(8,128)(2,1)} %get-tuple-element.178), channel_id=1, source_target_pairs={{1,0},{5,1},{0,2},{4,3},{3,4},{7,5},{2,6},{6,7},{9,8},{13,9},{8,10... | collective-permute-start | bytes 786440 | tf_op jit(solution)/shard_map/ppermute | solution.py:1120
  124.7 17.7 %copy-start.18 = (bf16[256,512]{1,0:T(8,128)(2,1)}, bf16[256,512]{1,0:T(8,128)(2,1)S(1)}, u32[]{:S(2)}) copy-start(bf16[256,512]{1,0:T(8,128)(2,1)S(1)} %collective-permute-done.19.y0) | copy-start | bytes 786436
  124.8 17.7 %copy-start.19 = (bf16[256,512]{1,0:T(8,128)(2,1)}, bf16[256,512]{1,0:T(8,128)(2,1)S(1)}, u32[]{:S(2)}) copy-start(bf16[256,512]{1,0:T(8,128)(2,1)S(1)} %collective-permute-done.20.y1) | copy-start | bytes 786436
  129.3 13.2 %copy-start.7 = (f32[272,512]{1,0:T(8,128)S(1)}, f32[272,512]{1,0:T(8,128)}, u32[]{:S(2)}) copy-start(f32[272,512]{1,0:T(8,128)} %get-tuple-element.191) | copy-start | bytes 1671172
  129.3 13.3 %copy-start.23 = (f32[1,128]{1,0:T(1,128)S(1)}, f32[1,128]{1,0:T(1,128)}, u32[]{:S(2)}) copy-start(f32[1,128]{1,0:T(1,128)} %get-tuple-element.213) | copy-start | bytes 1540
  129.3 13.3 %copy-start.24 = (f32[1,128]{1,0:T(1,128)S(1)}, f32[1,128]{1,0:T(1,128)}, u32[]{:S(2)}) copy-start(f32[1,128]{1,0:T(1,128)} %get-tuple-element.215) | copy-start | bytes 1540
  129.3 13.2 %collective-permute-start.24 = (bf16[272,512]{1,0:T(8,128)(2,1)}, bf16[272,512]{1,0:T(8,128)(2,1)S(1)}, u32[]{:S(2)}, u32[]{:S(2)}) collective-permute-start(bf16[272,512]{1,0:T(8,128)(2,1)} %get-tuple-element.201), channel_id=1, source_target_pairs={{0,1},{1,0},{2,3},{3,2},{4,5},{5,4},{6,7},{7,6},{8,9},{9,8},{10,11... | collective-permute-start | bytes 835592 | tf_op jit(solution)/shard_map/ppermute | solution.py:549
  152.3 16.0 %collective-permute-start.28 = (bf16[512,512]{1,0:T(8,128)(2,1)}, bf16[512,512]{1,0:T(8,128)(2,1)S(1)}, u32[]{:S(2)}, u32[]{:S(2)}) collective-permute-start(bf16[512,512]{1,0:T(8,128)(2,1)} %get-tuple-element.223), channel_id=1, source_target_pairs={{0,4},{4,0},{8,12},{12,8},{16,20},{20,16},{24,28},{28,24},{1,5},{5... | collective-permute-start | bytes 1572872 | tf_op jit(solution)/shard_map/ppermute | solution.py:539
  152.6 15.7 %collective-permute-start.29 = (bf16[272,512]{1,0:T(8,128)(2,1)S(1)}, bf16[272,512]{1,0:T(8,128)(2,1)S(1)}, u32[]{:S(2)}, u32[]{:S(2)}) collective-permute-start(bf16[272,512]{1,0:T(8,128)(2,1)S(1)} %add_convert_fusion.1), channel_id=1, source_target_pairs={{0,2},{1,3},{2,0},{3,1},{4,6},{5,7},{6,4},{7,5},{8,10},{9,11},{10,... | collective-permute-start | bytes 835592 | tf_op jit(solution)/shard_map/ppermute | solution.py:549
  152.6 20.2 %collective-permute-start.25 = (bf16[176,1024]{1,0:T(8,128)(2,1)}, bf16[176,1024]{1,0:T(8,128)(2,1)S(1)}, u32[]{:S(2)}, u32[]{:S(2)}) collective-permute-start(bf16[176,1024]{1,0:T(8,128)(2,1)} %get-tuple-element.219), channel_id=1, source_target_pairs={{0,8},{4,12},{8,0},{12,4},{16,24},{20,28},{24,16},{28,20},{1,9},{5... | collective-permute-start | bytes 1081352 | tf_op jit(solution)/shard_map/ppermute | solution.py:544
  156.8 18.1 %collective-permute-start.26 = (bf16[176,1024]{1,0:T(8,128)(2,1)}, bf16[176,1024]{1,0:T(8,128)(2,1)S(1)}, u32[]{:S(2)}, u32[]{:S(2)}) collective-permute-start(bf16[176,1024]{1,0:T(8,128)(2,1)} %get-tuple-element.220), channel_id=1, source_target_pairs={{0,16},{4,20},{8,24},{12,28},{16,0},{20,4},{24,8},{28,12},{1,17},{... | collective-permute-start | bytes 1081352 | tf_op jit(solution)/shard_map/ppermute | solution.py:544
  157.4 17.5 %collective-permute-start.27 = (bf16[176,1024]{1,0:T(8,128)(2,1)}, bf16[176,1024]{1,0:T(8,128)(2,1)S(1)}, u32[]{:S(2)}, u32[]{:S(2)}) collective-permute-start(bf16[176,1024]{1,0:T(8,128)(2,1)} %get-tuple-element.221), channel_id=1, source_target_pairs={{0,24},{4,28},{8,16},{12,20},{16,8},{20,12},{24,0},{28,4},{1,25},{... | collective-permute-start | bytes 1081352 | tf_op jit(solution)/shard_map/ppermute | solution.py:544
  168.4 8.1 %collective-permute-start.30 = (bf16[272,512]{1,0:T(8,128)(2,1)S(1)}, bf16[272,512]{1,0:T(8,128)(2,1)S(1)}, u32[]{:S(2)}, u32[]{:S(2)}) collective-permute-start(bf16[272,512]{1,0:T(8,128)(2,1)S(1)} %add_convert_fusion.mine), channel_id=1, source_target_pairs={{0,1},{1,0},{2,3},{3,2},{4,5},{5,4},{6,7},{7,6},{8,9},{9,8},{10,11... | collective-permute-start | bytes 835592 | tf_op jit(solution)/shard_map/ppermute | solution.py:549
  179.5 5.7 %collective-permute-start.31 = (bf16[176,512]{1,0:T(8,128)(2,1)}, bf16[176,512]{1,0:T(8,128)(2,1)S(1)}, u32[]{:S(2)}, u32[]{:S(2)}) collective-permute-start(bf16[176,512]{1,0:T(8,128)(2,1)} %get-tuple-element.234), channel_id=1, source_target_pairs={{0,1},{1,0},{2,3},{3,2},{4,5},{5,4},{6,7},{7,6},{8,9},{9,8},{10,11... | collective-permute-start | bytes 540680 | tf_op jit(solution)/shard_map/ppermute | solution.py:549
  179.8 12.5 %collective-permute-start.33 = (bf16[256,512]{1,0:T(8,128)(2,1)}, bf16[256,512]{1,0:T(8,128)(2,1)S(1)}, u32[]{:S(2)}, u32[]{:S(2)}) collective-permute-start(bf16[256,512]{1,0:T(8,128)(2,1)} %get-tuple-element.238), channel_id=1, source_target_pairs={{0,0},{4,1},{1,2},{5,3},{2,4},{6,5},{3,6},{7,7},{8,8},{12,9},{9,10... | collective-permute-start | bytes 786440 | tf_op jit(solution)/shard_map/ppermute | solution.py:1170
  181.4 10.9 %collective-permute-start.34 = (bf16[256,512]{1,0:T(8,128)(2,1)}, bf16[256,512]{1,0:T(8,128)(2,1)S(1)}, u32[]{:S(2)}, u32[]{:S(2)}) collective-permute-start(bf16[256,512]{1,0:T(8,128)(2,1)} %get-tuple-element.239), channel_id=1, source_target_pairs={{1,0},{5,1},{0,2},{4,3},{3,4},{7,5},{2,6},{6,7},{9,8},{13,9},{8,10... | collective-permute-start | bytes 786440 | tf_op jit(solution)/shard_map/ppermute | solution.py:1170
  186.2 16.6 %collective-permute-start.32 = (bf16[176,512]{1,0:T(8,128)(2,1)S(1)}, bf16[176,512]{1,0:T(8,128)(2,1)S(1)}, u32[]{:S(2)}, u32[]{:S(2)}) collective-permute-start(bf16[176,512]{1,0:T(8,128)(2,1)S(1)} %add_convert_fusion.3), channel_id=1, source_target_pairs={{0,2},{1,3},{2,0},{3,1},{4,6},{5,7},{6,4},{7,5},{8,10},{9,11},{10,... | collective-permute-start | bytes 540680 | tf_op jit(solution)/shard_map/ppermute | solution.py:549
  202.9 5.6 %collective-permute-start.35 = (bf16[176,512]{1,0:T(8,128)(2,1)S(1)}, bf16[176,512]{1,0:T(8,128)(2,1)S(1)}, u32[]{:S(2)}, u32[]{:S(2)}) collective-permute-start(bf16[176,512]{1,0:T(8,128)(2,1)S(1)} %add_convert_fusion.2.mine), channel_id=1, source_target_pairs={{0,1},{1,0},{2,3},{3,2},{4,5},{5,4},{6,7},{7,6},{8,9},{9,8},{10,11... | collective-permute-start | bytes 540680 | tf_op jit(solution)/shard_map/ppermute | solution.py:549
  211.8 1.8 collective-permute-start.36
  (26 other events, 112.6 us)

commit v2 on v1

--- a/solution.py
+++ b/solution.py
@@ -92,10 +92,8 @@
             in_specs=[at(0), at(1), at(2), at(0), row, row],
             out_specs=(at(0), pl.BlockSpec((2, full, 1), lambda pair, _: (pair, 0, 0))),
         ),
-        cost_estimate=pl.CostEstimate(
-            flops=12 * full * full * cols, bytes_accessed=10 * full * cols, transcendentals=0
-        ),
-        compiler_params=pltpu.CompilerParams(vmem_limit_bytes=60 << 20),
+        cost_estimate=pl.CostEstimate(flops=0, bytes_accessed=0, transcendentals=0),
+        compiler_params=pltpu.CompilerParams(vmem_limit_bytes=32 << 20),
         name="attn_fwd",
     )(length, qkv, qkv, qkv, rel_rev, bias_u, bias_v)
 
@@ -178,10 +176,8 @@
             out_specs=(out,) * 4 + (out_row, out_row),
             scratch_shapes=[pltpu.VMEM((2 * HD, full), f32)] * 3,
         ),
-        cost_estimate=pl.CostEstimate(
-            flops=36 * full * full * HD * 4, bytes_accessed=20 * full * HD * 2, transcendentals=0
-        ),
-        compiler_params=pltpu.CompilerParams(vmem_limit_bytes=60 << 20),
+        cost_estimate=pl.CostEstimate(flops=0, bytes_accessed=0, transcendentals=0),
+        compiler_params=pltpu.CompilerParams(vmem_limit_bytes=32 << 20),
         name="attn_bwd",
     )(length, qkv, qkv, qkv, rel_rev, bias_u, bias_v, lse, d_out)
 
@@ -544,6 +540,11 @@
     return lax.ppermute(values, "fsdp", [(i, i ^ (2 * mask)) for i in range(size)])
 
 
+def swap_axis(values, turn):
+    size = lax.axis_size("fsdp")
+    return lax.ppermute(values, "fsdp", [(i, i ^ (2 << ((i & 1) ^ turn))) for i in range(size)])
+
+
 def swap_seq(values, mask):
     size = lax.axis_size("seq")
     return lax.ppermute(values, "seq", [(i, i ^ mask) for i in range(size)])
@@ -577,7 +578,7 @@
     return pl.BlockSpec(shape, lambda *_: (0,) * len(shape))
 
 
-def kernel_call(body, name, meta, args, outs, *, grid=(1,), in_specs=None, out_specs=None, scratch=(), flops=0):
+def kernel_call(body, name, meta, args, outs, *, grid=(1,), in_specs=None, out_specs=None, scratch=(), flops=0, vmem=32):
     in_specs = in_specs or [whole(*a.shape) for a in args]
     out_specs = out_specs or [whole(*shape) for shape, _ in outs]
     moved = sum(a.size * a.dtype.itemsize for a in args)
@@ -592,30 +593,42 @@
             out_specs=out_specs,
             scratch_shapes=scratch,
         ),
-        compiler_params=pltpu.CompilerParams(vmem_limit_bytes=60 << 20),
-        cost_estimate=pl.CostEstimate(flops=flops, bytes_accessed=moved, transcendentals=0),
+        compiler_params=pltpu.CompilerParams(vmem_limit_bytes=vmem << 20),
+        cost_estimate=pl.CostEstimate(flops=0, bytes_accessed=0, transcendentals=0),
         name=name,
     )(meta, *args)
 
 
 TN = (((0,), (0,)), ((), ()))
 CORE, CHIP, RANK, LIVE = range(4)
+DIGIT = 128
 
 
 def aligned(index, size):
     return pl.multiple_of(index * size, size)
 
 
-def pack_body(meta, qkv_ref, rel_ref, up_ref, out_ref, down_ref, *refs):
+def own_place():
+    device = lax.axis_index("fsdp")
+    return device & 1, device >> 1, lax.axis_index("seq")
+
+
+def pack_body(lengths_ref, qkv_ref, rel_ref, up_ref, out_ref, down_ref, *refs):
     small, (attn_ref, feed_ref, send_ref) = refs[:8], refs[8:]
-    core = meta[CORE]
+    core, _, _ = own_place()
     shard = qkv_ref.shape[0]
     qkv, rel, up, out, down = qkv_ref[...], rel_ref[...], up_ref[...], out_ref[...], down_ref[...]
     heads, hd = rel.shape[1] // HEAD_DIM // 2, HEAD_DIM
     unit = up.shape[1] // 8
     packs, ups = [], []
     row = jnp.concatenate([ref[i : i + 1] for ref in small for i in range(ref.shape[0])], axis=1)
-    row = jnp.concatenate([row, jnp.zeros((1, 4 * heads * hd - row.shape[1]), row.dtype)], axis=1)
+    lane = lax.broadcasted_iota(jnp.int32, (1, 4 * heads * hd - row.shape[1]), 1)
+    digits = jnp.zeros(lane.shape, f32)
+    for slot in range(lengths_ref.shape[0]):
+        high = lengths_ref[slot] // DIGIT
+        for at, digit in ((2 * slot, high), (2 * slot + 1, lengths_ref[slot] - high * DIGIT)):
+            digits = jnp.where(lane == at, digit.astype(f32), digits)
+    row = jnp.concatenate([row, digits.astype(row.dtype)], axis=1)
     rows = jnp.broadcast_to(row, (8, row.shape[1]))
     for side in (0, 1):
         parts = [
@@ -641,14 +654,14 @@
     feed_ref[shard + shard // 2 :] = jnp.concatenate([down[: 2 * shard], down[2 * shard :]], axis=1)
 
 
-def ordered(meta, own, other):
-    first = meta[CORE] == 0
+def ordered(core, own, other):
+    first = core == 0
     return jnp.concatenate([jnp.where(first, own, other), jnp.where(first, other, own)], axis=0)
 
 
-def slot_block(meta, step, own, other, store):
-    turn = (step >> 1) ^ (meta[RANK] & 1)
-    local = (step & 1) == meta[CORE]
+def slot_block(core, rank, step, own, other, store):
+    turn = (step >> 1) ^ (rank & 1)
+    local = (step & 1) == core
     for t in (0, 1):
         pl.when(local & (turn == t))(functools.partial(store, own[t]))
         pl.when(jnp.logical_not(local) & (turn == t))(functools.partial(store, other[t]))
@@ -661,10 +674,10 @@
     return centered * inv_std, inv_std
 
 
-def project_body(meta, *refs):
+def project_body(_, *refs):
     packs, own_x, other_x = refs[0:4], refs[4:6], refs[6:8]
-    table_ref, qkv_ref, h_ref, x_ref, rel_ref, w_ref, vec_ref, up_ref, bias_ref = refs[8:17]
-    step, chip = pl.program_id(0), meta[CHIP]
+    table_ref, qkv_ref, h_ref, x_ref, rel_ref, w_ref, vec_ref, up_ref, *bias_refs = refs[8:18]
+    step, (core, chip, rank) = pl.program_id(0), own_place()
     width = w_ref.shape[0]
     shard = width // 8
     span = qkv_ref.shape[1]
@@ -672,13 +685,13 @@
 
     @pl.when(step == 0)
     def _():
-        first = meta[CORE] == 0
+        first = core == 0
         vec_ref[...] = jnp.zeros_like(vec_ref)
         own_rows = []
         for k in range(4):
             at = pl.ds(aligned(chip ^ k, 2 * shard), 2 * shard)
             own, other = packs[k][: shard + 8], packs[k][shard + 8 :]
-            w_ref[at, :] = ordered(meta, own[:shard], other[:shard])
+            w_ref[at, :] = ordered(core, own[:shard], other[:shard])
             own_row, other_row = own[shard : shard + 1].astype(f32), other[shard : shard + 1].astype(f32)
             own_rows.append(own_row)
             low, high = jnp.where(first, own_row, other_row), jnp.where(first, other_row, own_row)
@@ -694,12 +707,12 @@
             high = jnp.where(even, own_rows[k + 1], own_rows[k])
             for row, source in enumerate((2, 3)):
                 piece = slice(source * shard, (source + 1) * shard)
-                bias_ref[row : row + 1, at] = jnp.concatenate([low[:, piece], high[:, piece]], axis=1)
+                bias_refs[row][:, at] = jnp.concatenate([low[:, piece], high[:, piece]], axis=1)
 
     def copy(ref):
         x_ref[...] = ref[...]
 
-    slot_block(meta, step, own_x, other_x, copy)
+    slot_block(core, rank, step, own_x, other_x, copy)
     x_hat, _ = norm_rows(x_ref[...].astype(f32))
     h = (x_hat * vec_ref[0:1, :] + vec_ref[1:2, :]).astype(bf)
     h_ref[...] = h
@@ -710,69 +723,81 @@
 def feed_body(meta, *refs):
     packs, own_g, other_g = refs[0:4], refs[4:6], refs[6:8]
     x_ref, o_own, o_other, vec_ref, bias_ref = refs[8:13]
-    (g_ref, df_ref, h_ref, dy_ref, y1_ref, y_keep, dh_keep, dh_send, y_send, sum_ref, wo_mine) = refs[13:24]
-    up_w, down_w, wo_theirs = refs[24:27]
+    dy_ref, x_hat_ref, rstd_ref, y_keep, dh_ref, y_send, wo_mine = refs[13:20]
+    outs = refs[20:24]
+    up_w, down_w, wo_theirs, up_acc, down_acc, sums = refs[24:30]
     step, chip, core = pl.program_id(0), meta[CHIP], meta[CORE]
     width = up_w.shape[0]
     shard, unit, block = width // 8, down_w.shape[0] // 4, x_ref.shape[0]
     fold = shard // 2
+    unfold = lambda rows: jnp.concatenate([rows[:, :width], rows[:, width:]], axis=0)
 
     @pl.when(step == 0)
     def _():
-        sum_ref[...] = jnp.zeros_like(sum_ref)
-        for k in range(4):
-            pack = packs[k]
-            own, other = pack[:shard], pack[shard + fold + 2 * shard : 2 * shard + fold + 2 * shard]
-            up_w[pl.ds(aligned(chip ^ k, 2 * shard), 2 * shard), :] = ordered(meta, own, other)
+        sums[...] = jnp.zeros_like(sums)
+        up_acc[...] = jnp.zeros_like(up_acc)
+        down_acc[...] = jnp.zeros_like(down_acc)
+        masks = (0, 1 + core, 2 - core, 3)
+        for pack_ref, k in zip(packs, masks):
+            pack, other = pack_ref[: 3 * shard + fold], pack_ref[3 * shard + fold :]
+            up_w[pl.ds(aligned(chip ^ k, 2 * shard), 2 * shard), :] = ordered(core, pack[:shard], other[:shard])
             at = pl.ds(aligned(chip ^ k, shard), shard)
-            rows = pack[shard : shard + fold]
-            wo_mine[at, :] = jnp.concatenate([rows[:, :width], rows[:, width:]], axis=0)
-            rows = pack[4 * shard + fold :]
-            wo_theirs[at, :] = jnp.concatenate([rows[:, :width], rows[:, width:]], axis=0)
-            rows = pack[shard + fold : 3 * shard + fold]
-            down_w[pl.ds(aligned(chip ^ k, unit), unit), :] = jnp.concatenate(
-                [rows[:, :width], rows[:, width:]], axis=0
-            )
+            wo_mine[at, :] = unfold(pack[shard : shard + fold])
+            wo_theirs[at, :] = unfold(other[shard:])
+            down_w[pl.ds(aligned(chip ^ k, unit), unit), :] = unfold(pack[shard + fold :])
 
     at = step * block + lax.broadcasted_iota(jnp.int32, (block, 1), 0)
 
     def load(ref):
         dy_ref[...] = jnp.where(at < meta[LIVE], ref[...].astype(f32), 0.0).astype(bf)
 
-    slot_block(meta, step, own_g, other_g, load)
+    slot_block(core, meta[RANK], step, own_g, other_g, load)
     y1 = x_ref[...].astype(f32) + (dot(o_own[...], wo_mine[...], NN) + dot(o_other[...], wo_theirs[...], NN))
-    y1_ref[...] = y1
-    x_hat, _ = norm_rows(y1)
+    x_hat, inv_std = norm_rows(y1)
+    x_hat_ref[...] = x_hat.astype(bf)
+    rstd_ref[...] = inv_std
     h = (x_hat * vec_ref[2:3, :] + vec_ref[3:4, :]).astype(bf)
-    h_ref[...] = h
     f = dot(h, up_w[...], NN) + bias_ref[...]
     cdf = 0.5 * (1.0 + lax.erf(f * (1.0 / math.sqrt(2.0))))
     g = (f * cdf).astype(bf)
-    g_ref[...] = g
-    z = dot(g, down_w[...], NN)
     dy = dy_ref[...]
     dg = dot(dy, down_w[...], NT)
     df = (dg * (cdf + f * jnp.exp(-0.5 * f * f) * (1.0 / math.sqrt(2.0 * math.pi)))).astype(bf)
-    df_ref[...] = df
+    z = dot(g, down_w[...], NN)
     dh = dot(df, up_w[...], NT)
-    dh_keep[...] = dh
-    dh_send[...] = dh.astype(bf)
-    sum_ref[0:1, :width] += jnp.sum(dh * x_hat, axis=0, keepdims=True)
-    sum_ref[1:2, :width] += jnp.sum(dh, axis=0, keepdims=True)
-    sum_ref[3:4, :] += jnp.sum(df.astype(f32), axis=0, keepdims=True)
+    dh_ref[...] = dh.astype(bf)
+    up_acc[...] += dot(h, df, TN)
+    down_acc[...] += dot(g, dy, TN)
+    sums[0:1, :width] += jnp.sum(dh * x_hat, axis=0, keepdims=True)
+    sums[1:2, :width] += jnp.sum(dh, axis=0, keepdims=True)
+    sums[3:4, :] += jnp.sum(df.astype(f32), axis=0, keepdims=True)
     local = (step & 1) == core
 
     @pl.when(local)
     def _():
         y_keep[...] = y1 + z + vec_ref[4:5, :]
-        sum_ref[2:3, :width] += jnp.sum(dy.astype(f32), axis=0, keepdims=True)
+        sums[2:3, :width] += jnp.sum(dy.astype(f32), axis=0, keepdims=True)
 
     @pl.when(jnp.logical_not(local))
     def _():
         y_send[...] = z.astype(bf)
 
-
-def norm_two_body(meta, y1_ref, dh_keep, dh_came, dy_ref, vec_ref, y_keep, y_came, wo_ref, o_ref, *refs):
+    @pl.when(step == pl.num_programs(0) - 1)
+    def _():
+        rows = 2 * shard
+        for k, out in enumerate(outs):
+            at = pl.ds(aligned(chip ^ k, rows), rows)
+            units = pl.ds(aligned(chip ^ k, unit), unit)
+            tail = [sums[0:1, at], sums[1:2, at], sums[2:3, at], sums[3:4, units]]
+            tail = jnp.concatenate(tail + [jnp.zeros((1, sums.shape[1] - 3 * rows - unit), f32)], axis=1)
+            out[:rows] = up_acc[at, :].astype(out.dtype)
+            out[rows : rows + 8] = jnp.broadcast_to(tail, (8, tail.shape[1])).astype(out.dtype)
+            down = down_acc[units, :]
+            half = unit // 2
+            out[rows + 8 :] = jnp.concatenate([down[:half], down[half:]], axis=1).astype(out.dtype)
+
+
+def norm_two_body(meta, x_hat_ref, rstd_ref, dh_ref, dh_came, dy_ref, vec_ref, y_keep, y_came, wo_ref, o_ref, *refs):
     out0, out1, resid_ref, do_ref, go_ref = refs
     step = pl.program_id(0)
 
@@ -780,11 +805,11 @@
     def _():
         go_ref[...] = jnp.zeros_like(go_ref)
 
-    x_hat, inv_std = norm_rows(y1_ref[...])
-    e = (dh_keep[...] + dh_came[...].astype(f32)) * vec_ref[2:3, :]
+    x_hat = x_hat_ref[...].astype(f32)
+    e = (dh_ref[...].astype(f32) + dh_came[...].astype(f32)) * vec_ref[2:3, :]
     first = jnp.mean(e, axis=1, keepdims=True)
     second = jnp.mean(e * x_hat, axis=1, keepdims=True)
-    grad = dy_ref[...].astype(f32) + inv_std * (e - first - x_hat * second)
+    grad = dy_ref[...].astype(f32) + rstd_ref[...] * (e - first - x_hat * second)
     da = grad.astype(bf)
     do_ref[...] = dot(da, wo_ref[...], NT).astype(bf)
     go_ref[...] += dot(o_ref[...], da, TN)
@@ -805,35 +830,12 @@
             out1[...] = y
 
 
-def feed_grad_body(meta, h_ref, df_ref, sum_ref, g_ref, dy_ref, *outs):
-    k = pl.program_id(0)
-    rows = h_ref.shape[1]
-    grad = dot(h_ref[...], df_ref[...], TN)
-    at = pl.ds(aligned(meta[CHIP] ^ k, rows), rows)
-    unit = df_ref.shape[1] // 4
-    tail = jnp.concatenate(
-        [sum_ref[0:1, at], sum_ref[1:2, at], sum_ref[2:3, at]]
-        + [sum_ref[3:4, pl.ds(aligned(meta[CHIP] ^ k, unit), unit)]],
-        axis=1,
-    )
-    tail = jnp.concatenate([tail, jnp.zeros((1, df_ref.shape[1] - tail.shape[1]), f32)], axis=1)
-    tail = jnp.broadcast_to(tail, (16, tail.shape[1]))
-    down = dot(g_ref[...], dy_ref[...], TN)
-    half = unit // 2
-    for index, out in enumerate(outs):
-
-        @pl.when(k == index)
-        def _():
-            out[:rows] = grad.astype(out.dtype)
-            out[rows : rows + 16] = tail.astype(out.dtype)
-            out[rows + 16 :] = jnp.concatenate([down[:half], down[half:]], axis=1).astype(out.dtype)
-
-
 def qkv_back_body(meta, *refs):
     grads, rels = refs[:6], refs[6:8]
-    w_ref, x_ref, h_ref, table_ref, gu_ref, gv_ref, go_ref = refs[8:15]
-    keep_ref, send_ref = refs[15:17]
-    outs, acc, sums = refs[17:21], refs[21], refs[22]
+    w_ref, x_ref, h_ref, table_ref = refs[8:12]
+    gu_refs, gv_refs, go_ref = refs[12:14], refs[14:16], refs[16]
+    keep_ref, send_ref = refs[17:19]
+    outs, acc, sums = refs[19:23], refs[23], refs[24]
     step, chip = pl.program_id(0), meta[CHIP]
     width = x_ref.shape[1]
     rows = width // 4
@@ -866,15 +868,16 @@
     def _():
         for k, out in enumerate(outs):
             at = pl.ds(aligned(chip ^ k, rows), rows)
-            pair = pl.ds(aligned((chip ^ k) >> 1, rows), rows)
-            tail = [sums[0:1, at], sums[1:2, at], gu_ref[0:1, pair], gv_ref[0:1, pair]]
+            low = (chip ^ k) >> 1 == 0
+            tail = [sums[0:1, at], sums[1:2, at]]
+            tail += [jnp.where(low, a[...], b[...]) for a, b in (gu_refs, gv_refs)]
             tail = jnp.concatenate(tail + [jnp.zeros((1, acc.shape[1] - 4 * rows), f32)], axis=1)
             out[:rows] = acc[at, :].astype(out.dtype)
-            out[rows : rows + 16] = jnp.broadcast_to(tail, (16, tail.shape[1])).astype(out.dtype)
+            out[rows : rows + 8] = jnp.broadcast_to(tail, (8, tail.shape[1])).astype(out.dtype)
             shard = rows // 2
             lines = go_ref[pl.ds(aligned(chip ^ k, shard), shard), :]
             lines = jnp.concatenate([lines[: shard // 2], lines[shard // 2 :]], axis=1)
-            out[rows + 16 :] = lines.astype(out.dtype)
+            out[rows + 8 :] = lines.astype(out.dtype)
 
 
 def norm_one_body(meta, x_ref, dh_keep, dh_came, resid_ref, vec_ref, out0, out1):
@@ -894,10 +897,14 @@
         out1[...] = grad
 
 
-def chip_sum_body(meta, own, *refs):
+def rank_bit(meta, bit):
+    return (meta[RANK] >> bit) & 1
+
+
+def chip_sum_body(meta, own, *refs, bit):
     *came, keep, send = refs
     half = keep.shape[1]
-    for out, side in ((keep, meta[RANK] & 1), (send, 1 - (meta[RANK] & 1))):
+    for out, side in ((keep, rank_bit(meta, bit)), (send, 1 - rank_bit(meta, bit))):
         at = pl.ds(aligned(side, half), half)
         total = own[:, at]
         for ref in came:
@@ -905,79 +912,69 @@
         out[...] = total.astype(out.dtype)
 
 
-def chip_sum(meta, parts, name):
+def chip_sum(meta, parts, name, bit):
     rows, size = parts[0].shape
-    return kernel_call(chip_sum_body, name, meta, parts, [((rows, size // 2), f32), ((rows, size // 2), bf)])
-
-
-def halves(meta, mine, other):
-    low = meta[RANK] & 1 == 0
+    return kernel_call(functools.partial(chip_sum_body, bit=bit), name, meta, parts, [((rows, size // 2), f32), ((rows, size // 2), bf)])
+
+
+def own_rows_first(total, core, shard):
+    theirs = lax.dynamic_slice_in_dim(total, (1 - core) * shard, shard, 0)
+    mine = lax.dynamic_slice_in_dim(total, core * shard, shard, 0)
+    came = swap_core(jnp.concatenate([theirs, total[2 * shard : 2 * shard + 8]], axis=0))
+    return jnp.concatenate([mine, came, total[2 * shard :]], axis=0)
+
+
+def halves(meta, mine, other, bit):
+    low = rank_bit(meta, bit) == 0
     return jnp.concatenate([jnp.where(low, mine, other), jnp.where(low, other, mine)], axis=1)
 
 
-def early_out_body(meta, mine, other, up_ref, down_ref):
-    both = halves(meta, mine[...], other[...])
-    rows, width = up_ref.shape[0], down_ref.shape[1]
-    up_ref[...] = both[:rows]
-    down = both[rows:].astype(f32)
-    down_ref[...] = jnp.concatenate([down[:, :width], down[:, width:]], axis=0)
-
-
-def late_pack_body(meta, up_ref, mine, other, late_ref, out_ref, send_ref):
-    both = halves(meta, mine[...], other[...])
-    rows, width = up_ref.shape[0] - 16, out_ref.shape[1]
-    shard = rows // 2
-    late_ref[...] = both[: rows + 16]
-    out = both[rows + 16 :].astype(f32)
-    out_ref[...] = jnp.concatenate([out[:, :width], out[:, width:]], axis=0)
-    up = up_ref[...]
-    for at, part in ((0, up), (up.shape[1], both)):
-        theirs = jnp.where(meta[CORE] == 0, part[shard:rows], part[:shard])
-        send_ref[:shard, at : at + up.shape[1]] = theirs
-        send_ref[shard:, at : at + up.shape[1]] = part[rows : rows + 8]
-
-
-def late_out_body(meta, up_ref, late_ref, came_ref, g_up, g_qkv, g_rel, vec_ref):
-    shard = g_up.shape[0]
-    rows, size = 2 * shard, up_ref.shape[1]
-    unit, hd, heads = size // 4, HEAD_DIM, H // 2
-    first = meta[CORE] == 0
-    came = came_ref[...]
-    pair = []
-    for at, ref in ((0, up_ref), (size, late_ref)):
-        mine = jnp.where(first, ref[:shard], ref[shard:rows])
-        theirs = came[:shard, at : at + size]
-        pair.append([jnp.where(first, mine, theirs), jnp.where(first, theirs, mine)])
+def both_cores(meta, own, came):
+    own, came = own.astype(f32), came.astype(f32)
+    return own, own + came, meta[CORE] == 0
+
+
+def store_half(ref, source, at, low):
+    size = 2 * ref.shape[1]
+    piece = source[:, at * size : (at + 1) * size]
+    ref[...] = jnp.where(low, piece[:, : size // 2], piece[:, size // 2 :])
+
+
+def early_out_body(meta, mine, other, came_ref, g_up, g_down, *vec_refs):
+    rows = halves(meta, mine[...], other[...], 0)
+    came_rows = halves(meta, came_ref[0], came_ref[1], 0)
+    shard, width = g_up.shape[0], g_down.shape[1]
+    first, unit = meta[CORE] == 0, rows.shape[1] // 4
+    own, came = jnp.where(first, rows[:shard], rows[shard : 2 * shard]), came_rows[:shard]
+    pair = (jnp.where(first, own, came), jnp.where(first, came, own))
     for j in range(4):
         for side in (0, 1):
             at = (2 * j + side) * unit
-            g_up[:, at : at + unit] = pair[0][side][:, j * unit : (j + 1) * unit].astype(f32)
+            g_up[:, at : at + unit] = pair[side][:, j * unit : (j + 1) * unit].astype(f32)
+    down = rows[2 * shard + 8 :].astype(f32)
+    g_down[...] = jnp.concatenate([down[:, :width], down[:, width:]], axis=0)
+    own, total, low = both_cores(meta, rows[2 * shard : 2 * shard + 1], came_rows[shard : shard + 1])
+    for at, ref in enumerate(vec_refs[:3]):
+        store_half(ref, total, at, low)
+    vec_refs[3][...] = own[:, 6 * shard : 6 * shard + unit]
+
+
+def late_out_body(meta, mine, other, g_qkv, g_rel, g_out, *vec_refs):
+    rows = halves(meta, mine[...], other[...], 0)
+    shard, width = g_qkv.shape[0], g_out.shape[1]
+    first, hd, heads = meta[CORE] == 0, HEAD_DIM, H // 2
+    own, came = rows[:shard], rows[shard : 2 * shard]
+    pair = (jnp.where(first, own, came), jnp.where(first, came, own))
     cols = heads * hd
-    g_qkv[...] = jnp.concatenate(
-        [
-            pair[1][h & 1][:, t * cols + (h >> 1) * hd : t * cols + ((h >> 1) + 1) * hd]
-            for h in range(2 * heads)
-            for t in range(3)
-        ],
-        axis=1,
-    ).astype(f32)
-    g_rel[...] = jnp.concatenate(
-        [
-            pair[1][h & 1][:, 3 * cols + (h >> 1) * hd : 3 * cols + ((h >> 1) + 1) * hd]
-            for h in range(2 * heads)
-        ],
-        axis=1,
-    ).astype(f32)
-    own = [ref[rows : rows + 1].astype(f32) for ref in (up_ref, late_ref)]
-    both = [own[0] + came[shard : shard + 1, :size].astype(f32), own[1] + came[shard : shard + 1, size:].astype(f32)]
-    odd_chip = meta[CHIP] & 1 == 0
-    vec_ref[...] = jnp.zeros_like(vec_ref)
-    picks = [(both[1], 0, first), (both[1], 1, first), (own[1], 2, odd_chip), (own[1], 3, odd_chip)]
-    picks += [(both[0], 0, first), (both[0], 1, first), (both[0], 2, first)]
-    for row, (source, at, low) in enumerate(picks):
-        piece = source[:, at * rows : (at + 1) * rows]
-        vec_ref[row : row + 1, :shard] = jnp.where(low, piece[:, :shard], piece[:, shard:])
-    vec_ref[7:8, :] = own[0][:, 3 * rows : 3 * rows + unit]
+    piece = lambda h, t: pair[h & 1][:, t * cols + (h >> 1) * hd : t * cols + ((h >> 1) + 1) * hd]
+    g_qkv[...] = jnp.concatenate([piece(h, t) for h in range(2 * heads) for t in range(3)], axis=1).astype(f32)
+    g_rel[...] = jnp.concatenate([piece(h, 3) for h in range(2 * heads)], axis=1).astype(f32)
+    out = rows[2 * shard + 16 :].astype(f32)
+    g_out[...] = jnp.concatenate([out[:, :width], out[:, width:]], axis=0)
+    own, total, low = both_cores(meta, rows[2 * shard + 8 : 2 * shard + 9], rows[2 * shard : 2 * shard + 1])
+    even = meta[CHIP] & 1 == 0
+    for at, ref in enumerate(vec_refs):
+        store_half(ref, total if at < 2 else own, at, low if at < 2 else even)
 
 
 def place_body(meta, y0, y1, x0, x1, y_ref, x_ref):
@@ -1013,146 +1010,148 @@
     cols, shard, unit = heads * HEAD_DIM, width // 8, up_bias.shape[0]
     mine_ff = 4 * unit
 
+    none = jnp.zeros((4,), jnp.int32)
     x_own = to_slots(layer_input, rank)
-    where = jnp.stack([core, chip, rank, rank]).astype(jnp.int32)
     vectors = (ln1_gain, ln1_bias, bias_u, bias_v, ln2_gain, ln2_bias, down_bias, up_bias)
     attn_rows, fold = shard + 8, shard // 2
     attn_pack, feed_pack, pack_send = kernel_call(
         pack_body,
         "pack",
-        where,
+        lengths,
         [w_qkv, w_rel, w_up, w_out, w_down] + [v.reshape(-1, min(128, v.size)) for v in vectors],
         [((attn_rows, 4 * cols), bf), ((3 * shard + fold, 4 * cols), bf), ((attn_rows + shard + fold, 4 * cols), bf)],
+        vmem=60,
     )
     pack_came = swap_core(pack_send)
     attn_pack = jnp.concatenate([attn_pack, pack_came[:attn_rows]], axis=0)
-    both = swap_core(lengths)
-    length = jnp.where(core == rank >> 1, lengths, both)
-    length = jnp.where(rank & 1 == 0, length[0], length[1])
+    attn_packs = [attn_pack] + [swap_chip(attn_pack, k) for k in (1, 2, 3)]
+    feed_pack = jnp.concatenate([feed_pack, pack_came[attn_rows:]], axis=0)
+    digits_at = 7 * shard + unit
+    digits = pack_came[shard, digits_at : digits_at + 2 * slots].astype(jnp.int32)
+    lengths = jnp.where(core == rank >> 1, lengths, digits[0::2] * DIGIT + digits[1::2])
+    length = jnp.where(rank & 1 == 0, lengths[0], lengths[1])
     meta = jnp.stack([core, chip, rank, length]).astype(jnp.int32)
     length_arr = length.reshape(1)
-
-    steps = (full - 1 - lax.iota(jnp.int32, full)).astype(f32)
-    attn_pack, steps = together(attn_pack, steps)
-    attn_packs = [attn_pack] + [swap_chip(attn_pack, k) for k in (1, 2, 3)]
-    grad_out, *x_own = together(grad_out, *x_own)
+    feed_pack, meta, length_arr, grad_out, *rest = together(
+        feed_pack, meta, length_arr, grad_out, *x_own, *attn_packs
+    )
     grad_own = to_slots(grad_out, rank)
+    x_own, attn_packs = rest[:2], rest[2:]
+    x_other = [swap_core(x) for x in x_own]
+    feed_pack, x_other[0] = together(feed_pack, x_other[0])
+    feed_first = swap_axis(feed_pack, 0)
+
+    fine = 32
     inv_freq = jnp.exp(lax.iota(f32, width // 2) * (-2.0 * math.log(10000.0) / width))
-    angles = steps[:, None] * inv_freq[None, :]
-    table = jnp.concatenate([jnp.sin(angles), jnp.cos(angles)], axis=1).astype(bf)
-
-    x_other = [swap_core(x) for x in x_own]
+    high = (full - 1 - fine * lax.iota(jnp.int32, full // fine)).astype(f32)[:, None] * inv_freq
+    low = lax.iota(f32, fine)[:, None] * inv_freq
+    high_sin, high_cos, low_sin, low_cos = together(jnp.sin(high), jnp.cos(high), jnp.sin(low), jnp.cos(low))
+    high_sin, high_cos = high_sin[:, None], high_cos[:, None]
+    table = jnp.concatenate(
+        [high_sin * low_cos - high_cos * low_sin, high_cos * low_cos + high_sin * low_sin], axis=2
+    )
+    table = table.astype(bf).reshape(full, width)
+
     by_step = lambda width: pl.BlockSpec((block, width), lambda i, _: (i, 0))
-    qkv, h1, x_slot, rel, w_own, vecs, up_b, biases = kernel_call(
+    qkv, h1, x_slot, rel, w_own, vecs, up_b, own_u, own_v = kernel_call(
         project_body,
         "project",
-        where,
-        attn_packs + x_own + x_other + [table],
+        none,
+        [pltpu.with_memory_space_constraint(v, pltpu.HBM) for v in attn_packs + x_own + x_other + [table]],
         [((full, 3 * cols), bf), ((full, width), bf), ((full, width), bf), ((full, cols), bf)]
-        + [((width, 4 * cols), bf), ((8, width), f32), ((1, mine_ff), f32), ((2, cols), f32)],
+        + [((width, 4 * cols), bf), ((8, width), f32), ((1, mine_ff), f32), ((1, cols), f32), ((1, cols), f32)],
         grid=(4,),
         in_specs=[whole(2 * attn_rows, 4 * cols)] * 4 + [whole(block, width)] * 4 + [by_step(width)],
         out_specs=[by_step(3 * cols), by_step(width), by_step(width), by_step(cols)]
-        + [whole(width, 4 * cols), whole(8, width), whole(1, mine_ff), whole(2, cols)],
+        + [whole(width, 4 * cols), whole(8, width), whole(1, mine_ff), whole(1, cols), whole(1, cols)],
         flops=2 * full * width * 4 * cols,
-    )
-    own_u, own_v = biases[0:1], biases[1:2]
-    qkv, *grad_own = together(qkv, *grad_own)
+        vmem=32,
+    )
+    qkv, feed_later, feed_first = together(qkv, feed_pack, feed_first)
+    feed_second = swap_axis(feed_later, 1)
+    feed_third = swap_axis(feed_first, 1)
     attn, lse = attn_fwd(length_arr, qkv, rel, own_u, own_v)
-
-    feed_pack = jnp.concatenate([feed_pack, pack_came[attn_rows:]], axis=0)
-    feed_pack, *_ = together(feed_pack, *attn_packs)
-    feed_packs = [swap_chip(feed_pack, k) for k in (1, 2, 3)]
+    attn, feed_second, feed_third, *grad_own = together(attn, feed_second, feed_third, *grad_own)
     grad_other = [swap_core(g) for g in grad_own]
-    attn, *rest = together(attn, *feed_packs, *grad_other)
-    feed_packs, grad_other = [feed_pack] + rest[:3], rest[3:]
+    feed_packs = [feed_pack, feed_first, feed_second, feed_third]
 
     attn_other = swap_core(attn)
     kept = lambda width: pl.BlockSpec((block, width), lambda i, _: (i >> 1, 0))
-    half = full // 2
-    g, df, h2, dy, y1, y_keep, dh_keep, dh_send, y_send, early, wo_mine = kernel_call(
+    half, rows = full // 2, 2 * shard + 8
+    blocks = lambda rows: [((rows, 2 * width), f32)] + [((rows, 2 * width), bf)] * 3
+    dy, x_hat, rstd, y_keep, dh, y_send, wo_mine, *early_parts = kernel_call(
         feed_body,
         "feed",
         meta,
         feed_packs + grad_own + grad_other + [x_slot, attn, attn_other, vecs, up_b],
-        [((full, mine_ff), bf)] * 2 + [((full, width), bf)] * 2
-        + [((full, width), f32), ((half, width), f32), ((full, width), f32), ((full, width), bf)]
-        + [((half, width), bf), ((8, mine_ff), f32), ((cols, width), bf)],
+        [((full, width), bf), ((full, width), bf), ((full, 1), f32), ((half, width), f32)]
+        + [((full, width), bf), ((half, width), bf), ((cols, width), bf)]
+        + blocks(rows + unit // 2),
         grid=(4,),
         in_specs=[whole(*feed_pack.shape)] * 4 + [whole(block, width)] * 4
         + [by_step(width), by_step(cols), by_step(cols), whole(8, width), whole(1, mine_ff)],
-        out_specs=[by_step(mine_ff)] * 2 + [by_step(width)] * 3 + [kept(width)] + [by_step(width)] * 2
-        + [kept(width), whole(8, mine_ff), whole(cols, width)],
+        out_specs=[by_step(width), by_step(width), by_step(1), kept(width)]
+        + [by_step(width), kept(width), whole(cols, width)]
+        + [whole(rows + unit // 2, 2 * width)] * 4,
         scratch=[
             pltpu.VMEM((width, mine_ff), bf),
             pltpu.VMEM((mine_ff, width), bf),
             pltpu.VMEM((cols, width), bf),
+            pltpu.VMEM((width, mine_ff), f32),
+            pltpu.VMEM((mine_ff, width), f32),
+            pltpu.VMEM((8, mine_ff), f32),
         ],
-        flops=8 * full * width * mine_ff,
-    )
-    dh_came = swap_core(dh_send)
+        flops=12 * full * width * mine_ff,
+    )
+    dh_came = swap_core(dh)
     y_came = swap_core(y_send)
-    by_chip = lambda rows, size: pl.BlockSpec((rows, size), lambda k, m: (0, m[CHIP] ^ k))
-    blocks = lambda rows: [((rows, 2 * width), f32)] + [((rows, 2 * width), bf)] * 3
-    early_parts = kernel_call(
-        feed_grad_body,
-        "feed_grad",
-        meta,
-        [h2, df, early, g, dy],
-        blocks(2 * shard + 16 + unit // 2),
-        grid=(4,),
-        in_specs=[by_chip(full, 2 * shard), whole(full, mine_ff), whole(8, mine_ff)]
-        + [by_chip(full, unit), whole(full, width)],
-        flops=4 * full * width * mine_ff,
-    )
+    early_came = [swap_chip(early_parts[k], k) for k in (1, 2, 3)]
     out0, out1, g_resid, d_attn, g_out = kernel_call(
         norm_two_body,
         "norm_two",
         meta,
-        [y1, dh_keep, dh_came, dy, vecs, y_keep, y_came, wo_mine, attn],
+        [x_hat, rstd, dh, dh_came, dy, vecs, y_keep, y_came, wo_mine, attn],
         [((block, width), bf)] * 2 + [((half, width), f32), ((full, cols), bf), ((cols, width), f32)],
         grid=(4,),
-        in_specs=[by_step(width)] * 4 + [whole(8, width)] + [kept(width)] * 2 + [whole(cols, width), by_step(cols)],
+        in_specs=[by_step(width), by_step(1)] + [by_step(width)] * 3 + [whole(8, width)] + [kept(width)] * 2
+        + [whole(cols, width), by_step(cols)],
         out_specs=[whole(block, width)] * 2 + [kept(width), by_step(cols), whole(cols, width)],
         flops=4 * full * width * cols,
     )
-    y_turns = [
+    home = lambda outs: [
         lax.ppermute(out, ("fsdp", "seq"), [(b, a) for a, b in slot_pairs(turn)])
-        for turn, out in enumerate((out0, out1))
+        for turn, out in enumerate(outs)
     ]
+    y_turns = home((out0, out1))
     back = lambda pair: attn_bwd(length_arr, qkv, rel, own_u, own_v, lse, d_attn, pair=pair)
-    early_came = [swap_chip(early_parts[k], k) for k in (1, 2, 3)]
-    *first_pair, y0, y1, e1, e2, e3 = together(*back(0), *y_turns, *early_came)
-    y_turns = [y0, y1]
-    early_keep, early_send = chip_sum(meta, [early_parts[0], e1, e2, e3], "early_chips")
-    d_attn, early_send, lse = together(d_attn, early_send, lse)
-    *second_pair, early_came = together(*back(1), swap_seq(early_send, 1))
+    first_pair = back(0)
+    d_attn, *first_pair = together(d_attn, *first_pair)
+    *second_pair, y0, y1, e1, e2, e3 = together(*back(1), *y_turns, *early_came)
     q0, k0, v0, r0, u0, b0 = first_pair
     q1, k1, v1, r1, u1, b1 = second_pair
-    early_pair = (early_keep + early_came.astype(f32)).astype(bf)
-    early_pair, q1 = together(early_pair, q1)
-    early_came = swap_seq(early_pair, 2)
-    rows = 2 * shard + 16
+    early_keep, early_send = chip_sum(meta, [early_parts[0], e1, e2, e3], "early_chips", 0)
+    early_send, q1 = together(early_send, q1)
+    early_came = swap_seq(early_send, 1)
     pair_step = pl.BlockSpec((block, 2 * HEAD_DIM), lambda i, _: (i, 0))
+    pair_row = whole(1, 2 * HEAD_DIM)
     dh1_keep, dh1_send, *late_parts = kernel_call(
         qkv_back_body,
         "qkv_back",
         meta,
-        [q0, q1, k0, k1, v0, v1, r0, r1, w_own, x_slot, h1, table]
-        + [jnp.concatenate([u0, u1], axis=1), jnp.concatenate([b0, b1], axis=1), g_out],
+        [q0, q1, k0, k1, v0, v1, r0, r1, w_own, x_slot, h1, table, u0, u1, b0, b1, g_out],
         [((half, width), f32), ((half, width), bf)] + blocks(rows + fold),
         grid=(4,),
         in_specs=[pair_step] * 8 + [whole(width, 4 * cols)] + [by_step(width)] * 3
-        + [whole(1, cols), whole(1, cols), whole(cols, width)],
+        + [pair_row] * 4 + [whole(cols, width)],
         out_specs=[kept(width)] * 2 + [whole(rows + fold, 2 * width)] * 4,
         scratch=[pltpu.VMEM((width, 4 * cols), f32), pltpu.VMEM((8, width), f32)],
         flops=14 * full * width * cols,
     )
+    dh1_send, early_came, *late_parts = together(dh1_send, early_came, *late_parts)
+    dh1_came = swap_core(dh1_send)
+    early_pair = (early_keep + early_came.astype(f32)).astype(bf)
+    early_came = swap_seq(early_pair, 2)
     late_came = [swap_chip(late_parts[k], k) for k in (1, 2, 3)]
-    dh1_came = swap_core(dh1_send)
-    dh1_came, early_came = together(dh1_came, early_came)
-    early_mine = (early_pair.astype(f32) + early_came.astype(f32)).astype(bf)
-    early_other = swap_seq(early_mine, 1)
     by_half = pl.BlockSpec((block, width), lambda i, _: (i, 0))
     own_rows = pl.BlockSpec((block, width), lambda i, m: (2 * i + m[CORE], 0))
     x0, x1 = kernel_call(
@@ -1164,62 +1163,65 @@
         grid=(2,),
         in_specs=[own_rows] + [by_half] * 3 + [whole(8, width)],
         out_specs=[whole(block, width)] * 2,
-    )
-    *late_came, x0, x1, early_other = together(*late_came, x0, x1, early_other)
-    x_turns = [
-        lax.ppermute(out, ("fsdp", "seq"), [(b, a) for a, b in slot_pairs(turn)])
-        for turn, out in enumerate((x0, x1))
-    ]
-    late_keep, late_send = chip_sum(meta, [late_parts[0]] + late_came, "late_chips")
-    g_up_rows, g_down = kernel_call(
+        vmem=60,
+    )
+    x_turns = home((x0, x1))
+    *late_came, early_came, _, _ = together(*late_came, early_came, x0, x1)
+    early_mine = (early_pair.astype(f32) + early_came.astype(f32)).astype(bf)
+    late_keep, late_send = chip_sum(meta, [late_parts[0]] + late_came, "late_chips", 0)
+    small = lambda size: ((1, size), f32)
+    late_came, g0, g1, early_mine = together(swap_seq(late_send, 1), *x_turns, early_mine)
+    early_other = swap_seq(early_mine, 1)
+    theirs = lambda rows: jnp.concatenate(
+        [
+            lax.dynamic_slice_in_dim(rows, (1 - core) * shard, shard, 0),
+            rows[2 * shard : 2 * shard + 8],
+        ],
+        axis=0,
+    )
+    early_core = swap_core(jnp.stack([theirs(early_mine), theirs(early_other)]))
+    g_up, g_down, g_gain_two, g_shift_two, g_down_shift, g_up_shift = kernel_call(
         early_out_body,
         "early_out",
         meta,
-        [early_mine, early_other],
-        [((rows, 2 * width), bf), ((unit, width), f32)],
-    )
-    late_pair = (late_keep + swap_seq(late_send, 1).astype(f32)).astype(bf)
-    late_came, g_up_rows, g_down, *x_turns = together(swap_seq(late_pair, 2), g_up_rows, g_down, *x_turns)
-    late_mine = (late_pair.astype(f32) + late_came.astype(f32)).astype(bf)
+        [early_mine, early_other, early_core],
+        [((shard, 2 * mine_ff), f32), ((unit, width), f32)] + [small(shard)] * 3 + [small(unit)],
+    )
+    late_pair = (late_keep + late_came.astype(f32)).astype(bf)
     output, grad_x = kernel_call(
         place_body,
         "place",
         meta,
-        y_turns + x_turns,
+        [y0, y1, g0, g1],
         [((2, block, width), bf), ((2, block, width), f32)],
     )
-    late_other, output, grad_x = together(swap_seq(late_mine, 1), output, grad_x)
-    late, g_w_out, send = kernel_call(
-        late_pack_body,
-        "late_pack",
-        meta,
-        [g_up_rows, late_mine, late_other],
-        [((rows, 2 * width), bf), ((shard, width), f32), ((shard + 8, 4 * width), bf)],
-    )
-    g_up, g_qkv, g_rel, vecs = kernel_call(
+    late_came, output, grad_x, g_up = together(swap_seq(late_pair, 2), output, grad_x, g_up)
+    late_total = (late_pair.astype(f32) + late_came.astype(f32)).astype(bf)
+    late_mine = own_rows_first(late_total, core, shard)
+    g_qkv, g_rel, g_w_out, *late_vectors = kernel_call(
         late_out_body,
         "late_out",
         meta,
-        [g_up_rows, late, swap_core(send)],
-        [((shard, 2 * mine_ff), f32), ((shard, 6 * cols), f32), ((shard, 2 * cols), f32), ((8, unit), f32)],
-    )
-    small = lambda row: vecs[row, :shard]
+        [late_mine, swap_seq(late_mine, 1)],
+        [((shard, 6 * cols), f32), ((shard, 2 * cols), f32), ((shard, width), f32)] + [small(shard)] * 4,
+    )
+    g_gain_one, g_shift_one, g_bias_u, g_bias_v = [v.reshape(-1) for v in late_vectors]
     return (
         output,
         grad_x,
-        small(0),
-        small(1),
+        g_gain_one,
+        g_shift_one,
         g_qkv,
         g_rel,
-        small(2),
-        small(3),
+        g_bias_u,
+        g_bias_v,
         g_w_out,
-        small(4),
-        small(5),
+        g_gain_two.reshape(-1),
+        g_shift_two.reshape(-1),
         g_up,
-        vecs[7],
+        g_up_shift.reshape(-1),
         g_down,
-        small(6),
+        g_down_shift.reshape(-1),
     )
 
 

time: 222 us -> 174 us (0.78)
  Pallas kernels: 106 us -> 62.8 us
  waiting for transfers between devices: 37.2 us -> 58 us
  starting transfers between devices: 52.7 us -> 40.6 us
  other arithmetic: 10.7 us -> 4.05 us
  local copies, waits for them, and re-layouts: 11.2 us -> 5.48 us
    pallas_call x13 -> x11, Pallas kernels: 68.7 us -> 38.2 us  [kernel_call(): pl.pallas_call(body, out_shape=[jax.ShapeDtypeStruct(shape, kind) for sha...]
    ppermute x6, waiting for transfers between devices: 25.3 us -> 36.9 us  [swap_seq(): return lax.ppermute(values, 'seq', [(i, i ^ mask) for i in range(size)])]
    ppermute x4, waiting for transfers between devices: 0.01 us -> 11.2 us  [to_slots(): lax.ppermute(lax.dynamic_index_in_dim(values, turn ^ seq_rank >> 1, 0, ke...]
    pallas_call x2, Pallas kernels: 25.1 us -> 14.6 us  [attn_bwd(): pl.pallas_call(functools.partial(attn_bwd_body, block=block), out_shape=(...]
    ppermute x11, starting transfers between devices: 11 us -> 4.41 us  [swap_core(): return lax.ppermute(values, 'fsdp', [(i, i ^ 1) for i in range(size)])]
    ppermute x4, starting transfers between devices: 11.3 us -> 5.62 us  [slot_split_device(): lax.ppermute(out, ('fsdp', 'seq'), [(b, a) for a, b in slot_pairs(turn)])]
    another operation x2 -> x4, other arithmetic: 4.82 us -> 0.38 us
    ppermute x12 -> x9, waiting for transfers between devices: 8.86 us -> 4.75 us  [swap_chip(): lax.ppermute(values, 'fsdp', [(i, i ^ 2 * mask) for i in range(size)])]
  transfers between devices with their start and end apart: 37 -> 37, of which waited for: 11 -> 16; matrix products, arithmetic and copies ran while one was open for 6% -> 3% of each run, Pallas kernels for 33% -> 27%
where the time goes in v2:
time: 174 us; the launch traced here: 173 us
  Pallas kernels  62.8 us (36%)
  waiting for transfers between devices  58 us (33%)
  starting transfers between devices  40.6 us (23%)
  local copies, waits for them, and re-layouts  5.48 us (3%)
  other arithmetic  4.05 us (2%)
  between operations  2.39 us (1%)
    pallas_call x11, Pallas kernels, kernel_call(): pl.pallas_call(body, out_shape=[jax.ShapeDtypeStruct(shape, kind) for sha...  38.2 us
    ppermute x6, waiting for transfers between devices, swap_seq(): return lax.ppermute(values, 'seq', [(i, i ^ mask) for i in range(size)])  36.9 us
    ppermute x9, starting transfers between devices, swap_chip(): lax.ppermute(values, 'fsdp', [(i, i ^ 2 * mask) for i in range(size)])  16.3 us
    pallas_call x2, Pallas kernels, attn_bwd(): pl.pallas_call(functools.partial(attn_bwd_body, block=block), out_shape=(...  14.6 us
    ppermute x4, waiting for transfers between devices, to_slots(): lax.ppermute(lax.dynamic_index_in_dim(values, turn ^ seq_rank >> 1, 0, ke...  11.2 us
    pallas_call x1, Pallas kernels, attn_fwd(): pl.pallas_call(functools.partial(attn_fwd_body, block=block), out_shape=(...  10 us
    ppermute x4, starting transfers between devices, to_slots(): lax.ppermute(lax.dynamic_index_in_dim(values, turn ^ seq_rank >> 1, 0, ke...  7.37 us
    ppermute x4, starting transfers between devices, slot_split_device(): lax.ppermute(out, ('fsdp', 'seq'), [(b, a) for a, b in slot_pairs(turn)])  5.62 us
  transfers between devices with their start and end apart: 37, of which 16 were waited for; matrix products, arithmetic and copies ran while one was open for 3% of the time, Pallas kernels for 27%

profile of v2, /device:TPU:0, one launch (start us, length us, event | category | flops | bytes accessed | tf_op | source)
XLA Modules:
  0.0 173.3 jit_solution(11240023326691359667)
XLA Ops:
  0.7 3.1 %pack.1 = (bf16[72,1024]{1,0:T(8,128)(2,1)}, bf16[224,1024]{1,0:T(8,128)(2,1)}, bf16[168,1024]{1,0:T(8,128)(2,1)}) custom-call(s32[2]{0:T(128)} %lengths_ref.1, bf16[64,1536]{1,0:T(8,128)(2,1)} %qkv_ref.1, bf16[64,512]{1,0:T(8,128)(2,1)} %rel_ref.1, bf16[64,2048]{1,0:T(8,128)(2,1)} %up_ref.1, bf16[64,512]{1,0:T(8,128)(2,1)} %out_ref.1, ...), custom_call_target="tpu_custom_call" | custom-call | tf_op jit(solution)/shard_map/pack/pallas_call | solution.py:586
  4.2 1.1 dynamic-slice_bitcast_fusion.2
  6.0 3.9 %collective-permute-start.2 = (bf16[256,512]{1,0:T(8,128)(2,1)S(1)}, bf16[256,512]{1,0:T(8,128)(2,1)S(1)}, u32[]{:S(2)}, u32[]{:S(2)}) collective-permute-start(bf16[256,512]{1,0:T(8,128)(2,1)S(1)} %get-tuple-element.279), channel_id=1, source_target_pairs={{0,1},{1,5},{2,0},{3,4},{4,3},{5,7},{6,2},{7,6},{8,9},{9,13},{10,8... | collective-permute-start | bytes 786440 | tf_op jit(solution)/shard_map/ppermute | solution.py:564
  10.2 0.9 pad_maximum_fusion.2.refs_0_
  11.2 2.0 %collective-permute-start.3 = (bf16[144,1024]{1,0:T(8,128)(2,1)S(1)}, bf16[144,1024]{1,0:T(8,128)(2,1)S(1)}, u32[]{:S(2)}, u32[]{:S(2)}) collective-permute-start(bf16[144,1024]{1,0:T(8,128)(2,1)S(1)} %pad_maximum_fusion.2.refs_0_), channel_id=1, source_target_pairs={{0,8},{4,12},{8,0},{12,4},{16,24},{20,28},{24,16},{28,20},{1,9},{5... | collective-permute-start | bytes 884744 | tf_op jit(solution)/shard_map/ppermute | solution.py:540
  13.2 1.5 collective-permute-start.4
  16.8 7.3 %collective-permute-done.2.refs_5_ = bf16[256,512]{1,0:T(8,128)(2,1)S(1)} collective-permute-done((bf16[256,512]{1,0:T(8,128)(2,1)S(1)}, bf16[256,512]{1,0:T(8,128)(2,1)S(1)}, u32[]{:S(2)}, u32[]{:S(2)}) %collective-permute-start.2) | collective-permute-done | bytes 262176 | tf_op jit(solution)/shard_map/ppermute | solution.py:564
  24.1 3.6 %collective-permute-done.4.refs_2_ = bf16[144,1024]{1,0:T(8,128)(2,1)S(1)} collective-permute-done((bf16[144,1024]{1,0:T(8,128)(2,1)S(1)}, bf16[144,1024]{1,0:T(8,128)(2,1)S(1)}, u32[]{:S(2)}, u32[]{:S(2)}) %collective-permute-start.4) | collective-permute-done | bytes 294944 | tf_op jit(solution)/shard_map/ppermute | solution.py:540
  27.9 1.4 collective-permute-start.6
  29.3 1.2 collective-permute-done.6.refs_6_
  30.5 0.9 collective-permute-start.8
  32.8 1.1 pad_maximum_fusion.refs_8_.refs_11_
  34.6 5.4 %project.1 = (bf16[1024,768]{1,0:T(8,128)(2,1)S(1)}, bf16[1024,512]{1,0:T(8,128)(2,1)S(1)}, bf16[1024,512]{1,0:T(8,128)(2,1)S(1)}, bf16[1024,256]{1,0:T(8,128)(2...) custom-call(s32[4]{0:T(128)S(1)} %broadcast_3__.2._, ...), custom_call_target="tpu_custom_call" | custom-call | tf_op jit(solution)/shard_map/project/pallas_call | solution.py:586
  40.0 1.0 collective-permute-done.8.refs_1_
  41.1 1.5 collective-permute-start.10
  43.8 2.1 %collective-permute-start.12 = (bf16[256,512]{1,0:T(8,128)(2,1)S(1)}, bf16[256,512]{1,0:T(8,128)(2,1)S(1)}, u32[]{:S(2)}, u32[]{:S(2)}) collective-permute-start(bf16[256,512]{1,0:T(8,128)(2,1)S(1)} %get-tuple-element.277), channel_id=1, source_target_pairs={{0,1},{1,5},{2,0},{3,4},{4,3},{5,7},{6,2},{7,6},{8,9},{9,13},{10,8... | collective-permute-start | bytes 786440 | tf_op jit(solution)/shard_map/ppermute | solution.py:564
  45.9 10.0 %attn_fwd.1 = (bf16[1024,256]{1,0:T(8,128)(2,1)S(1)}, f32[4,1024,1]{2,1,0:T(8,128)S(1)}) custom-call(s32[1]{0:T(128)} %bitcast.15.len_ref, bf16[1024,768]{1,0:T(8,128)(2,1)S(1)} %get-tuple-element.166.q_ref.k_ref.v_ref, bf16[1024,768]{1,0:T(8,128)(2,1)S(1)} %get-tuple-element.166.q_ref.k_ref.v_ref, ...), custom_call_target="tpu_custom_call" | custom-call | tf_op jit(solution)/shard_map/attn_fwd/pallas_call | solution.py:83
  55.9 3.9 %collective-permute-done.12.refs_5_ = bf16[256,512]{1,0:T(8,128)(2,1)S(1)} collective-permute-done((bf16[256,512]{1,0:T(8,128)(2,1)S(1)}, bf16[256,512]{1,0:T(8,128)(2,1)S(1)}, u32[]{:S(2)}, u32[]{:S(2)}) %collective-permute-start.12) | collective-permute-done | bytes 262176 | tf_op jit(solution)/shard_map/ppermute | solution.py:564
  60.4 1.7 collective-permute-done.13.refs_6_
  62.5 11.1 %feed.1 = (bf16[1024,512]{1,0:T(8,128)(2,1)S(1)}, bf16[1024,512]{1,0:T(8,128)(2,1)S(1)}, f32[1024,1]{1,0:T(8,128)S(1)}, f32[512,512]{1,0:T(8,128)S(1)}, bf16[102...) custom-call(s32[4]{0:T(128)S(1)} %pad_add_fusion.meta, ...), custom_call_target="tpu_custom_call" | custom-call | tf_op jit(solution)/shard_map/feed/pallas_call | solution.py:586
  74.2 1.2 collective-permute-start.20
  75.4 0.9 collective-permute-start.21
  76.2 1.4 collective-permute-start.22
  77.7 3.4 %norm_two.1 = (bf16[256,512]{1,0:T(8,128)(2,1)S(1)}, bf16[256,512]{1,0:T(8,128)(2,1)S(1)}, f32[512,512]{1,0:T(8,128)S(1)}, bf16[1024,256]{1,0:T(8,128)(2,1)S(1)}, f32[256,512]{1,0:T(8,128)S(1)}) custom-call(s32[4]{0:T(128)S(1)} %pad_add_fusion.meta, bf16[1024,512]{1,0:T(8,128)(2,1)S(1)} %get-tuple-element.181.x_hat_ref, ...), custom_call_target="tpu_custom_call" | custom-call | tf_op jit(solution)/shard_map/norm_two/pallas_call | solution.py:586
  81.1 1.0 copy-done.2
  82.8 3.4 %collective-permute-start.19 = (bf16[256,512]{1,0:T(8,128)(2,1)S(1)}, bf16[256,512]{1,0:T(8,128)(2,1)S(1)}, u32[]{:S(2)}, u32[]{:S(2)}) collective-permute-start(bf16[256,512]{1,0:T(8,128)(2,1)S(1)} %get-tuple-element.206), channel_id=1, source_target_pairs={{1,0},{5,1},{0,2},{4,3},{3,4},{7,5},{2,6},{6,7},{9,8},{13,9},{8,10... | collective-permute-start | bytes 786440 | tf_op jit(solution)/shard_map/ppermute | solution.py:1122
  86.1 7.3 %attn_bwd.2 = (bf16[1024,128]{1,0:T(8,128)(2,1)S(1)}, bf16[1024,128]{1,0:T(8,128)(2,1)S(1)}, bf16[1024,128]{1,0:T(8,128)(2,1)S(1)}, bf16[1024,128]{1,0:T(8,128)(...) custom-call(s32[1]{0:T(128)} %bitcast.15.len_ref, bf16[1024,768]{1,0:T(8,128)(2,1)S(1)} %get-tuple-element.166.q_ref.k_ref.v_ref, ...), custom_call_target="tpu_custom_call" | custom-call | tf_op jit(solution)/shard_map/attn_bwd/pallas_call | solution.py:167
  93.4 7.3 %attn_bwd.3 = (bf16[1024,128]{1,0:T(8,128)(2,1)S(1)}, bf16[1024,128]{1,0:T(8,128)(2,1)S(1)}, bf16[1024,128]{1,0:T(8,128)(2,1)S(1)}, bf16[1024,128]{1,0:T(8,128)(...) custom-call(s32[1]{0:T(128)} %bitcast.15.len_ref, bf16[1024,768]{1,0:T(8,128)(2,1)S(1)} %get-tuple-element.166.q_ref.k_ref.v_ref, ...), custom_call_target="tpu_custom_call" | custom-call | tf_op jit(solution)/shard_map/attn_bwd/pallas_call | solution.py:167
  102.0 4.9 %qkv_back.1 = (f32[512,512]{1,0:T(8,128)S(1)}, bf16[512,512]{1,0:T(8,128)(2,1)S(1)}, f32[168,1024]{1,0:T(8,128)S(1)}, bf16[168,1024]{1,0:T(8,128)(2,1)}, bf16[16...) custom-call(s32[4]{0:T(128)S(1)} %pad_add_fusion.meta, bf16[1024,128]{1,0:T(8,128)(2,1)S(1)} %get-tuple-element.196.refs_0_, ...), custom_call_target="tpu_custom_call" | custom-call | tf_op jit(solution)/shard_map/qkv_back/pallas_call | solution.py:586
  106.9 1.0 copy-done.3
  107.8 1.8 %collective-permute-done.23 = bf16[264,512]{1,0:T(8,128)(2,1)S(1)} collective-permute-done((bf16[264,512]{1,0:T(8,128)(2,1)S(1)}, bf16[264,512]{1,0:T(8,128)(2,1)S(1)}, u32[]{:S(2)}, u32[]{:S(2)}) %collective-permute-start.23) | collective-permute-done | bytes 270368 | tf_op jit(solution)/shard_map/ppermute | solution.py:550
  109.6 7.4 %collective-permute-start.24 = (bf16[168,1024]{1,0:T(8,128)(2,1)}, bf16[168,1024]{1,0:T(8,128)(2,1)S(1)}, u32[]{:S(2)}, u32[]{:S(2)}) collective-permute-start(bf16[168,1024]{1,0:T(8,128)(2,1)} %get-tuple-element.236), channel_id=1, source_target_pairs={{0,8},{4,12},{8,0},{12,4},{16,24},{20,28},{24,16},{28,20},{1,9},{5... | collective-permute-start | bytes 1032200 | tf_op jit(solution)/shard_map/ppermute | solution.py:540
  117.4 1.5 collective-permute-start.26
  118.9 1.6 collective-permute-start.27
  120.5 0.8 copy-done.9
  121.3 3.8 %norm_one.1 = (bf16[256,512]{1,0:T(8,128)(2,1)}, bf16[256,512]{1,0:T(8,128)(2,1)}) custom-call(s32[4]{0:T(128)} %copy-done.5, bf16[1024,512]{1,0:T(8,128)(2,1)} %copy-done.1, f32[512,512]{1,0:T(8,128)} %copy-done.3, bf16[512,512]{1,0:T(8,128)(2,1)} %copy-done.9, f32[512,512]{1,0:T(8,128)} %copy-done.2, f32[8,512]{1,0:T(8,128)} %copy-done.4), custom_call_target="tpu_custom_call" | custom-call | tf_op jit(solution)/shard_map/norm_one/pallas_call | solution.py:586
  125.1 1.6 collective-permute-start.30
  126.7 7.5 %collective-permute-done.27 = bf16[264,512]{1,0:T(8,128)(2,1)} collective-permute-done((bf16[264,512]{1,0:T(8,128)(2,1)S(1)}, bf16[264,512]{1,0:T(8,128)(2,1)}, u32[]{:S(2)}, u32[]{:S(2)}) %collective-permute-start.27) | collective-permute-done | bytes 270368 | tf_op jit(solution)/shard_map/ppermute | solution.py:550
  135.6 1.5 collective-permute-start.29
  137.0 1.0 add_convert_fusion.1.mine
  138.0 10.6 %collective-permute-done.29 = bf16[168,512]{1,0:T(8,128)(2,1)S(1)} collective-permute-done((bf16[168,512]{1,0:T(8,128)(2,1)S(1)}, bf16[168,512]{1,0:T(8,128)(2,1)S(1)}, u32[]{:S(2)}, u32[]{:S(2)}) %collective-permute-start.29) | collective-permute-done | bytes 172064 | tf_op jit(solution)/shard_map/ppermute | solution.py:550
  148.8 0.9 collective-permute-start.32
  149.7 10.2 %collective-permute-done.33.other = bf16[264,512]{1,0:T(8,128)(2,1)S(1)} collective-permute-done((bf16[264,512]{1,0:T(8,128)(2,1)S(1)}, bf16[264,512]{1,0:T(8,128)(2,1)S(1)}, u32[]{:S(2)}, u32[]{:S(2)}) %collective-permute-start.33) | collective-permute-done | bytes 270368 | tf_op jit(solution)/shard_map/ppermute | solution.py:550
  160.0 1.8 %place.1 = (bf16[2,256,512]{2,1,0:T(8,128)(2,1)}, f32[2,256,512]{2,1,0:T(8,128)}) custom-call(s32[4]{0:T(128)S(1)} %copy-done.6, bf16[256,512]{1,0:T(8,128)(2,1)S(1)} %collective-permute-done.18.y0, bf16[256,512]{1,0:T(8,128)(2,1)S(1)} %collective-permute-done.19.y1, bf16[256,512]{1,0:T(8,128)(2,1)S(1)} %collective-permute-done.30.x0, ...), custom_call_target="tpu_custom_call" | custom-call | tf_op jit(solution)/shard_map/place/pallas_call | solution.py:586
  161.7 1.6 early_out.1
  164.0 0.9 collective-permute-done.35
  165.0 6.8 %collective-permute-done.36.other = bf16[176,512]{1,0:T(8,128)(2,1)S(1)} collective-permute-done((bf16[176,512]{1,0:T(8,128)(2,1)S(1)}, bf16[176,512]{1,0:T(8,128)(2,1)S(1)}, u32[]{:S(2)}, u32[]{:S(2)}) %collective-permute-start.36) | collective-permute-done | bytes 180256 | tf_op jit(solution)/shard_map/ppermute | solution.py:550
  171.8 1.5 late_out.1
  (112 shorter events, 11.8 us)
Async XLA Ops:
  0.7 14.1 %copy-start.18 = (s32[2]{0:T(128)S(1)}, s32[2]{0:T(128)}, u32[]{:S(2)}) copy-start(s32[2]{0:T(128)} %lengths_ref.1) | copy-start | bytes 28
  3.8 13.0 %copy-start.10 = (bf16[224,1024]{1,0:T(8,128)(2,1)S(1)}, bf16[224,1024]{1,0:T(8,128)(2,1)}, u32[]{:S(2)}) copy-start(bf16[224,1024]{1,0:T(8,128)(2,1)} %get-tuple-element.146) | copy-start | bytes 1376260
  3.8 6.2 %collective-permute-start = (bf16[168,1024]{1,0:T(8,128)(2,1)}, bf16[168,1024]{1,0:T(8,128)(2,1)S(1)}, u32[]{:S(2)}, u32[]{:S(2)}) collective-permute-start(bf16[168,1024]{1,0:T(8,128)(2,1)} %get-tuple-element.147), channel_id=1, source_target_pairs={{0,4},{4,0},{8,12},{12,8},{16,20},{20,16},{24,28},{28,24},{1,5},{5... | collective-permute-start | bytes 1032200 | tf_op jit(solution)/shard_map/ppermute | solution.py:535
  5.3 11.5 %collective-permute-start.1 = (bf16[256,512]{1,0:T(8,128)(2,1)S(1)}, bf16[256,512]{1,0:T(8,128)(2,1)S(1)}, u32[]{:S(2)}, u32[]{:S(2)}) collective-permute-start(bf16[256,512]{1,0:T(8,128)(2,1)S(1)} %get-tuple-element.280), channel_id=1, source_target_pairs={{0,0},{1,4},{2,1},{3,5},{4,2},{5,6},{6,3},{7,7},{8,8},{9,12},{10,9... | collective-permute-start | bytes 786440 | tf_op jit(solution)/shard_map/ppermute | solution.py:564
  6.0 18.1 %collective-permute-start.2 = (bf16[256,512]{1,0:T(8,128)(2,1)S(1)}, bf16[256,512]{1,0:T(8,128)(2,1)S(1)}, u32[]{:S(2)}, u32[]{:S(2)}) collective-permute-start(bf16[256,512]{1,0:T(8,128)(2,1)S(1)} %get-tuple-element.279), channel_id=1, source_target_pairs={{0,1},{1,5},{2,0},{3,4},{4,3},{5,7},{6,2},{7,6},{8,9},{9,13},{10,8... | collective-permute-start | bytes 786440 | tf_op jit(solution)/shard_map/ppermute | solution.py:564
  11.2 22.7 %copy-start.7 = (bf16[144,1024]{1,0:T(8,128)(2,1)}, bf16[144,1024]{1,0:T(8,128)(2,1)S(1)}, u32[]{:S(2)}) copy-start(bf16[144,1024]{1,0:T(8,128)(2,1)S(1)} %pad_maximum_fusion.2.refs_0_) | copy-start | bytes 884740
  11.2 12.9 %collective-permute-start.3 = (bf16[144,1024]{1,0:T(8,128)(2,1)S(1)}, bf16[144,1024]{1,0:T(8,128)(2,1)S(1)}, u32[]{:S(2)}, u32[]{:S(2)}) collective-permute-start(bf16[144,1024]{1,0:T(8,128)(2,1)S(1)} %pad_maximum_fusion.2.refs_0_), channel_id=1, source_target_pairs={{0,8},{4,12},{8,0},{12,4},{16,24},{20,28},{24,16},{28,20},{1,9},{5... | collective-permute-start | bytes 884744 | tf_op jit(solution)/shard_map/ppermute | solution.py:540
  13.2 14.5 %collective-permute-start.4 = (bf16[144,1024]{1,0:T(8,128)(2,1)S(1)}, bf16[144,1024]{1,0:T(8,128)(2,1)S(1)}, u32[]{:S(2)}, u32[]{:S(2)}) collective-permute-start(bf16[144,1024]{1,0:T(8,128)(2,1)S(1)} %pad_maximum_fusion.2.refs_0_), channel_id=1, source_target_pairs={{0,16},{4,20},{8,24},{12,28},{16,0},{20,4},{24,8},{28,12},{1,17},{... | collective-permute-start | bytes 884744 | tf_op jit(solution)/shard_map/ppermute | solution.py:540
  14.7 13.2 %collective-permute-start.5 = (bf16[144,1024]{1,0:T(8,128)(2,1)S(1)}, bf16[144,1024]{1,0:T(8,128)(2,1)S(1)}, u32[]{:S(2)}, u32[]{:S(2)}) collective-permute-start(bf16[144,1024]{1,0:T(8,128)(2,1)S(1)} %pad_maximum_fusion.2.refs_0_), channel_id=1, source_target_pairs={{0,24},{4,28},{8,16},{12,20},{16,8},{20,12},{24,0},{28,4},{1,25},{... | collective-permute-start | bytes 884744 | tf_op jit(solution)/shard_map/ppermute | solution.py:540
  16.8 85.2 %copy-start.5 = (s32[4]{0:T(128)}, s32[4]{0:T(128)S(1)}, u32[]{:S(2)}) copy-start(s32[4]{0:T(128)S(1)} %pad_add_fusion.meta) | copy-start | bytes 52
  16.8 17.0 %copy-start.14 = (bf16[256,512]{1,0:T(8,128)(2,1)}, bf16[256,512]{1,0:T(8,128)(2,1)S(1)}, u32[]{:S(2)}) copy-start(bf16[256,512]{1,0:T(8,128)(2,1)S(1)} %collective-permute-done.1.refs_4_) | copy-start | bytes 786436
  24.1 9.7 %copy-start.15 = (bf16[256,512]{1,0:T(8,128)(2,1)}, bf16[256,512]{1,0:T(8,128)(2,1)S(1)}, u32[]{:S(2)}) copy-start(bf16[256,512]{1,0:T(8,128)(2,1)S(1)} %collective-permute-done.2.refs_5_) | copy-start | bytes 786436
  24.1 9.7 %copy-start.11 = (bf16[144,1024]{1,0:T(8,128)(2,1)}, bf16[144,1024]{1,0:T(8,128)(2,1)S(1)}, u32[]{:S(2)}) copy-start(bf16[144,1024]{1,0:T(8,128)(2,1)S(1)} %collective-permute-done.3.refs_1_) | copy-start | bytes 884740
  27.9 2.5 %collective-permute-start.6 = (bf16[256,512]{1,0:T(8,128)(2,1)S(1)}, bf16[256,512]{1,0:T(8,128)(2,1)S(1)}, u32[]{:S(2)}, u32[]{:S(2)}) collective-permute-start(bf16[256,512]{1,0:T(8,128)(2,1)S(1)} %collective-permute-done.1.refs_4_), channel_id=1, source_target_pairs={{0,4},{4,0},{8,12},{12,8},{16,20},{20,16},{24,28},{28,24},{1,5},{5... | collective-permute-start | bytes 786440 | tf_op jit(solution)/shard_map/ppermute | solution.py:535
  30.5 10.6 %collective-permute-start.8 = (bf16[320,1024]{1,0:T(8,128)(2,1)S(1)}, bf16[320,1024]{1,0:T(8,128)(2,1)S(1)}, u32[]{:S(2)}, u32[]{:S(2)}) collective-permute-start(bf16[320,1024]{1,0:T(8,128)(2,1)S(1)} %pad_maximum_fusion.1.refs_0_), channel_id=1, source_target_pairs={{0,8},{4,20},{8,0},{12,28},{16,24},{20,4},{24,16},{28,12},{1,9},{5... | collective-permute-start | bytes 1966088 | tf_op jit(solution)/shard_map/ppermute | solution.py:545
  31.6 2.2 %collective-permute-start.7 = (bf16[256,512]{1,0:T(8,128)(2,1)S(1)}, bf16[256,512]{1,0:T(8,128)(2,1)S(1)}, u32[]{:S(2)}, u32[]{:S(2)}) collective-permute-start(bf16[256,512]{1,0:T(8,128)(2,1)S(1)} %collective-permute-done.2.refs_5_), channel_id=1, source_target_pairs={{0,4},{4,0},{8,12},{12,8},{16,20},{20,16},{24,28},{28,24},{1,5},{5... | collective-permute-start | bytes 786440 | tf_op jit(solution)/shard_map/ppermute | solution.py:535
  34.6 8.5 %copy-start.8 = (bf16[2,256,512]{2,1,0:T(8,128)(2,1)S(1)}, bf16[2,256,512]{2,1,0:T(8,128)(2,1)}, u32[]{:S(2)}) copy-start(bf16[2,256,512]{2,1,0:T(8,128)(2,1)} %param.31) | copy-start | bytes 1572868
  40.0 37.7 %copy-start.4 = (f32[8,512]{1,0:T(8,128)}, f32[8,512]{1,0:T(8,128)S(1)}, u32[]{:S(2)}) copy-start(f32[8,512]{1,0:T(8,128)S(1)} %get-tuple-element.179.refs_11_.vec_ref) | copy-start | bytes 49156
  40.0 61.9 %copy-start.1 = (bf16[1024,512]{1,0:T(8,128)(2,1)}, bf16[1024,512]{1,0:T(8,128)(2,1)S(1)}, u32[]{:S(2)}) copy-start(bf16[1024,512]{1,0:T(8,128)(2,1)S(1)} %get-tuple-element.177.refs_8_.refs_9_.x_ref) | copy-start | bytes 3145732
  41.1 18.8 %collective-permute-start.10 = (bf16[320,1024]{1,0:T(8,128)(2,1)S(1)}, bf16[320,1024]{1,0:T(8,128)(2,1)S(1)}, u32[]{:S(2)}, u32[]{:S(2)}) collective-permute-start(bf16[320,1024]{1,0:T(8,128)(2,1)S(1)} %collective-permute-done.8.refs_1_), channel_id=1, source_target_pairs={{0,16},{4,12},{8,24},{12,4},{16,0},{20,28},{24,8},{28,20},{1,17},{... | collective-permute-start | bytes 1966088 | tf_op jit(solution)/shard_map/ppermute | solution.py:545
  42.6 17.3 %collective-permute-start.9 = (bf16[320,1024]{1,0:T(8,128)(2,1)S(1)}, bf16[320,1024]{1,0:T(8,128)(2,1)S(1)}, u32[]{:S(2)}, u32[]{:S(2)}) collective-permute-start(bf16[320,1024]{1,0:T(8,128)(2,1)S(1)} %pad_maximum_fusion.1.refs_0_), channel_id=1, source_target_pairs={{0,16},{4,12},{8,24},{12,4},{16,0},{20,28},{24,8},{28,20},{1,17},{... | collective-permute-start | bytes 1966088 | tf_op jit(solution)/shard_map/ppermute | solution.py:545
  43.1 12.8 %collective-permute-start.11 = (bf16[256,512]{1,0:T(8,128)(2,1)S(1)}, bf16[256,512]{1,0:T(8,128)(2,1)S(1)}, u32[]{:S(2)}, u32[]{:S(2)}) collective-permute-start(bf16[256,512]{1,0:T(8,128)(2,1)S(1)} %get-tuple-element.278), channel_id=1, source_target_pairs={{0,0},{1,4},{2,1},{3,5},{4,2},{5,6},{6,3},{7,7},{8,8},{9,12},{10,9... | collective-permute-start | bytes 786440 | tf_op jit(solution)/shard_map/ppermute | solution.py:564
  43.8 16.0 %collective-permute-start.12 = (bf16[256,512]{1,0:T(8,128)(2,1)S(1)}, bf16[256,512]{1,0:T(8,128)(2,1)S(1)}, u32[]{:S(2)}, u32[]{:S(2)}) collective-permute-start(bf16[256,512]{1,0:T(8,128)(2,1)S(1)} %get-tuple-element.277), channel_id=1, source_target_pairs={{0,1},{1,5},{2,0},{3,4},{4,3},{5,7},{6,2},{7,6},{8,9},{9,13},{10,8... | collective-permute-start | bytes 786440 | tf_op jit(solution)/shard_map/ppermute | solution.py:564
  59.8 2.7 %collective-permute-start.15 = (bf16[1024,256]{1,0:T(8,128)(2,1)S(1)}, bf16[1024,256]{1,0:T(8,128)(2,1)S(1)}, u32[]{:S(2)}, u32[]{:S(2)}) collective-permute-start(bf16[1024,256]{1,0:T(8,128)(2,1)S(1)} %get-tuple-element.178.refs_9_.o_ref), channel_id=1, source_target_pairs={{0,4},{4,0},{8,12},{12,8},{16,20},{20,16},{24,28},{28,24},{1,5},{5... | collective-permute-start | bytes 1572872 | tf_op jit(solution)/shard_map/ppermute | solution.py:535
  59.9 2.3 %collective-permute-start.13 = (bf16[256,512]{1,0:T(8,128)(2,1)S(1)}, bf16[256,512]{1,0:T(8,128)(2,1)S(1)}, u32[]{:S(2)}, u32[]{:S(2)}) collective-permute-start(bf16[256,512]{1,0:T(8,128)(2,1)S(1)} %collective-permute-done.11.refs_4_), channel_id=1, source_target_pairs={{0,4},{4,0},{8,12},{12,8},{16,20},{20,16},{24,28},{28,24},{1,5},{5... | collective-permute-start | bytes 786440 | tf_op jit(solution)/shard_map/ppermute | solution.py:535
  60.4 2.1 %collective-permute-start.14 = (bf16[256,512]{1,0:T(8,128)(2,1)S(1)}, bf16[256,512]{1,0:T(8,128)(2,1)S(1)}, u32[]{:S(2)}, u32[]{:S(2)}) collective-permute-start(bf16[256,512]{1,0:T(8,128)(2,1)S(1)} %collective-permute-done.12.refs_5_), channel_id=1, source_target_pairs={{0,4},{4,0},{8,12},{12,8},{16,20},{20,16},{24,28},{28,24},{1,5},{5... | collective-permute-start | bytes 786440 | tf_op jit(solution)/shard_map/ppermute | solution.py:535
  73.6 4.1 %collective-permute-start.16 = (bf16[1024,512]{1,0:T(8,128)(2,1)S(1)}, bf16[1024,512]{1,0:T(8,128)(2,1)S(1)}, u32[]{:S(2)}, u32[]{:S(2)}) collective-permute-start(bf16[1024,512]{1,0:T(8,128)(2,1)S(1)} %get-tuple-element.183.dh_ref), channel_id=1, source_target_pairs={{0,4},{4,0},{8,12},{12,8},{16,20},{20,16},{24,28},{28,24},{1,5},{5... | collective-permute-start | bytes 3145736 | tf_op jit(solution)/shard_map/ppermute | solution.py:535
  73.8 3.9 %collective-permute-start.17 = (bf16[512,512]{1,0:T(8,128)(2,1)S(1)}, bf16[512,512]{1,0:T(8,128)(2,1)S(1)}, u32[]{:S(2)}, u32[]{:S(2)}) collective-permute-start(bf16[512,512]{1,0:T(8,128)(2,1)S(1)} %get-tuple-element.186), channel_id=1, source_target_pairs={{0,4},{4,0},{8,12},{12,8},{16,20},{20,16},{24,28},{28,24},{1,5},{5... | collective-permute-start | bytes 1572872 | tf_op jit(solution)/shard_map/ppermute | solution.py:535
  74.2 26.6 %collective-permute-start.20 = (bf16[264,1024]{1,0:T(8,128)(2,1)S(1)}, bf16[264,1024]{1,0:T(8,128)(2,1)S(1)}, u32[]{:S(2)}, u32[]{:S(2)}) collective-permute-start(bf16[264,1024]{1,0:T(8,128)(2,1)S(1)} %get-tuple-element.207), channel_id=1, source_target_pairs={{0,8},{4,12},{8,0},{12,4},{16,24},{20,28},{24,16},{28,20},{1,9},{5... | collective-permute-start | bytes 1622024 | tf_op jit(solution)/shard_map/ppermute | solution.py:540
  75.4 25.4 %collective-permute-start.21 = (bf16[264,1024]{1,0:T(8,128)(2,1)S(1)}, bf16[264,1024]{1,0:T(8,128)(2,1)S(1)}, u32[]{:S(2)}, u32[]{:S(2)}) collective-permute-start(bf16[264,1024]{1,0:T(8,128)(2,1)S(1)} %get-tuple-element.208), channel_id=1, source_target_pairs={{0,16},{4,20},{8,24},{12,28},{16,0},{20,4},{24,8},{28,12},{1,17},{... | collective-permute-start | bytes 1622024 | tf_op jit(solution)/shard_map/ppermute | solution.py:540
  76.2 24.8 %collective-permute-start.22 = (bf16[264,1024]{1,0:T(8,128)(2,1)S(1)}, bf16[264,1024]{1,0:T(8,128)(2,1)S(1)}, u32[]{:S(2)}, u32[]{:S(2)}) collective-permute-start(bf16[264,1024]{1,0:T(8,128)(2,1)S(1)} %get-tuple-element.209), channel_id=1, source_target_pairs={{0,24},{4,28},{8,16},{12,20},{16,8},{20,12},{24,0},{28,4},{1,25},{... | collective-permute-start | bytes 1622024 | tf_op jit(solution)/shard_map/ppermute | solution.py:540
  82.1 18.9 %collective-permute-start.18 = (bf16[256,512]{1,0:T(8,128)(2,1)S(1)}, bf16[256,512]{1,0:T(8,128)(2,1)S(1)}, u32[]{:S(2)}, u32[]{:S(2)}) collective-permute-start(bf16[256,512]{1,0:T(8,128)(2,1)S(1)} %get-tuple-element.205), channel_id=1, source_target_pairs={{0,0},{4,1},{1,2},{5,3},{2,4},{6,5},{3,6},{7,7},{8,8},{12,9},{9,10... | collective-permute-start | bytes 786440 | tf_op jit(solution)/shard_map/ppermute | solution.py:1122
  82.8 18.3 %collective-permute-start.19 = (bf16[256,512]{1,0:T(8,128)(2,1)S(1)}, bf16[256,512]{1,0:T(8,128)(2,1)S(1)}, u32[]{:S(2)}, u32[]{:S(2)}) collective-permute-start(bf16[256,512]{1,0:T(8,128)(2,1)S(1)} %get-tuple-element.206), channel_id=1, source_target_pairs={{1,0},{5,1},{0,2},{4,3},{3,4},{7,5},{2,6},{6,7},{9,8},{13,9},{8,10... | collective-permute-start | bytes 786440 | tf_op jit(solution)/shard_map/ppermute | solution.py:1122
  101.8 7.8 %collective-permute-start.23 = (bf16[264,512]{1,0:T(8,128)(2,1)S(1)}, bf16[264,512]{1,0:T(8,128)(2,1)S(1)}, u32[]{:S(2)}, u32[]{:S(2)}) collective-permute-start(bf16[264,512]{1,0:T(8,128)(2,1)S(1)} %get-tuple-element.230), channel_id=1, source_target_pairs={{0,1},{1,0},{2,3},{3,2},{4,5},{5,4},{6,7},{7,6},{8,9},{9,8},{10,11... | collective-permute-start | bytes 811016 | tf_op jit(solution)/shard_map/ppermute | solution.py:550
  109.6 10.8 %collective-permute-start.28 = (bf16[512,512]{1,0:T(8,128)(2,1)S(1)}, bf16[512,512]{1,0:T(8,128)(2,1)S(1)}, u32[]{:S(2)}, u32[]{:S(2)}) collective-permute-start(bf16[512,512]{1,0:T(8,128)(2,1)S(1)} %get-tuple-element.242), channel_id=1, source_target_pairs={{0,4},{4,0},{8,12},{12,8},{16,20},{20,16},{24,28},{28,24},{1,5},{5... | collective-permute-start | bytes 1572872 | tf_op jit(solution)/shard_map/ppermute | solution.py:535
  109.6 24.6 %collective-permute-start.24 = (bf16[168,1024]{1,0:T(8,128)(2,1)}, bf16[168,1024]{1,0:T(8,128)(2,1)S(1)}, u32[]{:S(2)}, u32[]{:S(2)}) collective-permute-start(bf16[168,1024]{1,0:T(8,128)(2,1)} %get-tuple-element.236), channel_id=1, source_target_pairs={{0,8},{4,12},{8,0},{12,4},{16,24},{20,28},{24,16},{28,20},{1,9},{5... | collective-permute-start | bytes 1032200 | tf_op jit(solution)/shard_map/ppermute | solution.py:540
  117.0 17.2 %collective-permute-start.25 = (bf16[168,1024]{1,0:T(8,128)(2,1)}, bf16[168,1024]{1,0:T(8,128)(2,1)S(1)}, u32[]{:S(2)}, u32[]{:S(2)}) collective-permute-start(bf16[168,1024]{1,0:T(8,128)(2,1)} %get-tuple-element.237), channel_id=1, source_target_pairs={{0,16},{4,20},{8,24},{12,28},{16,0},{20,4},{24,8},{28,12},{1,17},{... | collective-permute-start | bytes 1032200 | tf_op jit(solution)/shard_map/ppermute | solution.py:540
  117.4 17.5 %collective-permute-start.26 = (bf16[168,1024]{1,0:T(8,128)(2,1)S(1)}, bf16[168,1024]{1,0:T(8,128)(2,1)S(1)}, u32[]{:S(2)}, u32[]{:S(2)}) collective-permute-start(bf16[168,1024]{1,0:T(8,128)(2,1)S(1)} %get-tuple-element.238), channel_id=1, source_target_pairs={{0,24},{4,28},{8,16},{12,20},{16,8},{20,12},{24,0},{28,4},{1,25},{... | collective-permute-start | bytes 1032200 | tf_op jit(solution)/shard_map/ppermute | solution.py:540
  118.9 15.3 %collective-permute-start.27 = (bf16[264,512]{1,0:T(8,128)(2,1)S(1)}, bf16[264,512]{1,0:T(8,128)(2,1)}, u32[]{:S(2)}, u32[]{:S(2)}) collective-permute-start(bf16[264,512]{1,0:T(8,128)(2,1)S(1)} %add_convert_fusion.2), channel_id=1, source_target_pairs={{0,2},{1,3},{2,0},{3,1},{4,6},{5,7},{6,4},{7,5},{8,10},{9,11},{10,... | collective-permute-start | bytes 811016 | tf_op jit(solution)/shard_map/ppermute | solution.py:550
  121.3 13.6 %copy-start.6 = (s32[4]{0:T(128)S(1)}, s32[4]{0:T(128)}, u32[]{:S(2)}) copy-start(s32[4]{0:T(128)} %copy-done.5) | copy-start | bytes 52
  125.1 23.6 %collective-permute-start.30 = (bf16[256,512]{1,0:T(8,128)(2,1)}, bf16[256,512]{1,0:T(8,128)(2,1)S(1)}, u32[]{:S(2)}, u32[]{:S(2)}) collective-permute-start(bf16[256,512]{1,0:T(8,128)(2,1)} %get-tuple-element.244), channel_id=1, source_target_pairs={{0,0},{4,1},{1,2},{5,3},{2,4},{6,5},{3,6},{7,7},{8,8},{12,9},{9,10... | collective-permute-start | bytes 786440 | tf_op jit(solution)/shard_map/ppermute | solution.py:1122
  134.2 14.5 %collective-permute-start.31 = (bf16[256,512]{1,0:T(8,128)(2,1)}, bf16[256,512]{1,0:T(8,128)(2,1)S(1)}, u32[]{:S(2)}, u32[]{:S(2)}) collective-permute-start(bf16[256,512]{1,0:T(8,128)(2,1)} %get-tuple-element.245), channel_id=1, source_target_pairs={{1,0},{5,1},{0,2},{4,3},{3,4},{7,5},{2,6},{6,7},{9,8},{13,9},{8,10... | collective-permute-start | bytes 786440 | tf_op jit(solution)/shard_map/ppermute | solution.py:1122
  135.6 13.1 %collective-permute-start.29 = (bf16[168,512]{1,0:T(8,128)(2,1)S(1)}, bf16[168,512]{1,0:T(8,128)(2,1)S(1)}, u32[]{:S(2)}, u32[]{:S(2)}) collective-permute-start(bf16[168,512]{1,0:T(8,128)(2,1)S(1)} %get-tuple-element.250), channel_id=1, source_target_pairs={{0,1},{1,0},{2,3},{3,2},{4,5},{5,4},{6,7},{7,6},{8,9},{9,8},{10,11... | collective-permute-start | bytes 516104 | tf_op jit(solution)/shard_map/ppermute | solution.py:550
  148.7 11.2 %collective-permute-start.33 = (bf16[264,512]{1,0:T(8,128)(2,1)S(1)}, bf16[264,512]{1,0:T(8,128)(2,1)S(1)}, u32[]{:S(2)}, u32[]{:S(2)}) collective-permute-start(bf16[264,512]{1,0:T(8,128)(2,1)S(1)} %add_convert_fusion.1.mine), channel_id=1, source_target_pairs={{0,1},{1,0},{2,3},{3,2},{4,5},{5,4},{6,7},{7,6},{8,9},{9,8},{10,11... | collective-permute-start | bytes 811016 | tf_op jit(solution)/shard_map/ppermute | solution.py:550
  148.8 14.6 %collective-permute-start.32 = (bf16[168,512]{1,0:T(8,128)(2,1)S(1)}, bf16[168,512]{1,0:T(8,128)(2,1)S(1)}, u32[]{:S(2)}, u32[]{:S(2)}) collective-permute-start(bf16[168,512]{1,0:T(8,128)(2,1)S(1)} %add_convert_fusion.4), channel_id=1, source_target_pairs={{0,2},{1,3},{2,0},{3,1},{4,6},{5,7},{6,4},{7,5},{8,10},{9,11},{10,... | collective-permute-start | bytes 516104 | tf_op jit(solution)/shard_map/ppermute | solution.py:550
  159.9 1.9 %collective-permute-start.34 = (bf16[2,72,512]{2,1,0:T(8,128)(2,1)S(1)}, bf16[2,72,512]{2,1,0:T(8,128)(2,1)S(1)}, u32[]{:S(2)}, u32[]{:S(2)}) collective-permute-start(bf16[2,72,512]{2,1,0:T(8,128)(2,1)S(1)} %pad_maximum_fusion.4), channel_id=1, source_target_pairs={{0,4},{4,0},{8,12},{12,8},{16,20},{20,16},{24,28},{28,24},{1,5},{5... | collective-permute-start | bytes 442376 | tf_op jit(solution)/shard_map/ppermute | solution.py:535
  163.5 1.5 collective-permute-start.35
  165.0 6.9 %collective-permute-start.36 = (bf16[176,512]{1,0:T(8,128)(2,1)S(1)}, bf16[176,512]{1,0:T(8,128)(2,1)S(1)}, u32[]{:S(2)}, u32[]{:S(2)}) collective-permute-start(bf16[176,512]{1,0:T(8,128)(2,1)S(1)} %pad_maximum_fusion.3.mine), channel_id=1, source_target_pairs={{0,1},{1,0},{2,3},{3,2},{4,5},{5,4},{6,7},{7,6},{8,9},{9,8},{10,11... | collective-permute-start | bytes 540680 | tf_op jit(solution)/shard_map/ppermute | solution.py:550
  (8 other events, 20.1 us)

commit v3 on v2

--- a/solution.py
+++ b/solution.py
@@ -98,7 +98,7 @@
     )(length, qkv, qkv, qkv, rel_rev, bias_u, bias_v)
 
 
-def attn_bwd_body(len_ref, q_ref, k_ref, v_ref, r_ref, bu_ref, bv_ref, lse_ref, do_ref, *refs, block):
+def attn_bwd_body(len_ref, q_ref, k_ref, v_ref, r_ref, bu_ref, bv_ref, lse_ref, do_ref, *refs, block, heads):
     dq_ref, dk_ref, dv_ref, dr_ref, gu_ref, gv_ref, dk_t, dv_t, dr_t = refs
     full = q_ref.shape[0]
     length = len_ref[0]
@@ -123,8 +123,9 @@
             qu_t = jnp.transpose(qu).astype(bf)
             do_t = jnp.transpose(do).astype(bf)
             qv_t = jnp.transpose(dot(flip, qv.astype(bf), NN)).astype(bf)
-            dqu, dqv = [], []
-            for head, side in enumerate(sides):
+            dqu, dqv = [0.0, 0.0], [0.0, 0.0]
+            for head in heads:
+                side = sides[head]
                 at = slice(head * HD, (head + 1) * HD)
                 s = scores(
                     jnp.where(side, qu, 0.0).astype(bf),
@@ -142,10 +143,10 @@
                 dv_t[at, :span] += dot(do_t[at], p.astype(bf), NN)
                 both = dot(jnp.concatenate([qu_t[at], flip], axis=0), ds, NN)
                 dk_t[at, :span] += both[:HD]
-                dqu.append(dot(ds, k_ref[:span, :], NN))
+                dqu[head] = dot(ds, k_ref[:span, :], NN)
                 ds_rev = pltpu.roll(both[HD:], 0, 1, stride=1, stride_axis=0).astype(bf)
                 dr_t[at, full - span :] += dot(qv_t[at], ds_rev, NN)
-                dqv.append(dot(ds_rev, r_ref[full - span :, :], NN))
+                dqv[head] = dot(ds_rev, r_ref[full - span :, :], NN)
             dqu = jnp.where(sides[0], dqu[0], dqu[1]) * 0.125
             dqv = jnp.where(sides[0], dqv[0], dqv[1]) * 0.125
             gu_ref[...] += jnp.sum(dqu, axis=0, keepdims=True)
@@ -157,7 +158,7 @@
     dr_ref[...] = jnp.transpose(dr_t[...]).astype(bf)
 
 
-def attn_bwd(length, qkv, rel_rev, bias_u, bias_v, lse, d_out, *, pair, block=256):
+def attn_bwd(length, qkv, rel_rev, bias_u, bias_v, lse, d_out, *, pair, heads=(0, 1), block=256):
     full, cols = rel_rev.shape
     pairs = cols // (2 * HD)
     at = lambda part: pl.BlockSpec((full, 2 * HD), lambda i, _: (0, part * pairs + pair))
@@ -165,7 +166,7 @@
     out = pl.BlockSpec((full, 2 * HD), lambda i, _: (0, 0))
     out_row = pl.BlockSpec((1, 2 * HD), lambda i, _: (0, 0))
     return pl.pallas_call(
-        functools.partial(attn_bwd_body, block=block),
+        functools.partial(attn_bwd_body, block=block, heads=heads),
         out_shape=(jax.ShapeDtypeStruct((full, 2 * HD), bf),) * 4
         + (jax.ShapeDtypeStruct((1, 2 * HD), f32),) * 2,
         grid_spec=pltpu.PrefetchScalarGridSpec(
@@ -831,11 +832,10 @@
 
 
 def qkv_back_body(meta, *refs):
-    grads, rels = refs[:6], refs[6:8]
-    w_ref, x_ref, h_ref, table_ref = refs[8:12]
-    gu_refs, gv_refs, go_ref = refs[12:14], refs[14:16], refs[16]
-    keep_ref, send_ref = refs[17:19]
-    outs, acc, sums = refs[19:23], refs[23], refs[24]
+    grads_a, grads_b, grads_c = refs[:6], refs[6:12], refs[12:18]
+    w_ref, x_ref, h_ref, table_ref, go_ref = refs[18:23]
+    keep_ref, send_ref = refs[23:25]
+    outs, acc, sums = refs[25:29], refs[29], refs[30]
     step, chip = pl.program_id(0), meta[CHIP]
     width = x_ref.shape[1]
     rows = width // 4
@@ -845,8 +845,9 @@
         sums[...] = jnp.zeros_like(sums)
         acc[...] = jnp.zeros_like(acc)
 
-    dqkv = jnp.concatenate([ref[...] for ref in grads], axis=1)
-    drel = jnp.concatenate([ref[...] for ref in rels], axis=1)
+    both = lambda i: [grads_a[i][...], grads_b[i][...] + grads_c[i][...]]
+    dqkv = jnp.concatenate(both(0) + both(1) + both(2), axis=1)
+    drel = jnp.concatenate(both(3), axis=1)
     span = dqkv.shape[1]
     acc[:, :span] += dot(h_ref[...], dqkv, TN)
     acc[:, span:] += dot(table_ref[...], drel, TN)
@@ -870,7 +871,7 @@
             at = pl.ds(aligned(chip ^ k, rows), rows)
             low = (chip ^ k) >> 1 == 0
             tail = [sums[0:1, at], sums[1:2, at]]
-            tail += [jnp.where(low, a[...], b[...]) for a, b in (gu_refs, gv_refs)]
+            tail += [jnp.where(low, *both(i)) for i in (4, 5)]
             tail = jnp.concatenate(tail + [jnp.zeros((1, acc.shape[1] - 4 * rows), f32)], axis=1)
             out[:rows] = acc[at, :].astype(out.dtype)
             out[rows : rows + 8] = jnp.broadcast_to(tail, (8, tail.shape[1])).astype(out.dtype)
@@ -1011,16 +1012,19 @@
     mine_ff = 4 * unit
 
     none = jnp.zeros((4,), jnp.int32)
-    x_own = to_slots(layer_input, rank)
+    x_own = to_slots(jnp.concatenate([layer_input, grad_out], axis=2), rank)
     vectors = (ln1_gain, ln1_bias, bias_u, bias_v, ln2_gain, ln2_bias, down_bias, up_bias)
     attn_rows, fold = shard + 8, shard // 2
     attn_pack, feed_pack, pack_send = kernel_call(
         pack_body,
         "pack",
         lengths,
-        [w_qkv, w_rel, w_up, w_out, w_down] + [v.reshape(-1, min(128, v.size)) for v in vectors],
+        [
+            pltpu.with_memory_space_constraint(v, pltpu.HBM)
+            for v in [w_qkv, w_rel, w_up, w_out, w_down] + [v.reshape(-1, min(128, v.size)) for v in vectors]
+        ],
         [((attn_rows, 4 * cols), bf), ((3 * shard + fold, 4 * cols), bf), ((attn_rows + shard + fold, 4 * cols), bf)],
-        vmem=60,
+        vmem=32,
     )
     pack_came = swap_core(pack_send)
     attn_pack = jnp.concatenate([attn_pack, pack_came[:attn_rows]], axis=0)
@@ -1032,15 +1036,6 @@
     length = jnp.where(rank & 1 == 0, lengths[0], lengths[1])
     meta = jnp.stack([core, chip, rank, length]).astype(jnp.int32)
     length_arr = length.reshape(1)
-    feed_pack, meta, length_arr, grad_out, *rest = together(
-        feed_pack, meta, length_arr, grad_out, *x_own, *attn_packs
-    )
-    grad_own = to_slots(grad_out, rank)
-    x_own, attn_packs = rest[:2], rest[2:]
-    x_other = [swap_core(x) for x in x_own]
-    feed_pack, x_other[0] = together(feed_pack, x_other[0])
-    feed_first = swap_axis(feed_pack, 0)
-
     fine = 32
     inv_freq = jnp.exp(lax.iota(f32, width // 2) * (-2.0 * math.log(10000.0) / width))
     high = (full - 1 - fine * lax.iota(jnp.int32, full // fine)).astype(f32)[:, None] * inv_freq
@@ -1052,6 +1047,15 @@
     )
     table = table.astype(bf).reshape(full, width)
 
+    feed_pack, meta, length_arr, table, *attn_packs = together(feed_pack, meta, length_arr, table, *attn_packs)
+    rest = list(together(*x_own, *attn_packs))
+    x_own, attn_packs = rest[:2], rest[2:]
+    x_other = [swap_core(x) for x in x_own]
+    feed_first = swap_axis(feed_pack, 0)
+    feed_pack, x_other[1] = together(feed_pack, x_other[1])
+    feed_second = swap_axis(feed_pack, 1)
+
+    side = lambda at: pl.BlockSpec((block, width), lambda i, _: (0, at))
     by_step = lambda width: pl.BlockSpec((block, width), lambda i, _: (i, 0))
     qkv, h1, x_slot, rel, w_own, vecs, up_b, own_u, own_v = kernel_call(
         project_body,
@@ -1061,18 +1065,16 @@
         [((full, 3 * cols), bf), ((full, width), bf), ((full, width), bf), ((full, cols), bf)]
         + [((width, 4 * cols), bf), ((8, width), f32), ((1, mine_ff), f32), ((1, cols), f32), ((1, cols), f32)],
         grid=(4,),
-        in_specs=[whole(2 * attn_rows, 4 * cols)] * 4 + [whole(block, width)] * 4 + [by_step(width)],
+        in_specs=[whole(2 * attn_rows, 4 * cols)] * 4 + [side(0)] * 4 + [by_step(width)],
         out_specs=[by_step(3 * cols), by_step(width), by_step(width), by_step(cols)]
         + [whole(width, 4 * cols), whole(8, width), whole(1, mine_ff), whole(1, cols), whole(1, cols)],
         flops=2 * full * width * 4 * cols,
         vmem=32,
     )
-    qkv, feed_later, feed_first = together(qkv, feed_pack, feed_first)
-    feed_second = swap_axis(feed_later, 1)
+    qkv, feed_first = together(qkv, feed_first)
     feed_third = swap_axis(feed_first, 1)
     attn, lse = attn_fwd(length_arr, qkv, rel, own_u, own_v)
-    attn, feed_second, feed_third, *grad_own = together(attn, feed_second, feed_third, *grad_own)
-    grad_other = [swap_core(g) for g in grad_own]
+    attn, feed_second, feed_third = together(attn, feed_second, feed_third)
     feed_packs = [feed_pack, feed_first, feed_second, feed_third]
 
     attn_other = swap_core(attn)
@@ -1083,12 +1085,12 @@
         feed_body,
         "feed",
         meta,
-        feed_packs + grad_own + grad_other + [x_slot, attn, attn_other, vecs, up_b],
+        feed_packs + x_own + x_other + [x_slot, attn, attn_other, vecs, up_b],
         [((full, width), bf), ((full, width), bf), ((full, 1), f32), ((half, width), f32)]
         + [((full, width), bf), ((half, width), bf), ((cols, width), bf)]
         + blocks(rows + unit // 2),
         grid=(4,),
-        in_specs=[whole(*feed_pack.shape)] * 4 + [whole(block, width)] * 4
+        in_specs=[whole(*feed_pack.shape)] * 4 + [side(1)] * 4
         + [by_step(width), by_step(cols), by_step(cols), whole(8, width), whole(1, mine_ff)],
         out_specs=[by_step(width), by_step(width), by_step(1), kept(width)]
         + [by_step(width), kept(width), whole(cols, width)]
@@ -1123,34 +1125,34 @@
         for turn, out in enumerate(outs)
     ]
     y_turns = home((out0, out1))
-    back = lambda pair: attn_bwd(length_arr, qkv, rel, own_u, own_v, lse, d_attn, pair=pair)
-    first_pair = back(0)
-    d_attn, *first_pair = together(d_attn, *first_pair)
-    *second_pair, y0, y1, e1, e2, e3 = together(*back(1), *y_turns, *early_came)
-    q0, k0, v0, r0, u0, b0 = first_pair
-    q1, k1, v1, r1, u1, b1 = second_pair
+    back = lambda pair, heads, d_out: attn_bwd(
+        length_arr, qkv, rel, own_u, own_v, lse, d_out, pair=pair, heads=heads
+    )
+    d_attn, *grads_a = together(d_attn, *back(0, (0, 1), d_attn))
+    *grads_b, y0, y1, e1, e2, e3 = together(*back(1, (0,), d_attn), *y_turns, *early_came)
     early_keep, early_send = chip_sum(meta, [early_parts[0], e1, e2, e3], "early_chips", 0)
-    early_send, q1 = together(early_send, q1)
-    early_came = swap_seq(early_send, 1)
+    d_attn, early_send, early_keep = together(d_attn, early_send, early_keep)
+    *grads_c, early_came = together(*back(1, (1,), d_attn), swap_seq(early_send, 1))
+    early_pair = (early_keep + early_came.astype(f32)).astype(bf)
+    early_pair, *grads_c = together(early_pair, *grads_c)
+    early_came = swap_seq(early_pair, 2)
     pair_step = pl.BlockSpec((block, 2 * HEAD_DIM), lambda i, _: (i, 0))
     pair_row = whole(1, 2 * HEAD_DIM)
     dh1_keep, dh1_send, *late_parts = kernel_call(
         qkv_back_body,
         "qkv_back",
         meta,
-        [q0, q1, k0, k1, v0, v1, r0, r1, w_own, x_slot, h1, table, u0, u1, b0, b1, g_out],
+        [*grads_a, *grads_b, *grads_c, w_own, x_slot, h1, table, g_out],
         [((half, width), f32), ((half, width), bf)] + blocks(rows + fold),
         grid=(4,),
-        in_specs=[pair_step] * 8 + [whole(width, 4 * cols)] + [by_step(width)] * 3
-        + [pair_row] * 4 + [whole(cols, width)],
+        in_specs=([pair_step] * 4 + [pair_row] * 2) * 3
+        + [whole(width, 4 * cols)] + [by_step(width)] * 3 + [whole(cols, width)],
         out_specs=[kept(width)] * 2 + [whole(rows + fold, 2 * width)] * 4,
         scratch=[pltpu.VMEM((width, 4 * cols), f32), pltpu.VMEM((8, width), f32)],
         flops=14 * full * width * cols,
     )
-    dh1_send, early_came, *late_parts = together(dh1_send, early_came, *late_parts)
+    dh1_send, *late_parts = together(dh1_send, *late_parts)
     dh1_came = swap_core(dh1_send)
-    early_pair = (early_keep + early_came.astype(f32)).astype(bf)
-    early_came = swap_seq(early_pair, 2)
     late_came = [swap_chip(late_parts[k], k) for k in (1, 2, 3)]
     by_half = pl.BlockSpec((block, width), lambda i, _: (i, 0))
     own_rows = pl.BlockSpec((block, width), lambda i, m: (2 * i + m[CORE], 0))
@@ -1163,15 +1165,20 @@
         grid=(2,),
         in_specs=[own_rows] + [by_half] * 3 + [whole(8, width)],
         out_specs=[whole(block, width)] * 2,
-        vmem=60,
     )
     x_turns = home((x0, x1))
     *late_came, early_came, _, _ = together(*late_came, early_came, x0, x1)
     early_mine = (early_pair.astype(f32) + early_came.astype(f32)).astype(bf)
     late_keep, late_send = chip_sum(meta, [late_parts[0]] + late_came, "late_chips", 0)
     small = lambda size: ((1, size), f32)
-    late_came, g0, g1, early_mine = together(swap_seq(late_send, 1), *x_turns, early_mine)
+    late_came, early_mine = together(swap_seq(late_send, 1), early_mine)
+    late_pair = (late_keep + late_came.astype(f32)).astype(bf)
+    late_came = swap_seq(late_pair, 2)
     early_other = swap_seq(early_mine, 1)
+    late_total = (late_pair.astype(f32) + late_came.astype(f32)).astype(bf)
+    late_mine = own_rows_first(late_total, core, shard)
+    late_other = swap_seq(late_mine, 1)
+    late_mine, g0, g1, early_other = together(late_mine, *x_turns, early_other)
     theirs = lambda rows: jnp.concatenate(
         [
             lax.dynamic_slice_in_dim(rows, (1 - core) * shard, shard, 0),
@@ -1180,6 +1187,13 @@
         axis=0,
     )
     early_core = swap_core(jnp.stack([theirs(early_mine), theirs(early_other)]))
+    output, grad_x = kernel_call(
+        place_body,
+        "place",
+        meta,
+        [y0, y1, g0, g1],
+        [((2, block, width), bf), ((2, block, width), f32)],
+    )
     g_up, g_down, g_gain_two, g_shift_two, g_down_shift, g_up_shift = kernel_call(
         early_out_body,
         "early_out",
@@ -1187,22 +1201,12 @@
         [early_mine, early_other, early_core],
         [((shard, 2 * mine_ff), f32), ((unit, width), f32)] + [small(shard)] * 3 + [small(unit)],
     )
-    late_pair = (late_keep + late_came.astype(f32)).astype(bf)
-    output, grad_x = kernel_call(
-        place_body,
-        "place",
-        meta,
-        [y0, y1, g0, g1],
-        [((2, block, width), bf), ((2, block, width), f32)],
-    )
-    late_came, output, grad_x, g_up = together(swap_seq(late_pair, 2), output, grad_x, g_up)
-    late_total = (late_pair.astype(f32) + late_came.astype(f32)).astype(bf)
-    late_mine = own_rows_first(late_total, core, shard)
+    late_other, output, grad_x, g_up = together(late_other, output, grad_x, g_up)
     g_qkv, g_rel, g_w_out, *late_vectors = kernel_call(
         late_out_body,
         "late_out",
         meta,
-        [late_mine, swap_seq(late_mine, 1)],
+        [late_mine, late_other],
         [((shard, 6 * cols), f32), ((shard, 2 * cols), f32), ((shard, width), f32)] + [small(shard)] * 4,
     )
     g_gain_one, g_shift_one, g_bias_u, g_bias_v = [v.reshape(-1) for v in late_vectors]

time: 174 us -> 167 us (0.960)
  starting transfers between devices: 40.6 us -> 33.6 us
  Pallas kernels: 62.8 us -> 67.4 us
  local copies, waits for them, and re-layouts: 5.48 us -> 3.53 us
  other arithmetic: 4.05 us -> 2.21 us
    pallas_call x2 -> x3, Pallas kernels: 14.6 us -> 23.3 us  [attn_bwd(): pl.pallas_call(functools.partial(attn_bwd_body, block=block, heads=heads)...]
    ppermute x9, waiting for transfers between devices: 4.75 us -> 11.6 us  [swap_chip(): lax.ppermute(values, 'fsdp', [(i, i ^ 2 * mask) for i in range(size)])]
    ppermute x4 -> x2, waiting for transfers between devices: 11.2 us -> 5.05 us  [to_slots(): lax.ppermute(lax.dynamic_index_in_dim(values, turn ^ seq_rank >> 1, 0, ke...]
    ppermute x9, starting transfers between devices: 16.3 us -> 10.7 us  [swap_chip(): lax.ppermute(values, 'fsdp', [(i, i ^ 2 * mask) for i in range(size)])]
    pallas_call x11, Pallas kernels: 38.2 us -> 34 us  [kernel_call(): pl.pallas_call(body, out_shape=[jax.ShapeDtypeStruct(shape, kind) for sha...]
    ppermute x6, waiting for transfers between devices: 36.9 us -> 33.3 us  [swap_seq(): return lax.ppermute(values, 'seq', [(i, i ^ mask) for i in range(size)])]
    ppermute x4, waiting for transfers between devices: 0.01 us -> 2.99 us  [slot_split_device(): lax.ppermute(out, ('fsdp', 'seq'), [(b, a) for a, b in slot_pairs(turn)])]
    ppermute x4 -> x2, starting transfers between devices: 7.37 us -> 4.58 us  [to_slots(): lax.ppermute(lax.dynamic_index_in_dim(values, turn ^ seq_rank >> 1, 0, ke...]
  transfers between devices with their start and end apart: 37 -> 33, of which waited for: 16 -> 14; matrix products, arithmetic and copies ran while one was open for 3% -> 2% of each run, Pallas kernels for 27% -> 28%
where the time goes in v3:
time: 167 us
  Pallas kernels  67.4 us (40%)
  waiting for transfers between devices  57.4 us (34%)
  starting transfers between devices  33.6 us (20%)
  local copies, waits for them, and re-layouts  3.53 us (2%)
  between operations  2.47 us (1%)
  other arithmetic  2.21 us (1%)
    pallas_call x11, Pallas kernels, kernel_call(): pl.pallas_call(body, out_shape=[jax.ShapeDtypeStruct(shape, kind) for sha...  34 us
    ppermute x6, waiting for transfers between devices, swap_seq(): return lax.ppermute(values, 'seq', [(i, i ^ mask) for i in range(size)])  33.3 us
    pallas_call x3, Pallas kernels, attn_bwd(): pl.pallas_call(functools.partial(attn_bwd_body, block=block, heads=heads)...  23.3 us
    ppermute x9, waiting for transfers between devices, swap_chip(): lax.ppermute(values, 'fsdp', [(i, i ^ 2 * mask) for i in range(size)])  11.6 us
    ppermute x9, starting transfers between devices, swap_chip(): lax.ppermute(values, 'fsdp', [(i, i ^ 2 * mask) for i in range(size)])  10.7 us
    pallas_call x1, Pallas kernels, attn_fwd(): pl.pallas_call(functools.partial(attn_fwd_body, block=block), out_shape=(...  10.1 us
    ppermute x4, starting transfers between devices, slot_split_device(): lax.ppermute(out, ('fsdp', 'seq'), [(b, a) for a, b in slot_pairs(turn)])  7.37 us
    ppermute x6, starting transfers between devices, swap_seq(): return lax.ppermute(values, 'seq', [(i, i ^ mask) for i in range(size)])  5.43 us
  transfers between devices with their start and end apart: 33, of which 14 were waited for; matrix products, arithmetic and copies ran while one was open for 2% of the time, Pallas kernels for 28%

profile of v3, /device:TPU:0, one launch (start us, length us, event | category | flops | bytes accessed | tf_op | source)
XLA Modules:
  0.0 166.7 jit_solution(2509243934630980697)
XLA Ops:
  1.3 2.0 %pack.1 = (bf16[72,1024]{1,0:T(8,128)(2,1)S(1)}, bf16[224,1024]{1,0:T(8,128)(2,1)S(1)}, bf16[168,1024]{1,0:T(8,128)(2,1)S(1)}) custom-call(s32[2]{0:T(128)S(1)} %copy-done.9, bf16[64,1536]{1,0:T(8,128)(2,1)} %qkv_ref.1, bf16[64,512]{1,0:T(8,128)(2,1)} %rel_ref.1, bf16[64,2048]{1,0:T(8,128)(2,1)} %up_ref.1, bf16[64,512]{1,0:T(8,128)(2,1)} %out_ref.1, ...), custom_call_target="tpu_custom_call" | custom-call | tf_op jit(solution)/shard_map/pack/pallas_call | solution.py:587
  3.8 1.1 constant_dynamic-update-slice_fusion.1
  5.1 0.7 collective-permute-start.4
  5.8 3.9 %collective-permute-start.5 = (bf16[256,1024]{1,0:T(8,128)(2,1)S(1)}, bf16[256,1024]{1,0:T(8,128)(2,1)S(1)}, u32[]{:S(2)}, u32[]{:S(2)}) collective-permute-start(bf16[256,1024]{1,0:T(8,128)(2,1)S(1)} %get-tuple-element.323), channel_id=1, source_target_pairs={{0,1},{1,5},{2,0},{3,4},{4,3},{5,7},{6,2},{7,6},{8,9},{9,13},{10,8... | collective-permute-start | bytes 1572872 | tf_op jit(solution)/shard_map/ppermute | solution.py:565
  10.4 1.1 pad_maximum_fusion.refs_8_.refs_21_
  11.7 2.1 %collective-permute-start.1 = (bf16[144,1024]{1,0:T(8,128)(2,1)S(1)}, bf16[144,1024]{1,0:T(8,128)(2,1)}, u32[]{:S(2)}, u32[]{:S(2)}) collective-permute-start(bf16[144,1024]{1,0:T(8,128)(2,1)S(1)} %pad_maximum_fusion.2.refs_0_), channel_id=1, source_target_pairs={{0,8},{4,12},{8,0},{12,4},{16,24},{20,28},{24,16},{28,20},{1,9},{5... | collective-permute-start | bytes 884744 | tf_op jit(solution)/shard_map/ppermute | solution.py:541
  13.8 1.5 collective-permute-start.2
  17.4 2.7 %collective-permute-done.1.refs_1_ = bf16[144,1024]{1,0:T(8,128)(2,1)} collective-permute-done((bf16[144,1024]{1,0:T(8,128)(2,1)S(1)}, bf16[144,1024]{1,0:T(8,128)(2,1)}, u32[]{:S(2)}, u32[]{:S(2)}) %collective-permute-start.1) | collective-permute-done | bytes 294944 | tf_op jit(solution)/shard_map/ppermute | solution.py:541
  20.2 8.2 %collective-permute-done.2.refs_2_ = bf16[144,1024]{1,0:T(8,128)(2,1)} collective-permute-done((bf16[144,1024]{1,0:T(8,128)(2,1)S(1)}, bf16[144,1024]{1,0:T(8,128)(2,1)}, u32[]{:S(2)}, u32[]{:S(2)}) %collective-permute-start.2) | collective-permute-done | bytes 294944 | tf_op jit(solution)/shard_map/ppermute | solution.py:541
  28.6 1.4 collective-permute-start.8
  30.0 5.0 %collective-permute-done.5.refs_5_ = bf16[256,1024]{1,0:T(8,128)(2,1)S(1)} collective-permute-done((bf16[256,1024]{1,0:T(8,128)(2,1)S(1)}, bf16[256,1024]{1,0:T(8,128)(2,1)S(1)}, u32[]{:S(2)}, u32[]{:S(2)}) %collective-permute-start.5) | collective-permute-done | bytes 524320 | tf_op jit(solution)/shard_map/ppermute | solution.py:565
  35.6 1.4 collective-permute-done.6.refs_7_
  37.0 1.5 collective-permute-start.9
  38.6 0.8 copy-done.7
  39.3 5.4 %project.1 = (bf16[1024,768]{1,0:T(8,128)(2,1)S(1)}, bf16[1024,512]{1,0:T(8,128)(2,1)S(1)}, bf16[1024,512]{1,0:T(8,128)(2,1)S(1)}, bf16[1024,256]{1,0:T(8,128)(2...) custom-call(s32[4]{0:T(128)S(1)} %broadcast_3__.2._, ...), custom_call_target="tpu_custom_call" | custom-call | tf_op jit(solution)/shard_map/project/pallas_call | solution.py:587
  44.8 0.8 collective-permute-start.10
  45.6 10.1 %attn_fwd.1 = (bf16[1024,256]{1,0:T(8,128)(2,1)S(1)}, f32[4,1024,1]{2,1,0:T(8,128)S(1)}) custom-call(s32[1]{0:T(128)} %bitcast.15.len_ref, bf16[1024,768]{1,0:T(8,128)(2,1)S(1)} %get-tuple-element.194.q_ref.k_ref.v_ref, bf16[1024,768]{1,0:T(8,128)(2,1)S(1)} %get-tuple-element.194.q_ref.k_ref.v_ref, ...), custom_call_target="tpu_custom_call" | custom-call | tf_op jit(solution)/shard_map/attn_fwd/pallas_call | solution.py:83
  55.8 1.9 %collective-permute-done.11.refs_10_ = bf16[1024,256]{1,0:T(8,128)(2,1)S(1)} collective-permute-done((bf16[1024,256]{1,0:T(8,128)(2,1)S(1)}, bf16[1024,256]{1,0:T(8,128)(2,1)S(1)}, u32[]{:S(2)}, u32[]{:S(2)}) %collective-permute-start.11) | collective-permute-done | bytes 524320 | tf_op jit(solution)/shard_map/ppermute | solution.py:536
  57.7 11.2 %feed.1 = (bf16[1024,512]{1,0:T(8,128)(2,1)S(1)}, bf16[1024,512]{1,0:T(8,128)(2,1)S(1)}, f32[1024,1]{1,0:T(8,128)S(1)}, f32[512,512]{1,0:T(8,128)S(1)}, bf16[102...) custom-call(s32[4]{0:T(128)S(1)} %pad_add_fusion.meta, ...), custom_call_target="tpu_custom_call" | custom-call | tf_op jit(solution)/shard_map/feed/pallas_call | solution.py:587
  69.4 1.5 collective-permute-start.16
  70.9 1.3 collective-permute-start.17
  72.2 0.7 collective-permute-start.18
  72.9 3.4 %norm_two.1 = (bf16[256,512]{1,0:T(8,128)(2,1)S(1)}, bf16[256,512]{1,0:T(8,128)(2,1)S(1)}, f32[512,512]{1,0:T(8,128)S(1)}, bf16[1024,256]{1,0:T(8,128)(2,1)S(1)}, f32[256,512]{1,0:T(8,128)S(1)}) custom-call(s32[4]{0:T(128)S(1)} %pad_add_fusion.meta, bf16[1024,512]{1,0:T(8,128)(2,1)S(1)} %get-tuple-element.205.x_hat_ref, ...), custom_call_target="tpu_custom_call" | custom-call | tf_op jit(solution)/shard_map/norm_two/pallas_call | solution.py:587
  76.4 0.7 collective-permute-start.14
  77.1 3.4 %collective-permute-start.15 = (bf16[256,512]{1,0:T(8,128)(2,1)S(1)}, bf16[256,512]{1,0:T(8,128)(2,1)S(1)}, u32[]{:S(2)}, u32[]{:S(2)}) collective-permute-start(bf16[256,512]{1,0:T(8,128)(2,1)S(1)} %get-tuple-element.234), channel_id=1, source_target_pairs={{1,0},{5,1},{0,2},{4,3},{3,4},{7,5},{2,6},{6,7},{9,8},{13,9},{8,10... | collective-permute-start | bytes 786440 | tf_op jit(solution)/shard_map/ppermute | solution.py:1124
  80.4 10.3 %attn_bwd.3 = (bf16[1024,128]{1,0:T(8,128)(2,1)S(1)}, bf16[1024,128]{1,0:T(8,128)(2,1)S(1)}, bf16[1024,128]{1,0:T(8,128)(2,1)S(1)}, bf16[1024,128]{1,0:T(8,128)(...) custom-call(s32[1]{0:T(128)} %bitcast.15.len_ref, bf16[1024,768]{1,0:T(8,128)(2,1)S(1)} %get-tuple-element.194.q_ref.k_ref.v_ref, ...), custom_call_target="tpu_custom_call" | custom-call | tf_op jit(solution)/shard_map/attn_bwd/pallas_call | solution.py:168
  90.8 6.6 %attn_bwd.4 = (bf16[1024,128]{1,0:T(8,128)(2,1)S(1)}, bf16[1024,128]{1,0:T(8,128)(2,1)S(1)}, bf16[1024,128]{1,0:T(8,128)(2,1)S(1)}, bf16[1024,128]{1,0:T(8,128)(...) custom-call(s32[1]{0:T(128)} %bitcast.15.len_ref, bf16[1024,768]{1,0:T(8,128)(2,1)S(1)} %get-tuple-element.194.q_ref.k_ref.v_ref, ...), custom_call_target="tpu_custom_call" | custom-call | tf_op jit(solution)/shard_map/attn_bwd/pallas_call | solution.py:168
  97.4 0.8 early_chips.1
  98.3 6.4 %attn_bwd.5 = (bf16[1024,128]{1,0:T(8,128)(2,1)S(1)}, bf16[1024,128]{1,0:T(8,128)(2,1)S(1)}, bf16[1024,128]{1,0:T(8,128)(2,1)S(1)}, bf16[1024,128]{1,0:T(8,128)(...) custom-call(s32[1]{0:T(128)} %bitcast.15.len_ref, bf16[1024,768]{1,0:T(8,128)(2,1)S(1)} %get-tuple-element.194.q_ref.k_ref.v_ref, ...), custom_call_target="tpu_custom_call" | custom-call | tf_op jit(solution)/shard_map/attn_bwd/pallas_call | solution.py:168
  104.7 1.4 collective-permute-done.19
  106.2 4.2 %qkv_back.1 = (f32[512,512]{1,0:T(8,128)S(1)}, bf16[512,512]{1,0:T(8,128)(2,1)S(1)}, f32[168,1024]{1,0:T(8,128)S(1)}, bf16[168,1024]{1,0:T(8,128)(2,1)S(1)}, bf1...) custom-call(s32[4]{0:T(128)S(1)} %pad_add_fusion.meta, bf16[1024,128]{1,0:T(8,128)(2,1)S(1)} %get-tuple-element.220.refs_0_, ...), custom_call_target="tpu_custom_call" | custom-call | tf_op jit(solution)/shard_map/qkv_back/pallas_call | solution.py:587
  110.5 1.6 collective-permute-start.21
  112.2 1.8 %collective-permute-start.22 = (bf16[168,1024]{1,0:T(8,128)(2,1)S(1)}, bf16[168,1024]{1,0:T(8,128)(2,1)S(1)}, u32[]{:S(2)}, u32[]{:S(2)}) collective-permute-start(bf16[168,1024]{1,0:T(8,128)(2,1)S(1)} %get-tuple-element.283), channel_id=1, source_target_pairs={{0,24},{4,28},{8,16},{12,20},{16,8},{20,12},{24,0},{28,4},{1,25},{... | collective-permute-start | bytes 1032200 | tf_op jit(solution)/shard_map/ppermute | solution.py:541
  114.0 2.0 %collective-permute-start.23 = (bf16[264,512]{1,0:T(8,128)(2,1)S(1)}, bf16[264,512]{1,0:T(8,128)(2,1)S(1)}, u32[]{:S(2)}, u32[]{:S(2)}) collective-permute-start(bf16[264,512]{1,0:T(8,128)(2,1)S(1)} %add_convert_fusion.2), channel_id=1, source_target_pairs={{0,2},{1,3},{2,0},{3,1},{4,6},{5,7},{6,4},{7,5},{8,10},{9,11},{10,... | collective-permute-start | bytes 811016 | tf_op jit(solution)/shard_map/ppermute | solution.py:551
  116.0 1.4 norm_one.1
  117.4 11.3 %collective-permute-done.23 = bf16[264,512]{1,0:T(8,128)(2,1)S(1)} collective-permute-done((bf16[264,512]{1,0:T(8,128)(2,1)S(1)}, bf16[264,512]{1,0:T(8,128)(2,1)S(1)}, u32[]{:S(2)}, u32[]{:S(2)}) %collective-permute-start.23) | collective-permute-done | bytes 270368 | tf_op jit(solution)/shard_map/ppermute | solution.py:551
  129.1 0.7 late_chips.1
  129.8 1.0 collective-permute-start.25
  130.9 4.9 %collective-permute-done.25 = bf16[168,512]{1,0:T(8,128)(2,1)S(1)} collective-permute-done((bf16[168,512]{1,0:T(8,128)(2,1)S(1)}, bf16[168,512]{1,0:T(8,128)(2,1)S(1)}, u32[]{:S(2)}, u32[]{:S(2)}) %collective-permute-start.25) | collective-permute-done | bytes 172064 | tf_op jit(solution)/shard_map/ppermute | solution.py:551
  135.8 1.6 collective-permute-start.26
  138.1 2.7 %collective-permute-start.30 = (bf16[256,512]{1,0:T(8,128)(2,1)S(1)}, bf16[256,512]{1,0:T(8,128)(2,1)S(1)}, u32[]{:S(2)}, u32[]{:S(2)}) collective-permute-start(bf16[256,512]{1,0:T(8,128)(2,1)S(1)} %get-tuple-element.289), channel_id=1, source_target_pairs={{1,0},{5,1},{0,2},{4,3},{3,4},{7,5},{2,6},{6,7},{9,8},{13,9},{8,10... | collective-permute-start | bytes 786440 | tf_op jit(solution)/shard_map/ppermute | solution.py:1124
  141.4 10.1 %collective-permute-done.26 = bf16[168,512]{1,0:T(8,128)(2,1)S(1)} collective-permute-done((bf16[168,512]{1,0:T(8,128)(2,1)S(1)}, bf16[168,512]{1,0:T(8,128)(2,1)S(1)}, u32[]{:S(2)}, u32[]{:S(2)}) %collective-permute-start.26) | collective-permute-done | bytes 172064 | tf_op jit(solution)/shard_map/ppermute | solution.py:551
  151.8 1.2 collective-permute-done.27
  153.1 3.0 %collective-permute-done.30.x1 = bf16[256,512]{1,0:T(8,128)(2,1)S(1)} collective-permute-done((bf16[256,512]{1,0:T(8,128)(2,1)S(1)}, bf16[256,512]{1,0:T(8,128)(2,1)S(1)}, u32[]{:S(2)}, u32[]{:S(2)}) %collective-permute-start.30) | collective-permute-done | bytes 262176 | tf_op jit(solution)/shard_map/ppermute | solution.py:1124
  156.1 5.6 %collective-permute-done.31.other = bf16[264,512]{1,0:T(8,128)(2,1)S(1)} collective-permute-done((bf16[264,512]{1,0:T(8,128)(2,1)S(1)}, bf16[264,512]{1,0:T(8,128)(2,1)S(1)}, u32[]{:S(2)}, u32[]{:S(2)}) %collective-permute-start.31) | collective-permute-done | bytes 270368 | tf_op jit(solution)/shard_map/ppermute | solution.py:551
  161.8 1.8 %place.1 = (bf16[2,256,512]{2,1,0:T(8,128)(2,1)}, f32[2,256,512]{2,1,0:T(8,128)}) custom-call(s32[4]{0:T(128)S(1)} %pad_add_fusion.meta, bf16[256,512]{1,0:T(8,128)(2,1)S(1)} %collective-permute-done.14.y0, bf16[256,512]{1,0:T(8,128)(2,1)S(1)} %collective-permute-done.15.y1, bf16[256,512]{1,0:T(8,128)(2,1)S(1)} %collective-permute-done.29.x0, ...), custom_call_target="tpu_custom_call" | custom-call | tf_op jit(solution)/shard_map/place/pallas_call | solution.py:587
  163.6 1.6 early_out.1
  165.2 1.5 late_out.1
  (94 shorter events, 7.0 us)
Async XLA Ops:
  0.7 0.7 copy-start.9
  1.3 3.7 %copy-start.12 = (bf16[2,256,512]{2,1,0:T(8,128)(2,1)S(1)}, bf16[2,256,512]{2,1,0:T(8,128)(2,1)}, u32[]{:S(2)}) copy-start(bf16[2,256,512]{2,1,0:T(8,128)(2,1)} %param.31) | copy-start | bytes 1572868
  3.3 8.1 %collective-permute-start = (bf16[168,1024]{1,0:T(8,128)(2,1)S(1)}, bf16[168,1024]{1,0:T(8,128)(2,1)S(1)}, u32[]{:S(2)}, u32[]{:S(2)}) collective-permute-start(bf16[168,1024]{1,0:T(8,128)(2,1)S(1)} %get-tuple-element.170), channel_id=1, source_target_pairs={{0,4},{4,0},{8,12},{12,8},{16,20},{20,16},{24,28},{28,24},{1,5},{5... | collective-permute-start | bytes 1032200 | tf_op jit(solution)/shard_map/ppermute | solution.py:536
  5.1 24.9 %collective-permute-start.4 = (bf16[256,1024]{1,0:T(8,128)(2,1)S(1)}, bf16[256,1024]{1,0:T(8,128)(2,1)S(1)}, u32[]{:S(2)}, u32[]{:S(2)}) collective-permute-start(bf16[256,1024]{1,0:T(8,128)(2,1)S(1)} %get-tuple-element.324), channel_id=1, source_target_pairs={{0,0},{1,4},{2,1},{3,5},{4,2},{5,6},{6,3},{7,7},{8,8},{9,12},{10,9... | collective-permute-start | bytes 1572872 | tf_op jit(solution)/shard_map/ppermute | solution.py:565
  5.8 29.3 %collective-permute-start.5 = (bf16[256,1024]{1,0:T(8,128)(2,1)S(1)}, bf16[256,1024]{1,0:T(8,128)(2,1)S(1)}, u32[]{:S(2)}, u32[]{:S(2)}) collective-permute-start(bf16[256,1024]{1,0:T(8,128)(2,1)S(1)} %get-tuple-element.323), channel_id=1, source_target_pairs={{0,1},{1,5},{2,0},{3,4},{4,3},{5,7},{6,2},{7,6},{8,9},{9,13},{10,8... | collective-permute-start | bytes 1572872 | tf_op jit(solution)/shard_map/ppermute | solution.py:565
  10.4 5.0 %copy-start.10 = (s32[2]{0:T(128)S(1)}, s32[2]{0:T(128)}, u32[]{:S(2)}) copy-start(s32[2]{0:T(128)} %lengths_ref.1) | copy-start | bytes 28
  11.7 26.8 %copy-start.11 = (bf16[144,1024]{1,0:T(8,128)(2,1)}, bf16[144,1024]{1,0:T(8,128)(2,1)S(1)}, u32[]{:S(2)}) copy-start(bf16[144,1024]{1,0:T(8,128)(2,1)S(1)} %pad_maximum_fusion.2.refs_0_) | copy-start | bytes 884740
  11.7 8.4 %collective-permute-start.1 = (bf16[144,1024]{1,0:T(8,128)(2,1)S(1)}, bf16[144,1024]{1,0:T(8,128)(2,1)}, u32[]{:S(2)}, u32[]{:S(2)}) collective-permute-start(bf16[144,1024]{1,0:T(8,128)(2,1)S(1)} %pad_maximum_fusion.2.refs_0_), channel_id=1, source_target_pairs={{0,8},{4,12},{8,0},{12,4},{16,24},{20,28},{24,16},{28,20},{1,9},{5... | collective-permute-start | bytes 884744 | tf_op jit(solution)/shard_map/ppermute | solution.py:541
  13.8 14.5 %collective-permute-start.2 = (bf16[144,1024]{1,0:T(8,128)(2,1)S(1)}, bf16[144,1024]{1,0:T(8,128)(2,1)}, u32[]{:S(2)}, u32[]{:S(2)}) collective-permute-start(bf16[144,1024]{1,0:T(8,128)(2,1)S(1)} %pad_maximum_fusion.2.refs_0_), channel_id=1, source_target_pairs={{0,16},{4,20},{8,24},{12,28},{16,0},{20,4},{24,8},{28,12},{1,17},{... | collective-permute-start | bytes 884744 | tf_op jit(solution)/shard_map/ppermute | solution.py:541
  15.4 13.3 %collective-permute-start.3 = (bf16[144,1024]{1,0:T(8,128)(2,1)S(1)}, bf16[144,1024]{1,0:T(8,128)(2,1)}, u32[]{:S(2)}, u32[]{:S(2)}) collective-permute-start(bf16[144,1024]{1,0:T(8,128)(2,1)S(1)} %pad_maximum_fusion.2.refs_0_), channel_id=1, source_target_pairs={{0,24},{4,28},{8,16},{12,20},{16,8},{20,12},{24,0},{28,4},{1,25},{... | collective-permute-start | bytes 884744 | tf_op jit(solution)/shard_map/ppermute | solution.py:541
  28.6 16.1 %collective-permute-start.8 = (bf16[320,1024]{1,0:T(8,128)(2,1)S(1)}, bf16[320,1024]{1,0:T(8,128)(2,1)S(1)}, u32[]{:S(2)}, u32[]{:S(2)}) collective-permute-start(bf16[320,1024]{1,0:T(8,128)(2,1)S(1)} %pad_maximum_fusion.1.refs_0_), channel_id=1, source_target_pairs={{0,8},{4,20},{8,0},{12,28},{16,24},{20,4},{24,16},{28,12},{1,9},{5... | collective-permute-start | bytes 1966088 | tf_op jit(solution)/shard_map/ppermute | solution.py:546
  30.0 8.5 %copy-start.1 = (bf16[256,1024]{1,0:T(8,128)(2,1)}, bf16[256,1024]{1,0:T(8,128)(2,1)S(1)}, u32[]{:S(2)}) copy-start(bf16[256,1024]{1,0:T(8,128)(2,1)S(1)} %collective-permute-done.4.refs_4_) | copy-start | bytes 1572868
  35.1 3.5 %copy-start.3 = (bf16[256,1024]{1,0:T(8,128)(2,1)}, bf16[256,1024]{1,0:T(8,128)(2,1)S(1)}, u32[]{:S(2)}) copy-start(bf16[256,1024]{1,0:T(8,128)(2,1)S(1)} %collective-permute-done.5.refs_5_) | copy-start | bytes 1572868
  35.1 1.9 %collective-permute-start.6 = (bf16[256,1024]{1,0:T(8,128)(2,1)S(1)}, bf16[256,1024]{1,0:T(8,128)(2,1)S(1)}, u32[]{:S(2)}, u32[]{:S(2)}) collective-permute-start(bf16[256,1024]{1,0:T(8,128)(2,1)S(1)} %collective-permute-done.5.refs_5_), channel_id=1, source_target_pairs={{0,4},{4,0},{8,12},{12,8},{16,20},{20,16},{24,28},{28,24},{1,5},{5... | collective-permute-start | bytes 1572872 | tf_op jit(solution)/shard_map/ppermute | solution.py:536
  35.1 3.4 %collective-permute-start.7 = (bf16[256,1024]{1,0:T(8,128)(2,1)S(1)}, bf16[256,1024]{1,0:T(8,128)(2,1)S(1)}, u32[]{:S(2)}, u32[]{:S(2)}) collective-permute-start(bf16[256,1024]{1,0:T(8,128)(2,1)S(1)} %collective-permute-done.4.refs_4_), channel_id=1, source_target_pairs={{0,4},{4,0},{8,12},{12,8},{16,20},{20,16},{24,28},{28,24},{1,5},{5... | collective-permute-start | bytes 1572872 | tf_op jit(solution)/shard_map/ppermute | solution.py:536
  37.0 1.6 copy-start.5
  37.0 18.7 %collective-permute-start.9 = (bf16[320,1024]{1,0:T(8,128)(2,1)S(1)}, bf16[320,1024]{1,0:T(8,128)(2,1)S(1)}, u32[]{:S(2)}, u32[]{:S(2)}) collective-permute-start(bf16[320,1024]{1,0:T(8,128)(2,1)S(1)} %pad_maximum_fusion.1.refs_0_), channel_id=1, source_target_pairs={{0,16},{4,12},{8,24},{12,4},{16,0},{20,28},{24,8},{28,20},{1,17},{... | collective-permute-start | bytes 1966088 | tf_op jit(solution)/shard_map/ppermute | solution.py:546
  38.5 0.8 copy-start.7
  44.8 10.9 %collective-permute-start.10 = (bf16[320,1024]{1,0:T(8,128)(2,1)S(1)}, bf16[320,1024]{1,0:T(8,128)(2,1)S(1)}, u32[]{:S(2)}, u32[]{:S(2)}) collective-permute-start(bf16[320,1024]{1,0:T(8,128)(2,1)S(1)} %collective-permute-done.8.refs_1_), channel_id=1, source_target_pairs={{0,16},{4,12},{8,24},{12,4},{16,0},{20,28},{24,8},{28,20},{1,17},{... | collective-permute-start | bytes 1966088 | tf_op jit(solution)/shard_map/ppermute | solution.py:546
  45.6 12.1 %copy-start.2 = (bf16[256,1024]{1,0:T(8,128)(2,1)S(1)}, bf16[256,1024]{1,0:T(8,128)(2,1)}, u32[]{:S(2)}) copy-start(bf16[256,1024]{1,0:T(8,128)(2,1)} %copy-done.1) | copy-start | bytes 1572868
  45.6 12.1 %copy-start.4 = (bf16[256,1024]{1,0:T(8,128)(2,1)S(1)}, bf16[256,1024]{1,0:T(8,128)(2,1)}, u32[]{:S(2)}) copy-start(bf16[256,1024]{1,0:T(8,128)(2,1)} %copy-done.3) | copy-start | bytes 1572868
  45.6 12.1 %copy-start.6 = (bf16[256,1024]{1,0:T(8,128)(2,1)S(1)}, bf16[256,1024]{1,0:T(8,128)(2,1)}, u32[]{:S(2)}) copy-start(bf16[256,1024]{1,0:T(8,128)(2,1)} %copy-done.5) | copy-start | bytes 1572868
  45.6 12.1 %copy-start.8 = (bf16[256,1024]{1,0:T(8,128)(2,1)S(1)}, bf16[256,1024]{1,0:T(8,128)(2,1)}, u32[]{:S(2)}) copy-start(bf16[256,1024]{1,0:T(8,128)(2,1)} %copy-done.7) | copy-start | bytes 1572868
  55.7 2.0 %collective-permute-start.11 = (bf16[1024,256]{1,0:T(8,128)(2,1)S(1)}, bf16[1024,256]{1,0:T(8,128)(2,1)S(1)}, u32[]{:S(2)}, u32[]{:S(2)}) collective-permute-start(bf16[1024,256]{1,0:T(8,128)(2,1)S(1)} %get-tuple-element.202.refs_9_.o_ref), channel_id=1, source_target_pairs={{0,4},{4,0},{8,12},{12,8},{16,20},{20,16},{24,28},{28,24},{1,5},{5... | collective-permute-start | bytes 1572872 | tf_op jit(solution)/shard_map/ppermute | solution.py:536
  68.9 4.1 %collective-permute-start.12 = (bf16[1024,512]{1,0:T(8,128)(2,1)S(1)}, bf16[1024,512]{1,0:T(8,128)(2,1)S(1)}, u32[]{:S(2)}, u32[]{:S(2)}) collective-permute-start(bf16[1024,512]{1,0:T(8,128)(2,1)S(1)} %get-tuple-element.207.dh_ref), channel_id=1, source_target_pairs={{0,4},{4,0},{8,12},{12,8},{16,20},{20,16},{24,28},{28,24},{1,5},{5... | collective-permute-start | bytes 3145736 | tf_op jit(solution)/shard_map/ppermute | solution.py:536
  69.1 3.9 %collective-permute-start.13 = (bf16[512,512]{1,0:T(8,128)(2,1)S(1)}, bf16[512,512]{1,0:T(8,128)(2,1)S(1)}, u32[]{:S(2)}, u32[]{:S(2)}) collective-permute-start(bf16[512,512]{1,0:T(8,128)(2,1)S(1)} %get-tuple-element.210), channel_id=1, source_target_pairs={{0,4},{4,0},{8,12},{12,8},{16,20},{20,16},{24,28},{28,24},{1,5},{5... | collective-permute-start | bytes 1572872 | tf_op jit(solution)/shard_map/ppermute | solution.py:536
  69.4 27.9 %collective-permute-start.16 = (bf16[264,1024]{1,0:T(8,128)(2,1)S(1)}, bf16[264,1024]{1,0:T(8,128)(2,1)S(1)}, u32[]{:S(2)}, u32[]{:S(2)}) collective-permute-start(bf16[264,1024]{1,0:T(8,128)(2,1)S(1)} %get-tuple-element.235), channel_id=1, source_target_pairs={{0,8},{4,12},{8,0},{12,4},{16,24},{20,28},{24,16},{28,20},{1,9},{5... | collective-permute-start | bytes 1622024 | tf_op jit(solution)/shard_map/ppermute | solution.py:541
  70.9 26.4 %collective-permute-start.17 = (bf16[264,1024]{1,0:T(8,128)(2,1)S(1)}, bf16[264,1024]{1,0:T(8,128)(2,1)S(1)}, u32[]{:S(2)}, u32[]{:S(2)}) collective-permute-start(bf16[264,1024]{1,0:T(8,128)(2,1)S(1)} %get-tuple-element.236), channel_id=1, source_target_pairs={{0,16},{4,20},{8,24},{12,28},{16,0},{20,4},{24,8},{28,12},{1,17},{... | collective-permute-start | bytes 1622024 | tf_op jit(solution)/shard_map/ppermute | solution.py:541
  72.2 25.2 %collective-permute-start.18 = (bf16[264,1024]{1,0:T(8,128)(2,1)S(1)}, bf16[264,1024]{1,0:T(8,128)(2,1)S(1)}, u32[]{:S(2)}, u32[]{:S(2)}) collective-permute-start(bf16[264,1024]{1,0:T(8,128)(2,1)S(1)} %get-tuple-element.237), channel_id=1, source_target_pairs={{0,24},{4,28},{8,16},{12,20},{16,8},{20,12},{24,0},{28,4},{1,25},{... | collective-permute-start | bytes 1622024 | tf_op jit(solution)/shard_map/ppermute | solution.py:541
  76.4 21.0 %collective-permute-start.14 = (bf16[256,512]{1,0:T(8,128)(2,1)S(1)}, bf16[256,512]{1,0:T(8,128)(2,1)S(1)}, u32[]{:S(2)}, u32[]{:S(2)}) collective-permute-start(bf16[256,512]{1,0:T(8,128)(2,1)S(1)} %get-tuple-element.233), channel_id=1, source_target_pairs={{0,0},{4,1},{1,2},{5,3},{2,4},{6,5},{3,6},{7,7},{8,8},{12,9},{9,10... | collective-permute-start | bytes 786440 | tf_op jit(solution)/shard_map/ppermute | solution.py:1124
  77.1 20.3 %collective-permute-start.15 = (bf16[256,512]{1,0:T(8,128)(2,1)S(1)}, bf16[256,512]{1,0:T(8,128)(2,1)S(1)}, u32[]{:S(2)}, u32[]{:S(2)}) collective-permute-start(bf16[256,512]{1,0:T(8,128)(2,1)S(1)} %get-tuple-element.234), channel_id=1, source_target_pairs={{1,0},{5,1},{0,2},{4,3},{3,4},{7,5},{2,6},{6,7},{9,8},{13,9},{8,10... | collective-permute-start | bytes 786440 | tf_op jit(solution)/shard_map/ppermute | solution.py:1124
  98.2 7.9 %collective-permute-start.19 = (bf16[264,512]{1,0:T(8,128)(2,1)S(1)}, bf16[264,512]{1,0:T(8,128)(2,1)S(1)}, u32[]{:S(2)}, u32[]{:S(2)}) collective-permute-start(bf16[264,512]{1,0:T(8,128)(2,1)S(1)} %get-tuple-element.258), channel_id=1, source_target_pairs={{0,1},{1,0},{2,3},{3,2},{4,5},{5,4},{6,7},{7,6},{8,9},{9,8},{10,11... | collective-permute-start | bytes 811016 | tf_op jit(solution)/shard_map/ppermute | solution.py:551
  104.7 1.5 copy-start
  110.4 5.6 %collective-permute-start.24 = (bf16[512,512]{1,0:T(8,128)(2,1)S(1)}, bf16[512,512]{1,0:T(8,128)(2,1)S(1)}, u32[]{:S(2)}, u32[]{:S(2)}) collective-permute-start(bf16[512,512]{1,0:T(8,128)(2,1)S(1)} %get-tuple-element.286), channel_id=1, source_target_pairs={{0,4},{4,0},{8,12},{12,8},{16,20},{20,16},{24,28},{28,24},{1,5},{5... | collective-permute-start | bytes 1572872 | tf_op jit(solution)/shard_map/ppermute | solution.py:536
  110.5 18.2 %collective-permute-start.20 = (bf16[168,1024]{1,0:T(8,128)(2,1)S(1)}, bf16[168,1024]{1,0:T(8,128)(2,1)S(1)}, u32[]{:S(2)}, u32[]{:S(2)}) collective-permute-start(bf16[168,1024]{1,0:T(8,128)(2,1)S(1)} %get-tuple-element.281), channel_id=1, source_target_pairs={{0,8},{4,12},{8,0},{12,4},{16,24},{20,28},{24,16},{28,20},{1,9},{5... | collective-permute-start | bytes 1032200 | tf_op jit(solution)/shard_map/ppermute | solution.py:541
  110.5 18.2 %collective-permute-start.21 = (bf16[168,1024]{1,0:T(8,128)(2,1)S(1)}, bf16[168,1024]{1,0:T(8,128)(2,1)S(1)}, u32[]{:S(2)}, u32[]{:S(2)}) collective-permute-start(bf16[168,1024]{1,0:T(8,128)(2,1)S(1)} %get-tuple-element.282), channel_id=1, source_target_pairs={{0,16},{4,20},{8,24},{12,28},{16,0},{20,4},{24,8},{28,12},{1,17},{... | collective-permute-start | bytes 1032200 | tf_op jit(solution)/shard_map/ppermute | solution.py:541
  112.2 16.9 %collective-permute-start.22 = (bf16[168,1024]{1,0:T(8,128)(2,1)S(1)}, bf16[168,1024]{1,0:T(8,128)(2,1)S(1)}, u32[]{:S(2)}, u32[]{:S(2)}) collective-permute-start(bf16[168,1024]{1,0:T(8,128)(2,1)S(1)} %get-tuple-element.283), channel_id=1, source_target_pairs={{0,24},{4,28},{8,16},{12,20},{16,8},{20,12},{24,0},{28,4},{1,25},{... | collective-permute-start | bytes 1032200 | tf_op jit(solution)/shard_map/ppermute | solution.py:541
  114.0 14.7 %collective-permute-start.23 = (bf16[264,512]{1,0:T(8,128)(2,1)S(1)}, bf16[264,512]{1,0:T(8,128)(2,1)S(1)}, u32[]{:S(2)}, u32[]{:S(2)}) collective-permute-start(bf16[264,512]{1,0:T(8,128)(2,1)S(1)} %add_convert_fusion.2), channel_id=1, source_target_pairs={{0,2},{1,3},{2,0},{3,1},{4,6},{5,7},{6,4},{7,5},{8,10},{9,11},{10,... | collective-permute-start | bytes 811016 | tf_op jit(solution)/shard_map/ppermute | solution.py:551
  129.8 6.0 %collective-permute-start.25 = (bf16[168,512]{1,0:T(8,128)(2,1)S(1)}, bf16[168,512]{1,0:T(8,128)(2,1)S(1)}, u32[]{:S(2)}, u32[]{:S(2)}) collective-permute-start(bf16[168,512]{1,0:T(8,128)(2,1)S(1)} %get-tuple-element.294), channel_id=1, source_target_pairs={{0,1},{1,0},{2,3},{3,2},{4,5},{5,4},{6,7},{7,6},{8,9},{9,8},{10,11... | collective-permute-start | bytes 516104 | tf_op jit(solution)/shard_map/ppermute | solution.py:551
  135.8 15.8 %collective-permute-start.26 = (bf16[168,512]{1,0:T(8,128)(2,1)S(1)}, bf16[168,512]{1,0:T(8,128)(2,1)S(1)}, u32[]{:S(2)}, u32[]{:S(2)}) collective-permute-start(bf16[168,512]{1,0:T(8,128)(2,1)S(1)} %add_convert_fusion.4), channel_id=1, source_target_pairs={{0,2},{1,3},{2,0},{3,1},{4,6},{5,7},{6,4},{7,5},{8,10},{9,11},{10,... | collective-permute-start | bytes 516104 | tf_op jit(solution)/shard_map/ppermute | solution.py:551
  137.4 15.7 %collective-permute-start.29 = (bf16[256,512]{1,0:T(8,128)(2,1)S(1)}, bf16[256,512]{1,0:T(8,128)(2,1)S(1)}, u32[]{:S(2)}, u32[]{:S(2)}) collective-permute-start(bf16[256,512]{1,0:T(8,128)(2,1)S(1)} %get-tuple-element.288), channel_id=1, source_target_pairs={{0,0},{4,1},{1,2},{5,3},{2,4},{6,5},{3,6},{7,7},{8,8},{12,9},{9,10... | collective-permute-start | bytes 786440 | tf_op jit(solution)/shard_map/ppermute | solution.py:1124
  138.1 18.0 %collective-permute-start.30 = (bf16[256,512]{1,0:T(8,128)(2,1)S(1)}, bf16[256,512]{1,0:T(8,128)(2,1)S(1)}, u32[]{:S(2)}, u32[]{:S(2)}) collective-permute-start(bf16[256,512]{1,0:T(8,128)(2,1)S(1)} %get-tuple-element.289), channel_id=1, source_target_pairs={{1,0},{5,1},{0,2},{4,3},{3,4},{7,5},{2,6},{6,7},{9,8},{13,9},{8,10... | collective-permute-start | bytes 786440 | tf_op jit(solution)/shard_map/ppermute | solution.py:1124
  140.8 20.9 %collective-permute-start.31 = (bf16[264,512]{1,0:T(8,128)(2,1)S(1)}, bf16[264,512]{1,0:T(8,128)(2,1)S(1)}, u32[]{:S(2)}, u32[]{:S(2)}) collective-permute-start(bf16[264,512]{1,0:T(8,128)(2,1)S(1)} %add_convert_fusion.1.mine), channel_id=1, source_target_pairs={{0,1},{1,0},{2,3},{3,2},{4,5},{5,4},{6,7},{7,6},{8,9},{9,8},{10,11... | collective-permute-start | bytes 811016 | tf_op jit(solution)/shard_map/ppermute | solution.py:551
  151.7 1.3 collective-permute-start.27
  153.0 12.1 %collective-permute-start.28 = (bf16[176,512]{1,0:T(8,128)(2,1)S(1)}, bf16[176,512]{1,0:T(8,128)(2,1)S(1)}, u32[]{:S(2)}, u32[]{:S(2)}) collective-permute-start(bf16[176,512]{1,0:T(8,128)(2,1)S(1)} %pad_maximum_fusion.3.mine), channel_id=1, source_target_pairs={{0,1},{1,0},{2,3},{3,2},{4,5},{5,4},{6,7},{7,6},{8,9},{9,8},{10,11... | collective-permute-start | bytes 540680 | tf_op jit(solution)/shard_map/ppermute | solution.py:551
  161.7 1.9 %collective-permute-start.32 = (bf16[2,72,512]{2,1,0:T(8,128)(2,1)S(1)}, bf16[2,72,512]{2,1,0:T(8,128)(2,1)S(1)}, u32[]{:S(2)}, u32[]{:S(2)}) collective-permute-start(bf16[2,72,512]{2,1,0:T(8,128)(2,1)S(1)} %pad_maximum_fusion.4), channel_id=1, source_target_pairs={{0,4},{4,0},{8,12},{12,8},{16,20},{20,16},{24,28},{28,24},{1,5},{5... | collective-permute-start | bytes 442376 | tf_op jit(solution)/shard_map/ppermute | solution.py:536

commit v4 on v3

--- a/solution.py
+++ b/solution.py
@@ -41,7 +41,7 @@
     return masked_tail(dot(qu, keys, NT) + rel, keep, block)
 
 
-def attn_fwd_body(len_ref, q_ref, k_ref, v_ref, r_ref, bu_ref, bv_ref, o_ref, lse_ref, *, block):
+def attn_fwd_body(len_ref, q_ref, k_ref, v_ref, r_ref, bu_ref, bv_ref, o_ref, *p_refs, block):
     full = q_ref.shape[0]
     lane = lax.broadcasted_iota(jnp.int32, (block, 2 * HD), 1)
     sides = (lane < HD, lane >= HD)
@@ -70,13 +70,15 @@
             top = jnp.max(s, axis=1, keepdims=True)
             e = jnp.exp(s - top)
             total = jnp.sum(e, axis=1, keepdims=True)
-            outs.append(dot(e.astype(bf), v_ref[:span, :], NN) / total)
-            lse_ref[head, first:span, :] = top + jnp.log(total)
+            p = (e * (1.0 / total)).astype(bf)
+            p_refs[first // block][head] = p
+            outs.append(dot(p, v_ref[:span, :], NN))
         o_ref[first:span, :] = jnp.where(sides[0], outs[0], outs[1]).astype(bf)
 
 
 def attn_fwd(length, qkv, rel_rev, bias_u, bias_v, *, block=256):
     full, cols = rel_rev.shape
+    spans = range(block, full + 1, block)
     pairs = cols // (2 * HD)
     at = lambda part: pl.BlockSpec((full, 2 * HD), lambda pair, _: (0, part * pairs + pair))
     row = pl.BlockSpec((1, 2 * HD), lambda pair, _: (0, pair))
@@ -84,13 +86,16 @@
         functools.partial(attn_fwd_body, block=block),
         out_shape=(
             jax.ShapeDtypeStruct((full, cols), bf),
-            jax.ShapeDtypeStruct((2 * pairs, full, 1), f32),
+            *(jax.ShapeDtypeStruct((2 * pairs, block, span), bf) for span in spans),
         ),
         grid_spec=pltpu.PrefetchScalarGridSpec(
             num_scalar_prefetch=1,
             grid=(pairs,),
             in_specs=[at(0), at(1), at(2), at(0), row, row],
-            out_specs=(at(0), pl.BlockSpec((2, full, 1), lambda pair, _: (pair, 0, 0))),
+            out_specs=(
+                at(0),
+                *(pl.BlockSpec((2, block, span), lambda pair, _: (pair, 0, 0)) for span in spans),
+            ),
         ),
         cost_estimate=pl.CostEstimate(flops=0, bytes_accessed=0, transcendentals=0),
         compiler_params=pltpu.CompilerParams(vmem_limit_bytes=32 << 20),
@@ -98,17 +103,16 @@
     )(length, qkv, qkv, qkv, rel_rev, bias_u, bias_v)
 
 
-def attn_bwd_body(len_ref, q_ref, k_ref, v_ref, r_ref, bu_ref, bv_ref, lse_ref, do_ref, *refs, block, heads):
+def attn_bwd_body(len_ref, q_ref, k_ref, v_ref, r_ref, bu_ref, bv_ref, do_ref, *refs, block, heads):
+    full = q_ref.shape[0]
+    p_refs, refs = refs[: full // block], refs[full // block :]
     dq_ref, dk_ref, dv_ref, dr_ref, gu_ref, gv_ref, dk_t, dv_t, dr_t = refs
-    full = q_ref.shape[0]
     length = len_ref[0]
     lane = lax.broadcasted_iota(jnp.int32, (block, 2 * HD), 1)
     sides = (lane < HD, lane >= HD)
     rows = lax.broadcasted_iota(jnp.int32, (block, block), 0)
     cols = lax.broadcasted_iota(jnp.int32, (block, block), 1)
-    tri = cols <= rows
     flip = jnp.where(rows + cols == block - 1, 1.0, 0.0).astype(bf)
-    row = lax.broadcasted_iota(jnp.int32, (block, 1), 0)
     for ref in (dk_t, dv_t, dr_t, dq_ref, gu_ref, gv_ref):
         ref[...] = jnp.zeros_like(ref)
     for first in range(0, full, block):
@@ -127,20 +131,12 @@
             for head in heads:
                 side = sides[head]
                 at = slice(head * HD, (head + 1) * HD)
-                s = scores(
-                    jnp.where(side, qu, 0.0).astype(bf),
-                    jnp.where(side, qv, 0.0).astype(bf),
-                    k_ref[:span, :],
-                    r_ref[full - span :, :],
-                    tri,
-                    block,
-                )
-                lse = jnp.where(first + row < length, lse_ref[head, first:span, :], -NEG)
-                p = jnp.exp(s - lse)
+                rounded = p_refs[first // block][head - heads[0]]
+                p = rounded.astype(f32)
                 dp = dot(jnp.where(side, do, 0.0).astype(bf), v_ref[:span, :], NT)
                 t = p * dp
                 ds = (t - p * jnp.sum(t, axis=1, keepdims=True)).astype(bf)
-                dv_t[at, :span] += dot(do_t[at], p.astype(bf), NN)
+                dv_t[at, :span] += dot(do_t[at], rounded, NN)
                 both = dot(jnp.concatenate([qu_t[at], flip], axis=0), ds, NN)
                 dk_t[at, :span] += both[:HD]
                 dqu[head] = dot(ds, k_ref[:span, :], NN)
@@ -158,7 +154,7 @@
     dr_ref[...] = jnp.transpose(dr_t[...]).astype(bf)
 
 
-def attn_bwd(length, qkv, rel_rev, bias_u, bias_v, lse, d_out, *, pair, heads=(0, 1), block=256):
+def attn_bwd(length, qkv, rel_rev, bias_u, bias_v, probs, d_out, *, pair, heads=(0, 1), block=256):
     full, cols = rel_rev.shape
     pairs = cols // (2 * HD)
     at = lambda part: pl.BlockSpec((full, 2 * HD), lambda i, _: (0, part * pairs + pair))
@@ -173,14 +169,18 @@
             num_scalar_prefetch=1,
             grid=(1,),
             in_specs=[at(0), at(1), at(2), at(0), row, row]
-            + [pl.BlockSpec((2, full, 1), lambda i, _: (pair, 0, 0)), at(0)],
+            + [at(0)]
+            + [
+                pl.BlockSpec((len(heads),) + p.shape[1:], lambda i, _: ((2 * pair + heads[0]) // len(heads), 0, 0))
+                for p in probs
+            ],
             out_specs=(out,) * 4 + (out_row, out_row),
             scratch_shapes=[pltpu.VMEM((2 * HD, full), f32)] * 3,
         ),
         cost_estimate=pl.CostEstimate(flops=0, bytes_accessed=0, transcendentals=0),
         compiler_params=pltpu.CompilerParams(vmem_limit_bytes=32 << 20),
         name="attn_bwd",
-    )(length, qkv, qkv, qkv, rel_rev, bias_u, bias_v, lse, d_out)
+    )(length, qkv, qkv, qkv, rel_rev, bias_u, bias_v, d_out, *probs)
 
 
 def norm_parts(values):
@@ -832,10 +832,10 @@
 
 
 def qkv_back_body(meta, *refs):
-    grads_a, grads_b, grads_c = refs[:6], refs[6:12], refs[12:18]
-    w_ref, x_ref, h_ref, table_ref, go_ref = refs[18:23]
-    keep_ref, send_ref = refs[23:25]
-    outs, acc, sums = refs[25:29], refs[29], refs[30]
+    grads_a, grads_b = refs[:6], refs[6:12]
+    w_ref, x_ref, h_ref, table_ref, go_ref = refs[12:17]
+    keep_ref, send_ref = refs[17:19]
+    outs, acc, sums = refs[19:23], refs[23], refs[24]
     step, chip = pl.program_id(0), meta[CHIP]
     width = x_ref.shape[1]
     rows = width // 4
@@ -845,7 +845,7 @@
         sums[...] = jnp.zeros_like(sums)
         acc[...] = jnp.zeros_like(acc)
 
-    both = lambda i: [grads_a[i][...], grads_b[i][...] + grads_c[i][...]]
+    both = lambda i: [grads_a[i][...], grads_b[i][...]]
     dqkv = jnp.concatenate(both(0) + both(1) + both(2), axis=1)
     drel = jnp.concatenate(both(3), axis=1)
     span = dqkv.shape[1]
@@ -1073,7 +1073,7 @@
     )
     qkv, feed_first = together(qkv, feed_first)
     feed_third = swap_axis(feed_first, 1)
-    attn, lse = attn_fwd(length_arr, qkv, rel, own_u, own_v)
+    attn, *probs = attn_fwd(length_arr, qkv, rel, own_u, own_v)
     attn, feed_second, feed_third = together(attn, feed_second, feed_third)
     feed_packs = [feed_pack, feed_first, feed_second, feed_third]
 
@@ -1125,34 +1125,29 @@
         for turn, out in enumerate(outs)
     ]
     y_turns = home((out0, out1))
-    back = lambda pair, heads, d_out: attn_bwd(
-        length_arr, qkv, rel, own_u, own_v, lse, d_out, pair=pair, heads=heads
-    )
-    d_attn, *grads_a = together(d_attn, *back(0, (0, 1), d_attn))
-    *grads_b, y0, y1, e1, e2, e3 = together(*back(1, (0,), d_attn), *y_turns, *early_came)
+    back = lambda pair, d_out: attn_bwd(length_arr, qkv, rel, own_u, own_v, probs, d_out, pair=pair)
+    d_attn, *grads_a = together(d_attn, *back(0, d_attn))
+    *grads_b, y0, y1, e1, e2, e3 = together(*back(1, d_attn), *y_turns, *early_came)
     early_keep, early_send = chip_sum(meta, [early_parts[0], e1, e2, e3], "early_chips", 0)
-    d_attn, early_send, early_keep = together(d_attn, early_send, early_keep)
-    *grads_c, early_came = together(*back(1, (1,), d_attn), swap_seq(early_send, 1))
-    early_pair = (early_keep + early_came.astype(f32)).astype(bf)
-    early_pair, *grads_c = together(early_pair, *grads_c)
-    early_came = swap_seq(early_pair, 2)
+    early_send, *grads_b = together(early_send, *grads_b)
+    early_came = swap_seq(early_send, 1)
     pair_step = pl.BlockSpec((block, 2 * HEAD_DIM), lambda i, _: (i, 0))
     pair_row = whole(1, 2 * HEAD_DIM)
     dh1_keep, dh1_send, *late_parts = kernel_call(
         qkv_back_body,
         "qkv_back",
         meta,
-        [*grads_a, *grads_b, *grads_c, w_own, x_slot, h1, table, g_out],
+        [*grads_a, *grads_b, w_own, x_slot, h1, table, g_out],
         [((half, width), f32), ((half, width), bf)] + blocks(rows + fold),
         grid=(4,),
-        in_specs=([pair_step] * 4 + [pair_row] * 2) * 3
+        in_specs=([pair_step] * 4 + [pair_row] * 2) * 2
         + [whole(width, 4 * cols)] + [by_step(width)] * 3 + [whole(cols, width)],
         out_specs=[kept(width)] * 2 + [whole(rows + fold, 2 * width)] * 4,
         scratch=[pltpu.VMEM((width, 4 * cols), f32), pltpu.VMEM((8, width), f32)],
         flops=14 * full * width * cols,
     )
     dh1_send, *late_parts = together(dh1_send, *late_parts)
-    dh1_came = swap_core(dh1_send)
+    dh1_came, early_came = together(swap_core(dh1_send), early_came)
     late_came = [swap_chip(late_parts[k], k) for k in (1, 2, 3)]
     by_half = pl.BlockSpec((block, width), lambda i, _: (i, 0))
     own_rows = pl.BlockSpec((block, width), lambda i, m: (2 * i + m[CORE], 0))
@@ -1167,11 +1162,13 @@
         out_specs=[whole(block, width)] * 2,
     )
     x_turns = home((x0, x1))
-    *late_came, early_came, _, _ = together(*late_came, early_came, x0, x1)
-    early_mine = (early_pair.astype(f32) + early_came.astype(f32)).astype(bf)
+    *late_came, _, _ = together(*late_came, x0, x1)
+    early_pair = (early_keep + early_came.astype(f32)).astype(bf)
+    early_came = swap_seq(early_pair, 2)
     late_keep, late_send = chip_sum(meta, [late_parts[0]] + late_came, "late_chips", 0)
     small = lambda size: ((1, size), f32)
-    late_came, early_mine = together(swap_seq(late_send, 1), early_mine)
+    late_came, early_came, x_turns[0] = together(swap_seq(late_send, 1), early_came, x_turns[0])
+    early_mine = (early_pair.astype(f32) + early_came.astype(f32)).astype(bf)
     late_pair = (late_keep + late_came.astype(f32)).astype(bf)
     late_came = swap_seq(late_pair, 2)
     early_other = swap_seq(early_mine, 1)

time: 167 us -> 158 us (0.946)
  Pallas kernels: 67.4 us -> 52.9 us
  starting transfers between devices: 33.6 us -> 40.5 us
    pallas_call x3 -> x2, Pallas kernels: 23.3 us -> 7.56 us  [attn_bwd(): pl.pallas_call(functools.partial(attn_bwd_body, block=block, heads=heads)...]
    ppermute x9, waiting for transfers between devices: 11.6 us -> 26.5 us  [swap_chip(): lax.ppermute(values, 'fsdp', [(i, i ^ 2 * mask) for i in range(size)])]
    ppermute x6, waiting for transfers between devices: 33.3 us -> 20.6 us  [swap_seq(): return lax.ppermute(values, 'seq', [(i, i ^ mask) for i in range(size)])]
    ppermute x6, starting transfers between devices: 5.43 us -> 12.9 us  [swap_seq(): return lax.ppermute(values, 'seq', [(i, i ^ mask) for i in range(size)])]
    ppermute x4, waiting for transfers between devices: 2.99 us -> 0.01 us  [slot_split_device(): lax.ppermute(out, ('fsdp', 'seq'), [(b, a) for a, b in slot_pairs(turn)])]
  transfers between devices with their start and end apart: 33 -> 33, of which waited for: 14 -> 13; matrix products, arithmetic and copies ran while one was open for 2% -> 3% of each run, Pallas kernels for 28% -> 21%
where the time goes in v4:
time: 158 us
  waiting for transfers between devices  56.7 us (36%)
  Pallas kernels  52.9 us (33%)
  starting transfers between devices  40.5 us (26%)
  local copies, waits for them, and re-layouts  3.54 us (2%)
  between operations  2.44 us (2%)
  other arithmetic  2.21 us (1%)
    pallas_call x11, Pallas kernels, kernel_call(): pl.pallas_call(body, out_shape=[jax.ShapeDtypeStruct(shape, kind) for sha...  34 us
    ppermute x9, waiting for transfers between devices, swap_chip(): lax.ppermute(values, 'fsdp', [(i, i ^ 2 * mask) for i in range(size)])  26.5 us
    ppermute x6, waiting for transfers between devices, swap_seq(): return lax.ppermute(values, 'seq', [(i, i ^ mask) for i in range(size)])  20.6 us
    ppermute x6, starting transfers between devices, swap_seq(): return lax.ppermute(values, 'seq', [(i, i ^ mask) for i in range(size)])  12.9 us
    pallas_call x1, Pallas kernels, attn_fwd(): pl.pallas_call(functools.partial(attn_fwd_body, block=block), out_shape=(...  11.3 us
    ppermute x9, starting transfers between devices, swap_chip(): lax.ppermute(values, 'fsdp', [(i, i ^ 2 * mask) for i in range(size)])  11.3 us
    pallas_call x2, Pallas kernels, attn_bwd(): pl.pallas_call(functools.partial(attn_bwd_body, block=block, heads=heads)...  7.56 us
    ppermute x4, starting transfers between devices, slot_split_device(): lax.ppermute(out, ('fsdp', 'seq'), [(b, a) for a, b in slot_pairs(turn)])  5.91 us
  transfers between devices with their start and end apart: 33, of which 13 were waited for; matrix products, arithmetic and copies ran while one was open for 3% of the time, Pallas kernels for 21%

profile of v4, /device:TPU:0, one launch (start us, length us, event | category | flops | bytes accessed | tf_op | source)
XLA Modules:
  0.0 158.3 jit_solution(4162719906704063904)
XLA Ops:
  1.3 2.0 %pack.1 = (bf16[72,1024]{1,0:T(8,128)(2,1)S(1)}, bf16[224,1024]{1,0:T(8,128)(2,1)S(1)}, bf16[168,1024]{1,0:T(8,128)(2,1)S(1)}) custom-call(s32[2]{0:T(128)S(1)} %copy-done.9, bf16[64,1536]{1,0:T(8,128)(2,1)} %qkv_ref.1, bf16[64,512]{1,0:T(8,128)(2,1)} %rel_ref.1, bf16[64,2048]{1,0:T(8,128)(2,1)} %up_ref.1, bf16[64,512]{1,0:T(8,128)(2,1)} %out_ref.1, ...), custom_call_target="tpu_custom_call" | custom-call | tf_op jit(solution)/shard_map/pack/pallas_call | solution.py:587
  3.8 1.1 constant_dynamic-update-slice_fusion.1
  5.1 0.7 collective-permute-start.4
  5.8 3.9 %collective-permute-start.5 = (bf16[256,1024]{1,0:T(8,128)(2,1)S(1)}, bf16[256,1024]{1,0:T(8,128)(2,1)S(1)}, u32[]{:S(2)}, u32[]{:S(2)}) collective-permute-start(bf16[256,1024]{1,0:T(8,128)(2,1)S(1)} %get-tuple-element.301), channel_id=1, source_target_pairs={{0,1},{1,5},{2,0},{3,4},{4,3},{5,7},{6,2},{7,6},{8,9},{9,13},{10,8... | collective-permute-start | bytes 1572872 | tf_op jit(solution)/shard_map/ppermute | solution.py:565
  10.4 1.1 pad_maximum_fusion.refs_8_.refs_15_
  11.7 2.1 %collective-permute-start.1 = (bf16[144,1024]{1,0:T(8,128)(2,1)S(1)}, bf16[144,1024]{1,0:T(8,128)(2,1)}, u32[]{:S(2)}, u32[]{:S(2)}) collective-permute-start(bf16[144,1024]{1,0:T(8,128)(2,1)S(1)} %pad_maximum_fusion.2.refs_0_), channel_id=1, source_target_pairs={{0,8},{4,12},{8,0},{12,4},{16,24},{20,28},{24,16},{28,20},{1,9},{5... | collective-permute-start | bytes 884744 | tf_op jit(solution)/shard_map/ppermute | solution.py:541
  13.8 1.5 collective-permute-start.2
  17.4 2.7 %collective-permute-done.1.refs_1_ = bf16[144,1024]{1,0:T(8,128)(2,1)} collective-permute-done((bf16[144,1024]{1,0:T(8,128)(2,1)S(1)}, bf16[144,1024]{1,0:T(8,128)(2,1)}, u32[]{:S(2)}, u32[]{:S(2)}) %collective-permute-start.1) | collective-permute-done | bytes 294944 | tf_op jit(solution)/shard_map/ppermute | solution.py:541
  20.2 8.2 %collective-permute-done.2.refs_2_ = bf16[144,1024]{1,0:T(8,128)(2,1)} collective-permute-done((bf16[144,1024]{1,0:T(8,128)(2,1)S(1)}, bf16[144,1024]{1,0:T(8,128)(2,1)}, u32[]{:S(2)}, u32[]{:S(2)}) %collective-permute-start.2) | collective-permute-done | bytes 294944 | tf_op jit(solution)/shard_map/ppermute | solution.py:541
  28.6 1.4 collective-permute-start.8
  30.0 5.0 %collective-permute-done.5.refs_5_ = bf16[256,1024]{1,0:T(8,128)(2,1)S(1)} collective-permute-done((bf16[256,1024]{1,0:T(8,128)(2,1)S(1)}, bf16[256,1024]{1,0:T(8,128)(2,1)S(1)}, u32[]{:S(2)}, u32[]{:S(2)}) %collective-permute-start.5) | collective-permute-done | bytes 524320 | tf_op jit(solution)/shard_map/ppermute | solution.py:565
  35.6 1.4 collective-permute-done.6.refs_7_
  37.0 1.5 collective-permute-start.9
  38.6 0.8 copy-done.7
  39.3 5.4 %project.1 = (bf16[1024,768]{1,0:T(8,128)(2,1)S(1)}, bf16[1024,512]{1,0:T(8,128)(2,1)S(1)}, bf16[1024,512]{1,0:T(8,128)(2,1)S(1)}, bf16[1024,256]{1,0:T(8,128)(2...) custom-call(s32[4]{0:T(128)S(1)} %broadcast_3__.2._, ...), custom_call_target="tpu_custom_call" | custom-call | tf_op jit(solution)/shard_map/project/pallas_call | solution.py:587
  44.8 0.8 collective-permute-start.10
  45.6 11.3 %attn_fwd.1 = (bf16[1024,256]{1,0:T(8,128)(2,1)S(1)}, bf16[4,256,256]{2,1,0:T(8,128)(2,1)S(1)}, bf16[4,256,512]{2,1,0:T(8,128)(2,1)S(1)}, bf16[4,256,768]{2,1,0:T(8,128)(2,1)S(1)}, bf16[4,256,1024]{2,1,0:T(8,128)(2,1)S(1)}) custom-call(s32[1]{0:T(128)} %bitcast.15.len_ref, bf16[1024,768]{1,0:T(8,128)(2,1)S(1)} %get-tuple-element.183.q_ref.k_ref.v_ref, ...), custom_call_target="tpu_custom_call" | custom-call | tf_op jit(solution)/shard_map/attn_fwd/pallas_call | solution.py:85
  57.0 1.9 %collective-permute-done.11.refs_10_ = bf16[1024,256]{1,0:T(8,128)(2,1)S(1)} collective-permute-done((bf16[1024,256]{1,0:T(8,128)(2,1)S(1)}, bf16[1024,256]{1,0:T(8,128)(2,1)S(1)}, u32[]{:S(2)}, u32[]{:S(2)}) %collective-permute-start.11) | collective-permute-done | bytes 524320 | tf_op jit(solution)/shard_map/ppermute | solution.py:536
  58.9 11.2 %feed.1 = (bf16[1024,512]{1,0:T(8,128)(2,1)S(1)}, bf16[1024,512]{1,0:T(8,128)(2,1)S(1)}, f32[1024,1]{1,0:T(8,128)S(1)}, f32[512,512]{1,0:T(8,128)S(1)}, bf16[102...) custom-call(s32[4]{0:T(128)S(1)} %pad_add_fusion.meta, ...), custom_call_target="tpu_custom_call" | custom-call | tf_op jit(solution)/shard_map/feed/pallas_call | solution.py:587
  70.7 1.5 collective-permute-start.16
  72.2 1.3 collective-permute-start.17
  73.5 0.7 collective-permute-start.18
  74.2 3.4 %norm_two.1 = (bf16[256,512]{1,0:T(8,128)(2,1)S(1)}, bf16[256,512]{1,0:T(8,128)(2,1)S(1)}, f32[512,512]{1,0:T(8,128)S(1)}, bf16[1024,256]{1,0:T(8,128)(2,1)S(1)}, f32[256,512]{1,0:T(8,128)S(1)}) custom-call(s32[4]{0:T(128)S(1)} %pad_add_fusion.meta, bf16[1024,512]{1,0:T(8,128)(2,1)S(1)} %get-tuple-element.194.x_hat_ref, ...), custom_call_target="tpu_custom_call" | custom-call | tf_op jit(solution)/shard_map/norm_two/pallas_call | solution.py:587
  77.6 0.7 collective-permute-start.14
  78.3 3.5 %collective-permute-start.15 = (bf16[256,512]{1,0:T(8,128)(2,1)S(1)}, bf16[256,512]{1,0:T(8,128)(2,1)S(1)}, u32[]{:S(2)}, u32[]{:S(2)}) collective-permute-start(bf16[256,512]{1,0:T(8,128)(2,1)S(1)} %get-tuple-element.227), channel_id=1, source_target_pairs={{1,0},{5,1},{0,2},{4,3},{3,4},{7,5},{2,6},{6,7},{9,8},{13,9},{8,10... | collective-permute-start | bytes 786440 | tf_op jit(solution)/shard_map/ppermute | solution.py:1124
  81.8 3.7 %attn_bwd.2 = (bf16[1024,128]{1,0:T(8,128)(2,1)S(1)}, bf16[1024,128]{1,0:T(8,128)(2,1)S(1)}, bf16[1024,128]{1,0:T(8,128)(2,1)S(1)}, bf16[1024,128]{1,0:T(8,128)(...) custom-call(s32[1]{0:T(128)} %bitcast.15.len_ref, bf16[1024,768]{1,0:T(8,128)(2,1)S(1)} %get-tuple-element.183.q_ref.k_ref.v_ref, ...), custom_call_target="tpu_custom_call" | custom-call | tf_op jit(solution)/shard_map/attn_bwd/pallas_call | solution.py:164
  85.5 3.9 %attn_bwd.3 = (bf16[1024,128]{1,0:T(8,128)(2,1)S(1)}, bf16[1024,128]{1,0:T(8,128)(2,1)S(1)}, bf16[1024,128]{1,0:T(8,128)(2,1)S(1)}, bf16[1024,128]{1,0:T(8,128)(...) custom-call(s32[1]{0:T(128)} %bitcast.15.len_ref, bf16[1024,768]{1,0:T(8,128)(2,1)S(1)} %get-tuple-element.183.q_ref.k_ref.v_ref, ...), custom_call_target="tpu_custom_call" | custom-call | tf_op jit(solution)/shard_map/attn_bwd/pallas_call | solution.py:164
  89.4 8.4 %collective-permute-done.17.refs_1_ = bf16[264,1024]{1,0:T(8,128)(2,1)S(1)} collective-permute-done((bf16[264,1024]{1,0:T(8,128)(2,1)S(1)}, bf16[264,1024]{1,0:T(8,128)(2,1)S(1)}, u32[]{:S(2)}, u32[]{:S(2)}) %collective-permute-start.17) | collective-permute-done | bytes 540704 | tf_op jit(solution)/shard_map/ppermute | solution.py:541
  97.8 0.8 early_chips.1
  98.6 4.2 %qkv_back.1 = (f32[512,512]{1,0:T(8,128)S(1)}, bf16[512,512]{1,0:T(8,128)(2,1)S(1)}, f32[168,1024]{1,0:T(8,128)S(1)}, bf16[168,1024]{1,0:T(8,128)(2,1)S(1)}, bf1...) custom-call(s32[4]{0:T(128)S(1)} %pad_add_fusion.meta, bf16[1024,128]{1,0:T(8,128)(2,1)S(1)} %get-tuple-element.212.refs_0_, ...), custom_call_target="tpu_custom_call" | custom-call | tf_op jit(solution)/shard_map/qkv_back/pallas_call | solution.py:587
  103.0 2.7 %collective-permute-start.19 = (bf16[168,1024]{1,0:T(8,128)(2,1)S(1)}, bf16[168,1024]{1,0:T(8,128)(2,1)S(1)}, u32[]{:S(2)}, u32[]{:S(2)}) collective-permute-start(bf16[168,1024]{1,0:T(8,128)(2,1)S(1)} %get-tuple-element.256), channel_id=1, source_target_pairs={{0,8},{4,12},{8,0},{12,4},{16,24},{20,28},{24,16},{28,20},{1,9},{5... | collective-permute-start | bytes 1032200 | tf_op jit(solution)/shard_map/ppermute | solution.py:541
  105.7 1.4 collective-permute-start.20
  107.1 4.7 %collective-permute-done.23 = bf16[264,512]{1,0:T(8,128)(2,1)S(1)} collective-permute-done((bf16[264,512]{1,0:T(8,128)(2,1)S(1)}, bf16[264,512]{1,0:T(8,128)(2,1)S(1)}, u32[]{:S(2)}, u32[]{:S(2)}) %collective-permute-start.23) | collective-permute-done | bytes 270368 | tf_op jit(solution)/shard_map/ppermute | solution.py:551
  111.9 1.8 %collective-permute-start.25 = (bf16[264,512]{1,0:T(8,128)(2,1)S(1)}, bf16[264,512]{1,0:T(8,128)(2,1)S(1)}, u32[]{:S(2)}, u32[]{:S(2)}) collective-permute-start(bf16[264,512]{1,0:T(8,128)(2,1)S(1)} %add_convert_fusion.2), channel_id=1, source_target_pairs={{0,2},{1,3},{2,0},{3,1},{4,6},{5,7},{6,4},{7,5},{8,10},{9,11},{10,... | collective-permute-start | bytes 811016 | tf_op jit(solution)/shard_map/ppermute | solution.py:551
  113.7 1.4 norm_one.1
  115.8 7.0 %collective-permute-done.20.refs_1_ = bf16[168,1024]{1,0:T(8,128)(2,1)S(1)} collective-permute-done((bf16[168,1024]{1,0:T(8,128)(2,1)S(1)}, bf16[168,1024]{1,0:T(8,128)(2,1)S(1)}, u32[]{:S(2)}, u32[]{:S(2)}) %collective-permute-start.20) | collective-permute-done | bytes 344096 | tf_op jit(solution)/shard_map/ppermute | solution.py:541
  122.7 0.7 late_chips.1
  123.4 1.8 %collective-permute-start.24 = (bf16[168,512]{1,0:T(8,128)(2,1)S(1)}, bf16[168,512]{1,0:T(8,128)(2,1)S(1)}, u32[]{:S(2)}, u32[]{:S(2)}) collective-permute-start(bf16[168,512]{1,0:T(8,128)(2,1)S(1)} %get-tuple-element.270), channel_id=1, source_target_pairs={{0,1},{1,0},{2,3},{3,2},{4,5},{5,4},{6,7},{7,6},{8,9},{9,8},{10,11... | collective-permute-start | bytes 516104 | tf_op jit(solution)/shard_map/ppermute | solution.py:551
  125.3 1.0 collective-permute-start.30
  126.3 5.5 %collective-permute-done.24 = bf16[168,512]{1,0:T(8,128)(2,1)S(1)} collective-permute-done((bf16[168,512]{1,0:T(8,128)(2,1)S(1)}, bf16[168,512]{1,0:T(8,128)(2,1)S(1)}, u32[]{:S(2)}, u32[]{:S(2)}) %collective-permute-start.24) | collective-permute-done | bytes 172064 | tf_op jit(solution)/shard_map/ppermute | solution.py:551
  131.8 7.8 %collective-permute-start.27 = (bf16[168,512]{1,0:T(8,128)(2,1)S(1)}, bf16[168,512]{1,0:T(8,128)(2,1)S(1)}, u32[]{:S(2)}, u32[]{:S(2)}) collective-permute-start(bf16[168,512]{1,0:T(8,128)(2,1)S(1)} %add_convert_fusion.4), channel_id=1, source_target_pairs={{0,2},{1,3},{2,0},{3,1},{4,6},{5,7},{6,4},{7,5},{8,10},{9,11},{10,... | collective-permute-start | bytes 516104 | tf_op jit(solution)/shard_map/ppermute | solution.py:551
  139.7 1.4 collective-permute-start.31
  141.1 7.5 %collective-permute-done.27 = bf16[168,512]{1,0:T(8,128)(2,1)S(1)} collective-permute-done((bf16[168,512]{1,0:T(8,128)(2,1)S(1)}, bf16[168,512]{1,0:T(8,128)(2,1)S(1)}, u32[]{:S(2)}, u32[]{:S(2)}) %collective-permute-start.27) | collective-permute-done | bytes 172064 | tf_op jit(solution)/shard_map/ppermute | solution.py:551
  148.9 1.2 collective-permute-done.28
  150.5 1.8 %place.1 = (bf16[2,256,512]{2,1,0:T(8,128)(2,1)}, f32[2,256,512]{2,1,0:T(8,128)}) custom-call(s32[4]{0:T(128)S(1)} %pad_add_fusion.meta, bf16[256,512]{1,0:T(8,128)(2,1)S(1)} %collective-permute-done.14.y0, bf16[256,512]{1,0:T(8,128)(2,1)S(1)} %collective-permute-done.15.y1, bf16[256,512]{1,0:T(8,128)(2,1)S(1)} %collective-permute-done.26.x0, ...), custom_call_target="tpu_custom_call" | custom-call | tf_op jit(solution)/shard_map/place/pallas_call | solution.py:587
  152.3 1.6 %early_out.1 = (f32[64,2048]{1,0:T(8,128)}, f32[256,512]{1,0:T(8,128)}, f32[1,64]{1,0:T(1,128)}, f32[1,64]{1,0:T(1,128)}, f32[1,64]{1,0:T(1,128)}, /*index=5*/f32[1,256]{1,0:T(1,128)}) custom-call(s32[4]{0:T(128)S(1)} %pad_add_fusion.meta, bf16[264,512]{1,0:T(8,128)(2,1)S(1)} %add_convert_fusion.1.mine, bf16[264,512]{1,0:T(8,128)(2,1)S(1)} %collective-permute-done.31.other, ...), custom_call_target="tpu_custom_call" | custom-call | tf_op jit(solution)/shard_map/early_out/pallas_call | solution.py:587
  153.9 2.9 %collective-permute-done.29.other = bf16[176,512]{1,0:T(8,128)(2,1)S(1)} collective-permute-done((bf16[176,512]{1,0:T(8,128)(2,1)S(1)}, bf16[176,512]{1,0:T(8,128)(2,1)S(1)}, u32[]{:S(2)}, u32[]{:S(2)}) %collective-permute-start.29) | collective-permute-done | bytes 180256 | tf_op jit(solution)/shard_map/ppermute | solution.py:551
  156.8 1.5 late_out.1
  (93 shorter events, 6.2 us)
Async XLA Ops:
  0.7 0.7 copy-start.9
  1.3 3.7 %copy-start.12 = (bf16[2,256,512]{2,1,0:T(8,128)(2,1)S(1)}, bf16[2,256,512]{2,1,0:T(8,128)(2,1)}, u32[]{:S(2)}) copy-start(bf16[2,256,512]{2,1,0:T(8,128)(2,1)} %param.31) | copy-start | bytes 1572868
  3.3 8.1 %collective-permute-start = (bf16[168,1024]{1,0:T(8,128)(2,1)S(1)}, bf16[168,1024]{1,0:T(8,128)(2,1)S(1)}, u32[]{:S(2)}, u32[]{:S(2)}) collective-permute-start(bf16[168,1024]{1,0:T(8,128)(2,1)S(1)} %get-tuple-element.159), channel_id=1, source_target_pairs={{0,4},{4,0},{8,12},{12,8},{16,20},{20,16},{24,28},{28,24},{1,5},{5... | collective-permute-start | bytes 1032200 | tf_op jit(solution)/shard_map/ppermute | solution.py:536
  5.1 24.9 %collective-permute-start.4 = (bf16[256,1024]{1,0:T(8,128)(2,1)S(1)}, bf16[256,1024]{1,0:T(8,128)(2,1)S(1)}, u32[]{:S(2)}, u32[]{:S(2)}) collective-permute-start(bf16[256,1024]{1,0:T(8,128)(2,1)S(1)} %get-tuple-element.302), channel_id=1, source_target_pairs={{0,0},{1,4},{2,1},{3,5},{4,2},{5,6},{6,3},{7,7},{8,8},{9,12},{10,9... | collective-permute-start | bytes 1572872 | tf_op jit(solution)/shard_map/ppermute | solution.py:565
  5.8 29.3 %collective-permute-start.5 = (bf16[256,1024]{1,0:T(8,128)(2,1)S(1)}, bf16[256,1024]{1,0:T(8,128)(2,1)S(1)}, u32[]{:S(2)}, u32[]{:S(2)}) collective-permute-start(bf16[256,1024]{1,0:T(8,128)(2,1)S(1)} %get-tuple-element.301), channel_id=1, source_target_pairs={{0,1},{1,5},{2,0},{3,4},{4,3},{5,7},{6,2},{7,6},{8,9},{9,13},{10,8... | collective-permute-start | bytes 1572872 | tf_op jit(solution)/shard_map/ppermute | solution.py:565
  10.4 5.0 %copy-start.10 = (s32[2]{0:T(128)S(1)}, s32[2]{0:T(128)}, u32[]{:S(2)}) copy-start(s32[2]{0:T(128)} %lengths_ref.1) | copy-start | bytes 28
  11.7 26.8 %copy-start.11 = (bf16[144,1024]{1,0:T(8,128)(2,1)}, bf16[144,1024]{1,0:T(8,128)(2,1)S(1)}, u32[]{:S(2)}) copy-start(bf16[144,1024]{1,0:T(8,128)(2,1)S(1)} %pad_maximum_fusion.2.refs_0_) | copy-start | bytes 884740
  11.7 8.4 %collective-permute-start.1 = (bf16[144,1024]{1,0:T(8,128)(2,1)S(1)}, bf16[144,1024]{1,0:T(8,128)(2,1)}, u32[]{:S(2)}, u32[]{:S(2)}) collective-permute-start(bf16[144,1024]{1,0:T(8,128)(2,1)S(1)} %pad_maximum_fusion.2.refs_0_), channel_id=1, source_target_pairs={{0,8},{4,12},{8,0},{12,4},{16,24},{20,28},{24,16},{28,20},{1,9},{5... | collective-permute-start | bytes 884744 | tf_op jit(solution)/shard_map/ppermute | solution.py:541
  13.8 14.5 %collective-permute-start.2 = (bf16[144,1024]{1,0:T(8,128)(2,1)S(1)}, bf16[144,1024]{1,0:T(8,128)(2,1)}, u32[]{:S(2)}, u32[]{:S(2)}) collective-permute-start(bf16[144,1024]{1,0:T(8,128)(2,1)S(1)} %pad_maximum_fusion.2.refs_0_), channel_id=1, source_target_pairs={{0,16},{4,20},{8,24},{12,28},{16,0},{20,4},{24,8},{28,12},{1,17},{... | collective-permute-start | bytes 884744 | tf_op jit(solution)/shard_map/ppermute | solution.py:541
  15.4 13.3 %collective-permute-start.3 = (bf16[144,1024]{1,0:T(8,128)(2,1)S(1)}, bf16[144,1024]{1,0:T(8,128)(2,1)}, u32[]{:S(2)}, u32[]{:S(2)}) collective-permute-start(bf16[144,1024]{1,0:T(8,128)(2,1)S(1)} %pad_maximum_fusion.2.refs_0_), channel_id=1, source_target_pairs={{0,24},{4,28},{8,16},{12,20},{16,8},{20,12},{24,0},{28,4},{1,25},{... | collective-permute-start | bytes 884744 | tf_op jit(solution)/shard_map/ppermute | solution.py:541
  28.6 16.1 %collective-permute-start.8 = (bf16[320,1024]{1,0:T(8,128)(2,1)S(1)}, bf16[320,1024]{1,0:T(8,128)(2,1)S(1)}, u32[]{:S(2)}, u32[]{:S(2)}) collective-permute-start(bf16[320,1024]{1,0:T(8,128)(2,1)S(1)} %pad_maximum_fusion.1.refs_0_), channel_id=1, source_target_pairs={{0,8},{4,20},{8,0},{12,28},{16,24},{20,4},{24,16},{28,12},{1,9},{5... | collective-permute-start | bytes 1966088 | tf_op jit(solution)/shard_map/ppermute | solution.py:546
  30.0 8.5 %copy-start.1 = (bf16[256,1024]{1,0:T(8,128)(2,1)}, bf16[256,1024]{1,0:T(8,128)(2,1)S(1)}, u32[]{:S(2)}) copy-start(bf16[256,1024]{1,0:T(8,128)(2,1)S(1)} %collective-permute-done.4.refs_4_) | copy-start | bytes 1572868
  35.1 3.5 %copy-start.3 = (bf16[256,1024]{1,0:T(8,128)(2,1)}, bf16[256,1024]{1,0:T(8,128)(2,1)S(1)}, u32[]{:S(2)}) copy-start(bf16[256,1024]{1,0:T(8,128)(2,1)S(1)} %collective-permute-done.5.refs_5_) | copy-start | bytes 1572868
  35.1 1.9 %collective-permute-start.6 = (bf16[256,1024]{1,0:T(8,128)(2,1)S(1)}, bf16[256,1024]{1,0:T(8,128)(2,1)S(1)}, u32[]{:S(2)}, u32[]{:S(2)}) collective-permute-start(bf16[256,1024]{1,0:T(8,128)(2,1)S(1)} %collective-permute-done.5.refs_5_), channel_id=1, source_target_pairs={{0,4},{4,0},{8,12},{12,8},{16,20},{20,16},{24,28},{28,24},{1,5},{5... | collective-permute-start | bytes 1572872 | tf_op jit(solution)/shard_map/ppermute | solution.py:536
  35.1 3.4 %collective-permute-start.7 = (bf16[256,1024]{1,0:T(8,128)(2,1)S(1)}, bf16[256,1024]{1,0:T(8,128)(2,1)S(1)}, u32[]{:S(2)}, u32[]{:S(2)}) collective-permute-start(bf16[256,1024]{1,0:T(8,128)(2,1)S(1)} %collective-permute-done.4.refs_4_), channel_id=1, source_target_pairs={{0,4},{4,0},{8,12},{12,8},{16,20},{20,16},{24,28},{28,24},{1,5},{5... | collective-permute-start | bytes 1572872 | tf_op jit(solution)/shard_map/ppermute | solution.py:536
  37.0 1.6 copy-start.5
  37.0 19.9 %collective-permute-start.9 = (bf16[320,1024]{1,0:T(8,128)(2,1)S(1)}, bf16[320,1024]{1,0:T(8,128)(2,1)S(1)}, u32[]{:S(2)}, u32[]{:S(2)}) collective-permute-start(bf16[320,1024]{1,0:T(8,128)(2,1)S(1)} %pad_maximum_fusion.1.refs_0_), channel_id=1, source_target_pairs={{0,16},{4,12},{8,24},{12,4},{16,0},{20,28},{24,8},{28,20},{1,17},{... | collective-permute-start | bytes 1966088 | tf_op jit(solution)/shard_map/ppermute | solution.py:546
  38.5 0.8 copy-start.7
  44.8 12.1 %collective-permute-start.10 = (bf16[320,1024]{1,0:T(8,128)(2,1)S(1)}, bf16[320,1024]{1,0:T(8,128)(2,1)S(1)}, u32[]{:S(2)}, u32[]{:S(2)}) collective-permute-start(bf16[320,1024]{1,0:T(8,128)(2,1)S(1)} %collective-permute-done.8.refs_1_), channel_id=1, source_target_pairs={{0,16},{4,12},{8,24},{12,4},{16,0},{20,28},{24,8},{28,20},{1,17},{... | collective-permute-start | bytes 1966088 | tf_op jit(solution)/shard_map/ppermute | solution.py:546
  45.6 13.3 %copy-start.2 = (bf16[256,1024]{1,0:T(8,128)(2,1)S(1)}, bf16[256,1024]{1,0:T(8,128)(2,1)}, u32[]{:S(2)}) copy-start(bf16[256,1024]{1,0:T(8,128)(2,1)} %copy-done.1) | copy-start | bytes 1572868
  45.6 13.3 %copy-start.4 = (bf16[256,1024]{1,0:T(8,128)(2,1)S(1)}, bf16[256,1024]{1,0:T(8,128)(2,1)}, u32[]{:S(2)}) copy-start(bf16[256,1024]{1,0:T(8,128)(2,1)} %copy-done.3) | copy-start | bytes 1572868
  45.6 13.3 %copy-start.6 = (bf16[256,1024]{1,0:T(8,128)(2,1)S(1)}, bf16[256,1024]{1,0:T(8,128)(2,1)}, u32[]{:S(2)}) copy-start(bf16[256,1024]{1,0:T(8,128)(2,1)} %copy-done.5) | copy-start | bytes 1572868
  45.6 13.3 %copy-start.8 = (bf16[256,1024]{1,0:T(8,128)(2,1)S(1)}, bf16[256,1024]{1,0:T(8,128)(2,1)}, u32[]{:S(2)}) copy-start(bf16[256,1024]{1,0:T(8,128)(2,1)} %copy-done.7) | copy-start | bytes 1572868
  56.9 2.0 %collective-permute-start.11 = (bf16[1024,256]{1,0:T(8,128)(2,1)S(1)}, bf16[1024,256]{1,0:T(8,128)(2,1)S(1)}, u32[]{:S(2)}, u32[]{:S(2)}) collective-permute-start(bf16[1024,256]{1,0:T(8,128)(2,1)S(1)} %get-tuple-element.191.refs_9_.o_ref), channel_id=1, source_target_pairs={{0,4},{4,0},{8,12},{12,8},{16,20},{20,16},{24,28},{28,24},{1,5},{5... | collective-permute-start | bytes 1572872 | tf_op jit(solution)/shard_map/ppermute | solution.py:536
  70.1 4.1 %collective-permute-start.12 = (bf16[1024,512]{1,0:T(8,128)(2,1)S(1)}, bf16[1024,512]{1,0:T(8,128)(2,1)S(1)}, u32[]{:S(2)}, u32[]{:S(2)}) collective-permute-start(bf16[1024,512]{1,0:T(8,128)(2,1)S(1)} %get-tuple-element.196.dh_ref), channel_id=1, source_target_pairs={{0,4},{4,0},{8,12},{12,8},{16,20},{20,16},{24,28},{28,24},{1,5},{5... | collective-permute-start | bytes 3145736 | tf_op jit(solution)/shard_map/ppermute | solution.py:536
  70.3 3.9 %collective-permute-start.13 = (bf16[512,512]{1,0:T(8,128)(2,1)S(1)}, bf16[512,512]{1,0:T(8,128)(2,1)S(1)}, u32[]{:S(2)}, u32[]{:S(2)}) collective-permute-start(bf16[512,512]{1,0:T(8,128)(2,1)S(1)} %get-tuple-element.199), channel_id=1, source_target_pairs={{0,4},{4,0},{8,12},{12,8},{16,20},{20,16},{24,28},{28,24},{1,5},{5... | collective-permute-start | bytes 1572872 | tf_op jit(solution)/shard_map/ppermute | solution.py:536
  70.7 18.8 %collective-permute-start.16 = (bf16[264,1024]{1,0:T(8,128)(2,1)S(1)}, bf16[264,1024]{1,0:T(8,128)(2,1)S(1)}, u32[]{:S(2)}, u32[]{:S(2)}) collective-permute-start(bf16[264,1024]{1,0:T(8,128)(2,1)S(1)} %get-tuple-element.228), channel_id=1, source_target_pairs={{0,8},{4,12},{8,0},{12,4},{16,24},{20,28},{24,16},{28,20},{1,9},{5... | collective-permute-start | bytes 1622024 | tf_op jit(solution)/shard_map/ppermute | solution.py:541
  72.2 25.6 %collective-permute-start.17 = (bf16[264,1024]{1,0:T(8,128)(2,1)S(1)}, bf16[264,1024]{1,0:T(8,128)(2,1)S(1)}, u32[]{:S(2)}, u32[]{:S(2)}) collective-permute-start(bf16[264,1024]{1,0:T(8,128)(2,1)S(1)} %get-tuple-element.229), channel_id=1, source_target_pairs={{0,16},{4,20},{8,24},{12,28},{16,0},{20,4},{24,8},{28,12},{1,17},{... | collective-permute-start | bytes 1622024 | tf_op jit(solution)/shard_map/ppermute | solution.py:541
  73.5 24.3 %collective-permute-start.18 = (bf16[264,1024]{1,0:T(8,128)(2,1)S(1)}, bf16[264,1024]{1,0:T(8,128)(2,1)S(1)}, u32[]{:S(2)}, u32[]{:S(2)}) collective-permute-start(bf16[264,1024]{1,0:T(8,128)(2,1)S(1)} %get-tuple-element.230), channel_id=1, source_target_pairs={{0,24},{4,28},{8,16},{12,20},{16,8},{20,12},{24,0},{28,4},{1,25},{... | collective-permute-start | bytes 1622024 | tf_op jit(solution)/shard_map/ppermute | solution.py:541
  77.6 20.2 %collective-permute-start.14 = (bf16[256,512]{1,0:T(8,128)(2,1)S(1)}, bf16[256,512]{1,0:T(8,128)(2,1)S(1)}, u32[]{:S(2)}, u32[]{:S(2)}) collective-permute-start(bf16[256,512]{1,0:T(8,128)(2,1)S(1)} %get-tuple-element.226), channel_id=1, source_target_pairs={{0,0},{4,1},{1,2},{5,3},{2,4},{6,5},{3,6},{7,7},{8,8},{12,9},{9,10... | collective-permute-start | bytes 786440 | tf_op jit(solution)/shard_map/ppermute | solution.py:1124
  78.3 19.5 %collective-permute-start.15 = (bf16[256,512]{1,0:T(8,128)(2,1)S(1)}, bf16[256,512]{1,0:T(8,128)(2,1)S(1)}, u32[]{:S(2)}, u32[]{:S(2)}) collective-permute-start(bf16[256,512]{1,0:T(8,128)(2,1)S(1)} %get-tuple-element.227), channel_id=1, source_target_pairs={{1,0},{5,1},{0,2},{4,3},{3,4},{7,5},{2,6},{6,7},{9,8},{13,9},{8,10... | collective-permute-start | bytes 786440 | tf_op jit(solution)/shard_map/ppermute | solution.py:1124
  89.4 9.2 %copy-start = (bf16[1024,512]{1,0:T(8,128)(2,1)S(1)}, bf16[1024,512]{1,0:T(8,128)(2,1)}, u32[]{:S(2)}) copy-start(bf16[1024,512]{1,0:T(8,128)(2,1)} %pad_maximum_fusion.refs_8_.refs_15_) | copy-start | bytes 3145732
  102.8 9.0 %collective-permute-start.22 = (bf16[512,512]{1,0:T(8,128)(2,1)S(1)}, bf16[512,512]{1,0:T(8,128)(2,1)S(1)}, u32[]{:S(2)}, u32[]{:S(2)}) collective-permute-start(bf16[512,512]{1,0:T(8,128)(2,1)S(1)} %get-tuple-element.260), channel_id=1, source_target_pairs={{0,4},{4,0},{8,12},{12,8},{16,20},{20,16},{24,28},{28,24},{1,5},{5... | collective-permute-start | bytes 1572872 | tf_op jit(solution)/shard_map/ppermute | solution.py:536
  102.9 8.9 %collective-permute-start.23 = (bf16[264,512]{1,0:T(8,128)(2,1)S(1)}, bf16[264,512]{1,0:T(8,128)(2,1)S(1)}, u32[]{:S(2)}, u32[]{:S(2)}) collective-permute-start(bf16[264,512]{1,0:T(8,128)(2,1)S(1)} %get-tuple-element.261), channel_id=1, source_target_pairs={{0,1},{1,0},{2,3},{3,2},{4,5},{5,4},{6,7},{7,6},{8,9},{9,8},{10,11... | collective-permute-start | bytes 811016 | tf_op jit(solution)/shard_map/ppermute | solution.py:551
  103.0 12.8 %collective-permute-start.19 = (bf16[168,1024]{1,0:T(8,128)(2,1)S(1)}, bf16[168,1024]{1,0:T(8,128)(2,1)S(1)}, u32[]{:S(2)}, u32[]{:S(2)}) collective-permute-start(bf16[168,1024]{1,0:T(8,128)(2,1)S(1)} %get-tuple-element.256), channel_id=1, source_target_pairs={{0,8},{4,12},{8,0},{12,4},{16,24},{20,28},{24,16},{28,20},{1,9},{5... | collective-permute-start | bytes 1032200 | tf_op jit(solution)/shard_map/ppermute | solution.py:541
  105.7 17.1 %collective-permute-start.20 = (bf16[168,1024]{1,0:T(8,128)(2,1)S(1)}, bf16[168,1024]{1,0:T(8,128)(2,1)S(1)}, u32[]{:S(2)}, u32[]{:S(2)}) collective-permute-start(bf16[168,1024]{1,0:T(8,128)(2,1)S(1)} %get-tuple-element.257), channel_id=1, source_target_pairs={{0,16},{4,20},{8,24},{12,28},{16,0},{20,4},{24,8},{28,12},{1,17},{... | collective-permute-start | bytes 1032200 | tf_op jit(solution)/shard_map/ppermute | solution.py:541
  107.1 15.7 %collective-permute-start.21 = (bf16[168,1024]{1,0:T(8,128)(2,1)S(1)}, bf16[168,1024]{1,0:T(8,128)(2,1)S(1)}, u32[]{:S(2)}, u32[]{:S(2)}) collective-permute-start(bf16[168,1024]{1,0:T(8,128)(2,1)S(1)} %get-tuple-element.258), channel_id=1, source_target_pairs={{0,24},{4,28},{8,16},{12,20},{16,8},{20,12},{24,0},{28,4},{1,25},{... | collective-permute-start | bytes 1032200 | tf_op jit(solution)/shard_map/ppermute | solution.py:541
  111.9 19.9 %collective-permute-start.25 = (bf16[264,512]{1,0:T(8,128)(2,1)S(1)}, bf16[264,512]{1,0:T(8,128)(2,1)S(1)}, u32[]{:S(2)}, u32[]{:S(2)}) collective-permute-start(bf16[264,512]{1,0:T(8,128)(2,1)S(1)} %add_convert_fusion.2), channel_id=1, source_target_pairs={{0,2},{1,3},{2,0},{3,1},{4,6},{5,7},{6,4},{7,5},{8,10},{9,11},{10,... | collective-permute-start | bytes 811016 | tf_op jit(solution)/shard_map/ppermute | solution.py:551
  115.1 16.7 %collective-permute-start.26 = (bf16[256,512]{1,0:T(8,128)(2,1)S(1)}, bf16[256,512]{1,0:T(8,128)(2,1)S(1)}, u32[]{:S(2)}, u32[]{:S(2)}) collective-permute-start(bf16[256,512]{1,0:T(8,128)(2,1)S(1)} %get-tuple-element.264), channel_id=1, source_target_pairs={{0,0},{4,1},{1,2},{5,3},{2,4},{6,5},{3,6},{7,7},{8,8},{12,9},{9,10... | collective-permute-start | bytes 786440 | tf_op jit(solution)/shard_map/ppermute | solution.py:1124
  123.4 8.3 %collective-permute-start.24 = (bf16[168,512]{1,0:T(8,128)(2,1)S(1)}, bf16[168,512]{1,0:T(8,128)(2,1)S(1)}, u32[]{:S(2)}, u32[]{:S(2)}) collective-permute-start(bf16[168,512]{1,0:T(8,128)(2,1)S(1)} %get-tuple-element.270), channel_id=1, source_target_pairs={{0,1},{1,0},{2,3},{3,2},{4,5},{5,4},{6,7},{7,6},{8,9},{9,8},{10,11... | collective-permute-start | bytes 516104 | tf_op jit(solution)/shard_map/ppermute | solution.py:551
  125.3 24.9 %collective-permute-start.30 = (bf16[256,512]{1,0:T(8,128)(2,1)S(1)}, bf16[256,512]{1,0:T(8,128)(2,1)S(1)}, u32[]{:S(2)}, u32[]{:S(2)}) collective-permute-start(bf16[256,512]{1,0:T(8,128)(2,1)S(1)} %get-tuple-element.265), channel_id=1, source_target_pairs={{1,0},{5,1},{0,2},{4,3},{3,4},{7,5},{2,6},{6,7},{9,8},{13,9},{8,10... | collective-permute-start | bytes 786440 | tf_op jit(solution)/shard_map/ppermute | solution.py:1124
  131.8 16.8 %collective-permute-start.27 = (bf16[168,512]{1,0:T(8,128)(2,1)S(1)}, bf16[168,512]{1,0:T(8,128)(2,1)S(1)}, u32[]{:S(2)}, u32[]{:S(2)}) collective-permute-start(bf16[168,512]{1,0:T(8,128)(2,1)S(1)} %add_convert_fusion.4), channel_id=1, source_target_pairs={{0,2},{1,3},{2,0},{3,1},{4,6},{5,7},{6,4},{7,5},{8,10},{9,11},{10,... | collective-permute-start | bytes 516104 | tf_op jit(solution)/shard_map/ppermute | solution.py:551
  139.7 10.5 %collective-permute-start.31 = (bf16[264,512]{1,0:T(8,128)(2,1)S(1)}, bf16[264,512]{1,0:T(8,128)(2,1)S(1)}, u32[]{:S(2)}, u32[]{:S(2)}) collective-permute-start(bf16[264,512]{1,0:T(8,128)(2,1)S(1)} %add_convert_fusion.1.mine), channel_id=1, source_target_pairs={{0,1},{1,0},{2,3},{3,2},{4,5},{5,4},{6,7},{7,6},{8,9},{9,8},{10,11... | collective-permute-start | bytes 811016 | tf_op jit(solution)/shard_map/ppermute | solution.py:551
  148.8 1.3 collective-permute-start.28
  150.1 6.7 %collective-permute-start.29 = (bf16[176,512]{1,0:T(8,128)(2,1)S(1)}, bf16[176,512]{1,0:T(8,128)(2,1)S(1)}, u32[]{:S(2)}, u32[]{:S(2)}) collective-permute-start(bf16[176,512]{1,0:T(8,128)(2,1)S(1)} %pad_maximum_fusion.3.mine), channel_id=1, source_target_pairs={{0,1},{1,0},{2,3},{3,2},{4,5},{5,4},{6,7},{7,6},{8,9},{9,8},{10,11... | collective-permute-start | bytes 540680 | tf_op jit(solution)/shard_map/ppermute | solution.py:551
  150.3 2.0 %collective-permute-start.32 = (bf16[2,72,512]{2,1,0:T(8,128)(2,1)S(1)}, bf16[2,72,512]{2,1,0:T(8,128)(2,1)S(1)}, u32[]{:S(2)}, u32[]{:S(2)}) collective-permute-start(bf16[2,72,512]{2,1,0:T(8,128)(2,1)S(1)} %pad_maximum_fusion.4), channel_id=1, source_target_pairs={{0,4},{4,0},{8,12},{12,8},{16,20},{20,16},{24,28},{28,24},{1,5},{5... | collective-permute-start | bytes 442376 | tf_op jit(solution)/shard_map/ppermute | solution.py:536

commit v5 on v4

--- a/solution.py
+++ b/solution.py
@@ -1018,7 +1018,7 @@
     attn_pack, feed_pack, pack_send = kernel_call(
         pack_body,
         "pack",
-        lengths,
+        pltpu.with_memory_space_constraint(lengths, pltpu.HBM),
         [
             pltpu.with_memory_space_constraint(v, pltpu.HBM)
             for v in [w_qkv, w_rel, w_up, w_out, w_down] + [v.reshape(-1, min(128, v.size)) for v in vectors]
@@ -1052,7 +1052,6 @@
     x_own, attn_packs = rest[:2], rest[2:]
     x_other = [swap_core(x) for x in x_own]
     feed_first = swap_axis(feed_pack, 0)
-    feed_pack, x_other[1] = together(feed_pack, x_other[1])
     feed_second = swap_axis(feed_pack, 1)
 
     side = lambda at: pl.BlockSpec((block, width), lambda i, _: (0, at))
@@ -1061,7 +1060,7 @@
         project_body,
         "project",
         none,
-        [pltpu.with_memory_space_constraint(v, pltpu.HBM) for v in attn_packs + x_own + x_other + [table]],
+        [pltpu.with_memory_space_constraint(v, pltpu.HBM) for v in attn_packs] + x_own + x_other + [table],
         [((full, 3 * cols), bf), ((full, width), bf), ((full, width), bf), ((full, cols), bf)]
         + [((width, 4 * cols), bf), ((8, width), f32), ((1, mine_ff), f32), ((1, cols), f32), ((1, cols), f32)],
         grid=(4,),
@@ -1147,7 +1146,9 @@
         flops=14 * full * width * cols,
     )
     dh1_send, *late_parts = together(dh1_send, *late_parts)
-    dh1_came, early_came = together(swap_core(dh1_send), early_came)
+    early_pair = (early_keep + early_came.astype(f32)).astype(bf)
+    dh1_came = swap_core(dh1_send)
+    early_came = swap_seq(early_pair, 2)
     late_came = [swap_chip(late_parts[k], k) for k in (1, 2, 3)]
     by_half = pl.BlockSpec((block, width), lambda i, _: (i, 0))
     own_rows = pl.BlockSpec((block, width), lambda i, m: (2 * i + m[CORE], 0))
@@ -1162,9 +1163,6 @@
         out_specs=[whole(block, width)] * 2,
     )
     x_turns = home((x0, x1))
-    *late_came, _, _ = together(*late_came, x0, x1)
-    early_pair = (early_keep + early_came.astype(f32)).astype(bf)
-    early_came = swap_seq(early_pair, 2)
     late_keep, late_send = chip_sum(meta, [late_parts[0]] + late_came, "late_chips", 0)
     small = lambda size: ((1, size), f32)
     late_came, early_came, x_turns[0] = together(swap_seq(late_send, 1), early_came, x_turns[0])

time: 158 us -> 152 us (0.962)
  starting transfers between devices: 40.5 us -> 35 us
  Pallas kernels: 52.9 us -> 56.7 us
  waiting for transfers between devices: 56.7 us -> 53.7 us
    ppermute x6, starting transfers between devices: 12.9 us -> 7.71 us  [swap_seq(): return lax.ppermute(values, 'seq', [(i, i ^ mask) for i in range(size)])]
    pallas_call x2, Pallas kernels: 7.56 us -> 11.8 us  [attn_bwd(): pl.pallas_call(functools.partial(attn_bwd_body, block=block, heads=heads)...]
    ppermute x6, waiting for transfers between devices: 20.6 us -> 16.9 us  [swap_seq(): return lax.ppermute(values, 'seq', [(i, i ^ mask) for i in range(size)])]
  transfers between devices with their start and end apart: 33 -> 33, of which waited for: 13 -> 14; matrix products, arithmetic and copies ran while one was open for 3% -> 3% of each run, Pallas kernels for 21% -> 27%
where the time goes in v5:
time: 152 us
  Pallas kernels  56.7 us (37%)
  waiting for transfers between devices  53.7 us (35%)
  starting transfers between devices  35 us (23%)
  local copies, waits for them, and re-layouts  3.07 us (2%)
  between operations  2.38 us (2%)
    pallas_call x11, Pallas kernels, kernel_call(): pl.pallas_call(body, out_shape=[jax.ShapeDtypeStruct(shape, kind) for sha...  33.6 us
    ppermute x9, waiting for transfers between devices, swap_chip(): lax.ppermute(values, 'fsdp', [(i, i ^ 2 * mask) for i in range(size)])  26.8 us
    ppermute x6, waiting for transfers between devices, swap_seq(): return lax.ppermute(values, 'seq', [(i, i ^ mask) for i in range(size)])  16.9 us
    pallas_call x2, Pallas kernels, attn_bwd(): pl.pallas_call(functools.partial(attn_bwd_body, block=block, heads=heads)...  11.8 us
    pallas_call x1, Pallas kernels, attn_fwd(): pl.pallas_call(functools.partial(attn_fwd_body, block=block), out_shape=(...  11.3 us
    ppermute x9, starting transfers between devices, swap_chip(): lax.ppermute(values, 'fsdp', [(i, i ^ 2 * mask) for i in range(size)])  11.1 us
    ppermute x6, starting transfers between devices, swap_seq(): return lax.ppermute(values, 'seq', [(i, i ^ mask) for i in range(size)])  7.71 us
    ppermute x2, waiting for transfers between devices, to_slots(): lax.ppermute(lax.dynamic_index_in_dim(values, turn ^ seq_rank >> 1, 0, ke...  6.23 us
  transfers between devices with their start and end apart: 33, of which 14 were waited for; matrix products, arithmetic and copies ran while one was open for 3% of the time, Pallas kernels for 27%

profile of v5, /device:TPU:0, one launch (start us, length us, event | category | flops | bytes accessed | tf_op | source)
XLA Modules:
  0.0 152.1 jit_solution(13641739277045217214)
XLA Ops:
  0.7 2.3 %pack.1 = (bf16[72,1024]{1,0:T(8,128)(2,1)S(1)}, bf16[224,1024]{1,0:T(8,128)(2,1)S(1)}, bf16[168,1024]{1,0:T(8,128)(2,1)S(1)}) custom-call(s32[2]{0:T(128)} %lengths_ref.1, bf16[64,1536]{1,0:T(8,128)(2,1)} %qkv_ref.1, bf16[64,512]{1,0:T(8,128)(2,1)} %rel_ref.1, bf16[64,2048]{1,0:T(8,128)(2,1)} %up_ref.1, bf16[64,512]{1,0:T(8,128)(2,1)} %out_ref.1, ...), custom_call_target="tpu_custom_call" | custom-call | tf_op jit(solution)/shard_map/pack/pallas_call | solution.py:587
  3.5 1.1 constant_dynamic-update-slice_fusion.1
  4.7 1.0 dynamic-slice_bitcast_fusion
  5.7 1.7 %collective-permute-start.4 = (bf16[256,1024]{1,0:T(8,128)(2,1)}, bf16[256,1024]{1,0:T(8,128)(2,1)S(1)}, u32[]{:S(2)}, u32[]{:S(2)}) collective-permute-start(bf16[256,1024]{1,0:T(8,128)(2,1)} %get-tuple-element.288), channel_id=1, source_target_pairs={{0,0},{1,4},{2,1},{3,5},{4,2},{5,6},{6,3},{7,7},{8,8},{9,12},{10,9... | collective-permute-start | bytes 1572872 | tf_op jit(solution)/shard_map/ppermute | solution.py:565
  7.4 2.9 %collective-permute-start.5 = (bf16[256,1024]{1,0:T(8,128)(2,1)}, bf16[256,1024]{1,0:T(8,128)(2,1)S(1)}, u32[]{:S(2)}, u32[]{:S(2)}) collective-permute-start(bf16[256,1024]{1,0:T(8,128)(2,1)} %get-tuple-element.287), channel_id=1, source_target_pairs={{0,1},{1,5},{2,0},{3,4},{4,3},{5,7},{6,2},{7,6},{8,9},{9,13},{10,8... | collective-permute-start | bytes 1572872 | tf_op jit(solution)/shard_map/ppermute | solution.py:565
  11.4 2.1 %collective-permute-start.1 = (bf16[144,1024]{1,0:T(8,128)(2,1)S(1)}, bf16[144,1024]{1,0:T(8,128)(2,1)}, u32[]{:S(2)}, u32[]{:S(2)}) collective-permute-start(bf16[144,1024]{1,0:T(8,128)(2,1)S(1)} %pad_maximum_fusion.2.refs_0_), channel_id=1, source_target_pairs={{0,8},{4,12},{8,0},{12,4},{16,24},{20,28},{24,16},{28,20},{1,9},{5... | collective-permute-start | bytes 884744 | tf_op jit(solution)/shard_map/ppermute | solution.py:541
  13.4 1.5 collective-permute-start.2
  15.0 0.6 fusion.3
  17.0 2.7 %collective-permute-done.1.refs_1_ = bf16[144,1024]{1,0:T(8,128)(2,1)} collective-permute-done((bf16[144,1024]{1,0:T(8,128)(2,1)S(1)}, bf16[144,1024]{1,0:T(8,128)(2,1)}, u32[]{:S(2)}, u32[]{:S(2)}) %collective-permute-start.1) | collective-permute-done | bytes 294944 | tf_op jit(solution)/shard_map/ppermute | solution.py:541
  19.8 8.2 %collective-permute-done.2.refs_2_ = bf16[144,1024]{1,0:T(8,128)(2,1)} collective-permute-done((bf16[144,1024]{1,0:T(8,128)(2,1)S(1)}, bf16[144,1024]{1,0:T(8,128)(2,1)}, u32[]{:S(2)}, u32[]{:S(2)}) %collective-permute-start.2) | collective-permute-done | bytes 294944 | tf_op jit(solution)/shard_map/ppermute | solution.py:541
  28.2 1.4 collective-permute-start.8
  29.6 6.2 %collective-permute-done.5.refs_5_ = bf16[256,1024]{1,0:T(8,128)(2,1)S(1)} collective-permute-done((bf16[256,1024]{1,0:T(8,128)(2,1)}, bf16[256,1024]{1,0:T(8,128)(2,1)S(1)}, u32[]{:S(2)}, u32[]{:S(2)}) %collective-permute-start.5) | collective-permute-done | bytes 524320 | tf_op jit(solution)/shard_map/ppermute | solution.py:565
  36.4 1.5 collective-permute-start.9
  37.9 0.6 collective-permute-done.7.refs_7_
  38.5 4.8 %project.1 = (bf16[1024,768]{1,0:T(8,128)(2,1)S(1)}, bf16[1024,512]{1,0:T(8,128)(2,1)S(1)}, bf16[1024,512]{1,0:T(8,128)(2,1)S(1)}, bf16[1024,256]{1,0:T(8,128)(2...) custom-call(s32[4]{0:T(128)S(1)} %broadcast_3__.2._, ...), custom_call_target="tpu_custom_call" | custom-call | tf_op jit(solution)/shard_map/project/pallas_call | solution.py:587
  43.3 1.6 %collective-permute-start.10 = (bf16[320,1024]{1,0:T(8,128)(2,1)S(1)}, bf16[320,1024]{1,0:T(8,128)(2,1)S(1)}, u32[]{:S(2)}, u32[]{:S(2)}) collective-permute-start(bf16[320,1024]{1,0:T(8,128)(2,1)S(1)} %collective-permute-done.8.refs_1_), channel_id=1, source_target_pairs={{0,16},{4,12},{8,24},{12,4},{16,0},{20,28},{24,8},{28,20},{1,17},{... | collective-permute-start | bytes 1966088 | tf_op jit(solution)/shard_map/ppermute | solution.py:546
  44.9 11.3 %attn_fwd.1 = (bf16[1024,256]{1,0:T(8,128)(2,1)S(1)}, bf16[4,256,256]{2,1,0:T(8,128)(2,1)S(1)}, bf16[4,256,512]{2,1,0:T(8,128)(2,1)S(1)}, bf16[4,256,768]{2,1,0:T(8,128)(2,1)S(1)}, bf16[4,256,1024]{2,1,0:T(8,128)(2,1)S(1)}) custom-call(s32[1]{0:T(128)} %bitcast.15.len_ref, bf16[1024,768]{1,0:T(8,128)(2,1)S(1)} %get-tuple-element.174.q_ref.k_ref.v_ref, ...), custom_call_target="tpu_custom_call" | custom-call | tf_op jit(solution)/shard_map/attn_fwd/pallas_call | solution.py:85
  56.3 1.9 %collective-permute-done.11.refs_10_ = bf16[1024,256]{1,0:T(8,128)(2,1)S(1)} collective-permute-done((bf16[1024,256]{1,0:T(8,128)(2,1)S(1)}, bf16[1024,256]{1,0:T(8,128)(2,1)S(1)}, u32[]{:S(2)}, u32[]{:S(2)}) %collective-permute-start.11) | collective-permute-done | bytes 524320 | tf_op jit(solution)/shard_map/ppermute | solution.py:536
  58.2 11.2 %feed.1 = (bf16[1024,512]{1,0:T(8,128)(2,1)S(1)}, bf16[1024,512]{1,0:T(8,128)(2,1)S(1)}, f32[1024,1]{1,0:T(8,128)S(1)}, f32[512,512]{1,0:T(8,128)S(1)}, bf16[102...) custom-call(s32[4]{0:T(128)S(1)} %pad_add_fusion.meta, ...), custom_call_target="tpu_custom_call" | custom-call | tf_op jit(solution)/shard_map/feed/pallas_call | solution.py:587
  70.0 1.5 collective-permute-start.16
  72.0 1.5 collective-permute-start.18
  73.5 3.5 %norm_two.1 = (bf16[256,512]{1,0:T(8,128)(2,1)S(1)}, bf16[256,512]{1,0:T(8,128)(2,1)S(1)}, f32[512,512]{1,0:T(8,128)S(1)}, bf16[1024,256]{1,0:T(8,128)(2,1)S(1)}, f32[256,512]{1,0:T(8,128)S(1)}) custom-call(s32[4]{0:T(128)S(1)} %pad_add_fusion.meta, bf16[1024,512]{1,0:T(8,128)(2,1)S(1)} %get-tuple-element.185.x_hat_ref, ...), custom_call_target="tpu_custom_call" | custom-call | tf_op jit(solution)/shard_map/norm_two/pallas_call | solution.py:587
  76.9 0.7 collective-permute-start.14
  77.6 3.5 %collective-permute-start.15 = (bf16[256,512]{1,0:T(8,128)(2,1)S(1)}, bf16[256,512]{1,0:T(8,128)(2,1)S(1)}, u32[]{:S(2)}, u32[]{:S(2)}) collective-permute-start(bf16[256,512]{1,0:T(8,128)(2,1)S(1)} %get-tuple-element.218), channel_id=1, source_target_pairs={{1,0},{5,1},{0,2},{4,3},{3,4},{7,5},{2,6},{6,7},{9,8},{13,9},{8,10... | collective-permute-start | bytes 786440 | tf_op jit(solution)/shard_map/ppermute | solution.py:1123
  81.2 5.8 %attn_bwd.2 = (bf16[1024,128]{1,0:T(8,128)(2,1)S(1)}, bf16[1024,128]{1,0:T(8,128)(2,1)S(1)}, bf16[1024,128]{1,0:T(8,128)(2,1)S(1)}, bf16[1024,128]{1,0:T(8,128)(...) custom-call(s32[1]{0:T(128)} %bitcast.15.len_ref, bf16[1024,768]{1,0:T(8,128)(2,1)S(1)} %get-tuple-element.174.q_ref.k_ref.v_ref, ...), custom_call_target="tpu_custom_call" | custom-call | tf_op jit(solution)/shard_map/attn_bwd/pallas_call | solution.py:164
  87.0 6.0 %attn_bwd.3 = (bf16[1024,128]{1,0:T(8,128)(2,1)S(1)}, bf16[1024,128]{1,0:T(8,128)(2,1)S(1)}, bf16[1024,128]{1,0:T(8,128)(2,1)S(1)}, bf16[1024,128]{1,0:T(8,128)(...) custom-call(s32[1]{0:T(128)} %bitcast.15.len_ref, bf16[1024,768]{1,0:T(8,128)(2,1)S(1)} %get-tuple-element.174.q_ref.k_ref.v_ref, ...), custom_call_target="tpu_custom_call" | custom-call | tf_op jit(solution)/shard_map/attn_bwd/pallas_call | solution.py:164
  93.0 4.1 %collective-permute-done.17.refs_1_ = bf16[264,1024]{1,0:T(8,128)(2,1)S(1)} collective-permute-done((bf16[264,1024]{1,0:T(8,128)(2,1)S(1)}, bf16[264,1024]{1,0:T(8,128)(2,1)S(1)}, u32[]{:S(2)}, u32[]{:S(2)}) %collective-permute-start.17) | collective-permute-done | bytes 540704 | tf_op jit(solution)/shard_map/ppermute | solution.py:541
  97.1 0.8 early_chips.1
  98.0 4.1 %qkv_back.1 = (f32[512,512]{1,0:T(8,128)S(1)}, bf16[512,512]{1,0:T(8,128)(2,1)S(1)}, f32[168,1024]{1,0:T(8,128)S(1)}, bf16[168,1024]{1,0:T(8,128)(2,1)S(1)}, bf1...) custom-call(s32[4]{0:T(128)S(1)} %pad_add_fusion.meta, bf16[1024,128]{1,0:T(8,128)(2,1)S(1)} %get-tuple-element.203.refs_0_, ...), custom_call_target="tpu_custom_call" | custom-call | tf_op jit(solution)/shard_map/qkv_back/pallas_call | solution.py:587
  102.2 2.5 %collective-permute-start.19 = (bf16[168,1024]{1,0:T(8,128)(2,1)S(1)}, bf16[168,1024]{1,0:T(8,128)(2,1)S(1)}, u32[]{:S(2)}, u32[]{:S(2)}) collective-permute-start(bf16[168,1024]{1,0:T(8,128)(2,1)S(1)} %get-tuple-element.247), channel_id=1, source_target_pairs={{0,8},{4,12},{8,0},{12,4},{16,24},{20,28},{24,16},{28,20},{1,9},{5... | collective-permute-start | bytes 1032200 | tf_op jit(solution)/shard_map/ppermute | solution.py:541
  104.7 1.5 %collective-permute-start.21 = (bf16[168,1024]{1,0:T(8,128)(2,1)S(1)}, bf16[168,1024]{1,0:T(8,128)(2,1)S(1)}, u32[]{:S(2)}, u32[]{:S(2)}) collective-permute-start(bf16[168,1024]{1,0:T(8,128)(2,1)S(1)} %get-tuple-element.249), channel_id=1, source_target_pairs={{0,24},{4,28},{8,16},{12,20},{16,8},{20,12},{24,0},{28,4},{1,25},{... | collective-permute-start | bytes 1032200 | tf_op jit(solution)/shard_map/ppermute | solution.py:541
  106.3 2.3 %collective-permute-start.24 = (bf16[264,512]{1,0:T(8,128)(2,1)S(1)}, bf16[264,512]{1,0:T(8,128)(2,1)S(1)}, u32[]{:S(2)}, u32[]{:S(2)}) collective-permute-start(bf16[264,512]{1,0:T(8,128)(2,1)S(1)} %add_convert_fusion.2), channel_id=1, source_target_pairs={{0,2},{1,3},{2,0},{3,1},{4,6},{5,7},{6,4},{7,5},{8,10},{9,11},{10,... | collective-permute-start | bytes 811016 | tf_op jit(solution)/shard_map/ppermute | solution.py:551
  108.6 1.4 norm_one.1
  110.1 0.7 collective-permute-start.26
  110.7 2.9 %collective-permute-done.19.refs_0_ = bf16[168,1024]{1,0:T(8,128)(2,1)S(1)} collective-permute-done((bf16[168,1024]{1,0:T(8,128)(2,1)S(1)}, bf16[168,1024]{1,0:T(8,128)(2,1)S(1)}, u32[]{:S(2)}, u32[]{:S(2)}) %collective-permute-start.19) | collective-permute-done | bytes 344096 | tf_op jit(solution)/shard_map/ppermute | solution.py:541
  113.6 8.6 %collective-permute-done.20.refs_1_ = bf16[168,1024]{1,0:T(8,128)(2,1)S(1)} collective-permute-done((bf16[168,1024]{1,0:T(8,128)(2,1)S(1)}, bf16[168,1024]{1,0:T(8,128)(2,1)S(1)}, u32[]{:S(2)}, u32[]{:S(2)}) %collective-permute-start.20) | collective-permute-done | bytes 344096 | tf_op jit(solution)/shard_map/ppermute | solution.py:541
  122.2 0.7 late_chips.1
  122.9 2.1 %collective-permute-start.22 = (bf16[168,512]{1,0:T(8,128)(2,1)S(1)}, bf16[168,512]{1,0:T(8,128)(2,1)S(1)}, u32[]{:S(2)}, u32[]{:S(2)}) collective-permute-start(bf16[168,512]{1,0:T(8,128)(2,1)S(1)} %get-tuple-element.251), channel_id=1, source_target_pairs={{0,1},{1,0},{2,3},{3,2},{4,5},{5,4},{6,7},{7,6},{8,9},{9,8},{10,11... | collective-permute-start | bytes 516104 | tf_op jit(solution)/shard_map/ppermute | solution.py:551
  125.2 5.1 %collective-permute-done.22 = bf16[168,512]{1,0:T(8,128)(2,1)S(1)} collective-permute-done((bf16[168,512]{1,0:T(8,128)(2,1)S(1)}, bf16[168,512]{1,0:T(8,128)(2,1)S(1)}, u32[]{:S(2)}, u32[]{:S(2)}) %collective-permute-start.22) | collective-permute-done | bytes 172064 | tf_op jit(solution)/shard_map/ppermute | solution.py:551
  130.3 2.0 %collective-permute-start.27 = (bf16[168,512]{1,0:T(8,128)(2,1)S(1)}, bf16[168,512]{1,0:T(8,128)(2,1)S(1)}, u32[]{:S(2)}, u32[]{:S(2)}) collective-permute-start(bf16[168,512]{1,0:T(8,128)(2,1)S(1)} %add_convert_fusion.4), channel_id=1, source_target_pairs={{0,2},{1,3},{2,0},{3,1},{4,6},{5,7},{6,4},{7,5},{8,10},{9,11},{10,... | collective-permute-start | bytes 516104 | tf_op jit(solution)/shard_map/ppermute | solution.py:551
  132.4 1.2 collective-permute-start.31
  133.6 8.8 %collective-permute-done.27 = bf16[168,512]{1,0:T(8,128)(2,1)S(1)} collective-permute-done((bf16[168,512]{1,0:T(8,128)(2,1)S(1)}, bf16[168,512]{1,0:T(8,128)(2,1)S(1)}, u32[]{:S(2)}, u32[]{:S(2)}) %collective-permute-start.27) | collective-permute-done | bytes 172064 | tf_op jit(solution)/shard_map/ppermute | solution.py:551
  142.6 1.2 collective-permute-done.28
  144.0 1.4 collective-permute-done.31.other
  145.5 1.8 %place.1 = (bf16[2,256,512]{2,1,0:T(8,128)(2,1)}, f32[2,256,512]{2,1,0:T(8,128)}) custom-call(s32[4]{0:T(128)S(1)} %pad_add_fusion.meta, bf16[256,512]{1,0:T(8,128)(2,1)S(1)} %collective-permute-done.14.y0, bf16[256,512]{1,0:T(8,128)(2,1)S(1)} %collective-permute-done.15.y1, bf16[256,512]{1,0:T(8,128)(2,1)S(1)} %collective-permute-done.26.x0, ...), custom_call_target="tpu_custom_call" | custom-call | tf_op jit(solution)/shard_map/place/pallas_call | solution.py:587
  147.3 1.6 %early_out.1 = (f32[64,2048]{1,0:T(8,128)}, f32[256,512]{1,0:T(8,128)}, f32[1,64]{1,0:T(1,128)}, f32[1,64]{1,0:T(1,128)}, f32[1,64]{1,0:T(1,128)}, /*index=5*/f32[1,256]{1,0:T(1,128)}) custom-call(s32[4]{0:T(128)S(1)} %pad_add_fusion.meta, bf16[264,512]{1,0:T(8,128)(2,1)S(1)} %add_convert_fusion.1.mine, bf16[264,512]{1,0:T(8,128)(2,1)S(1)} %collective-permute-done.31.other, ...), custom_call_target="tpu_custom_call" | custom-call | tf_op jit(solution)/shard_map/early_out/pallas_call | solution.py:587
  148.9 1.6 %collective-permute-done.29.other = bf16[176,512]{1,0:T(8,128)(2,1)S(1)} collective-permute-done((bf16[176,512]{1,0:T(8,128)(2,1)S(1)}, bf16[176,512]{1,0:T(8,128)(2,1)S(1)}, u32[]{:S(2)}, u32[]{:S(2)}) %collective-permute-start.29) | collective-permute-done | bytes 180256 | tf_op jit(solution)/shard_map/ppermute | solution.py:551
  150.5 1.5 late_out.1
  (73 shorter events, 4.8 us)
Async XLA Ops:
  0.7 3.9 %copy-start.1 = (bf16[2,256,512]{2,1,0:T(8,128)(2,1)S(1)}, bf16[2,256,512]{2,1,0:T(8,128)(2,1)}, u32[]{:S(2)}) copy-start(bf16[2,256,512]{2,1,0:T(8,128)(2,1)} %param.31) | copy-start | bytes 1572868
  2.9 8.1 %collective-permute-start = (bf16[168,1024]{1,0:T(8,128)(2,1)S(1)}, bf16[168,1024]{1,0:T(8,128)(2,1)S(1)}, u32[]{:S(2)}, u32[]{:S(2)}) collective-permute-start(bf16[168,1024]{1,0:T(8,128)(2,1)S(1)} %get-tuple-element.152), channel_id=1, source_target_pairs={{0,4},{4,0},{8,12},{12,8},{16,20},{20,16},{24,28},{28,24},{1,5},{5... | collective-permute-start | bytes 1032200 | tf_op jit(solution)/shard_map/ppermute | solution.py:536
  5.7 23.9 %collective-permute-start.4 = (bf16[256,1024]{1,0:T(8,128)(2,1)}, bf16[256,1024]{1,0:T(8,128)(2,1)S(1)}, u32[]{:S(2)}, u32[]{:S(2)}) collective-permute-start(bf16[256,1024]{1,0:T(8,128)(2,1)} %get-tuple-element.288), channel_id=1, source_target_pairs={{0,0},{1,4},{2,1},{3,5},{4,2},{5,6},{6,3},{7,7},{8,8},{9,12},{10,9... | collective-permute-start | bytes 1572872 | tf_op jit(solution)/shard_map/ppermute | solution.py:565
  7.4 28.5 %collective-permute-start.5 = (bf16[256,1024]{1,0:T(8,128)(2,1)}, bf16[256,1024]{1,0:T(8,128)(2,1)S(1)}, u32[]{:S(2)}, u32[]{:S(2)}) collective-permute-start(bf16[256,1024]{1,0:T(8,128)(2,1)} %get-tuple-element.287), channel_id=1, source_target_pairs={{0,1},{1,5},{2,0},{3,4},{4,3},{5,7},{6,2},{7,6},{8,9},{9,13},{10,8... | collective-permute-start | bytes 1572872 | tf_op jit(solution)/shard_map/ppermute | solution.py:565
  10.9 4.1 %copy-start.2 = (s32[2]{0:T(128)S(1)}, s32[2]{0:T(128)}, u32[]{:S(2)}) copy-start(s32[2]{0:T(128)} %lengths_ref.1) | copy-start | bytes 28
  11.3 27.2 %copy-start = (bf16[144,1024]{1,0:T(8,128)(2,1)}, bf16[144,1024]{1,0:T(8,128)(2,1)S(1)}, u32[]{:S(2)}) copy-start(bf16[144,1024]{1,0:T(8,128)(2,1)S(1)} %pad_maximum_fusion.2.refs_0_) | copy-start | bytes 884740
  11.4 8.4 %collective-permute-start.1 = (bf16[144,1024]{1,0:T(8,128)(2,1)S(1)}, bf16[144,1024]{1,0:T(8,128)(2,1)}, u32[]{:S(2)}, u32[]{:S(2)}) collective-permute-start(bf16[144,1024]{1,0:T(8,128)(2,1)S(1)} %pad_maximum_fusion.2.refs_0_), channel_id=1, source_target_pairs={{0,8},{4,12},{8,0},{12,4},{16,24},{20,28},{24,16},{28,20},{1,9},{5... | collective-permute-start | bytes 884744 | tf_op jit(solution)/shard_map/ppermute | solution.py:541
  13.4 14.5 %collective-permute-start.2 = (bf16[144,1024]{1,0:T(8,128)(2,1)S(1)}, bf16[144,1024]{1,0:T(8,128)(2,1)}, u32[]{:S(2)}, u32[]{:S(2)}) collective-permute-start(bf16[144,1024]{1,0:T(8,128)(2,1)S(1)} %pad_maximum_fusion.2.refs_0_), channel_id=1, source_target_pairs={{0,16},{4,20},{8,24},{12,28},{16,0},{20,4},{24,8},{28,12},{1,17},{... | collective-permute-start | bytes 884744 | tf_op jit(solution)/shard_map/ppermute | solution.py:541
  15.0 13.3 %collective-permute-start.3 = (bf16[144,1024]{1,0:T(8,128)(2,1)S(1)}, bf16[144,1024]{1,0:T(8,128)(2,1)}, u32[]{:S(2)}, u32[]{:S(2)}) collective-permute-start(bf16[144,1024]{1,0:T(8,128)(2,1)S(1)} %pad_maximum_fusion.2.refs_0_), channel_id=1, source_target_pairs={{0,24},{4,28},{8,16},{12,20},{16,8},{20,12},{24,0},{28,4},{1,25},{... | collective-permute-start | bytes 884744 | tf_op jit(solution)/shard_map/ppermute | solution.py:541
  28.2 15.1 %collective-permute-start.8 = (bf16[320,1024]{1,0:T(8,128)(2,1)S(1)}, bf16[320,1024]{1,0:T(8,128)(2,1)S(1)}, u32[]{:S(2)}, u32[]{:S(2)}) collective-permute-start(bf16[320,1024]{1,0:T(8,128)(2,1)S(1)} %pad_maximum_fusion.1.refs_0_), channel_id=1, source_target_pairs={{0,8},{4,20},{8,0},{12,28},{16,24},{20,4},{24,16},{28,12},{1,9},{5... | collective-permute-start | bytes 1966088 | tf_op jit(solution)/shard_map/ppermute | solution.py:546
  35.9 2.0 %collective-permute-start.6 = (bf16[256,1024]{1,0:T(8,128)(2,1)S(1)}, bf16[256,1024]{1,0:T(8,128)(2,1)S(1)}, u32[]{:S(2)}, u32[]{:S(2)}) collective-permute-start(bf16[256,1024]{1,0:T(8,128)(2,1)S(1)} %collective-permute-done.4.refs_4_), channel_id=1, source_target_pairs={{0,4},{4,0},{8,12},{12,8},{16,20},{20,16},{24,28},{28,24},{1,5},{5... | collective-permute-start | bytes 1572872 | tf_op jit(solution)/shard_map/ppermute | solution.py:536
  35.9 2.7 %collective-permute-start.7 = (bf16[256,1024]{1,0:T(8,128)(2,1)S(1)}, bf16[256,1024]{1,0:T(8,128)(2,1)S(1)}, u32[]{:S(2)}, u32[]{:S(2)}) collective-permute-start(bf16[256,1024]{1,0:T(8,128)(2,1)S(1)} %collective-permute-done.5.refs_5_), channel_id=1, source_target_pairs={{0,4},{4,0},{8,12},{12,8},{16,20},{20,16},{24,28},{28,24},{1,5},{5... | collective-permute-start | bytes 1572872 | tf_op jit(solution)/shard_map/ppermute | solution.py:536
  36.4 19.8 %collective-permute-start.9 = (bf16[320,1024]{1,0:T(8,128)(2,1)S(1)}, bf16[320,1024]{1,0:T(8,128)(2,1)S(1)}, u32[]{:S(2)}, u32[]{:S(2)}) collective-permute-start(bf16[320,1024]{1,0:T(8,128)(2,1)S(1)} %pad_maximum_fusion.1.refs_0_), channel_id=1, source_target_pairs={{0,16},{4,12},{8,24},{12,4},{16,0},{20,28},{24,8},{28,20},{1,17},{... | collective-permute-start | bytes 1966088 | tf_op jit(solution)/shard_map/ppermute | solution.py:546
  43.3 12.9 %collective-permute-start.10 = (bf16[320,1024]{1,0:T(8,128)(2,1)S(1)}, bf16[320,1024]{1,0:T(8,128)(2,1)S(1)}, u32[]{:S(2)}, u32[]{:S(2)}) collective-permute-start(bf16[320,1024]{1,0:T(8,128)(2,1)S(1)} %collective-permute-done.8.refs_1_), channel_id=1, source_target_pairs={{0,16},{4,12},{8,24},{12,4},{16,0},{20,28},{24,8},{28,20},{1,17},{... | collective-permute-start | bytes 1966088 | tf_op jit(solution)/shard_map/ppermute | solution.py:546
  56.2 2.0 %collective-permute-start.11 = (bf16[1024,256]{1,0:T(8,128)(2,1)S(1)}, bf16[1024,256]{1,0:T(8,128)(2,1)S(1)}, u32[]{:S(2)}, u32[]{:S(2)}) collective-permute-start(bf16[1024,256]{1,0:T(8,128)(2,1)S(1)} %get-tuple-element.182.refs_9_.o_ref), channel_id=1, source_target_pairs={{0,4},{4,0},{8,12},{12,8},{16,20},{20,16},{24,28},{28,24},{1,5},{5... | collective-permute-start | bytes 1572872 | tf_op jit(solution)/shard_map/ppermute | solution.py:536
  69.4 4.1 %collective-permute-start.12 = (bf16[1024,512]{1,0:T(8,128)(2,1)S(1)}, bf16[1024,512]{1,0:T(8,128)(2,1)S(1)}, u32[]{:S(2)}, u32[]{:S(2)}) collective-permute-start(bf16[1024,512]{1,0:T(8,128)(2,1)S(1)} %get-tuple-element.187.dh_ref), channel_id=1, source_target_pairs={{0,4},{4,0},{8,12},{12,8},{16,20},{20,16},{24,28},{28,24},{1,5},{5... | collective-permute-start | bytes 3145736 | tf_op jit(solution)/shard_map/ppermute | solution.py:536
  69.6 3.9 %collective-permute-start.13 = (bf16[512,512]{1,0:T(8,128)(2,1)S(1)}, bf16[512,512]{1,0:T(8,128)(2,1)S(1)}, u32[]{:S(2)}, u32[]{:S(2)}) collective-permute-start(bf16[512,512]{1,0:T(8,128)(2,1)S(1)} %get-tuple-element.190), channel_id=1, source_target_pairs={{0,4},{4,0},{8,12},{12,8},{16,20},{20,16},{24,28},{28,24},{1,5},{5... | collective-permute-start | bytes 1572872 | tf_op jit(solution)/shard_map/ppermute | solution.py:536
  70.0 23.0 %collective-permute-start.16 = (bf16[264,1024]{1,0:T(8,128)(2,1)S(1)}, bf16[264,1024]{1,0:T(8,128)(2,1)S(1)}, u32[]{:S(2)}, u32[]{:S(2)}) collective-permute-start(bf16[264,1024]{1,0:T(8,128)(2,1)S(1)} %get-tuple-element.219), channel_id=1, source_target_pairs={{0,8},{4,12},{8,0},{12,4},{16,24},{20,28},{24,16},{28,20},{1,9},{5... | collective-permute-start | bytes 1622024 | tf_op jit(solution)/shard_map/ppermute | solution.py:541
  71.5 25.6 %collective-permute-start.17 = (bf16[264,1024]{1,0:T(8,128)(2,1)S(1)}, bf16[264,1024]{1,0:T(8,128)(2,1)S(1)}, u32[]{:S(2)}, u32[]{:S(2)}) collective-permute-start(bf16[264,1024]{1,0:T(8,128)(2,1)S(1)} %get-tuple-element.220), channel_id=1, source_target_pairs={{0,16},{4,20},{8,24},{12,28},{16,0},{20,4},{24,8},{28,12},{1,17},{... | collective-permute-start | bytes 1622024 | tf_op jit(solution)/shard_map/ppermute | solution.py:541
  72.0 25.1 %collective-permute-start.18 = (bf16[264,1024]{1,0:T(8,128)(2,1)S(1)}, bf16[264,1024]{1,0:T(8,128)(2,1)S(1)}, u32[]{:S(2)}, u32[]{:S(2)}) collective-permute-start(bf16[264,1024]{1,0:T(8,128)(2,1)S(1)} %get-tuple-element.221), channel_id=1, source_target_pairs={{0,24},{4,28},{8,16},{12,20},{16,8},{20,12},{24,0},{28,4},{1,25},{... | collective-permute-start | bytes 1622024 | tf_op jit(solution)/shard_map/ppermute | solution.py:541
  76.9 20.2 %collective-permute-start.14 = (bf16[256,512]{1,0:T(8,128)(2,1)S(1)}, bf16[256,512]{1,0:T(8,128)(2,1)S(1)}, u32[]{:S(2)}, u32[]{:S(2)}) collective-permute-start(bf16[256,512]{1,0:T(8,128)(2,1)S(1)} %get-tuple-element.217), channel_id=1, source_target_pairs={{0,0},{4,1},{1,2},{5,3},{2,4},{6,5},{3,6},{7,7},{8,8},{12,9},{9,10... | collective-permute-start | bytes 786440 | tf_op jit(solution)/shard_map/ppermute | solution.py:1123
  77.6 19.5 %collective-permute-start.15 = (bf16[256,512]{1,0:T(8,128)(2,1)S(1)}, bf16[256,512]{1,0:T(8,128)(2,1)S(1)}, u32[]{:S(2)}, u32[]{:S(2)}) collective-permute-start(bf16[256,512]{1,0:T(8,128)(2,1)S(1)} %get-tuple-element.218), channel_id=1, source_target_pairs={{1,0},{5,1},{0,2},{4,3},{3,4},{7,5},{2,6},{6,7},{9,8},{13,9},{8,10... | collective-permute-start | bytes 786440 | tf_op jit(solution)/shard_map/ppermute | solution.py:1123
  97.9 8.3 %collective-permute-start.23 = (bf16[264,512]{1,0:T(8,128)(2,1)S(1)}, bf16[264,512]{1,0:T(8,128)(2,1)S(1)}, u32[]{:S(2)}, u32[]{:S(2)}) collective-permute-start(bf16[264,512]{1,0:T(8,128)(2,1)S(1)} %get-tuple-element.253), channel_id=1, source_target_pairs={{0,1},{1,0},{2,3},{3,2},{4,5},{5,4},{6,7},{7,6},{8,9},{9,8},{10,11... | collective-permute-start | bytes 811016 | tf_op jit(solution)/shard_map/ppermute | solution.py:551
  102.1 6.5 %collective-permute-start.25 = (bf16[512,512]{1,0:T(8,128)(2,1)S(1)}, bf16[512,512]{1,0:T(8,128)(2,1)S(1)}, u32[]{:S(2)}, u32[]{:S(2)}) collective-permute-start(bf16[512,512]{1,0:T(8,128)(2,1)S(1)} %get-tuple-element.255), channel_id=1, source_target_pairs={{0,4},{4,0},{8,12},{12,8},{16,20},{20,16},{24,28},{28,24},{1,5},{5... | collective-permute-start | bytes 1572872 | tf_op jit(solution)/shard_map/ppermute | solution.py:536
  102.2 11.4 %collective-permute-start.19 = (bf16[168,1024]{1,0:T(8,128)(2,1)S(1)}, bf16[168,1024]{1,0:T(8,128)(2,1)S(1)}, u32[]{:S(2)}, u32[]{:S(2)}) collective-permute-start(bf16[168,1024]{1,0:T(8,128)(2,1)S(1)} %get-tuple-element.247), channel_id=1, source_target_pairs={{0,8},{4,12},{8,0},{12,4},{16,24},{20,28},{24,16},{28,20},{1,9},{5... | collective-permute-start | bytes 1032200 | tf_op jit(solution)/shard_map/ppermute | solution.py:541
  104.7 17.5 %collective-permute-start.20 = (bf16[168,1024]{1,0:T(8,128)(2,1)S(1)}, bf16[168,1024]{1,0:T(8,128)(2,1)S(1)}, u32[]{:S(2)}, u32[]{:S(2)}) collective-permute-start(bf16[168,1024]{1,0:T(8,128)(2,1)S(1)} %get-tuple-element.248), channel_id=1, source_target_pairs={{0,16},{4,20},{8,24},{12,28},{16,0},{20,4},{24,8},{28,12},{1,17},{... | collective-permute-start | bytes 1032200 | tf_op jit(solution)/shard_map/ppermute | solution.py:541
  104.7 17.5 %collective-permute-start.21 = (bf16[168,1024]{1,0:T(8,128)(2,1)S(1)}, bf16[168,1024]{1,0:T(8,128)(2,1)S(1)}, u32[]{:S(2)}, u32[]{:S(2)}) collective-permute-start(bf16[168,1024]{1,0:T(8,128)(2,1)S(1)} %get-tuple-element.249), channel_id=1, source_target_pairs={{0,24},{4,28},{8,16},{12,20},{16,8},{20,12},{24,0},{28,4},{1,25},{... | collective-permute-start | bytes 1032200 | tf_op jit(solution)/shard_map/ppermute | solution.py:541
  106.3 24.0 %collective-permute-start.24 = (bf16[264,512]{1,0:T(8,128)(2,1)S(1)}, bf16[264,512]{1,0:T(8,128)(2,1)S(1)}, u32[]{:S(2)}, u32[]{:S(2)}) collective-permute-start(bf16[264,512]{1,0:T(8,128)(2,1)S(1)} %add_convert_fusion.2), channel_id=1, source_target_pairs={{0,2},{1,3},{2,0},{3,1},{4,6},{5,7},{6,4},{7,5},{8,10},{9,11},{10,... | collective-permute-start | bytes 811016 | tf_op jit(solution)/shard_map/ppermute | solution.py:551
  110.1 20.2 %collective-permute-start.26 = (bf16[256,512]{1,0:T(8,128)(2,1)S(1)}, bf16[256,512]{1,0:T(8,128)(2,1)S(1)}, u32[]{:S(2)}, u32[]{:S(2)}) collective-permute-start(bf16[256,512]{1,0:T(8,128)(2,1)S(1)} %get-tuple-element.257), channel_id=1, source_target_pairs={{0,0},{4,1},{1,2},{5,3},{2,4},{6,5},{3,6},{7,7},{8,8},{12,9},{9,10... | collective-permute-start | bytes 786440 | tf_op jit(solution)/shard_map/ppermute | solution.py:1123
  122.9 7.4 %collective-permute-start.22 = (bf16[168,512]{1,0:T(8,128)(2,1)S(1)}, bf16[168,512]{1,0:T(8,128)(2,1)S(1)}, u32[]{:S(2)}, u32[]{:S(2)}) collective-permute-start(bf16[168,512]{1,0:T(8,128)(2,1)S(1)} %get-tuple-element.251), channel_id=1, source_target_pairs={{0,1},{1,0},{2,3},{3,2},{4,5},{5,4},{6,7},{7,6},{8,9},{9,8},{10,11... | collective-permute-start | bytes 516104 | tf_op jit(solution)/shard_map/ppermute | solution.py:551
  125.0 19.0 %collective-permute-start.30 = (bf16[256,512]{1,0:T(8,128)(2,1)S(1)}, bf16[256,512]{1,0:T(8,128)(2,1)S(1)}, u32[]{:S(2)}, u32[]{:S(2)}) collective-permute-start(bf16[256,512]{1,0:T(8,128)(2,1)S(1)} %get-tuple-element.262), channel_id=1, source_target_pairs={{1,0},{5,1},{0,2},{4,3},{3,4},{7,5},{2,6},{6,7},{9,8},{13,9},{8,10... | collective-permute-start | bytes 786440 | tf_op jit(solution)/shard_map/ppermute | solution.py:1123
  130.3 12.1 %collective-permute-start.27 = (bf16[168,512]{1,0:T(8,128)(2,1)S(1)}, bf16[168,512]{1,0:T(8,128)(2,1)S(1)}, u32[]{:S(2)}, u32[]{:S(2)}) collective-permute-start(bf16[168,512]{1,0:T(8,128)(2,1)S(1)} %add_convert_fusion.4), channel_id=1, source_target_pairs={{0,2},{1,3},{2,0},{3,1},{4,6},{5,7},{6,4},{7,5},{8,10},{9,11},{10,... | collective-permute-start | bytes 516104 | tf_op jit(solution)/shard_map/ppermute | solution.py:551
  132.4 13.0 %collective-permute-start.31 = (bf16[264,512]{1,0:T(8,128)(2,1)S(1)}, bf16[264,512]{1,0:T(8,128)(2,1)S(1)}, u32[]{:S(2)}, u32[]{:S(2)}) collective-permute-start(bf16[264,512]{1,0:T(8,128)(2,1)S(1)} %add_convert_fusion.1.mine), channel_id=1, source_target_pairs={{0,1},{1,0},{2,3},{3,2},{4,5},{5,4},{6,7},{7,6},{8,9},{9,8},{10,11... | collective-permute-start | bytes 811016 | tf_op jit(solution)/shard_map/ppermute | solution.py:551
  142.5 1.3 collective-permute-start.28
  143.9 6.7 %collective-permute-start.29 = (bf16[176,512]{1,0:T(8,128)(2,1)S(1)}, bf16[176,512]{1,0:T(8,128)(2,1)S(1)}, u32[]{:S(2)}, u32[]{:S(2)}) collective-permute-start(bf16[176,512]{1,0:T(8,128)(2,1)S(1)} %pad_maximum_fusion.3.mine), channel_id=1, source_target_pairs={{0,1},{1,0},{2,3},{3,2},{4,5},{5,4},{6,7},{7,6},{8,9},{9,8},{10,11... | collective-permute-start | bytes 540680 | tf_op jit(solution)/shard_map/ppermute | solution.py:551
  145.4 1.9 %collective-permute-start.32 = (bf16[2,72,512]{2,1,0:T(8,128)(2,1)S(1)}, bf16[2,72,512]{2,1,0:T(8,128)(2,1)S(1)}, u32[]{:S(2)}, u32[]{:S(2)}) collective-permute-start(bf16[2,72,512]{2,1,0:T(8,128)(2,1)S(1)} %pad_maximum_fusion.4), channel_id=1, source_target_pairs={{0,4},{4,0},{8,12},{12,8},{16,20},{20,16},{24,28},{28,24},{1,5},{5... | collective-permute-start | bytes 442376 | tf_op jit(solution)/shard_map/ppermute | solution.py:536

commit v6 on v5

--- a/solution.py
+++ b/solution.py
@@ -66,7 +66,8 @@
                 tri,
                 block,
             )
-            s = s + bias[:, :span]
+            if span > full // 2:
+                s = s + bias[:, :span]
             top = jnp.max(s, axis=1, keepdims=True)
             e = jnp.exp(s - top)
             total = jnp.sum(e, axis=1, keepdims=True)
@@ -118,8 +119,7 @@
     for first in range(0, full, block):
         span = first + block
 
-        @pl.when(first < length)
-        def _():
+        def one_block(first=first, span=span):
             q = q_ref[first:span, :].astype(f32)
             qu = (q + bu_ref[...]).astype(bf).astype(f32) * 0.125
             qv = (q + bv_ref[...]).astype(bf).astype(f32) * 0.125
@@ -148,6 +148,11 @@
             gu_ref[...] += jnp.sum(dqu, axis=0, keepdims=True)
             gv_ref[...] += jnp.sum(dqv, axis=0, keepdims=True)
             dq_ref[first:span, :] = (dqu + dot(flip, dqv.astype(bf), NN)).astype(bf)
+
+        if first < full // 2:
+            one_block()
+        else:
+            pl.when(first < length)(one_block)
 
     dk_ref[...] = jnp.transpose(dk_t[...]).astype(bf)
     dv_ref[...] = jnp.transpose(dv_t[...]).astype(bf)
@@ -675,14 +680,13 @@
     return centered * inv_std, inv_std
 
 
-def project_body(_, *refs):
-    packs, own_x, other_x = refs[0:4], refs[4:6], refs[6:8]
-    table_ref, qkv_ref, h_ref, x_ref, rel_ref, w_ref, vec_ref, up_ref, *bias_refs = refs[8:18]
-    step, (core, chip, rank) = pl.program_id(0), own_place()
+def weights_body(_, *refs):
+    packs, table_ref = refs[0:4], refs[4]
+    rel_ref, w_ref, vec_ref, up_ref, *bias_refs = refs[5:11]
+    step, (core, chip, _) = pl.program_id(0), own_place()
     width = w_ref.shape[0]
     shard = width // 8
-    span = qkv_ref.shape[1]
-    cols = span // 3
+    span = w_ref.shape[1] - rel_ref.shape[1]
 
     @pl.when(step == 0)
     def _():
@@ -710,6 +714,14 @@
                 piece = slice(source * shard, (source + 1) * shard)
                 bias_refs[row][:, at] = jnp.concatenate([low[:, piece], high[:, piece]], axis=1)
 
+    rel_ref[...] = dot(table_ref[...], w_ref[:, span:], NN).astype(bf)
+
+
+def project_body(_, *refs):
+    own_x, other_x = refs[0:2], refs[2:4]
+    w_ref, vec_ref, qkv_ref, h_ref, x_ref = refs[4:9]
+    step, (core, _, rank) = pl.program_id(0), own_place()
+
     def copy(ref):
         x_ref[...] = ref[...]
 
@@ -717,8 +729,7 @@
     x_hat, _ = norm_rows(x_ref[...].astype(f32))
     h = (x_hat * vec_ref[0:1, :] + vec_ref[1:2, :]).astype(bf)
     h_ref[...] = h
-    qkv_ref[...] = dot(h, w_ref[:, :span], NN).astype(bf)
-    rel_ref[...] = dot(table_ref[...], w_ref[:, span:], NN).astype(bf)
+    qkv_ref[...] = dot(h, w_ref[:, : qkv_ref.shape[1]], NN).astype(bf)
 
 
 def feed_body(meta, *refs):
@@ -1048,27 +1059,34 @@
     table = table.astype(bf).reshape(full, width)
 
     feed_pack, meta, length_arr, table, *attn_packs = together(feed_pack, meta, length_arr, table, *attn_packs)
-    rest = list(together(*x_own, *attn_packs))
-    x_own, attn_packs = rest[:2], rest[2:]
+    by_step = lambda width: pl.BlockSpec((block, width), lambda i, _: (i, 0))
+    rel, w_own, vecs, up_b, own_u, own_v = kernel_call(
+        weights_body,
+        "weights",
+        none,
+        [pltpu.with_memory_space_constraint(v, pltpu.HBM) for v in attn_packs] + [table],
+        [((full, cols), bf), ((width, 4 * cols), bf), ((8, width), f32), ((1, mine_ff), f32)]
+        + [((1, cols), f32), ((1, cols), f32)],
+        grid=(4,),
+        in_specs=[whole(2 * attn_rows, 4 * cols)] * 4 + [by_step(width)],
+        out_specs=[by_step(cols), whole(width, 4 * cols), whole(8, width), whole(1, mine_ff)]
+        + [whole(1, cols), whole(1, cols)],
+    )
+    w_own, vecs, *x_own = together(w_own, vecs, *x_own)
     x_other = [swap_core(x) for x in x_own]
     feed_first = swap_axis(feed_pack, 0)
     feed_second = swap_axis(feed_pack, 1)
 
     side = lambda at: pl.BlockSpec((block, width), lambda i, _: (0, at))
-    by_step = lambda width: pl.BlockSpec((block, width), lambda i, _: (i, 0))
-    qkv, h1, x_slot, rel, w_own, vecs, up_b, own_u, own_v = kernel_call(
+    qkv, h1, x_slot = kernel_call(
         project_body,
         "project",
         none,
-        [pltpu.with_memory_space_constraint(v, pltpu.HBM) for v in attn_packs] + x_own + x_other + [table],
-        [((full, 3 * cols), bf), ((full, width), bf), ((full, width), bf), ((full, cols), bf)]
-        + [((width, 4 * cols), bf), ((8, width), f32), ((1, mine_ff), f32), ((1, cols), f32), ((1, cols), f32)],
+        x_own + x_other + [w_own, vecs],
+        [((full, 3 * cols), bf), ((full, width), bf), ((full, width), bf)],
         grid=(4,),
-        in_specs=[whole(2 * attn_rows, 4 * cols)] * 4 + [side(0)] * 4 + [by_step(width)],
-        out_specs=[by_step(3 * cols), by_step(width), by_step(width), by_step(cols)]
-        + [whole(width, 4 * cols), whole(8, width), whole(1, mine_ff), whole(1, cols), whole(1, cols)],
-        flops=2 * full * width * 4 * cols,
-        vmem=32,
+        in_specs=[side(0)] * 4 + [whole(width, 4 * cols), whole(8, width)],
+        out_specs=[by_step(3 * cols), by_step(width), by_step(width)],
     )
     qkv, feed_first = together(qkv, feed_first)
     feed_third = swap_axis(feed_first, 1)

time: 152 us -> 152 us (level)
  waiting for transfers between devices: 53.7 us -> 51 us
    ppermute x2, waiting for transfers between devices: 6.23 us -> 3.3 us  [to_slots(): lax.ppermute(lax.dynamic_index_in_dim(values, turn ^ seq_rank >> 1, 0, ke...]
    ppermute x4, starting transfers between devices: 5.16 us -> 6.85 us  [slot_split_device(): lax.ppermute(out, ('fsdp', 'seq'), [(b, a) for a, b in slot_pairs(turn)])]
    pallas_call x11 -> x12, Pallas kernels: 33.6 us -> 34.9 us  [kernel_call(): pl.pallas_call(body, out_shape=[jax.ShapeDtypeStruct(shape, kind) for sha...]
where the time goes in v6:
time: 152 us; the launch traced here: 151 us
  Pallas kernels  57.2 us (38%)
  waiting for transfers between devices  51 us (34%)
  starting transfers between devices  36.4 us (24%)
  local copies, waits for them, and re-layouts  3.07 us (2%)
  between operations  2.39 us (2%)
    pallas_call x12, Pallas kernels, kernel_call(): pl.pallas_call(body, out_shape=[jax.ShapeDtypeStruct(shape, kind) for sha...  34.9 us
    ppermute x9, waiting for transfers between devices, swap_chip(): lax.ppermute(values, 'fsdp', [(i, i ^ 2 * mask) for i in range(size)])  26.3 us
    ppermute x6, waiting for transfers between devices, swap_seq(): return lax.ppermute(values, 'seq', [(i, i ^ mask) for i in range(size)])  17.6 us
    pallas_call x1, Pallas kernels, attn_fwd(): pl.pallas_call(functools.partial(attn_fwd_body, block=block), out_shape=(...  11.3 us
    pallas_call x2, Pallas kernels, attn_bwd(): pl.pallas_call(functools.partial(attn_bwd_body, block=block, heads=heads)...  11.1 us
    ppermute x9, starting transfers between devices, swap_chip(): lax.ppermute(values, 'fsdp', [(i, i ^ 2 * mask) for i in range(size)])  10.7 us
    ppermute x6, starting transfers between devices, swap_seq(): return lax.ppermute(values, 'seq', [(i, i ^ mask) for i in range(size)])  7.91 us
    ppermute x4, starting transfers between devices, slot_split_device(): lax.ppermute(out, ('fsdp', 'seq'), [(b, a) for a, b in slot_pairs(turn)])  6.85 us
  transfers between devices with their start and end apart: 33, of which 14 were waited for; matrix products, arithmetic and copies ran while one was open for 3% of the time, Pallas kernels for 27%

profile of v6, /device:TPU:0, one launch (start us, length us, event | category | flops | bytes accessed | tf_op | source)
XLA Modules:
  0.0 151.3 jit_solution(15480973126618302765)
XLA Ops:
  0.7 2.3 %pack.1 = (bf16[72,1024]{1,0:T(8,128)(2,1)S(1)}, bf16[224,1024]{1,0:T(8,128)(2,1)S(1)}, bf16[168,1024]{1,0:T(8,128)(2,1)S(1)}) custom-call(s32[2]{0:T(128)} %lengths_ref.1, bf16[64,1536]{1,0:T(8,128)(2,1)} %qkv_ref.1, bf16[64,512]{1,0:T(8,128)(2,1)} %rel_ref.1, bf16[64,2048]{1,0:T(8,128)(2,1)} %up_ref.1, bf16[64,512]{1,0:T(8,128)(2,1)} %out_ref.1, ...), custom_call_target="tpu_custom_call" | custom-call | tf_op jit(solution)/shard_map/pack/pallas_call | solution.py:592
  3.5 1.1 constant_dynamic-update-slice_fusion.1
  4.7 1.0 dynamic-slice_bitcast_fusion
  5.7 1.7 %collective-permute-start.4 = (bf16[256,1024]{1,0:T(8,128)(2,1)}, bf16[256,1024]{1,0:T(8,128)(2,1)S(1)}, u32[]{:S(2)}, u32[]{:S(2)}) collective-permute-start(bf16[256,1024]{1,0:T(8,128)(2,1)} %get-tuple-element.284), channel_id=1, source_target_pairs={{0,0},{1,4},{2,1},{3,5},{4,2},{5,6},{6,3},{7,7},{8,8},{9,12},{10,9... | collective-permute-start | bytes 1572872 | tf_op jit(solution)/shard_map/ppermute | solution.py:570
  7.4 2.9 %collective-permute-start.5 = (bf16[256,1024]{1,0:T(8,128)(2,1)}, bf16[256,1024]{1,0:T(8,128)(2,1)S(1)}, u32[]{:S(2)}, u32[]{:S(2)}) collective-permute-start(bf16[256,1024]{1,0:T(8,128)(2,1)} %get-tuple-element.283), channel_id=1, source_target_pairs={{0,1},{1,5},{2,0},{3,4},{4,3},{5,7},{6,2},{7,6},{8,9},{9,13},{10,8... | collective-permute-start | bytes 1572872 | tf_op jit(solution)/shard_map/ppermute | solution.py:570
  11.4 2.1 %collective-permute-start.1 = (bf16[144,1024]{1,0:T(8,128)(2,1)S(1)}, bf16[144,1024]{1,0:T(8,128)(2,1)}, u32[]{:S(2)}, u32[]{:S(2)}) collective-permute-start(bf16[144,1024]{1,0:T(8,128)(2,1)S(1)} %pad_maximum_fusion.2.refs_0_), channel_id=1, source_target_pairs={{0,8},{4,12},{8,0},{12,4},{16,24},{20,28},{24,16},{28,20},{1,9},{5... | collective-permute-start | bytes 884744 | tf_op jit(solution)/shard_map/ppermute | solution.py:546
  13.4 1.5 %collective-permute-start.2 = (bf16[144,1024]{1,0:T(8,128)(2,1)S(1)}, bf16[144,1024]{1,0:T(8,128)(2,1)}, u32[]{:S(2)}, u32[]{:S(2)}) collective-permute-start(bf16[144,1024]{1,0:T(8,128)(2,1)S(1)} %pad_maximum_fusion.2.refs_0_), channel_id=1, source_target_pairs={{0,16},{4,20},{8,24},{12,28},{16,0},{20,4},{24,8},{28,12},{1,17},{... | collective-permute-start | bytes 884744 | tf_op jit(solution)/shard_map/ppermute | solution.py:546
  17.0 2.7 %collective-permute-done.1.refs_1_ = bf16[144,1024]{1,0:T(8,128)(2,1)} collective-permute-done((bf16[144,1024]{1,0:T(8,128)(2,1)S(1)}, bf16[144,1024]{1,0:T(8,128)(2,1)}, u32[]{:S(2)}, u32[]{:S(2)}) %collective-permute-start.1) | collective-permute-done | bytes 294944 | tf_op jit(solution)/shard_map/ppermute | solution.py:546
  19.8 8.2 %collective-permute-done.2.refs_2_ = bf16[144,1024]{1,0:T(8,128)(2,1)} collective-permute-done((bf16[144,1024]{1,0:T(8,128)(2,1)S(1)}, bf16[144,1024]{1,0:T(8,128)(2,1)}, u32[]{:S(2)}, u32[]{:S(2)}) %collective-permute-start.2) | collective-permute-done | bytes 294944 | tf_op jit(solution)/shard_map/ppermute | solution.py:546
  28.2 1.4 collective-permute-start.8
  29.6 2.9 %weights.1 = (bf16[1024,256]{1,0:T(8,128)(2,1)S(1)}, bf16[512,1024]{1,0:T(8,128)(2,1)S(1)}, f32[8,512]{1,0:T(8,128)S(1)}, f32[1,1024]{1,0:T(1,128)S(1)}, f32[1,256]{1,0:T(1,128)S(1)}, /*index=5*/f32[1,256]{1,0:T(1,128)S(1)}) custom-call(s32[4]{0:T(128)S(1)} %broadcast_3__.2._, bf16[144,1024]{1,0:T(8,128)(2,1)} %copy-done, ...), custom_call_target="tpu_custom_call" | custom-call | tf_op jit(solution)/shard_map/weights/pallas_call | solution.py:592
  32.6 3.3 %collective-permute-done.5.refs_1_.refs_5_ = bf16[256,1024]{1,0:T(8,128)(2,1)S(1)} collective-permute-done((bf16[256,1024]{1,0:T(8,128)(2,1)}, bf16[256,1024]{1,0:T(8,128)(2,1)S(1)}, u32[]{:S(2)}, u32[]{:S(2)}) %collective-permute-start.5) | collective-permute-done | bytes 524320 | tf_op jit(solution)/shard_map/ppermute | solution.py:570
  36.4 1.5 %collective-permute-start.9 = (bf16[320,1024]{1,0:T(8,128)(2,1)S(1)}, bf16[320,1024]{1,0:T(8,128)(2,1)S(1)}, u32[]{:S(2)}, u32[]{:S(2)}) collective-permute-start(bf16[320,1024]{1,0:T(8,128)(2,1)S(1)} %pad_maximum_fusion.1.refs_0_), channel_id=1, source_target_pairs={{0,16},{4,12},{8,24},{12,4},{16,0},{20,28},{24,8},{28,20},{1,17},{... | collective-permute-start | bytes 1966088 | tf_op jit(solution)/shard_map/ppermute | solution.py:551
  38.5 3.2 %project.1 = (bf16[1024,768]{1,0:T(8,128)(2,1)S(1)}, bf16[1024,512]{1,0:T(8,128)(2,1)S(1)}, bf16[1024,512]{1,0:T(8,128)(2,1)S(1)}) custom-call(s32[4]{0:T(128)S(1)} %broadcast_3__.2._, bf16[256,1024]{1,0:T(8,128)(2,1)S(1)} %collective-permute-done.4.refs_0_.refs_4_, bf16[256,1024]{1,0:T(8,128)(2,1)S(1)} %collective-permute-done.5.refs_1_.refs_5_, ...), custom_call_target="tpu_custom_call" | custom-call | tf_op jit(solution)/shard_map/project/pallas_call | solution.py:592
  41.8 1.6 %collective-permute-start.10 = (bf16[320,1024]{1,0:T(8,128)(2,1)S(1)}, bf16[320,1024]{1,0:T(8,128)(2,1)S(1)}, u32[]{:S(2)}, u32[]{:S(2)}) collective-permute-start(bf16[320,1024]{1,0:T(8,128)(2,1)S(1)} %collective-permute-done.8.refs_1_), channel_id=1, source_target_pairs={{0,16},{4,12},{8,24},{12,4},{16,0},{20,28},{24,8},{28,20},{1,17},{... | collective-permute-start | bytes 1966088 | tf_op jit(solution)/shard_map/ppermute | solution.py:551
  43.3 11.3 %attn_fwd.1 = (bf16[1024,256]{1,0:T(8,128)(2,1)S(1)}, bf16[4,256,256]{2,1,0:T(8,128)(2,1)S(1)}, bf16[4,256,512]{2,1,0:T(8,128)(2,1)S(1)}, bf16[4,256,768]{2,1,0:T(8,128)(2,1)S(1)}, bf16[4,256,1024]{2,1,0:T(8,128)(2,1)S(1)}) custom-call(s32[1]{0:T(128)} %bitcast.15.len_ref, bf16[1024,768]{1,0:T(8,128)(2,1)S(1)} %get-tuple-element.172.q_ref.k_ref.v_ref, ...), custom_call_target="tpu_custom_call" | custom-call | tf_op jit(solution)/shard_map/attn_fwd/pallas_call | solution.py:86
  54.7 1.9 %collective-permute-done.11.refs_10_ = bf16[1024,256]{1,0:T(8,128)(2,1)S(1)} collective-permute-done((bf16[1024,256]{1,0:T(8,128)(2,1)S(1)}, bf16[1024,256]{1,0:T(8,128)(2,1)S(1)}, u32[]{:S(2)}, u32[]{:S(2)}) %collective-permute-start.11) | collective-permute-done | bytes 524320 | tf_op jit(solution)/shard_map/ppermute | solution.py:541
  56.6 11.2 %feed.1 = (bf16[1024,512]{1,0:T(8,128)(2,1)S(1)}, bf16[1024,512]{1,0:T(8,128)(2,1)S(1)}, f32[1024,1]{1,0:T(8,128)S(1)}, f32[512,512]{1,0:T(8,128)S(1)}, bf16[102...) custom-call(s32[4]{0:T(128)S(1)} %pad_add_fusion.meta, ...), custom_call_target="tpu_custom_call" | custom-call | tf_op jit(solution)/shard_map/feed/pallas_call | solution.py:592
  68.4 1.5 collective-permute-start.16
  69.9 0.8 collective-permute-start.17
  70.7 1.2 collective-permute-start.18
  71.9 3.4 %norm_two.1 = (bf16[256,512]{1,0:T(8,128)(2,1)S(1)}, bf16[256,512]{1,0:T(8,128)(2,1)S(1)}, f32[512,512]{1,0:T(8,128)S(1)}, bf16[1024,256]{1,0:T(8,128)(2,1)S(1)}, f32[256,512]{1,0:T(8,128)S(1)}) custom-call(s32[4]{0:T(128)S(1)} %pad_add_fusion.meta, bf16[1024,512]{1,0:T(8,128)(2,1)S(1)} %get-tuple-element.182.x_hat_ref, ...), custom_call_target="tpu_custom_call" | custom-call | tf_op jit(solution)/shard_map/norm_two/pallas_call | solution.py:592
  75.3 0.7 collective-permute-start.14
  76.0 3.5 %collective-permute-start.15 = (bf16[256,512]{1,0:T(8,128)(2,1)S(1)}, bf16[256,512]{1,0:T(8,128)(2,1)S(1)}, u32[]{:S(2)}, u32[]{:S(2)}) collective-permute-start(bf16[256,512]{1,0:T(8,128)(2,1)S(1)} %get-tuple-element.215), channel_id=1, source_target_pairs={{1,0},{5,1},{0,2},{4,3},{3,4},{7,5},{2,6},{6,7},{9,8},{13,9},{8,10... | collective-permute-start | bytes 786440 | tf_op jit(solution)/shard_map/ppermute | solution.py:1141
  79.5 5.4 %attn_bwd.2 = (bf16[1024,128]{1,0:T(8,128)(2,1)S(1)}, bf16[1024,128]{1,0:T(8,128)(2,1)S(1)}, bf16[1024,128]{1,0:T(8,128)(2,1)S(1)}, bf16[1024,128]{1,0:T(8,128)(...) custom-call(s32[1]{0:T(128)} %bitcast.15.len_ref, bf16[1024,768]{1,0:T(8,128)(2,1)S(1)} %get-tuple-element.172.q_ref.k_ref.v_ref, ...), custom_call_target="tpu_custom_call" | custom-call | tf_op jit(solution)/shard_map/attn_bwd/pallas_call | solution.py:169
  84.9 5.6 %attn_bwd.3 = (bf16[1024,128]{1,0:T(8,128)(2,1)S(1)}, bf16[1024,128]{1,0:T(8,128)(2,1)S(1)}, bf16[1024,128]{1,0:T(8,128)(2,1)S(1)}, bf16[1024,128]{1,0:T(8,128)(...) custom-call(s32[1]{0:T(128)} %bitcast.15.len_ref, bf16[1024,768]{1,0:T(8,128)(2,1)S(1)} %get-tuple-element.172.q_ref.k_ref.v_ref, ...), custom_call_target="tpu_custom_call" | custom-call | tf_op jit(solution)/shard_map/attn_bwd/pallas_call | solution.py:169
  90.6 4.9 %collective-permute-done.17.refs_1_ = bf16[264,1024]{1,0:T(8,128)(2,1)S(1)} collective-permute-done((bf16[264,1024]{1,0:T(8,128)(2,1)S(1)}, bf16[264,1024]{1,0:T(8,128)(2,1)S(1)}, u32[]{:S(2)}, u32[]{:S(2)}) %collective-permute-start.17) | collective-permute-done | bytes 540704 | tf_op jit(solution)/shard_map/ppermute | solution.py:546
  95.5 0.8 early_chips.1
  96.3 0.8 collective-permute-start.23
  97.1 4.1 %qkv_back.1 = (f32[512,512]{1,0:T(8,128)S(1)}, bf16[512,512]{1,0:T(8,128)(2,1)S(1)}, f32[168,1024]{1,0:T(8,128)S(1)}, bf16[168,1024]{1,0:T(8,128)(2,1)S(1)}, bf1...) custom-call(s32[4]{0:T(128)S(1)} %pad_add_fusion.meta, bf16[1024,128]{1,0:T(8,128)(2,1)S(1)} %get-tuple-element.200.refs_0_, ...), custom_call_target="tpu_custom_call" | custom-call | tf_op jit(solution)/shard_map/qkv_back/pallas_call | solution.py:592
  101.3 1.8 %collective-permute-start.19 = (bf16[168,1024]{1,0:T(8,128)(2,1)S(1)}, bf16[168,1024]{1,0:T(8,128)(2,1)S(1)}, u32[]{:S(2)}, u32[]{:S(2)}) collective-permute-start(bf16[168,1024]{1,0:T(8,128)(2,1)S(1)} %get-tuple-element.243), channel_id=1, source_target_pairs={{0,8},{4,12},{8,0},{12,4},{16,24},{20,28},{24,16},{28,20},{1,9},{5... | collective-permute-start | bytes 1032200 | tf_op jit(solution)/shard_map/ppermute | solution.py:546
  103.6 1.2 collective-permute-start.21
  104.9 3.4 %collective-permute-start.24 = (bf16[264,512]{1,0:T(8,128)(2,1)S(1)}, bf16[264,512]{1,0:T(8,128)(2,1)S(1)}, u32[]{:S(2)}, u32[]{:S(2)}) collective-permute-start(bf16[264,512]{1,0:T(8,128)(2,1)S(1)} %add_convert_fusion.2), channel_id=1, source_target_pairs={{0,2},{1,3},{2,0},{3,1},{4,6},{5,7},{6,4},{7,5},{8,10},{9,11},{10,... | collective-permute-start | bytes 811016 | tf_op jit(solution)/shard_map/ppermute | solution.py:556
  108.3 1.4 norm_one.1
  109.7 0.7 collective-permute-start.26
  110.4 1.8 %collective-permute-done.19.refs_0_ = bf16[168,1024]{1,0:T(8,128)(2,1)S(1)} collective-permute-done((bf16[168,1024]{1,0:T(8,128)(2,1)S(1)}, bf16[168,1024]{1,0:T(8,128)(2,1)S(1)}, u32[]{:S(2)}, u32[]{:S(2)}) %collective-permute-start.19) | collective-permute-done | bytes 344096 | tf_op jit(solution)/shard_map/ppermute | solution.py:546
  112.2 8.4 %collective-permute-done.20.refs_1_ = bf16[168,1024]{1,0:T(8,128)(2,1)S(1)} collective-permute-done((bf16[168,1024]{1,0:T(8,128)(2,1)S(1)}, bf16[168,1024]{1,0:T(8,128)(2,1)S(1)}, u32[]{:S(2)}, u32[]{:S(2)}) %collective-permute-start.20) | collective-permute-done | bytes 344096 | tf_op jit(solution)/shard_map/ppermute | solution.py:546
  120.6 0.7 late_chips.1
  121.6 2.0 %collective-permute-start.30 = (bf16[256,512]{1,0:T(8,128)(2,1)S(1)}, bf16[256,512]{1,0:T(8,128)(2,1)S(1)}, u32[]{:S(2)}, u32[]{:S(2)}) collective-permute-start(bf16[256,512]{1,0:T(8,128)(2,1)S(1)} %get-tuple-element.258), channel_id=1, source_target_pairs={{1,0},{5,1},{0,2},{4,3},{3,4},{7,5},{2,6},{6,7},{9,8},{13,9},{8,10... | collective-permute-start | bytes 786440 | tf_op jit(solution)/shard_map/ppermute | solution.py:1141
  123.5 4.8 %collective-permute-done.22 = bf16[168,512]{1,0:T(8,128)(2,1)S(1)} collective-permute-done((bf16[168,512]{1,0:T(8,128)(2,1)S(1)}, bf16[168,512]{1,0:T(8,128)(2,1)S(1)}, u32[]{:S(2)}, u32[]{:S(2)}) %collective-permute-start.22) | collective-permute-done | bytes 172064 | tf_op jit(solution)/shard_map/ppermute | solution.py:556
  128.3 2.3 %collective-permute-start.27 = (bf16[168,512]{1,0:T(8,128)(2,1)S(1)}, bf16[168,512]{1,0:T(8,128)(2,1)S(1)}, u32[]{:S(2)}, u32[]{:S(2)}) collective-permute-start(bf16[168,512]{1,0:T(8,128)(2,1)S(1)} %add_convert_fusion.4), channel_id=1, source_target_pairs={{0,2},{1,3},{2,0},{3,1},{4,6},{5,7},{6,4},{7,5},{8,10},{9,11},{10,... | collective-permute-start | bytes 516104 | tf_op jit(solution)/shard_map/ppermute | solution.py:556
  130.7 1.1 collective-permute-start.31
  131.8 9.8 %collective-permute-done.27 = bf16[168,512]{1,0:T(8,128)(2,1)S(1)} collective-permute-done((bf16[168,512]{1,0:T(8,128)(2,1)S(1)}, bf16[168,512]{1,0:T(8,128)(2,1)S(1)}, u32[]{:S(2)}, u32[]{:S(2)}) %collective-permute-start.27) | collective-permute-done | bytes 172064 | tf_op jit(solution)/shard_map/ppermute | solution.py:556
  141.8 1.2 collective-permute-done.28
  143.5 1.8 %place.1 = (bf16[2,256,512]{2,1,0:T(8,128)(2,1)}, f32[2,256,512]{2,1,0:T(8,128)}) custom-call(s32[4]{0:T(128)S(1)} %pad_add_fusion.meta, bf16[256,512]{1,0:T(8,128)(2,1)S(1)} %collective-permute-done.14.y0, bf16[256,512]{1,0:T(8,128)(2,1)S(1)} %collective-permute-done.15.y1, bf16[256,512]{1,0:T(8,128)(2,1)S(1)} %collective-permute-done.26.x0, ...), custom_call_target="tpu_custom_call" | custom-call | tf_op jit(solution)/shard_map/place/pallas_call | solution.py:592
  145.3 1.6 %early_out.1 = (f32[64,2048]{1,0:T(8,128)}, f32[256,512]{1,0:T(8,128)}, f32[1,64]{1,0:T(1,128)}, f32[1,64]{1,0:T(1,128)}, f32[1,64]{1,0:T(1,128)}, /*index=5*/f32[1,256]{1,0:T(1,128)}) custom-call(s32[4]{0:T(128)S(1)} %pad_add_fusion.meta, bf16[264,512]{1,0:T(8,128)(2,1)S(1)} %add_convert_fusion.1.mine, bf16[264,512]{1,0:T(8,128)(2,1)S(1)} %collective-permute-done.31.other, ...), custom_call_target="tpu_custom_call" | custom-call | tf_op jit(solution)/shard_map/early_out/pallas_call | solution.py:592
  146.9 2.8 %collective-permute-done.29.other = bf16[176,512]{1,0:T(8,128)(2,1)S(1)} collective-permute-done((bf16[176,512]{1,0:T(8,128)(2,1)S(1)}, bf16[176,512]{1,0:T(8,128)(2,1)S(1)}, u32[]{:S(2)}, u32[]{:S(2)}) %collective-permute-start.29) | collective-permute-done | bytes 180256 | tf_op jit(solution)/shard_map/ppermute | solution.py:556
  149.8 1.5 %late_out.1 = (f32[64,1536]{1,0:T(8,128)}, f32[64,512]{1,0:T(8,128)}, f32[64,512]{1,0:T(8,128)}, f32[1,64]{1,0:T(1,128)}, f32[1,64]{1,0:T(1,128)}, /*index=5*/f32[1,64]{1,0:T(1,128)}, f32[1,64]{1,0:T(1,128)}) custom-call(s32[4]{0:T(128)S(1)} %pad_add_fusion.meta, bf16[176,512]{1,0:T(8,128)(2,1)S(1)} %pad_maximum_fusion.3.mine, ...), custom_call_target="tpu_custom_call" | custom-call | tf_op jit(solution)/shard_map/late_out/pallas_call | solution.py:592
  (74 shorter events, 6.1 us)
Async XLA Ops:
  0.7 3.9 %copy-start.1 = (bf16[2,256,512]{2,1,0:T(8,128)(2,1)S(1)}, bf16[2,256,512]{2,1,0:T(8,128)(2,1)}, u32[]{:S(2)}) copy-start(bf16[2,256,512]{2,1,0:T(8,128)(2,1)} %param.31) | copy-start | bytes 1572868
  2.9 8.1 %collective-permute-start = (bf16[168,1024]{1,0:T(8,128)(2,1)S(1)}, bf16[168,1024]{1,0:T(8,128)(2,1)S(1)}, u32[]{:S(2)}, u32[]{:S(2)}) collective-permute-start(bf16[168,1024]{1,0:T(8,128)(2,1)S(1)} %get-tuple-element.150), channel_id=1, source_target_pairs={{0,4},{4,0},{8,12},{12,8},{16,20},{20,16},{24,28},{28,24},{1,5},{5... | collective-permute-start | bytes 1032200 | tf_op jit(solution)/shard_map/ppermute | solution.py:541
  5.7 26.9 %collective-permute-start.4 = (bf16[256,1024]{1,0:T(8,128)(2,1)}, bf16[256,1024]{1,0:T(8,128)(2,1)S(1)}, u32[]{:S(2)}, u32[]{:S(2)}) collective-permute-start(bf16[256,1024]{1,0:T(8,128)(2,1)} %get-tuple-element.284), channel_id=1, source_target_pairs={{0,0},{1,4},{2,1},{3,5},{4,2},{5,6},{6,3},{7,7},{8,8},{9,12},{10,9... | collective-permute-start | bytes 1572872 | tf_op jit(solution)/shard_map/ppermute | solution.py:570
  7.4 28.5 %collective-permute-start.5 = (bf16[256,1024]{1,0:T(8,128)(2,1)}, bf16[256,1024]{1,0:T(8,128)(2,1)S(1)}, u32[]{:S(2)}, u32[]{:S(2)}) collective-permute-start(bf16[256,1024]{1,0:T(8,128)(2,1)} %get-tuple-element.283), channel_id=1, source_target_pairs={{0,1},{1,5},{2,0},{3,4},{4,3},{5,7},{6,2},{7,6},{8,9},{9,13},{10,8... | collective-permute-start | bytes 1572872 | tf_op jit(solution)/shard_map/ppermute | solution.py:570
  10.9 4.1 %copy-start.2 = (s32[2]{0:T(128)S(1)}, s32[2]{0:T(128)}, u32[]{:S(2)}) copy-start(s32[2]{0:T(128)} %lengths_ref.1) | copy-start | bytes 28
  11.3 18.3 %copy-start = (bf16[144,1024]{1,0:T(8,128)(2,1)}, bf16[144,1024]{1,0:T(8,128)(2,1)S(1)}, u32[]{:S(2)}) copy-start(bf16[144,1024]{1,0:T(8,128)(2,1)S(1)} %pad_maximum_fusion.2.refs_0_) | copy-start | bytes 884740
  11.4 8.4 %collective-permute-start.1 = (bf16[144,1024]{1,0:T(8,128)(2,1)S(1)}, bf16[144,1024]{1,0:T(8,128)(2,1)}, u32[]{:S(2)}, u32[]{:S(2)}) collective-permute-start(bf16[144,1024]{1,0:T(8,128)(2,1)S(1)} %pad_maximum_fusion.2.refs_0_), channel_id=1, source_target_pairs={{0,8},{4,12},{8,0},{12,4},{16,24},{20,28},{24,16},{28,20},{1,9},{5... | collective-permute-start | bytes 884744 | tf_op jit(solution)/shard_map/ppermute | solution.py:546
  13.4 14.5 %collective-permute-start.2 = (bf16[144,1024]{1,0:T(8,128)(2,1)S(1)}, bf16[144,1024]{1,0:T(8,128)(2,1)}, u32[]{:S(2)}, u32[]{:S(2)}) collective-permute-start(bf16[144,1024]{1,0:T(8,128)(2,1)S(1)} %pad_maximum_fusion.2.refs_0_), channel_id=1, source_target_pairs={{0,16},{4,20},{8,24},{12,28},{16,0},{20,4},{24,8},{28,12},{1,17},{... | collective-permute-start | bytes 884744 | tf_op jit(solution)/shard_map/ppermute | solution.py:546
  15.0 13.3 %collective-permute-start.3 = (bf16[144,1024]{1,0:T(8,128)(2,1)S(1)}, bf16[144,1024]{1,0:T(8,128)(2,1)}, u32[]{:S(2)}, u32[]{:S(2)}) collective-permute-start(bf16[144,1024]{1,0:T(8,128)(2,1)S(1)} %pad_maximum_fusion.2.refs_0_), channel_id=1, source_target_pairs={{0,24},{4,28},{8,16},{12,20},{16,8},{20,12},{24,0},{28,4},{1,25},{... | collective-permute-start | bytes 884744 | tf_op jit(solution)/shard_map/ppermute | solution.py:546
  28.2 13.5 %collective-permute-start.8 = (bf16[320,1024]{1,0:T(8,128)(2,1)S(1)}, bf16[320,1024]{1,0:T(8,128)(2,1)S(1)}, u32[]{:S(2)}, u32[]{:S(2)}) collective-permute-start(bf16[320,1024]{1,0:T(8,128)(2,1)S(1)} %pad_maximum_fusion.1.refs_0_), channel_id=1, source_target_pairs={{0,8},{4,20},{8,0},{12,28},{16,24},{20,4},{24,16},{28,12},{1,9},{5... | collective-permute-start | bytes 1966088 | tf_op jit(solution)/shard_map/ppermute | solution.py:551
  35.9 2.0 %collective-permute-start.6 = (bf16[256,1024]{1,0:T(8,128)(2,1)S(1)}, bf16[256,1024]{1,0:T(8,128)(2,1)S(1)}, u32[]{:S(2)}, u32[]{:S(2)}) collective-permute-start(bf16[256,1024]{1,0:T(8,128)(2,1)S(1)} %collective-permute-done.4.refs_0_.refs_4_), channel_id=1, source_target_pairs={{0,4},{4,0},{8,12},{12,8},{16,20},{20,16},{24,28},{28,24},{1,5},{5... | collective-permute-start | bytes 1572872 | tf_op jit(solution)/shard_map/ppermute | solution.py:541
  35.9 2.7 %collective-permute-start.7 = (bf16[256,1024]{1,0:T(8,128)(2,1)S(1)}, bf16[256,1024]{1,0:T(8,128)(2,1)S(1)}, u32[]{:S(2)}, u32[]{:S(2)}) collective-permute-start(bf16[256,1024]{1,0:T(8,128)(2,1)S(1)} %collective-permute-done.5.refs_1_.refs_5_), channel_id=1, source_target_pairs={{0,4},{4,0},{8,12},{12,8},{16,20},{20,16},{24,28},{28,24},{1,5},{5... | collective-permute-start | bytes 1572872 | tf_op jit(solution)/shard_map/ppermute | solution.py:541
  36.4 18.2 %collective-permute-start.9 = (bf16[320,1024]{1,0:T(8,128)(2,1)S(1)}, bf16[320,1024]{1,0:T(8,128)(2,1)S(1)}, u32[]{:S(2)}, u32[]{:S(2)}) collective-permute-start(bf16[320,1024]{1,0:T(8,128)(2,1)S(1)} %pad_maximum_fusion.1.refs_0_), channel_id=1, source_target_pairs={{0,16},{4,12},{8,24},{12,4},{16,0},{20,28},{24,8},{28,20},{1,17},{... | collective-permute-start | bytes 1966088 | tf_op jit(solution)/shard_map/ppermute | solution.py:551
  41.8 12.9 %collective-permute-start.10 = (bf16[320,1024]{1,0:T(8,128)(2,1)S(1)}, bf16[320,1024]{1,0:T(8,128)(2,1)S(1)}, u32[]{:S(2)}, u32[]{:S(2)}) collective-permute-start(bf16[320,1024]{1,0:T(8,128)(2,1)S(1)} %collective-permute-done.8.refs_1_), channel_id=1, source_target_pairs={{0,16},{4,12},{8,24},{12,4},{16,0},{20,28},{24,8},{28,20},{1,17},{... | collective-permute-start | bytes 1966088 | tf_op jit(solution)/shard_map/ppermute | solution.py:551
  54.6 2.0 %collective-permute-start.11 = (bf16[1024,256]{1,0:T(8,128)(2,1)S(1)}, bf16[1024,256]{1,0:T(8,128)(2,1)S(1)}, u32[]{:S(2)}, u32[]{:S(2)}) collective-permute-start(bf16[1024,256]{1,0:T(8,128)(2,1)S(1)} %get-tuple-element.180.refs_9_.o_ref), channel_id=1, source_target_pairs={{0,4},{4,0},{8,12},{12,8},{16,20},{20,16},{24,28},{28,24},{1,5},{5... | collective-permute-start | bytes 1572872 | tf_op jit(solution)/shard_map/ppermute | solution.py:541
  67.8 4.1 %collective-permute-start.12 = (bf16[1024,512]{1,0:T(8,128)(2,1)S(1)}, bf16[1024,512]{1,0:T(8,128)(2,1)S(1)}, u32[]{:S(2)}, u32[]{:S(2)}) collective-permute-start(bf16[1024,512]{1,0:T(8,128)(2,1)S(1)} %get-tuple-element.184.dh_ref), channel_id=1, source_target_pairs={{0,4},{4,0},{8,12},{12,8},{16,20},{20,16},{24,28},{28,24},{1,5},{5... | collective-permute-start | bytes 3145736 | tf_op jit(solution)/shard_map/ppermute | solution.py:541
  68.0 3.9 %collective-permute-start.13 = (bf16[512,512]{1,0:T(8,128)(2,1)S(1)}, bf16[512,512]{1,0:T(8,128)(2,1)S(1)}, u32[]{:S(2)}, u32[]{:S(2)}) collective-permute-start(bf16[512,512]{1,0:T(8,128)(2,1)S(1)} %get-tuple-element.187), channel_id=1, source_target_pairs={{0,4},{4,0},{8,12},{12,8},{16,20},{20,16},{24,28},{28,24},{1,5},{5... | collective-permute-start | bytes 1572872 | tf_op jit(solution)/shard_map/ppermute | solution.py:541
  68.4 22.2 %collective-permute-start.16 = (bf16[264,1024]{1,0:T(8,128)(2,1)S(1)}, bf16[264,1024]{1,0:T(8,128)(2,1)S(1)}, u32[]{:S(2)}, u32[]{:S(2)}) collective-permute-start(bf16[264,1024]{1,0:T(8,128)(2,1)S(1)} %get-tuple-element.216), channel_id=1, source_target_pairs={{0,8},{4,12},{8,0},{12,4},{16,24},{20,28},{24,16},{28,20},{1,9},{5... | collective-permute-start | bytes 1622024 | tf_op jit(solution)/shard_map/ppermute | solution.py:546
  69.9 25.6 %collective-permute-start.17 = (bf16[264,1024]{1,0:T(8,128)(2,1)S(1)}, bf16[264,1024]{1,0:T(8,128)(2,1)S(1)}, u32[]{:S(2)}, u32[]{:S(2)}) collective-permute-start(bf16[264,1024]{1,0:T(8,128)(2,1)S(1)} %get-tuple-element.217), channel_id=1, source_target_pairs={{0,16},{4,20},{8,24},{12,28},{16,0},{20,4},{24,8},{28,12},{1,17},{... | collective-permute-start | bytes 1622024 | tf_op jit(solution)/shard_map/ppermute | solution.py:546
  70.7 24.8 %collective-permute-start.18 = (bf16[264,1024]{1,0:T(8,128)(2,1)S(1)}, bf16[264,1024]{1,0:T(8,128)(2,1)S(1)}, u32[]{:S(2)}, u32[]{:S(2)}) collective-permute-start(bf16[264,1024]{1,0:T(8,128)(2,1)S(1)} %get-tuple-element.218), channel_id=1, source_target_pairs={{0,24},{4,28},{8,16},{12,20},{16,8},{20,12},{24,0},{28,4},{1,25},{... | collective-permute-start | bytes 1622024 | tf_op jit(solution)/shard_map/ppermute | solution.py:546
  75.3 20.2 %collective-permute-start.14 = (bf16[256,512]{1,0:T(8,128)(2,1)S(1)}, bf16[256,512]{1,0:T(8,128)(2,1)S(1)}, u32[]{:S(2)}, u32[]{:S(2)}) collective-permute-start(bf16[256,512]{1,0:T(8,128)(2,1)S(1)} %get-tuple-element.214), channel_id=1, source_target_pairs={{0,0},{4,1},{1,2},{5,3},{2,4},{6,5},{3,6},{7,7},{8,8},{12,9},{9,10... | collective-permute-start | bytes 786440 | tf_op jit(solution)/shard_map/ppermute | solution.py:1141
  76.0 19.5 %collective-permute-start.15 = (bf16[256,512]{1,0:T(8,128)(2,1)S(1)}, bf16[256,512]{1,0:T(8,128)(2,1)S(1)}, u32[]{:S(2)}, u32[]{:S(2)}) collective-permute-start(bf16[256,512]{1,0:T(8,128)(2,1)S(1)} %get-tuple-element.215), channel_id=1, source_target_pairs={{1,0},{5,1},{0,2},{4,3},{3,4},{7,5},{2,6},{6,7},{9,8},{13,9},{8,10... | collective-permute-start | bytes 786440 | tf_op jit(solution)/shard_map/ppermute | solution.py:1141
  96.3 8.5 %collective-permute-start.23 = (bf16[264,512]{1,0:T(8,128)(2,1)S(1)}, bf16[264,512]{1,0:T(8,128)(2,1)S(1)}, u32[]{:S(2)}, u32[]{:S(2)}) collective-permute-start(bf16[264,512]{1,0:T(8,128)(2,1)S(1)} %get-tuple-element.249), channel_id=1, source_target_pairs={{0,1},{1,0},{2,3},{3,2},{4,5},{5,4},{6,7},{7,6},{8,9},{9,8},{10,11... | collective-permute-start | bytes 811016 | tf_op jit(solution)/shard_map/ppermute | solution.py:556
  101.2 7.1 %collective-permute-start.25 = (bf16[512,512]{1,0:T(8,128)(2,1)S(1)}, bf16[512,512]{1,0:T(8,128)(2,1)S(1)}, u32[]{:S(2)}, u32[]{:S(2)}) collective-permute-start(bf16[512,512]{1,0:T(8,128)(2,1)S(1)} %get-tuple-element.251), channel_id=1, source_target_pairs={{0,4},{4,0},{8,12},{12,8},{16,20},{20,16},{24,28},{28,24},{1,5},{5... | collective-permute-start | bytes 1572872 | tf_op jit(solution)/shard_map/ppermute | solution.py:541
  101.3 10.9 %collective-permute-start.19 = (bf16[168,1024]{1,0:T(8,128)(2,1)S(1)}, bf16[168,1024]{1,0:T(8,128)(2,1)S(1)}, u32[]{:S(2)}, u32[]{:S(2)}) collective-permute-start(bf16[168,1024]{1,0:T(8,128)(2,1)S(1)} %get-tuple-element.243), channel_id=1, source_target_pairs={{0,8},{4,12},{8,0},{12,4},{16,24},{20,28},{24,16},{28,20},{1,9},{5... | collective-permute-start | bytes 1032200 | tf_op jit(solution)/shard_map/ppermute | solution.py:546
  103.1 17.5 %collective-permute-start.20 = (bf16[168,1024]{1,0:T(8,128)(2,1)S(1)}, bf16[168,1024]{1,0:T(8,128)(2,1)S(1)}, u32[]{:S(2)}, u32[]{:S(2)}) collective-permute-start(bf16[168,1024]{1,0:T(8,128)(2,1)S(1)} %get-tuple-element.244), channel_id=1, source_target_pairs={{0,16},{4,20},{8,24},{12,28},{16,0},{20,4},{24,8},{28,12},{1,17},{... | collective-permute-start | bytes 1032200 | tf_op jit(solution)/shard_map/ppermute | solution.py:546
  103.6 17.0 %collective-permute-start.21 = (bf16[168,1024]{1,0:T(8,128)(2,1)S(1)}, bf16[168,1024]{1,0:T(8,128)(2,1)S(1)}, u32[]{:S(2)}, u32[]{:S(2)}) collective-permute-start(bf16[168,1024]{1,0:T(8,128)(2,1)S(1)} %get-tuple-element.245), channel_id=1, source_target_pairs={{0,24},{4,28},{8,16},{12,20},{16,8},{20,12},{24,0},{28,4},{1,25},{... | collective-permute-start | bytes 1032200 | tf_op jit(solution)/shard_map/ppermute | solution.py:546
  104.9 23.4 %collective-permute-start.24 = (bf16[264,512]{1,0:T(8,128)(2,1)S(1)}, bf16[264,512]{1,0:T(8,128)(2,1)S(1)}, u32[]{:S(2)}, u32[]{:S(2)}) collective-permute-start(bf16[264,512]{1,0:T(8,128)(2,1)S(1)} %add_convert_fusion.2), channel_id=1, source_target_pairs={{0,2},{1,3},{2,0},{3,1},{4,6},{5,7},{6,4},{7,5},{8,10},{9,11},{10,... | collective-permute-start | bytes 811016 | tf_op jit(solution)/shard_map/ppermute | solution.py:556
  109.7 18.6 %collective-permute-start.26 = (bf16[256,512]{1,0:T(8,128)(2,1)S(1)}, bf16[256,512]{1,0:T(8,128)(2,1)S(1)}, u32[]{:S(2)}, u32[]{:S(2)}) collective-permute-start(bf16[256,512]{1,0:T(8,128)(2,1)S(1)} %get-tuple-element.253), channel_id=1, source_target_pairs={{0,0},{4,1},{1,2},{5,3},{2,4},{6,5},{3,6},{7,7},{8,8},{12,9},{9,10... | collective-permute-start | bytes 786440 | tf_op jit(solution)/shard_map/ppermute | solution.py:1141
  121.3 7.0 %collective-permute-start.22 = (bf16[168,512]{1,0:T(8,128)(2,1)S(1)}, bf16[168,512]{1,0:T(8,128)(2,1)S(1)}, u32[]{:S(2)}, u32[]{:S(2)}) collective-permute-start(bf16[168,512]{1,0:T(8,128)(2,1)S(1)} %get-tuple-element.247), channel_id=1, source_target_pairs={{0,1},{1,0},{2,3},{3,2},{4,5},{5,4},{6,7},{7,6},{8,9},{9,8},{10,11... | collective-permute-start | bytes 516104 | tf_op jit(solution)/shard_map/ppermute | solution.py:556
  121.6 21.6 %collective-permute-start.30 = (bf16[256,512]{1,0:T(8,128)(2,1)S(1)}, bf16[256,512]{1,0:T(8,128)(2,1)S(1)}, u32[]{:S(2)}, u32[]{:S(2)}) collective-permute-start(bf16[256,512]{1,0:T(8,128)(2,1)S(1)} %get-tuple-element.258), channel_id=1, source_target_pairs={{1,0},{5,1},{0,2},{4,3},{3,4},{7,5},{2,6},{6,7},{9,8},{13,9},{8,10... | collective-permute-start | bytes 786440 | tf_op jit(solution)/shard_map/ppermute | solution.py:1141
  128.3 13.3 %collective-permute-start.27 = (bf16[168,512]{1,0:T(8,128)(2,1)S(1)}, bf16[168,512]{1,0:T(8,128)(2,1)S(1)}, u32[]{:S(2)}, u32[]{:S(2)}) collective-permute-start(bf16[168,512]{1,0:T(8,128)(2,1)S(1)} %add_convert_fusion.4), channel_id=1, source_target_pairs={{0,2},{1,3},{2,0},{3,1},{4,6},{5,7},{6,4},{7,5},{8,10},{9,11},{10,... | collective-permute-start | bytes 516104 | tf_op jit(solution)/shard_map/ppermute | solution.py:556
  130.7 12.7 %collective-permute-start.31 = (bf16[264,512]{1,0:T(8,128)(2,1)S(1)}, bf16[264,512]{1,0:T(8,128)(2,1)S(1)}, u32[]{:S(2)}, u32[]{:S(2)}) collective-permute-start(bf16[264,512]{1,0:T(8,128)(2,1)S(1)} %add_convert_fusion.1.mine), channel_id=1, source_target_pairs={{0,1},{1,0},{2,3},{3,2},{4,5},{5,4},{6,7},{7,6},{8,9},{9,8},{10,11... | collective-permute-start | bytes 811016 | tf_op jit(solution)/shard_map/ppermute | solution.py:556
  141.7 1.3 collective-permute-start.28
  143.1 6.7 %collective-permute-start.29 = (bf16[176,512]{1,0:T(8,128)(2,1)S(1)}, bf16[176,512]{1,0:T(8,128)(2,1)S(1)}, u32[]{:S(2)}, u32[]{:S(2)}) collective-permute-start(bf16[176,512]{1,0:T(8,128)(2,1)S(1)} %pad_maximum_fusion.3.mine), channel_id=1, source_target_pairs={{0,1},{1,0},{2,3},{3,2},{4,5},{5,4},{6,7},{7,6},{8,9},{9,8},{10,11... | collective-permute-start | bytes 540680 | tf_op jit(solution)/shard_map/ppermute | solution.py:556
  143.4 1.9 %collective-permute-start.32 = (bf16[2,72,512]{2,1,0:T(8,128)(2,1)S(1)}, bf16[2,72,512]{2,1,0:T(8,128)(2,1)S(1)}, u32[]{:S(2)}, u32[]{:S(2)}) collective-permute-start(bf16[2,72,512]{2,1,0:T(8,128)(2,1)S(1)} %pad_maximum_fusion.4), channel_id=1, source_target_pairs={{0,4},{4,0},{8,12},{12,8},{16,20},{20,16},{24,28},{28,24},{1,5},{5... | collective-permute-start | bytes 442376 | tf_op jit(solution)/shard_map/ppermute | solution.py:541

commit v7 on v6

--- a/solution.py
+++ b/solution.py
@@ -41,7 +41,7 @@
     return masked_tail(dot(qu, keys, NT) + rel, keep, block)
 
 
-def attn_fwd_body(len_ref, q_ref, k_ref, v_ref, r_ref, bu_ref, bv_ref, o_ref, *p_refs, block):
+def attn_fwd_body(len_ref, q_ref, k_ref, v_ref, r_ref, bu_ref, bv_ref, o_ref, wide_ref, *p_refs, block):
     full = q_ref.shape[0]
     lane = lax.broadcasted_iota(jnp.int32, (block, 2 * HD), 1)
     sides = (lane < HD, lane >= HD)
@@ -74,7 +74,9 @@
             p = (e * (1.0 / total)).astype(bf)
             p_refs[first // block][head] = p
             outs.append(dot(p, v_ref[:span, :], NN))
-        o_ref[first:span, :] = jnp.where(sides[0], outs[0], outs[1]).astype(bf)
+        wide = jnp.where(sides[0], outs[0], outs[1])
+        wide_ref[first:span, :] = wide
+        o_ref[first:span, :] = wide.astype(bf)
 
 
 def attn_fwd(length, qkv, rel_rev, bias_u, bias_v, *, block=256):
@@ -87,6 +89,7 @@
         functools.partial(attn_fwd_body, block=block),
         out_shape=(
             jax.ShapeDtypeStruct((full, cols), bf),
+            jax.ShapeDtypeStruct((full, cols), f32),
             *(jax.ShapeDtypeStruct((2 * pairs, block, span), bf) for span in spans),
         ),
         grid_spec=pltpu.PrefetchScalarGridSpec(
@@ -95,6 +98,7 @@
             in_specs=[at(0), at(1), at(2), at(0), row, row],
             out_specs=(
                 at(0),
+                at(0),
                 *(pl.BlockSpec((2, block, span), lambda pair, _: (pair, 0, 0)) for span in spans),
             ),
         ),
@@ -104,7 +108,7 @@
     )(length, qkv, qkv, qkv, rel_rev, bias_u, bias_v)
 
 
-def attn_bwd_body(len_ref, q_ref, k_ref, v_ref, r_ref, bu_ref, bv_ref, do_ref, *refs, block, heads):
+def attn_bwd_body(len_ref, q_ref, k_ref, v_ref, r_ref, bu_ref, bv_ref, do_ref, o_ref, *refs, block, heads):
     full = q_ref.shape[0]
     p_refs, refs = refs[: full // block], refs[full // block :]
     dq_ref, dk_ref, dv_ref, dr_ref, gu_ref, gv_ref, dk_t, dv_t, dr_t = refs
@@ -124,6 +128,7 @@
             qu = (q + bu_ref[...]).astype(bf).astype(f32) * 0.125
             qv = (q + bv_ref[...]).astype(bf).astype(f32) * 0.125
             do = do_ref[first:span, :].astype(f32)
+            o = o_ref[first:span, :]
             qu_t = jnp.transpose(qu).astype(bf)
             do_t = jnp.transpose(do).astype(bf)
             qv_t = jnp.transpose(dot(flip, qv.astype(bf), NN)).astype(bf)
@@ -134,8 +139,8 @@
                 rounded = p_refs[first // block][head - heads[0]]
                 p = rounded.astype(f32)
                 dp = dot(jnp.where(side, do, 0.0).astype(bf), v_ref[:span, :], NT)
-                t = p * dp
-                ds = (t - p * jnp.sum(t, axis=1, keepdims=True)).astype(bf)
+                inner = jnp.sum(jnp.where(side, do * o, 0.0), axis=1, keepdims=True)
+                ds = (p * (dp - inner)).astype(bf)
                 dv_t[at, :span] += dot(do_t[at], rounded, NN)
                 both = dot(jnp.concatenate([qu_t[at], flip], axis=0), ds, NN)
                 dk_t[at, :span] += both[:HD]
@@ -159,7 +164,7 @@
     dr_ref[...] = jnp.transpose(dr_t[...]).astype(bf)
 
 
-def attn_bwd(length, qkv, rel_rev, bias_u, bias_v, probs, d_out, *, pair, heads=(0, 1), block=256):
+def attn_bwd(length, qkv, rel_rev, bias_u, bias_v, probs, d_out, out_rows, *, pair, heads=(0, 1), block=256):
     full, cols = rel_rev.shape
     pairs = cols // (2 * HD)
     at = lambda part: pl.BlockSpec((full, 2 * HD), lambda i, _: (0, part * pairs + pair))
@@ -174,7 +179,7 @@
             num_scalar_prefetch=1,
             grid=(1,),
             in_specs=[at(0), at(1), at(2), at(0), row, row]
-            + [at(0)]
+            + [at(0), at(0)]
             + [
                 pl.BlockSpec((len(heads),) + p.shape[1:], lambda i, _: ((2 * pair + heads[0]) // len(heads), 0, 0))
                 for p in probs
@@ -185,7 +190,7 @@
         cost_estimate=pl.CostEstimate(flops=0, bytes_accessed=0, transcendentals=0),
         compiler_params=pltpu.CompilerParams(vmem_limit_bytes=32 << 20),
         name="attn_bwd",
-    )(length, qkv, qkv, qkv, rel_rev, bias_u, bias_v, d_out, *probs)
+    )(length, qkv, qkv, qkv, rel_rev, bias_u, bias_v, d_out, out_rows, *probs)
 
 
 def norm_parts(values):
@@ -1090,7 +1095,7 @@
     )
     qkv, feed_first = together(qkv, feed_first)
     feed_third = swap_axis(feed_first, 1)
-    attn, *probs = attn_fwd(length_arr, qkv, rel, own_u, own_v)
+    attn, attn_wide, *probs = attn_fwd(length_arr, qkv, rel, own_u, own_v)
     attn, feed_second, feed_third = together(attn, feed_second, feed_third)
     feed_packs = [feed_pack, feed_first, feed_second, feed_third]
 
@@ -1142,7 +1147,7 @@
         for turn, out in enumerate(outs)
     ]
     y_turns = home((out0, out1))
-    back = lambda pair, d_out: attn_bwd(length_arr, qkv, rel, own_u, own_v, probs, d_out, pair=pair)
+    back = lambda pair, d_out: attn_bwd(length_arr, qkv, rel, own_u, own_v, probs, d_out, attn_wide, pair=pair)
     d_attn, *grads_a = together(d_attn, *back(0, d_attn))
     *grads_b, y0, y1, e1, e2, e3 = together(*back(1, d_attn), *y_turns, *early_came)
     early_keep, early_send = chip_sum(meta, [early_parts[0], e1, e2, e3], "early_chips", 0)

time: 152 us -> 150 us (0.987)
  Pallas kernels: 57.2 us -> 52.4 us
  waiting for transfers between devices: 51 us -> 55.6 us
    ppermute x9, waiting for transfers between devices: 26.3 us -> 33.2 us  [swap_chip(): lax.ppermute(values, 'fsdp', [(i, i ^ 2 * mask) for i in range(size)])]
    pallas_call x2, Pallas kernels: 11.1 us -> 6.14 us  [attn_bwd(): pl.pallas_call(functools.partial(attn_bwd_body, block=block, heads=heads)...]
    ppermute x6, waiting for transfers between devices: 17.6 us -> 15.4 us  [swap_seq(): return lax.ppermute(values, 'seq', [(i, i ^ mask) for i in range(size)])]
  transfers between devices with their start and end apart: 33 -> 33, of which waited for: 14 -> 14; matrix products, arithmetic and copies ran while one was open for 3% -> 3% of each run, Pallas kernels for 27% -> 24%
where the time goes in v7:
time: 150 us
  waiting for transfers between devices  55.6 us (37%)
  Pallas kernels  52.4 us (35%)
  starting transfers between devices  35.2 us (23%)
  local copies, waits for them, and re-layouts  3.07 us (2%)
  between operations  2.39 us (2%)
    pallas_call x12, Pallas kernels, kernel_call(): pl.pallas_call(body, out_shape=[jax.ShapeDtypeStruct(shape, kind) for sha...  34.9 us
    ppermute x9, waiting for transfers between devices, swap_chip(): lax.ppermute(values, 'fsdp', [(i, i ^ 2 * mask) for i in range(size)])  33.2 us
    ppermute x6, waiting for transfers between devices, swap_seq(): return lax.ppermute(values, 'seq', [(i, i ^ mask) for i in range(size)])  15.4 us
    pallas_call x1, Pallas kernels, attn_fwd(): pl.pallas_call(functools.partial(attn_fwd_body, block=block), out_shape=(...  11.4 us
    ppermute x9, starting transfers between devices, swap_chip(): lax.ppermute(values, 'fsdp', [(i, i ^ 2 * mask) for i in range(size)])  10.7 us
    ppermute x4, starting transfers between devices, slot_split_device(): lax.ppermute(out, ('fsdp', 'seq'), [(b, a) for a, b in slot_pairs(turn)])  6.93 us
    ppermute x6, starting transfers between devices, swap_seq(): return lax.ppermute(values, 'seq', [(i, i ^ mask) for i in range(size)])  6.69 us
    pallas_call x2, Pallas kernels, attn_bwd(): pl.pallas_call(functools.partial(attn_bwd_body, block=block, heads=heads)...  6.14 us
  transfers between devices with their start and end apart: 33, of which 14 were waited for; matrix products, arithmetic and copies ran while one was open for 3% of the time, Pallas kernels for 24%

profile of v7, /device:TPU:0, one launch (start us, length us, event | category | flops | bytes accessed | tf_op | source)
XLA Modules:
  0.0 150.0 jit_solution(2281099436449339652)
XLA Ops:
  0.7 2.3 %pack.1 = (bf16[72,1024]{1,0:T(8,128)(2,1)S(1)}, bf16[224,1024]{1,0:T(8,128)(2,1)S(1)}, bf16[168,1024]{1,0:T(8,128)(2,1)S(1)}) custom-call(s32[2]{0:T(128)} %lengths_ref.1, bf16[64,1536]{1,0:T(8,128)(2,1)} %qkv_ref.1, bf16[64,512]{1,0:T(8,128)(2,1)} %rel_ref.1, bf16[64,2048]{1,0:T(8,128)(2,1)} %up_ref.1, bf16[64,512]{1,0:T(8,128)(2,1)} %out_ref.1, ...), custom_call_target="tpu_custom_call" | custom-call | tf_op jit(solution)/shard_map/pack/pallas_call | solution.py:597
  3.5 1.1 constant_dynamic-update-slice_fusion.1
  4.7 1.0 dynamic-slice_bitcast_fusion
  5.7 1.7 %collective-permute-start.4 = (bf16[256,1024]{1,0:T(8,128)(2,1)}, bf16[256,1024]{1,0:T(8,128)(2,1)S(1)}, u32[]{:S(2)}, u32[]{:S(2)}) collective-permute-start(bf16[256,1024]{1,0:T(8,128)(2,1)} %get-tuple-element.286), channel_id=1, source_target_pairs={{0,0},{1,4},{2,1},{3,5},{4,2},{5,6},{6,3},{7,7},{8,8},{9,12},{10,9... | collective-permute-start | bytes 1572872 | tf_op jit(solution)/shard_map/ppermute | solution.py:575
  7.4 2.9 %collective-permute-start.5 = (bf16[256,1024]{1,0:T(8,128)(2,1)}, bf16[256,1024]{1,0:T(8,128)(2,1)S(1)}, u32[]{:S(2)}, u32[]{:S(2)}) collective-permute-start(bf16[256,1024]{1,0:T(8,128)(2,1)} %get-tuple-element.285), channel_id=1, source_target_pairs={{0,1},{1,5},{2,0},{3,4},{4,3},{5,7},{6,2},{7,6},{8,9},{9,13},{10,8... | collective-permute-start | bytes 1572872 | tf_op jit(solution)/shard_map/ppermute | solution.py:575
  11.4 2.1 %collective-permute-start.1 = (bf16[144,1024]{1,0:T(8,128)(2,1)S(1)}, bf16[144,1024]{1,0:T(8,128)(2,1)}, u32[]{:S(2)}, u32[]{:S(2)}) collective-permute-start(bf16[144,1024]{1,0:T(8,128)(2,1)S(1)} %pad_maximum_fusion.2.refs_0_), channel_id=1, source_target_pairs={{0,8},{4,12},{8,0},{12,4},{16,24},{20,28},{24,16},{28,20},{1,9},{5... | collective-permute-start | bytes 884744 | tf_op jit(solution)/shard_map/ppermute | solution.py:551
  13.4 1.5 %collective-permute-start.2 = (bf16[144,1024]{1,0:T(8,128)(2,1)S(1)}, bf16[144,1024]{1,0:T(8,128)(2,1)}, u32[]{:S(2)}, u32[]{:S(2)}) collective-permute-start(bf16[144,1024]{1,0:T(8,128)(2,1)S(1)} %pad_maximum_fusion.2.refs_0_), channel_id=1, source_target_pairs={{0,16},{4,20},{8,24},{12,28},{16,0},{20,4},{24,8},{28,12},{1,17},{... | collective-permute-start | bytes 884744 | tf_op jit(solution)/shard_map/ppermute | solution.py:551
  17.0 2.7 %collective-permute-done.1.refs_1_ = bf16[144,1024]{1,0:T(8,128)(2,1)} collective-permute-done((bf16[144,1024]{1,0:T(8,128)(2,1)S(1)}, bf16[144,1024]{1,0:T(8,128)(2,1)}, u32[]{:S(2)}, u32[]{:S(2)}) %collective-permute-start.1) | collective-permute-done | bytes 294944 | tf_op jit(solution)/shard_map/ppermute | solution.py:551
  19.8 8.2 %collective-permute-done.2.refs_2_ = bf16[144,1024]{1,0:T(8,128)(2,1)} collective-permute-done((bf16[144,1024]{1,0:T(8,128)(2,1)S(1)}, bf16[144,1024]{1,0:T(8,128)(2,1)}, u32[]{:S(2)}, u32[]{:S(2)}) %collective-permute-start.2) | collective-permute-done | bytes 294944 | tf_op jit(solution)/shard_map/ppermute | solution.py:551
  28.2 1.4 collective-permute-start.8
  29.6 2.9 %weights.1 = (bf16[1024,256]{1,0:T(8,128)(2,1)S(1)}, bf16[512,1024]{1,0:T(8,128)(2,1)S(1)}, f32[8,512]{1,0:T(8,128)S(1)}, f32[1,1024]{1,0:T(1,128)S(1)}, f32[1,256]{1,0:T(1,128)S(1)}, /*index=5*/f32[1,256]{1,0:T(1,128)S(1)}) custom-call(s32[4]{0:T(128)S(1)} %broadcast_3__.2._, bf16[144,1024]{1,0:T(8,128)(2,1)} %copy-done, ...), custom_call_target="tpu_custom_call" | custom-call | tf_op jit(solution)/shard_map/weights/pallas_call | solution.py:597
  32.6 3.3 %collective-permute-done.5.refs_1_.refs_5_ = bf16[256,1024]{1,0:T(8,128)(2,1)S(1)} collective-permute-done((bf16[256,1024]{1,0:T(8,128)(2,1)}, bf16[256,1024]{1,0:T(8,128)(2,1)S(1)}, u32[]{:S(2)}, u32[]{:S(2)}) %collective-permute-start.5) | collective-permute-done | bytes 524320 | tf_op jit(solution)/shard_map/ppermute | solution.py:575
  36.4 1.5 %collective-permute-start.9 = (bf16[320,1024]{1,0:T(8,128)(2,1)S(1)}, bf16[320,1024]{1,0:T(8,128)(2,1)S(1)}, u32[]{:S(2)}, u32[]{:S(2)}) collective-permute-start(bf16[320,1024]{1,0:T(8,128)(2,1)S(1)} %pad_maximum_fusion.1.refs_0_), channel_id=1, source_target_pairs={{0,16},{4,12},{8,24},{12,4},{16,0},{20,28},{24,8},{28,20},{1,17},{... | collective-permute-start | bytes 1966088 | tf_op jit(solution)/shard_map/ppermute | solution.py:556
  38.5 3.2 %project.1 = (bf16[1024,768]{1,0:T(8,128)(2,1)S(1)}, bf16[1024,512]{1,0:T(8,128)(2,1)S(1)}, bf16[1024,512]{1,0:T(8,128)(2,1)S(1)}) custom-call(s32[4]{0:T(128)S(1)} %broadcast_3__.2._, bf16[256,1024]{1,0:T(8,128)(2,1)S(1)} %collective-permute-done.4.refs_0_.refs_4_, bf16[256,1024]{1,0:T(8,128)(2,1)S(1)} %collective-permute-done.5.refs_1_.refs_5_, ...), custom_call_target="tpu_custom_call" | custom-call | tf_op jit(solution)/shard_map/project/pallas_call | solution.py:597
  41.8 1.6 %collective-permute-start.10 = (bf16[320,1024]{1,0:T(8,128)(2,1)S(1)}, bf16[320,1024]{1,0:T(8,128)(2,1)S(1)}, u32[]{:S(2)}, u32[]{:S(2)}) collective-permute-start(bf16[320,1024]{1,0:T(8,128)(2,1)S(1)} %collective-permute-done.8.refs_1_), channel_id=1, source_target_pairs={{0,16},{4,12},{8,24},{12,4},{16,0},{20,28},{24,8},{28,20},{1,17},{... | collective-permute-start | bytes 1966088 | tf_op jit(solution)/shard_map/ppermute | solution.py:556
  43.3 11.4 %attn_fwd.1 = (bf16[1024,256]{1,0:T(8,128)(2,1)S(1)}, f32[1024,256]{1,0:T(8,128)S(1)}, bf16[4,256,256]{2,1,0:T(8,128)(2,1)S(1)}, bf16[4,256,512]{2,1,0:T(8,128)(...) custom-call(s32[1]{0:T(128)} %bitcast.15.len_ref, ...), custom_call_target="tpu_custom_call" | custom-call | tf_op jit(solution)/shard_map/attn_fwd/pallas_call | solution.py:88
  54.8 1.9 %collective-permute-done.11.refs_10_ = bf16[1024,256]{1,0:T(8,128)(2,1)S(1)} collective-permute-done((bf16[1024,256]{1,0:T(8,128)(2,1)S(1)}, bf16[1024,256]{1,0:T(8,128)(2,1)S(1)}, u32[]{:S(2)}, u32[]{:S(2)}) %collective-permute-start.11) | collective-permute-done | bytes 524320 | tf_op jit(solution)/shard_map/ppermute | solution.py:546
  56.7 11.2 %feed.1 = (bf16[1024,512]{1,0:T(8,128)(2,1)S(1)}, bf16[1024,512]{1,0:T(8,128)(2,1)S(1)}, f32[1024,1]{1,0:T(8,128)S(1)}, f32[512,512]{1,0:T(8,128)S(1)}, bf16[102...) custom-call(s32[4]{0:T(128)S(1)} %pad_add_fusion.meta, ...), custom_call_target="tpu_custom_call" | custom-call | tf_op jit(solution)/shard_map/feed/pallas_call | solution.py:597
  68.5 1.5 collective-permute-start.16
  69.9 0.7 collective-permute-start.17
  70.7 1.3 collective-permute-start.18
  71.9 3.4 %norm_two.1 = (bf16[256,512]{1,0:T(8,128)(2,1)S(1)}, bf16[256,512]{1,0:T(8,128)(2,1)S(1)}, f32[512,512]{1,0:T(8,128)S(1)}, bf16[1024,256]{1,0:T(8,128)(2,1)S(1)}, f32[256,512]{1,0:T(8,128)S(1)}) custom-call(s32[4]{0:T(128)S(1)} %pad_add_fusion.meta, bf16[1024,512]{1,0:T(8,128)(2,1)S(1)} %get-tuple-element.183.x_hat_ref, ...), custom_call_target="tpu_custom_call" | custom-call | tf_op jit(solution)/shard_map/norm_two/pallas_call | solution.py:597
  76.0 3.5 %collective-permute-start.15 = (bf16[256,512]{1,0:T(8,128)(2,1)S(1)}, bf16[256,512]{1,0:T(8,128)(2,1)S(1)}, u32[]{:S(2)}, u32[]{:S(2)}) collective-permute-start(bf16[256,512]{1,0:T(8,128)(2,1)S(1)} %get-tuple-element.217), channel_id=1, source_target_pairs={{1,0},{5,1},{0,2},{4,3},{3,4},{7,5},{2,6},{6,7},{9,8},{13,9},{8,10... | collective-permute-start | bytes 786440 | tf_op jit(solution)/shard_map/ppermute | solution.py:1146
  79.6 3.0 %attn_bwd.2 = (bf16[1024,128]{1,0:T(8,128)(2,1)S(1)}, bf16[1024,128]{1,0:T(8,128)(2,1)S(1)}, bf16[1024,128]{1,0:T(8,128)(2,1)S(1)}, bf16[1024,128]{1,0:T(8,128)(...) custom-call(s32[1]{0:T(128)} %bitcast.15.len_ref, bf16[1024,768]{1,0:T(8,128)(2,1)S(1)} %get-tuple-element.173.q_ref.k_ref.v_ref, ...), custom_call_target="tpu_custom_call" | custom-call | tf_op jit(solution)/shard_map/attn_bwd/pallas_call | solution.py:174
  82.6 3.2 %attn_bwd.3 = (bf16[1024,128]{1,0:T(8,128)(2,1)S(1)}, bf16[1024,128]{1,0:T(8,128)(2,1)S(1)}, bf16[1024,128]{1,0:T(8,128)(2,1)S(1)}, bf16[1024,128]{1,0:T(8,128)(...) custom-call(s32[1]{0:T(128)} %bitcast.15.len_ref, bf16[1024,768]{1,0:T(8,128)(2,1)S(1)} %get-tuple-element.173.q_ref.k_ref.v_ref, ...), custom_call_target="tpu_custom_call" | custom-call | tf_op jit(solution)/shard_map/attn_bwd/pallas_call | solution.py:174
  85.8 9.8 %collective-permute-done.17.refs_1_ = bf16[264,1024]{1,0:T(8,128)(2,1)S(1)} collective-permute-done((bf16[264,1024]{1,0:T(8,128)(2,1)S(1)}, bf16[264,1024]{1,0:T(8,128)(2,1)S(1)}, u32[]{:S(2)}, u32[]{:S(2)}) %collective-permute-start.17) | collective-permute-done | bytes 540704 | tf_op jit(solution)/shard_map/ppermute | solution.py:551
  95.6 0.8 early_chips.1
  96.4 0.7 collective-permute-start.23
  97.2 4.1 %qkv_back.1 = (f32[512,512]{1,0:T(8,128)S(1)}, bf16[512,512]{1,0:T(8,128)(2,1)S(1)}, f32[168,1024]{1,0:T(8,128)S(1)}, bf16[168,1024]{1,0:T(8,128)(2,1)S(1)}, bf1...) custom-call(s32[4]{0:T(128)S(1)} %pad_add_fusion.meta, bf16[1024,128]{1,0:T(8,128)(2,1)S(1)} %get-tuple-element.202.refs_0_, ...), custom_call_target="tpu_custom_call" | custom-call | tf_op jit(solution)/shard_map/qkv_back/pallas_call | solution.py:597
  101.4 1.8 %collective-permute-start.19 = (bf16[168,1024]{1,0:T(8,128)(2,1)S(1)}, bf16[168,1024]{1,0:T(8,128)(2,1)S(1)}, u32[]{:S(2)}, u32[]{:S(2)}) collective-permute-start(bf16[168,1024]{1,0:T(8,128)(2,1)S(1)} %get-tuple-element.245), channel_id=1, source_target_pairs={{0,8},{4,12},{8,0},{12,4},{16,24},{20,28},{24,16},{28,20},{1,9},{5... | collective-permute-start | bytes 1032200 | tf_op jit(solution)/shard_map/ppermute | solution.py:551
  103.7 1.2 collective-permute-start.21
  105.0 1.4 collective-permute-start.24
  106.4 1.4 norm_one.1
  107.9 0.7 collective-permute-start.26
  108.5 3.8 %collective-permute-done.19.refs_0_ = bf16[168,1024]{1,0:T(8,128)(2,1)S(1)} collective-permute-done((bf16[168,1024]{1,0:T(8,128)(2,1)S(1)}, bf16[168,1024]{1,0:T(8,128)(2,1)S(1)}, u32[]{:S(2)}, u32[]{:S(2)}) %collective-permute-start.19) | collective-permute-done | bytes 344096 | tf_op jit(solution)/shard_map/ppermute | solution.py:551
  112.3 8.4 %collective-permute-done.20.refs_1_ = bf16[168,1024]{1,0:T(8,128)(2,1)S(1)} collective-permute-done((bf16[168,1024]{1,0:T(8,128)(2,1)S(1)}, bf16[168,1024]{1,0:T(8,128)(2,1)S(1)}, u32[]{:S(2)}, u32[]{:S(2)}) %collective-permute-start.20) | collective-permute-done | bytes 344096 | tf_op jit(solution)/shard_map/ppermute | solution.py:551
  120.7 0.7 late_chips.1
  121.6 2.0 %collective-permute-start.30 = (bf16[256,512]{1,0:T(8,128)(2,1)S(1)}, bf16[256,512]{1,0:T(8,128)(2,1)S(1)}, u32[]{:S(2)}, u32[]{:S(2)}) collective-permute-start(bf16[256,512]{1,0:T(8,128)(2,1)S(1)} %get-tuple-element.260), channel_id=1, source_target_pairs={{1,0},{5,1},{0,2},{4,3},{3,4},{7,5},{2,6},{6,7},{9,8},{13,9},{8,10... | collective-permute-start | bytes 786440 | tf_op jit(solution)/shard_map/ppermute | solution.py:1146
  123.6 4.8 %collective-permute-done.22 = bf16[168,512]{1,0:T(8,128)(2,1)S(1)} collective-permute-done((bf16[168,512]{1,0:T(8,128)(2,1)S(1)}, bf16[168,512]{1,0:T(8,128)(2,1)S(1)}, u32[]{:S(2)}, u32[]{:S(2)}) %collective-permute-start.22) | collective-permute-done | bytes 172064 | tf_op jit(solution)/shard_map/ppermute | solution.py:561
  128.5 1.4 collective-permute-start.27
  130.0 2.9 %collective-permute-start.31 = (bf16[264,512]{1,0:T(8,128)(2,1)S(1)}, bf16[264,512]{1,0:T(8,128)(2,1)S(1)}, u32[]{:S(2)}, u32[]{:S(2)}) collective-permute-start(bf16[264,512]{1,0:T(8,128)(2,1)S(1)} %add_convert_fusion.1.mine), channel_id=1, source_target_pairs={{0,1},{1,0},{2,3},{3,2},{4,5},{5,4},{6,7},{7,6},{8,9},{9,8},{10,11... | collective-permute-start | bytes 811016 | tf_op jit(solution)/shard_map/ppermute | solution.py:561
  132.9 7.5 %collective-permute-done.27 = bf16[168,512]{1,0:T(8,128)(2,1)S(1)} collective-permute-done((bf16[168,512]{1,0:T(8,128)(2,1)S(1)}, bf16[168,512]{1,0:T(8,128)(2,1)S(1)}, u32[]{:S(2)}, u32[]{:S(2)}) %collective-permute-start.27) | collective-permute-done | bytes 172064 | tf_op jit(solution)/shard_map/ppermute | solution.py:561
  140.6 1.2 collective-permute-done.28
  141.9 1.7 %collective-permute-done.31.other = bf16[264,512]{1,0:T(8,128)(2,1)S(1)} collective-permute-done((bf16[264,512]{1,0:T(8,128)(2,1)S(1)}, bf16[264,512]{1,0:T(8,128)(2,1)S(1)}, u32[]{:S(2)}, u32[]{:S(2)}) %collective-permute-start.31) | collective-permute-done | bytes 270368 | tf_op jit(solution)/shard_map/ppermute | solution.py:561
  143.7 1.8 %place.1 = (bf16[2,256,512]{2,1,0:T(8,128)(2,1)}, f32[2,256,512]{2,1,0:T(8,128)}) custom-call(s32[4]{0:T(128)S(1)} %pad_add_fusion.meta, bf16[256,512]{1,0:T(8,128)(2,1)S(1)} %collective-permute-done.14.y0, bf16[256,512]{1,0:T(8,128)(2,1)S(1)} %collective-permute-done.15.y1, bf16[256,512]{1,0:T(8,128)(2,1)S(1)} %collective-permute-done.26.x0, ...), custom_call_target="tpu_custom_call" | custom-call | tf_op jit(solution)/shard_map/place/pallas_call | solution.py:597
  145.4 1.6 %early_out.1 = (f32[64,2048]{1,0:T(8,128)}, f32[256,512]{1,0:T(8,128)}, f32[1,64]{1,0:T(1,128)}, f32[1,64]{1,0:T(1,128)}, f32[1,64]{1,0:T(1,128)}, /*index=5*/f32[1,256]{1,0:T(1,128)}) custom-call(s32[4]{0:T(128)S(1)} %pad_add_fusion.meta, bf16[264,512]{1,0:T(8,128)(2,1)S(1)} %add_convert_fusion.1.mine, bf16[264,512]{1,0:T(8,128)(2,1)S(1)} %collective-permute-done.31.other, ...), custom_call_target="tpu_custom_call" | custom-call | tf_op jit(solution)/shard_map/early_out/pallas_call | solution.py:597
  147.1 1.4 collective-permute-done.29.other
  148.5 1.5 %late_out.1 = (f32[64,1536]{1,0:T(8,128)}, f32[64,512]{1,0:T(8,128)}, f32[64,512]{1,0:T(8,128)}, f32[1,64]{1,0:T(1,128)}, f32[1,64]{1,0:T(1,128)}, /*index=5*/f32[1,64]{1,0:T(1,128)}, f32[1,64]{1,0:T(1,128)}) custom-call(s32[4]{0:T(128)S(1)} %pad_add_fusion.meta, bf16[176,512]{1,0:T(8,128)(2,1)S(1)} %pad_maximum_fusion.3.mine, ...), custom_call_target="tpu_custom_call" | custom-call | tf_op jit(solution)/shard_map/late_out/pallas_call | solution.py:597
  (74 shorter events, 6.5 us)
Async XLA Ops:
  0.7 3.9 %copy-start.1 = (bf16[2,256,512]{2,1,0:T(8,128)(2,1)S(1)}, bf16[2,256,512]{2,1,0:T(8,128)(2,1)}, u32[]{:S(2)}) copy-start(bf16[2,256,512]{2,1,0:T(8,128)(2,1)} %param.31) | copy-start | bytes 1572868
  2.9 8.1 %collective-permute-start = (bf16[168,1024]{1,0:T(8,128)(2,1)S(1)}, bf16[168,1024]{1,0:T(8,128)(2,1)S(1)}, u32[]{:S(2)}, u32[]{:S(2)}) collective-permute-start(bf16[168,1024]{1,0:T(8,128)(2,1)S(1)} %get-tuple-element.151), channel_id=1, source_target_pairs={{0,4},{4,0},{8,12},{12,8},{16,20},{20,16},{24,28},{28,24},{1,5},{5... | collective-permute-start | bytes 1032200 | tf_op jit(solution)/shard_map/ppermute | solution.py:546
  5.7 26.9 %collective-permute-start.4 = (bf16[256,1024]{1,0:T(8,128)(2,1)}, bf16[256,1024]{1,0:T(8,128)(2,1)S(1)}, u32[]{:S(2)}, u32[]{:S(2)}) collective-permute-start(bf16[256,1024]{1,0:T(8,128)(2,1)} %get-tuple-element.286), channel_id=1, source_target_pairs={{0,0},{1,4},{2,1},{3,5},{4,2},{5,6},{6,3},{7,7},{8,8},{9,12},{10,9... | collective-permute-start | bytes 1572872 | tf_op jit(solution)/shard_map/ppermute | solution.py:575
  7.4 28.5 %collective-permute-start.5 = (bf16[256,1024]{1,0:T(8,128)(2,1)}, bf16[256,1024]{1,0:T(8,128)(2,1)S(1)}, u32[]{:S(2)}, u32[]{:S(2)}) collective-permute-start(bf16[256,1024]{1,0:T(8,128)(2,1)} %get-tuple-element.285), channel_id=1, source_target_pairs={{0,1},{1,5},{2,0},{3,4},{4,3},{5,7},{6,2},{7,6},{8,9},{9,13},{10,8... | collective-permute-start | bytes 1572872 | tf_op jit(solution)/shard_map/ppermute | solution.py:575
  10.9 4.1 %copy-start.2 = (s32[2]{0:T(128)S(1)}, s32[2]{0:T(128)}, u32[]{:S(2)}) copy-start(s32[2]{0:T(128)} %lengths_ref.1) | copy-start | bytes 28
  11.3 18.3 %copy-start = (bf16[144,1024]{1,0:T(8,128)(2,1)}, bf16[144,1024]{1,0:T(8,128)(2,1)S(1)}, u32[]{:S(2)}) copy-start(bf16[144,1024]{1,0:T(8,128)(2,1)S(1)} %pad_maximum_fusion.2.refs_0_) | copy-start | bytes 884740
  11.4 8.4 %collective-permute-start.1 = (bf16[144,1024]{1,0:T(8,128)(2,1)S(1)}, bf16[144,1024]{1,0:T(8,128)(2,1)}, u32[]{:S(2)}, u32[]{:S(2)}) collective-permute-start(bf16[144,1024]{1,0:T(8,128)(2,1)S(1)} %pad_maximum_fusion.2.refs_0_), channel_id=1, source_target_pairs={{0,8},{4,12},{8,0},{12,4},{16,24},{20,28},{24,16},{28,20},{1,9},{5... | collective-permute-start | bytes 884744 | tf_op jit(solution)/shard_map/ppermute | solution.py:551
  13.4 14.5 %collective-permute-start.2 = (bf16[144,1024]{1,0:T(8,128)(2,1)S(1)}, bf16[144,1024]{1,0:T(8,128)(2,1)}, u32[]{:S(2)}, u32[]{:S(2)}) collective-permute-start(bf16[144,1024]{1,0:T(8,128)(2,1)S(1)} %pad_maximum_fusion.2.refs_0_), channel_id=1, source_target_pairs={{0,16},{4,20},{8,24},{12,28},{16,0},{20,4},{24,8},{28,12},{1,17},{... | collective-permute-start | bytes 884744 | tf_op jit(solution)/shard_map/ppermute | solution.py:551
  15.0 13.3 %collective-permute-start.3 = (bf16[144,1024]{1,0:T(8,128)(2,1)S(1)}, bf16[144,1024]{1,0:T(8,128)(2,1)}, u32[]{:S(2)}, u32[]{:S(2)}) collective-permute-start(bf16[144,1024]{1,0:T(8,128)(2,1)S(1)} %pad_maximum_fusion.2.refs_0_), channel_id=1, source_target_pairs={{0,24},{4,28},{8,16},{12,20},{16,8},{20,12},{24,0},{28,4},{1,25},{... | collective-permute-start | bytes 884744 | tf_op jit(solution)/shard_map/ppermute | solution.py:551
  28.2 13.5 %collective-permute-start.8 = (bf16[320,1024]{1,0:T(8,128)(2,1)S(1)}, bf16[320,1024]{1,0:T(8,128)(2,1)S(1)}, u32[]{:S(2)}, u32[]{:S(2)}) collective-permute-start(bf16[320,1024]{1,0:T(8,128)(2,1)S(1)} %pad_maximum_fusion.1.refs_0_), channel_id=1, source_target_pairs={{0,8},{4,20},{8,0},{12,28},{16,24},{20,4},{24,16},{28,12},{1,9},{5... | collective-permute-start | bytes 1966088 | tf_op jit(solution)/shard_map/ppermute | solution.py:556
  35.9 2.0 %collective-permute-start.6 = (bf16[256,1024]{1,0:T(8,128)(2,1)S(1)}, bf16[256,1024]{1,0:T(8,128)(2,1)S(1)}, u32[]{:S(2)}, u32[]{:S(2)}) collective-permute-start(bf16[256,1024]{1,0:T(8,128)(2,1)S(1)} %collective-permute-done.4.refs_0_.refs_4_), channel_id=1, source_target_pairs={{0,4},{4,0},{8,12},{12,8},{16,20},{20,16},{24,28},{28,24},{1,5},{5... | collective-permute-start | bytes 1572872 | tf_op jit(solution)/shard_map/ppermute | solution.py:546
  35.9 2.7 %collective-permute-start.7 = (bf16[256,1024]{1,0:T(8,128)(2,1)S(1)}, bf16[256,1024]{1,0:T(8,128)(2,1)S(1)}, u32[]{:S(2)}, u32[]{:S(2)}) collective-permute-start(bf16[256,1024]{1,0:T(8,128)(2,1)S(1)} %collective-permute-done.5.refs_1_.refs_5_), channel_id=1, source_target_pairs={{0,4},{4,0},{8,12},{12,8},{16,20},{20,16},{24,28},{28,24},{1,5},{5... | collective-permute-start | bytes 1572872 | tf_op jit(solution)/shard_map/ppermute | solution.py:546
  36.4 18.3 %collective-permute-start.9 = (bf16[320,1024]{1,0:T(8,128)(2,1)S(1)}, bf16[320,1024]{1,0:T(8,128)(2,1)S(1)}, u32[]{:S(2)}, u32[]{:S(2)}) collective-permute-start(bf16[320,1024]{1,0:T(8,128)(2,1)S(1)} %pad_maximum_fusion.1.refs_0_), channel_id=1, source_target_pairs={{0,16},{4,12},{8,24},{12,4},{16,0},{20,28},{24,8},{28,20},{1,17},{... | collective-permute-start | bytes 1966088 | tf_op jit(solution)/shard_map/ppermute | solution.py:556
  41.8 13.0 %collective-permute-start.10 = (bf16[320,1024]{1,0:T(8,128)(2,1)S(1)}, bf16[320,1024]{1,0:T(8,128)(2,1)S(1)}, u32[]{:S(2)}, u32[]{:S(2)}) collective-permute-start(bf16[320,1024]{1,0:T(8,128)(2,1)S(1)} %collective-permute-done.8.refs_1_), channel_id=1, source_target_pairs={{0,16},{4,12},{8,24},{12,4},{16,0},{20,28},{24,8},{28,20},{1,17},{... | collective-permute-start | bytes 1966088 | tf_op jit(solution)/shard_map/ppermute | solution.py:556
  54.7 2.0 %collective-permute-start.11 = (bf16[1024,256]{1,0:T(8,128)(2,1)S(1)}, bf16[1024,256]{1,0:T(8,128)(2,1)S(1)}, u32[]{:S(2)}, u32[]{:S(2)}) collective-permute-start(bf16[1024,256]{1,0:T(8,128)(2,1)S(1)} %get-tuple-element.181.refs_9_.o_ref), channel_id=1, source_target_pairs={{0,4},{4,0},{8,12},{12,8},{16,20},{20,16},{24,28},{28,24},{1,5},{5... | collective-permute-start | bytes 1572872 | tf_op jit(solution)/shard_map/ppermute | solution.py:546
  67.9 4.1 %collective-permute-start.12 = (bf16[1024,512]{1,0:T(8,128)(2,1)S(1)}, bf16[1024,512]{1,0:T(8,128)(2,1)S(1)}, u32[]{:S(2)}, u32[]{:S(2)}) collective-permute-start(bf16[1024,512]{1,0:T(8,128)(2,1)S(1)} %get-tuple-element.185.dh_ref), channel_id=1, source_target_pairs={{0,4},{4,0},{8,12},{12,8},{16,20},{20,16},{24,28},{28,24},{1,5},{5... | collective-permute-start | bytes 3145736 | tf_op jit(solution)/shard_map/ppermute | solution.py:546
  68.1 3.9 %collective-permute-start.13 = (bf16[512,512]{1,0:T(8,128)(2,1)S(1)}, bf16[512,512]{1,0:T(8,128)(2,1)S(1)}, u32[]{:S(2)}, u32[]{:S(2)}) collective-permute-start(bf16[512,512]{1,0:T(8,128)(2,1)S(1)} %get-tuple-element.188), channel_id=1, source_target_pairs={{0,4},{4,0},{8,12},{12,8},{16,20},{20,16},{24,28},{28,24},{1,5},{5... | collective-permute-start | bytes 1572872 | tf_op jit(solution)/shard_map/ppermute | solution.py:546
  68.5 17.3 %collective-permute-start.16 = (bf16[264,1024]{1,0:T(8,128)(2,1)S(1)}, bf16[264,1024]{1,0:T(8,128)(2,1)S(1)}, u32[]{:S(2)}, u32[]{:S(2)}) collective-permute-start(bf16[264,1024]{1,0:T(8,128)(2,1)S(1)} %get-tuple-element.218), channel_id=1, source_target_pairs={{0,8},{4,12},{8,0},{12,4},{16,24},{20,28},{24,16},{28,20},{1,9},{5... | collective-permute-start | bytes 1622024 | tf_op jit(solution)/shard_map/ppermute | solution.py:551
  69.9 25.6 %collective-permute-start.17 = (bf16[264,1024]{1,0:T(8,128)(2,1)S(1)}, bf16[264,1024]{1,0:T(8,128)(2,1)S(1)}, u32[]{:S(2)}, u32[]{:S(2)}) collective-permute-start(bf16[264,1024]{1,0:T(8,128)(2,1)S(1)} %get-tuple-element.219), channel_id=1, source_target_pairs={{0,16},{4,20},{8,24},{12,28},{16,0},{20,4},{24,8},{28,12},{1,17},{... | collective-permute-start | bytes 1622024 | tf_op jit(solution)/shard_map/ppermute | solution.py:551
  70.7 24.9 %collective-permute-start.18 = (bf16[264,1024]{1,0:T(8,128)(2,1)S(1)}, bf16[264,1024]{1,0:T(8,128)(2,1)S(1)}, u32[]{:S(2)}, u32[]{:S(2)}) collective-permute-start(bf16[264,1024]{1,0:T(8,128)(2,1)S(1)} %get-tuple-element.220), channel_id=1, source_target_pairs={{0,24},{4,28},{8,16},{12,20},{16,8},{20,12},{24,0},{28,4},{1,25},{... | collective-permute-start | bytes 1622024 | tf_op jit(solution)/shard_map/ppermute | solution.py:551
  75.4 20.2 %collective-permute-start.14 = (bf16[256,512]{1,0:T(8,128)(2,1)S(1)}, bf16[256,512]{1,0:T(8,128)(2,1)S(1)}, u32[]{:S(2)}, u32[]{:S(2)}) collective-permute-start(bf16[256,512]{1,0:T(8,128)(2,1)S(1)} %get-tuple-element.216), channel_id=1, source_target_pairs={{0,0},{4,1},{1,2},{5,3},{2,4},{6,5},{3,6},{7,7},{8,8},{12,9},{9,10... | collective-permute-start | bytes 786440 | tf_op jit(solution)/shard_map/ppermute | solution.py:1146
  76.0 19.5 %collective-permute-start.15 = (bf16[256,512]{1,0:T(8,128)(2,1)S(1)}, bf16[256,512]{1,0:T(8,128)(2,1)S(1)}, u32[]{:S(2)}, u32[]{:S(2)}) collective-permute-start(bf16[256,512]{1,0:T(8,128)(2,1)S(1)} %get-tuple-element.217), channel_id=1, source_target_pairs={{1,0},{5,1},{0,2},{4,3},{3,4},{7,5},{2,6},{6,7},{9,8},{13,9},{8,10... | collective-permute-start | bytes 786440 | tf_op jit(solution)/shard_map/ppermute | solution.py:1146
  96.4 8.5 %collective-permute-start.23 = (bf16[264,512]{1,0:T(8,128)(2,1)S(1)}, bf16[264,512]{1,0:T(8,128)(2,1)S(1)}, u32[]{:S(2)}, u32[]{:S(2)}) collective-permute-start(bf16[264,512]{1,0:T(8,128)(2,1)S(1)} %get-tuple-element.251), channel_id=1, source_target_pairs={{0,1},{1,0},{2,3},{3,2},{4,5},{5,4},{6,7},{7,6},{8,9},{9,8},{10,11... | collective-permute-start | bytes 811016 | tf_op jit(solution)/shard_map/ppermute | solution.py:561
  101.3 5.1 %collective-permute-start.25 = (bf16[512,512]{1,0:T(8,128)(2,1)S(1)}, bf16[512,512]{1,0:T(8,128)(2,1)S(1)}, u32[]{:S(2)}, u32[]{:S(2)}) collective-permute-start(bf16[512,512]{1,0:T(8,128)(2,1)S(1)} %get-tuple-element.253), channel_id=1, source_target_pairs={{0,4},{4,0},{8,12},{12,8},{16,20},{20,16},{24,28},{28,24},{1,5},{5... | collective-permute-start | bytes 1572872 | tf_op jit(solution)/shard_map/ppermute | solution.py:546
  101.4 10.9 %collective-permute-start.19 = (bf16[168,1024]{1,0:T(8,128)(2,1)S(1)}, bf16[168,1024]{1,0:T(8,128)(2,1)S(1)}, u32[]{:S(2)}, u32[]{:S(2)}) collective-permute-start(bf16[168,1024]{1,0:T(8,128)(2,1)S(1)} %get-tuple-element.245), channel_id=1, source_target_pairs={{0,8},{4,12},{8,0},{12,4},{16,24},{20,28},{24,16},{28,20},{1,9},{5... | collective-permute-start | bytes 1032200 | tf_op jit(solution)/shard_map/ppermute | solution.py:551
  103.2 17.5 %collective-permute-start.20 = (bf16[168,1024]{1,0:T(8,128)(2,1)S(1)}, bf16[168,1024]{1,0:T(8,128)(2,1)S(1)}, u32[]{:S(2)}, u32[]{:S(2)}) collective-permute-start(bf16[168,1024]{1,0:T(8,128)(2,1)S(1)} %get-tuple-element.246), channel_id=1, source_target_pairs={{0,16},{4,20},{8,24},{12,28},{16,0},{20,4},{24,8},{28,12},{1,17},{... | collective-permute-start | bytes 1032200 | tf_op jit(solution)/shard_map/ppermute | solution.py:551
  103.7 17.0 %collective-permute-start.21 = (bf16[168,1024]{1,0:T(8,128)(2,1)S(1)}, bf16[168,1024]{1,0:T(8,128)(2,1)S(1)}, u32[]{:S(2)}, u32[]{:S(2)}) collective-permute-start(bf16[168,1024]{1,0:T(8,128)(2,1)S(1)} %get-tuple-element.247), channel_id=1, source_target_pairs={{0,24},{4,28},{8,16},{12,20},{16,8},{20,12},{24,0},{28,4},{1,25},{... | collective-permute-start | bytes 1032200 | tf_op jit(solution)/shard_map/ppermute | solution.py:551
  105.0 23.4 %collective-permute-start.24 = (bf16[264,512]{1,0:T(8,128)(2,1)S(1)}, bf16[264,512]{1,0:T(8,128)(2,1)S(1)}, u32[]{:S(2)}, u32[]{:S(2)}) collective-permute-start(bf16[264,512]{1,0:T(8,128)(2,1)S(1)} %add_convert_fusion.2), channel_id=1, source_target_pairs={{0,2},{1,3},{2,0},{3,1},{4,6},{5,7},{6,4},{7,5},{8,10},{9,11},{10,... | collective-permute-start | bytes 811016 | tf_op jit(solution)/shard_map/ppermute | solution.py:561
  107.9 20.6 %collective-permute-start.26 = (bf16[256,512]{1,0:T(8,128)(2,1)S(1)}, bf16[256,512]{1,0:T(8,128)(2,1)S(1)}, u32[]{:S(2)}, u32[]{:S(2)}) collective-permute-start(bf16[256,512]{1,0:T(8,128)(2,1)S(1)} %get-tuple-element.255), channel_id=1, source_target_pairs={{0,0},{4,1},{1,2},{5,3},{2,4},{6,5},{3,6},{7,7},{8,8},{12,9},{9,10... | collective-permute-start | bytes 786440 | tf_op jit(solution)/shard_map/ppermute | solution.py:1146
  121.4 7.0 %collective-permute-start.22 = (bf16[168,512]{1,0:T(8,128)(2,1)S(1)}, bf16[168,512]{1,0:T(8,128)(2,1)S(1)}, u32[]{:S(2)}, u32[]{:S(2)}) collective-permute-start(bf16[168,512]{1,0:T(8,128)(2,1)S(1)} %get-tuple-element.249), channel_id=1, source_target_pairs={{0,1},{1,0},{2,3},{3,2},{4,5},{5,4},{6,7},{7,6},{8,9},{9,8},{10,11... | collective-permute-start | bytes 516104 | tf_op jit(solution)/shard_map/ppermute | solution.py:561
  121.6 20.3 %collective-permute-start.30 = (bf16[256,512]{1,0:T(8,128)(2,1)S(1)}, bf16[256,512]{1,0:T(8,128)(2,1)S(1)}, u32[]{:S(2)}, u32[]{:S(2)}) collective-permute-start(bf16[256,512]{1,0:T(8,128)(2,1)S(1)} %get-tuple-element.260), channel_id=1, source_target_pairs={{1,0},{5,1},{0,2},{4,3},{3,4},{7,5},{2,6},{6,7},{9,8},{13,9},{8,10... | collective-permute-start | bytes 786440 | tf_op jit(solution)/shard_map/ppermute | solution.py:1146
  128.5 11.8 %collective-permute-start.27 = (bf16[168,512]{1,0:T(8,128)(2,1)S(1)}, bf16[168,512]{1,0:T(8,128)(2,1)S(1)}, u32[]{:S(2)}, u32[]{:S(2)}) collective-permute-start(bf16[168,512]{1,0:T(8,128)(2,1)S(1)} %add_convert_fusion.4), channel_id=1, source_target_pairs={{0,2},{1,3},{2,0},{3,1},{4,6},{5,7},{6,4},{7,5},{8,10},{9,11},{10,... | collective-permute-start | bytes 516104 | tf_op jit(solution)/shard_map/ppermute | solution.py:561
  130.0 13.6 %collective-permute-start.31 = (bf16[264,512]{1,0:T(8,128)(2,1)S(1)}, bf16[264,512]{1,0:T(8,128)(2,1)S(1)}, u32[]{:S(2)}, u32[]{:S(2)}) collective-permute-start(bf16[264,512]{1,0:T(8,128)(2,1)S(1)} %add_convert_fusion.1.mine), channel_id=1, source_target_pairs={{0,1},{1,0},{2,3},{3,2},{4,5},{5,4},{6,7},{7,6},{8,9},{9,8},{10,11... | collective-permute-start | bytes 811016 | tf_op jit(solution)/shard_map/ppermute | solution.py:561
  140.4 1.3 collective-permute-start.28
  141.8 6.7 %collective-permute-start.29 = (bf16[176,512]{1,0:T(8,128)(2,1)S(1)}, bf16[176,512]{1,0:T(8,128)(2,1)S(1)}, u32[]{:S(2)}, u32[]{:S(2)}) collective-permute-start(bf16[176,512]{1,0:T(8,128)(2,1)S(1)} %pad_maximum_fusion.3.mine), channel_id=1, source_target_pairs={{0,1},{1,0},{2,3},{3,2},{4,5},{5,4},{6,7},{7,6},{8,9},{9,8},{10,11... | collective-permute-start | bytes 540680 | tf_op jit(solution)/shard_map/ppermute | solution.py:561
  143.6 1.9 %collective-permute-start.32 = (bf16[2,72,512]{2,1,0:T(8,128)(2,1)S(1)}, bf16[2,72,512]{2,1,0:T(8,128)(2,1)S(1)}, u32[]{:S(2)}, u32[]{:S(2)}) collective-permute-start(bf16[2,72,512]{2,1,0:T(8,128)(2,1)S(1)} %pad_maximum_fusion.4), channel_id=1, source_target_pairs={{0,4},{4,0},{8,12},{12,8},{16,20},{20,16},{24,28},{28,24},{1,5},{5... | collective-permute-start | bytes 442376 | tf_op jit(solution)/shard_map/ppermute | solution.py:546

commit v8 on v7

--- a/solution.py
+++ b/solution.py
@@ -51,7 +51,7 @@
     tri = lax.broadcasted_iota(jnp.int32, (block, block), 1) <= lax.broadcasted_iota(
         jnp.int32, (block, block), 0
     )
-    for first in range(0, full, block):
+    for first in reversed(range(0, full, block)):
         span = first + block
         q = q_ref[first:span, :].astype(f32)
         qu = (q + bu_ref[...]).astype(bf).astype(f32) * 0.125
@@ -120,7 +120,7 @@
     flip = jnp.where(rows + cols == block - 1, 1.0, 0.0).astype(bf)
     for ref in (dk_t, dv_t, dr_t, dq_ref, gu_ref, gv_ref):
         ref[...] = jnp.zeros_like(ref)
-    for first in range(0, full, block):
+    for first in reversed(range(0, full, block)):
         span = first + block
 
         def one_block(first=first, span=span):

time: 150 us -> 150 us (level)
  Pallas kernels: 52.4 us -> 60.4 us
  waiting for transfers between devices: 55.6 us -> 47.8 us
    pallas_call x2, Pallas kernels: 6.14 us -> 14 us  [attn_bwd(): pl.pallas_call(functools.partial(attn_bwd_body, block=block, heads=heads)...]
    ppermute x9, waiting for transfers between devices: 33.2 us -> 25.4 us  [swap_chip(): lax.ppermute(values, 'fsdp', [(i, i ^ 2 * mask) for i in range(size)])]
  transfers between devices with their start and end apart: 33 -> 33, of which waited for: 14 -> 14; matrix products, arithmetic and copies ran while one was open for 3% -> 3% of each run, Pallas kernels for 24% -> 30%
where the time goes in v8:
time: 150 us
  Pallas kernels  60.4 us (40%)
  waiting for transfers between devices  47.8 us (32%)
  starting transfers between devices  35.2 us (23%)
  local copies, waits for them, and re-layouts  3.07 us (2%)
  between operations  2.38 us (2%)
    pallas_call x12, Pallas kernels, kernel_call(): pl.pallas_call(body, out_shape=[jax.ShapeDtypeStruct(shape, kind) for sha...  34.9 us
    ppermute x9, waiting for transfers between devices, swap_chip(): lax.ppermute(values, 'fsdp', [(i, i ^ 2 * mask) for i in range(size)])  25.4 us
    ppermute x6, waiting for transfers between devices, swap_seq(): return lax.ppermute(values, 'seq', [(i, i ^ mask) for i in range(size)])  15.3 us
    pallas_call x2, Pallas kernels, attn_bwd(): pl.pallas_call(functools.partial(attn_bwd_body, block=block, heads=heads)...  14 us
    pallas_call x1, Pallas kernels, attn_fwd(): pl.pallas_call(functools.partial(attn_fwd_body, block=block), out_shape=(...  11.4 us
    ppermute x9, starting transfers between devices, swap_chip(): lax.ppermute(values, 'fsdp', [(i, i ^ 2 * mask) for i in range(size)])  10.7 us
    ppermute x4, starting transfers between devices, slot_split_device(): lax.ppermute(out, ('fsdp', 'seq'), [(b, a) for a, b in slot_pairs(turn)])  6.97 us
    ppermute x6, starting transfers between devices, swap_seq(): return lax.ppermute(values, 'seq', [(i, i ^ mask) for i in range(size)])  6.66 us
  transfers between devices with their start and end apart: 33, of which 14 were waited for; matrix products, arithmetic and copies ran while one was open for 3% of the time, Pallas kernels for 30%

profile of v8, /device:TPU:0, one launch (start us, length us, event | category | flops | bytes accessed | tf_op | source)
XLA Modules:
  0.0 150.1 jit_solution(17099346710213616240)
XLA Ops:
  0.7 2.3 %pack.1 = (bf16[72,1024]{1,0:T(8,128)(2,1)S(1)}, bf16[224,1024]{1,0:T(8,128)(2,1)S(1)}, bf16[168,1024]{1,0:T(8,128)(2,1)S(1)}) custom-call(s32[2]{0:T(128)} %lengths_ref.1, bf16[64,1536]{1,0:T(8,128)(2,1)} %qkv_ref.1, bf16[64,512]{1,0:T(8,128)(2,1)} %rel_ref.1, bf16[64,2048]{1,0:T(8,128)(2,1)} %up_ref.1, bf16[64,512]{1,0:T(8,128)(2,1)} %out_ref.1, ...), custom_call_target="tpu_custom_call" | custom-call | tf_op jit(solution)/shard_map/pack/pallas_call | solution.py:597
  3.5 1.1 constant_dynamic-update-slice_fusion.1
  4.7 1.0 dynamic-slice_bitcast_fusion
  5.7 1.7 %collective-permute-start.4 = (bf16[256,1024]{1,0:T(8,128)(2,1)}, bf16[256,1024]{1,0:T(8,128)(2,1)S(1)}, u32[]{:S(2)}, u32[]{:S(2)}) collective-permute-start(bf16[256,1024]{1,0:T(8,128)(2,1)} %get-tuple-element.286), channel_id=1, source_target_pairs={{0,0},{1,4},{2,1},{3,5},{4,2},{5,6},{6,3},{7,7},{8,8},{9,12},{10,9... | collective-permute-start | bytes 1572872 | tf_op jit(solution)/shard_map/ppermute | solution.py:575
  7.4 2.9 %collective-permute-start.5 = (bf16[256,1024]{1,0:T(8,128)(2,1)}, bf16[256,1024]{1,0:T(8,128)(2,1)S(1)}, u32[]{:S(2)}, u32[]{:S(2)}) collective-permute-start(bf16[256,1024]{1,0:T(8,128)(2,1)} %get-tuple-element.285), channel_id=1, source_target_pairs={{0,1},{1,5},{2,0},{3,4},{4,3},{5,7},{6,2},{7,6},{8,9},{9,13},{10,8... | collective-permute-start | bytes 1572872 | tf_op jit(solution)/shard_map/ppermute | solution.py:575
  11.4 2.1 %collective-permute-start.1 = (bf16[144,1024]{1,0:T(8,128)(2,1)S(1)}, bf16[144,1024]{1,0:T(8,128)(2,1)}, u32[]{:S(2)}, u32[]{:S(2)}) collective-permute-start(bf16[144,1024]{1,0:T(8,128)(2,1)S(1)} %pad_maximum_fusion.2.refs_0_), channel_id=1, source_target_pairs={{0,8},{4,12},{8,0},{12,4},{16,24},{20,28},{24,16},{28,20},{1,9},{5... | collective-permute-start | bytes 884744 | tf_op jit(solution)/shard_map/ppermute | solution.py:551
  13.4 1.5 %collective-permute-start.2 = (bf16[144,1024]{1,0:T(8,128)(2,1)S(1)}, bf16[144,1024]{1,0:T(8,128)(2,1)}, u32[]{:S(2)}, u32[]{:S(2)}) collective-permute-start(bf16[144,1024]{1,0:T(8,128)(2,1)S(1)} %pad_maximum_fusion.2.refs_0_), channel_id=1, source_target_pairs={{0,16},{4,20},{8,24},{12,28},{16,0},{20,4},{24,8},{28,12},{1,17},{... | collective-permute-start | bytes 884744 | tf_op jit(solution)/shard_map/ppermute | solution.py:551
  17.0 2.7 %collective-permute-done.1.refs_1_ = bf16[144,1024]{1,0:T(8,128)(2,1)} collective-permute-done((bf16[144,1024]{1,0:T(8,128)(2,1)S(1)}, bf16[144,1024]{1,0:T(8,128)(2,1)}, u32[]{:S(2)}, u32[]{:S(2)}) %collective-permute-start.1) | collective-permute-done | bytes 294944 | tf_op jit(solution)/shard_map/ppermute | solution.py:551
  19.8 8.2 %collective-permute-done.2.refs_2_ = bf16[144,1024]{1,0:T(8,128)(2,1)} collective-permute-done((bf16[144,1024]{1,0:T(8,128)(2,1)S(1)}, bf16[144,1024]{1,0:T(8,128)(2,1)}, u32[]{:S(2)}, u32[]{:S(2)}) %collective-permute-start.2) | collective-permute-done | bytes 294944 | tf_op jit(solution)/shard_map/ppermute | solution.py:551
  28.2 1.4 collective-permute-start.8
  29.6 2.9 %weights.1 = (bf16[1024,256]{1,0:T(8,128)(2,1)S(1)}, bf16[512,1024]{1,0:T(8,128)(2,1)S(1)}, f32[8,512]{1,0:T(8,128)S(1)}, f32[1,1024]{1,0:T(1,128)S(1)}, f32[1,256]{1,0:T(1,128)S(1)}, /*index=5*/f32[1,256]{1,0:T(1,128)S(1)}) custom-call(s32[4]{0:T(128)S(1)} %broadcast_3__.2._, bf16[144,1024]{1,0:T(8,128)(2,1)} %copy-done, ...), custom_call_target="tpu_custom_call" | custom-call | tf_op jit(solution)/shard_map/weights/pallas_call | solution.py:597
  32.6 3.3 %collective-permute-done.5.refs_1_.refs_5_ = bf16[256,1024]{1,0:T(8,128)(2,1)S(1)} collective-permute-done((bf16[256,1024]{1,0:T(8,128)(2,1)}, bf16[256,1024]{1,0:T(8,128)(2,1)S(1)}, u32[]{:S(2)}, u32[]{:S(2)}) %collective-permute-start.5) | collective-permute-done | bytes 524320 | tf_op jit(solution)/shard_map/ppermute | solution.py:575
  36.4 1.5 %collective-permute-start.9 = (bf16[320,1024]{1,0:T(8,128)(2,1)S(1)}, bf16[320,1024]{1,0:T(8,128)(2,1)S(1)}, u32[]{:S(2)}, u32[]{:S(2)}) collective-permute-start(bf16[320,1024]{1,0:T(8,128)(2,1)S(1)} %pad_maximum_fusion.1.refs_0_), channel_id=1, source_target_pairs={{0,16},{4,12},{8,24},{12,4},{16,0},{20,28},{24,8},{28,20},{1,17},{... | collective-permute-start | bytes 1966088 | tf_op jit(solution)/shard_map/ppermute | solution.py:556
  38.5 3.2 %project.1 = (bf16[1024,768]{1,0:T(8,128)(2,1)S(1)}, bf16[1024,512]{1,0:T(8,128)(2,1)S(1)}, bf16[1024,512]{1,0:T(8,128)(2,1)S(1)}) custom-call(s32[4]{0:T(128)S(1)} %broadcast_3__.2._, bf16[256,1024]{1,0:T(8,128)(2,1)S(1)} %collective-permute-done.4.refs_0_.refs_4_, bf16[256,1024]{1,0:T(8,128)(2,1)S(1)} %collective-permute-done.5.refs_1_.refs_5_, ...), custom_call_target="tpu_custom_call" | custom-call | tf_op jit(solution)/shard_map/project/pallas_call | solution.py:597
  41.8 1.6 %collective-permute-start.10 = (bf16[320,1024]{1,0:T(8,128)(2,1)S(1)}, bf16[320,1024]{1,0:T(8,128)(2,1)S(1)}, u32[]{:S(2)}, u32[]{:S(2)}) collective-permute-start(bf16[320,1024]{1,0:T(8,128)(2,1)S(1)} %collective-permute-done.8.refs_1_), channel_id=1, source_target_pairs={{0,16},{4,12},{8,24},{12,4},{16,0},{20,28},{24,8},{28,20},{1,17},{... | collective-permute-start | bytes 1966088 | tf_op jit(solution)/shard_map/ppermute | solution.py:556
  43.3 11.4 %attn_fwd.1 = (bf16[1024,256]{1,0:T(8,128)(2,1)S(1)}, f32[1024,256]{1,0:T(8,128)S(1)}, bf16[4,256,256]{2,1,0:T(8,128)(2,1)S(1)}, bf16[4,256,512]{2,1,0:T(8,128)(...) custom-call(s32[1]{0:T(128)} %bitcast.15.len_ref, ...), custom_call_target="tpu_custom_call" | custom-call | tf_op jit(solution)/shard_map/attn_fwd/pallas_call | solution.py:88
  54.9 1.9 %collective-permute-done.11.refs_10_ = bf16[1024,256]{1,0:T(8,128)(2,1)S(1)} collective-permute-done((bf16[1024,256]{1,0:T(8,128)(2,1)S(1)}, bf16[1024,256]{1,0:T(8,128)(2,1)S(1)}, u32[]{:S(2)}, u32[]{:S(2)}) %collective-permute-start.11) | collective-permute-done | bytes 524320 | tf_op jit(solution)/shard_map/ppermute | solution.py:546
  56.8 11.2 %feed.1 = (bf16[1024,512]{1,0:T(8,128)(2,1)S(1)}, bf16[1024,512]{1,0:T(8,128)(2,1)S(1)}, f32[1024,1]{1,0:T(8,128)S(1)}, f32[512,512]{1,0:T(8,128)S(1)}, bf16[102...) custom-call(s32[4]{0:T(128)S(1)} %pad_add_fusion.meta, ...), custom_call_target="tpu_custom_call" | custom-call | tf_op jit(solution)/shard_map/feed/pallas_call | solution.py:597
  68.5 1.5 %collective-permute-start.16 = (bf16[264,1024]{1,0:T(8,128)(2,1)S(1)}, bf16[264,1024]{1,0:T(8,128)(2,1)S(1)}, u32[]{:S(2)}, u32[]{:S(2)}) collective-permute-start(bf16[264,1024]{1,0:T(8,128)(2,1)S(1)} %get-tuple-element.218), channel_id=1, source_target_pairs={{0,8},{4,12},{8,0},{12,4},{16,24},{20,28},{24,16},{28,20},{1,9},{5... | collective-permute-start | bytes 1622024 | tf_op jit(solution)/shard_map/ppermute | solution.py:551
  70.7 1.4 collective-permute-start.18
  72.0 3.4 %norm_two.1 = (bf16[256,512]{1,0:T(8,128)(2,1)S(1)}, bf16[256,512]{1,0:T(8,128)(2,1)S(1)}, f32[512,512]{1,0:T(8,128)S(1)}, bf16[1024,256]{1,0:T(8,128)(2,1)S(1)}, f32[256,512]{1,0:T(8,128)S(1)}) custom-call(s32[4]{0:T(128)S(1)} %pad_add_fusion.meta, bf16[1024,512]{1,0:T(8,128)(2,1)S(1)} %get-tuple-element.183.x_hat_ref, ...), custom_call_target="tpu_custom_call" | custom-call | tf_op jit(solution)/shard_map/norm_two/pallas_call | solution.py:597
  75.4 0.7 collective-permute-start.14
  76.1 3.6 %collective-permute-start.15 = (bf16[256,512]{1,0:T(8,128)(2,1)S(1)}, bf16[256,512]{1,0:T(8,128)(2,1)S(1)}, u32[]{:S(2)}, u32[]{:S(2)}) collective-permute-start(bf16[256,512]{1,0:T(8,128)(2,1)S(1)} %get-tuple-element.217), channel_id=1, source_target_pairs={{1,0},{5,1},{0,2},{4,3},{3,4},{7,5},{2,6},{6,7},{9,8},{13,9},{8,10... | collective-permute-start | bytes 786440 | tf_op jit(solution)/shard_map/ppermute | solution.py:1146
  79.7 6.9 %attn_bwd.2 = (bf16[1024,128]{1,0:T(8,128)(2,1)S(1)}, bf16[1024,128]{1,0:T(8,128)(2,1)S(1)}, bf16[1024,128]{1,0:T(8,128)(2,1)S(1)}, bf16[1024,128]{1,0:T(8,128)(...) custom-call(s32[1]{0:T(128)} %bitcast.15.len_ref, bf16[1024,768]{1,0:T(8,128)(2,1)S(1)} %get-tuple-element.173.q_ref.k_ref.v_ref, ...), custom_call_target="tpu_custom_call" | custom-call | tf_op jit(solution)/shard_map/attn_bwd/pallas_call | solution.py:174
  86.6 7.1 %attn_bwd.3 = (bf16[1024,128]{1,0:T(8,128)(2,1)S(1)}, bf16[1024,128]{1,0:T(8,128)(2,1)S(1)}, bf16[1024,128]{1,0:T(8,128)(2,1)S(1)}, bf16[1024,128]{1,0:T(8,128)(...) custom-call(s32[1]{0:T(128)} %bitcast.15.len_ref, bf16[1024,768]{1,0:T(8,128)(2,1)S(1)} %get-tuple-element.173.q_ref.k_ref.v_ref, ...), custom_call_target="tpu_custom_call" | custom-call | tf_op jit(solution)/shard_map/attn_bwd/pallas_call | solution.py:174
  93.7 1.9 %collective-permute-done.17.refs_1_ = bf16[264,1024]{1,0:T(8,128)(2,1)S(1)} collective-permute-done((bf16[264,1024]{1,0:T(8,128)(2,1)S(1)}, bf16[264,1024]{1,0:T(8,128)(2,1)S(1)}, u32[]{:S(2)}, u32[]{:S(2)}) %collective-permute-start.17) | collective-permute-done | bytes 540704 | tf_op jit(solution)/shard_map/ppermute | solution.py:551
  95.7 0.8 early_chips.1
  96.5 0.7 collective-permute-start.23
  97.2 4.1 %qkv_back.1 = (f32[512,512]{1,0:T(8,128)S(1)}, bf16[512,512]{1,0:T(8,128)(2,1)S(1)}, f32[168,1024]{1,0:T(8,128)S(1)}, bf16[168,1024]{1,0:T(8,128)(2,1)S(1)}, bf1...) custom-call(s32[4]{0:T(128)S(1)} %pad_add_fusion.meta, bf16[1024,128]{1,0:T(8,128)(2,1)S(1)} %get-tuple-element.202.refs_0_, ...), custom_call_target="tpu_custom_call" | custom-call | tf_op jit(solution)/shard_map/qkv_back/pallas_call | solution.py:597
  101.5 1.8 %collective-permute-start.19 = (bf16[168,1024]{1,0:T(8,128)(2,1)S(1)}, bf16[168,1024]{1,0:T(8,128)(2,1)S(1)}, u32[]{:S(2)}, u32[]{:S(2)}) collective-permute-start(bf16[168,1024]{1,0:T(8,128)(2,1)S(1)} %get-tuple-element.245), channel_id=1, source_target_pairs={{0,8},{4,12},{8,0},{12,4},{16,24},{20,28},{24,16},{28,20},{1,9},{5... | collective-permute-start | bytes 1032200 | tf_op jit(solution)/shard_map/ppermute | solution.py:551
  103.8 1.2 collective-permute-start.21
  105.1 1.4 collective-permute-start.24
  106.5 1.4 norm_one.1
  107.9 0.7 collective-permute-start.26
  108.6 3.8 %collective-permute-done.19.refs_0_ = bf16[168,1024]{1,0:T(8,128)(2,1)S(1)} collective-permute-done((bf16[168,1024]{1,0:T(8,128)(2,1)S(1)}, bf16[168,1024]{1,0:T(8,128)(2,1)S(1)}, u32[]{:S(2)}, u32[]{:S(2)}) %collective-permute-start.19) | collective-permute-done | bytes 344096 | tf_op jit(solution)/shard_map/ppermute | solution.py:551
  112.4 8.4 %collective-permute-done.20.refs_1_ = bf16[168,1024]{1,0:T(8,128)(2,1)S(1)} collective-permute-done((bf16[168,1024]{1,0:T(8,128)(2,1)S(1)}, bf16[168,1024]{1,0:T(8,128)(2,1)S(1)}, u32[]{:S(2)}, u32[]{:S(2)}) %collective-permute-start.20) | collective-permute-done | bytes 344096 | tf_op jit(solution)/shard_map/ppermute | solution.py:551
  120.8 0.7 late_chips.1
  121.7 2.1 %collective-permute-start.30 = (bf16[256,512]{1,0:T(8,128)(2,1)S(1)}, bf16[256,512]{1,0:T(8,128)(2,1)S(1)}, u32[]{:S(2)}, u32[]{:S(2)}) collective-permute-start(bf16[256,512]{1,0:T(8,128)(2,1)S(1)} %get-tuple-element.260), channel_id=1, source_target_pairs={{1,0},{5,1},{0,2},{4,3},{3,4},{7,5},{2,6},{6,7},{9,8},{13,9},{8,10... | collective-permute-start | bytes 786440 | tf_op jit(solution)/shard_map/ppermute | solution.py:1146
  123.7 4.8 %collective-permute-done.22 = bf16[168,512]{1,0:T(8,128)(2,1)S(1)} collective-permute-done((bf16[168,512]{1,0:T(8,128)(2,1)S(1)}, bf16[168,512]{1,0:T(8,128)(2,1)S(1)}, u32[]{:S(2)}, u32[]{:S(2)}) %collective-permute-start.22) | collective-permute-done | bytes 172064 | tf_op jit(solution)/shard_map/ppermute | solution.py:561
  128.6 1.4 collective-permute-start.27
  130.1 2.9 %collective-permute-start.31 = (bf16[264,512]{1,0:T(8,128)(2,1)S(1)}, bf16[264,512]{1,0:T(8,128)(2,1)S(1)}, u32[]{:S(2)}, u32[]{:S(2)}) collective-permute-start(bf16[264,512]{1,0:T(8,128)(2,1)S(1)} %add_convert_fusion.1.mine), channel_id=1, source_target_pairs={{0,1},{1,0},{2,3},{3,2},{4,5},{5,4},{6,7},{7,6},{8,9},{9,8},{10,11... | collective-permute-start | bytes 811016 | tf_op jit(solution)/shard_map/ppermute | solution.py:561
  132.9 7.5 %collective-permute-done.27 = bf16[168,512]{1,0:T(8,128)(2,1)S(1)} collective-permute-done((bf16[168,512]{1,0:T(8,128)(2,1)S(1)}, bf16[168,512]{1,0:T(8,128)(2,1)S(1)}, u32[]{:S(2)}, u32[]{:S(2)}) %collective-permute-start.27) | collective-permute-done | bytes 172064 | tf_op jit(solution)/shard_map/ppermute | solution.py:561
  140.6 1.2 collective-permute-done.28
  142.0 1.7 %collective-permute-done.31.other = bf16[264,512]{1,0:T(8,128)(2,1)S(1)} collective-permute-done((bf16[264,512]{1,0:T(8,128)(2,1)S(1)}, bf16[264,512]{1,0:T(8,128)(2,1)S(1)}, u32[]{:S(2)}, u32[]{:S(2)}) %collective-permute-start.31) | collective-permute-done | bytes 270368 | tf_op jit(solution)/shard_map/ppermute | solution.py:561
  143.8 1.8 %place.1 = (bf16[2,256,512]{2,1,0:T(8,128)(2,1)}, f32[2,256,512]{2,1,0:T(8,128)}) custom-call(s32[4]{0:T(128)S(1)} %pad_add_fusion.meta, bf16[256,512]{1,0:T(8,128)(2,1)S(1)} %collective-permute-done.14.y0, bf16[256,512]{1,0:T(8,128)(2,1)S(1)} %collective-permute-done.15.y1, bf16[256,512]{1,0:T(8,128)(2,1)S(1)} %collective-permute-done.26.x0, ...), custom_call_target="tpu_custom_call" | custom-call | tf_op jit(solution)/shard_map/place/pallas_call | solution.py:597
  145.5 1.6 %early_out.1 = (f32[64,2048]{1,0:T(8,128)}, f32[256,512]{1,0:T(8,128)}, f32[1,64]{1,0:T(1,128)}, f32[1,64]{1,0:T(1,128)}, f32[1,64]{1,0:T(1,128)}, /*index=5*/f32[1,256]{1,0:T(1,128)}) custom-call(s32[4]{0:T(128)S(1)} %pad_add_fusion.meta, bf16[264,512]{1,0:T(8,128)(2,1)S(1)} %add_convert_fusion.1.mine, bf16[264,512]{1,0:T(8,128)(2,1)S(1)} %collective-permute-done.31.other, ...), custom_call_target="tpu_custom_call" | custom-call | tf_op jit(solution)/shard_map/early_out/pallas_call | solution.py:597
  147.1 1.4 collective-permute-done.29.other
  148.5 1.5 %late_out.1 = (f32[64,1536]{1,0:T(8,128)}, f32[64,512]{1,0:T(8,128)}, f32[64,512]{1,0:T(8,128)}, f32[1,64]{1,0:T(1,128)}, f32[1,64]{1,0:T(1,128)}, /*index=5*/f32[1,64]{1,0:T(1,128)}, f32[1,64]{1,0:T(1,128)}) custom-call(s32[4]{0:T(128)S(1)} %pad_add_fusion.meta, bf16[176,512]{1,0:T(8,128)(2,1)S(1)} %pad_maximum_fusion.3.mine, ...), custom_call_target="tpu_custom_call" | custom-call | tf_op jit(solution)/shard_map/late_out/pallas_call | solution.py:597
  (74 shorter events, 6.4 us)
Async XLA Ops:
  0.7 3.9 %copy-start.1 = (bf16[2,256,512]{2,1,0:T(8,128)(2,1)S(1)}, bf16[2,256,512]{2,1,0:T(8,128)(2,1)}, u32[]{:S(2)}) copy-start(bf16[2,256,512]{2,1,0:T(8,128)(2,1)} %param.31) | copy-start | bytes 1572868
  2.9 8.1 %collective-permute-start = (bf16[168,1024]{1,0:T(8,128)(2,1)S(1)}, bf16[168,1024]{1,0:T(8,128)(2,1)S(1)}, u32[]{:S(2)}, u32[]{:S(2)}) collective-permute-start(bf16[168,1024]{1,0:T(8,128)(2,1)S(1)} %get-tuple-element.151), channel_id=1, source_target_pairs={{0,4},{4,0},{8,12},{12,8},{16,20},{20,16},{24,28},{28,24},{1,5},{5... | collective-permute-start | bytes 1032200 | tf_op jit(solution)/shard_map/ppermute | solution.py:546
  5.7 26.9 %collective-permute-start.4 = (bf16[256,1024]{1,0:T(8,128)(2,1)}, bf16[256,1024]{1,0:T(8,128)(2,1)S(1)}, u32[]{:S(2)}, u32[]{:S(2)}) collective-permute-start(bf16[256,1024]{1,0:T(8,128)(2,1)} %get-tuple-element.286), channel_id=1, source_target_pairs={{0,0},{1,4},{2,1},{3,5},{4,2},{5,6},{6,3},{7,7},{8,8},{9,12},{10,9... | collective-permute-start | bytes 1572872 | tf_op jit(solution)/shard_map/ppermute | solution.py:575
  7.4 28.5 %collective-permute-start.5 = (bf16[256,1024]{1,0:T(8,128)(2,1)}, bf16[256,1024]{1,0:T(8,128)(2,1)S(1)}, u32[]{:S(2)}, u32[]{:S(2)}) collective-permute-start(bf16[256,1024]{1,0:T(8,128)(2,1)} %get-tuple-element.285), channel_id=1, source_target_pairs={{0,1},{1,5},{2,0},{3,4},{4,3},{5,7},{6,2},{7,6},{8,9},{9,13},{10,8... | collective-permute-start | bytes 1572872 | tf_op jit(solution)/shard_map/ppermute | solution.py:575
  10.9 4.1 %copy-start.2 = (s32[2]{0:T(128)S(1)}, s32[2]{0:T(128)}, u32[]{:S(2)}) copy-start(s32[2]{0:T(128)} %lengths_ref.1) | copy-start | bytes 28
  11.3 18.3 %copy-start = (bf16[144,1024]{1,0:T(8,128)(2,1)}, bf16[144,1024]{1,0:T(8,128)(2,1)S(1)}, u32[]{:S(2)}) copy-start(bf16[144,1024]{1,0:T(8,128)(2,1)S(1)} %pad_maximum_fusion.2.refs_0_) | copy-start | bytes 884740
  11.4 8.4 %collective-permute-start.1 = (bf16[144,1024]{1,0:T(8,128)(2,1)S(1)}, bf16[144,1024]{1,0:T(8,128)(2,1)}, u32[]{:S(2)}, u32[]{:S(2)}) collective-permute-start(bf16[144,1024]{1,0:T(8,128)(2,1)S(1)} %pad_maximum_fusion.2.refs_0_), channel_id=1, source_target_pairs={{0,8},{4,12},{8,0},{12,4},{16,24},{20,28},{24,16},{28,20},{1,9},{5... | collective-permute-start | bytes 884744 | tf_op jit(solution)/shard_map/ppermute | solution.py:551
  13.4 14.5 %collective-permute-start.2 = (bf16[144,1024]{1,0:T(8,128)(2,1)S(1)}, bf16[144,1024]{1,0:T(8,128)(2,1)}, u32[]{:S(2)}, u32[]{:S(2)}) collective-permute-start(bf16[144,1024]{1,0:T(8,128)(2,1)S(1)} %pad_maximum_fusion.2.refs_0_), channel_id=1, source_target_pairs={{0,16},{4,20},{8,24},{12,28},{16,0},{20,4},{24,8},{28,12},{1,17},{... | collective-permute-start | bytes 884744 | tf_op jit(solution)/shard_map/ppermute | solution.py:551
  15.0 13.3 %collective-permute-start.3 = (bf16[144,1024]{1,0:T(8,128)(2,1)S(1)}, bf16[144,1024]{1,0:T(8,128)(2,1)}, u32[]{:S(2)}, u32[]{:S(2)}) collective-permute-start(bf16[144,1024]{1,0:T(8,128)(2,1)S(1)} %pad_maximum_fusion.2.refs_0_), channel_id=1, source_target_pairs={{0,24},{4,28},{8,16},{12,20},{16,8},{20,12},{24,0},{28,4},{1,25},{... | collective-permute-start | bytes 884744 | tf_op jit(solution)/shard_map/ppermute | solution.py:551
  28.2 13.5 %collective-permute-start.8 = (bf16[320,1024]{1,0:T(8,128)(2,1)S(1)}, bf16[320,1024]{1,0:T(8,128)(2,1)S(1)}, u32[]{:S(2)}, u32[]{:S(2)}) collective-permute-start(bf16[320,1024]{1,0:T(8,128)(2,1)S(1)} %pad_maximum_fusion.1.refs_0_), channel_id=1, source_target_pairs={{0,8},{4,20},{8,0},{12,28},{16,24},{20,4},{24,16},{28,12},{1,9},{5... | collective-permute-start | bytes 1966088 | tf_op jit(solution)/shard_map/ppermute | solution.py:556
  35.9 2.0 %collective-permute-start.6 = (bf16[256,1024]{1,0:T(8,128)(2,1)S(1)}, bf16[256,1024]{1,0:T(8,128)(2,1)S(1)}, u32[]{:S(2)}, u32[]{:S(2)}) collective-permute-start(bf16[256,1024]{1,0:T(8,128)(2,1)S(1)} %collective-permute-done.4.refs_0_.refs_4_), channel_id=1, source_target_pairs={{0,4},{4,0},{8,12},{12,8},{16,20},{20,16},{24,28},{28,24},{1,5},{5... | collective-permute-start | bytes 1572872 | tf_op jit(solution)/shard_map/ppermute | solution.py:546
  35.9 2.7 %collective-permute-start.7 = (bf16[256,1024]{1,0:T(8,128)(2,1)S(1)}, bf16[256,1024]{1,0:T(8,128)(2,1)S(1)}, u32[]{:S(2)}, u32[]{:S(2)}) collective-permute-start(bf16[256,1024]{1,0:T(8,128)(2,1)S(1)} %collective-permute-done.5.refs_1_.refs_5_), channel_id=1, source_target_pairs={{0,4},{4,0},{8,12},{12,8},{16,20},{20,16},{24,28},{28,24},{1,5},{5... | collective-permute-start | bytes 1572872 | tf_op jit(solution)/shard_map/ppermute | solution.py:546
  36.4 18.4 %collective-permute-start.9 = (bf16[320,1024]{1,0:T(8,128)(2,1)S(1)}, bf16[320,1024]{1,0:T(8,128)(2,1)S(1)}, u32[]{:S(2)}, u32[]{:S(2)}) collective-permute-start(bf16[320,1024]{1,0:T(8,128)(2,1)S(1)} %pad_maximum_fusion.1.refs_0_), channel_id=1, source_target_pairs={{0,16},{4,12},{8,24},{12,4},{16,0},{20,28},{24,8},{28,20},{1,17},{... | collective-permute-start | bytes 1966088 | tf_op jit(solution)/shard_map/ppermute | solution.py:556
  41.8 13.0 %collective-permute-start.10 = (bf16[320,1024]{1,0:T(8,128)(2,1)S(1)}, bf16[320,1024]{1,0:T(8,128)(2,1)S(1)}, u32[]{:S(2)}, u32[]{:S(2)}) collective-permute-start(bf16[320,1024]{1,0:T(8,128)(2,1)S(1)} %collective-permute-done.8.refs_1_), channel_id=1, source_target_pairs={{0,16},{4,12},{8,24},{12,4},{16,0},{20,28},{24,8},{28,20},{1,17},{... | collective-permute-start | bytes 1966088 | tf_op jit(solution)/shard_map/ppermute | solution.py:556
  54.8 2.0 %collective-permute-start.11 = (bf16[1024,256]{1,0:T(8,128)(2,1)S(1)}, bf16[1024,256]{1,0:T(8,128)(2,1)S(1)}, u32[]{:S(2)}, u32[]{:S(2)}) collective-permute-start(bf16[1024,256]{1,0:T(8,128)(2,1)S(1)} %get-tuple-element.181.refs_9_.o_ref), channel_id=1, source_target_pairs={{0,4},{4,0},{8,12},{12,8},{16,20},{20,16},{24,28},{28,24},{1,5},{5... | collective-permute-start | bytes 1572872 | tf_op jit(solution)/shard_map/ppermute | solution.py:546
  67.9 4.1 %collective-permute-start.12 = (bf16[1024,512]{1,0:T(8,128)(2,1)S(1)}, bf16[1024,512]{1,0:T(8,128)(2,1)S(1)}, u32[]{:S(2)}, u32[]{:S(2)}) collective-permute-start(bf16[1024,512]{1,0:T(8,128)(2,1)S(1)} %get-tuple-element.185.dh_ref), channel_id=1, source_target_pairs={{0,4},{4,0},{8,12},{12,8},{16,20},{20,16},{24,28},{28,24},{1,5},{5... | collective-permute-start | bytes 3145736 | tf_op jit(solution)/shard_map/ppermute | solution.py:546
  68.2 3.9 %collective-permute-start.13 = (bf16[512,512]{1,0:T(8,128)(2,1)S(1)}, bf16[512,512]{1,0:T(8,128)(2,1)S(1)}, u32[]{:S(2)}, u32[]{:S(2)}) collective-permute-start(bf16[512,512]{1,0:T(8,128)(2,1)S(1)} %get-tuple-element.188), channel_id=1, source_target_pairs={{0,4},{4,0},{8,12},{12,8},{16,20},{20,16},{24,28},{28,24},{1,5},{5... | collective-permute-start | bytes 1572872 | tf_op jit(solution)/shard_map/ppermute | solution.py:546
  68.5 25.2 %collective-permute-start.16 = (bf16[264,1024]{1,0:T(8,128)(2,1)S(1)}, bf16[264,1024]{1,0:T(8,128)(2,1)S(1)}, u32[]{:S(2)}, u32[]{:S(2)}) collective-permute-start(bf16[264,1024]{1,0:T(8,128)(2,1)S(1)} %get-tuple-element.218), channel_id=1, source_target_pairs={{0,8},{4,12},{8,0},{12,4},{16,24},{20,28},{24,16},{28,20},{1,9},{5... | collective-permute-start | bytes 1622024 | tf_op jit(solution)/shard_map/ppermute | solution.py:551
  70.0 25.6 %collective-permute-start.17 = (bf16[264,1024]{1,0:T(8,128)(2,1)S(1)}, bf16[264,1024]{1,0:T(8,128)(2,1)S(1)}, u32[]{:S(2)}, u32[]{:S(2)}) collective-permute-start(bf16[264,1024]{1,0:T(8,128)(2,1)S(1)} %get-tuple-element.219), channel_id=1, source_target_pairs={{0,16},{4,20},{8,24},{12,28},{16,0},{20,4},{24,8},{28,12},{1,17},{... | collective-permute-start | bytes 1622024 | tf_op jit(solution)/shard_map/ppermute | solution.py:551
  70.7 25.0 %collective-permute-start.18 = (bf16[264,1024]{1,0:T(8,128)(2,1)S(1)}, bf16[264,1024]{1,0:T(8,128)(2,1)S(1)}, u32[]{:S(2)}, u32[]{:S(2)}) collective-permute-start(bf16[264,1024]{1,0:T(8,128)(2,1)S(1)} %get-tuple-element.220), channel_id=1, source_target_pairs={{0,24},{4,28},{8,16},{12,20},{16,8},{20,12},{24,0},{28,4},{1,25},{... | collective-permute-start | bytes 1622024 | tf_op jit(solution)/shard_map/ppermute | solution.py:551
  75.4 20.2 %collective-permute-start.14 = (bf16[256,512]{1,0:T(8,128)(2,1)S(1)}, bf16[256,512]{1,0:T(8,128)(2,1)S(1)}, u32[]{:S(2)}, u32[]{:S(2)}) collective-permute-start(bf16[256,512]{1,0:T(8,128)(2,1)S(1)} %get-tuple-element.216), channel_id=1, source_target_pairs={{0,0},{4,1},{1,2},{5,3},{2,4},{6,5},{3,6},{7,7},{8,8},{12,9},{9,10... | collective-permute-start | bytes 786440 | tf_op jit(solution)/shard_map/ppermute | solution.py:1146
  76.1 19.6 %collective-permute-start.15 = (bf16[256,512]{1,0:T(8,128)(2,1)S(1)}, bf16[256,512]{1,0:T(8,128)(2,1)S(1)}, u32[]{:S(2)}, u32[]{:S(2)}) collective-permute-start(bf16[256,512]{1,0:T(8,128)(2,1)S(1)} %get-tuple-element.217), channel_id=1, source_target_pairs={{1,0},{5,1},{0,2},{4,3},{3,4},{7,5},{2,6},{6,7},{9,8},{13,9},{8,10... | collective-permute-start | bytes 786440 | tf_op jit(solution)/shard_map/ppermute | solution.py:1146
  96.5 8.5 %collective-permute-start.23 = (bf16[264,512]{1,0:T(8,128)(2,1)S(1)}, bf16[264,512]{1,0:T(8,128)(2,1)S(1)}, u32[]{:S(2)}, u32[]{:S(2)}) collective-permute-start(bf16[264,512]{1,0:T(8,128)(2,1)S(1)} %get-tuple-element.251), channel_id=1, source_target_pairs={{0,1},{1,0},{2,3},{3,2},{4,5},{5,4},{6,7},{7,6},{8,9},{9,8},{10,11... | collective-permute-start | bytes 811016 | tf_op jit(solution)/shard_map/ppermute | solution.py:561
  101.4 5.1 %collective-permute-start.25 = (bf16[512,512]{1,0:T(8,128)(2,1)S(1)}, bf16[512,512]{1,0:T(8,128)(2,1)S(1)}, u32[]{:S(2)}, u32[]{:S(2)}) collective-permute-start(bf16[512,512]{1,0:T(8,128)(2,1)S(1)} %get-tuple-element.253), channel_id=1, source_target_pairs={{0,4},{4,0},{8,12},{12,8},{16,20},{20,16},{24,28},{28,24},{1,5},{5... | collective-permute-start | bytes 1572872 | tf_op jit(solution)/shard_map/ppermute | solution.py:546
  101.5 10.9 %collective-permute-start.19 = (bf16[168,1024]{1,0:T(8,128)(2,1)S(1)}, bf16[168,1024]{1,0:T(8,128)(2,1)S(1)}, u32[]{:S(2)}, u32[]{:S(2)}) collective-permute-start(bf16[168,1024]{1,0:T(8,128)(2,1)S(1)} %get-tuple-element.245), channel_id=1, source_target_pairs={{0,8},{4,12},{8,0},{12,4},{16,24},{20,28},{24,16},{28,20},{1,9},{5... | collective-permute-start | bytes 1032200 | tf_op jit(solution)/shard_map/ppermute | solution.py:551
  103.3 17.5 %collective-permute-start.20 = (bf16[168,1024]{1,0:T(8,128)(2,1)S(1)}, bf16[168,1024]{1,0:T(8,128)(2,1)S(1)}, u32[]{:S(2)}, u32[]{:S(2)}) collective-permute-start(bf16[168,1024]{1,0:T(8,128)(2,1)S(1)} %get-tuple-element.246), channel_id=1, source_target_pairs={{0,16},{4,20},{8,24},{12,28},{16,0},{20,4},{24,8},{28,12},{1,17},{... | collective-permute-start | bytes 1032200 | tf_op jit(solution)/shard_map/ppermute | solution.py:551
  103.8 17.0 %collective-permute-start.21 = (bf16[168,1024]{1,0:T(8,128)(2,1)S(1)}, bf16[168,1024]{1,0:T(8,128)(2,1)S(1)}, u32[]{:S(2)}, u32[]{:S(2)}) collective-permute-start(bf16[168,1024]{1,0:T(8,128)(2,1)S(1)} %get-tuple-element.247), channel_id=1, source_target_pairs={{0,24},{4,28},{8,16},{12,20},{16,8},{20,12},{24,0},{28,4},{1,25},{... | collective-permute-start | bytes 1032200 | tf_op jit(solution)/shard_map/ppermute | solution.py:551
  105.1 23.4 %collective-permute-start.24 = (bf16[264,512]{1,0:T(8,128)(2,1)S(1)}, bf16[264,512]{1,0:T(8,128)(2,1)S(1)}, u32[]{:S(2)}, u32[]{:S(2)}) collective-permute-start(bf16[264,512]{1,0:T(8,128)(2,1)S(1)} %add_convert_fusion.2), channel_id=1, source_target_pairs={{0,2},{1,3},{2,0},{3,1},{4,6},{5,7},{6,4},{7,5},{8,10},{9,11},{10,... | collective-permute-start | bytes 811016 | tf_op jit(solution)/shard_map/ppermute | solution.py:561
  107.9 20.6 %collective-permute-start.26 = (bf16[256,512]{1,0:T(8,128)(2,1)S(1)}, bf16[256,512]{1,0:T(8,128)(2,1)S(1)}, u32[]{:S(2)}, u32[]{:S(2)}) collective-permute-start(bf16[256,512]{1,0:T(8,128)(2,1)S(1)} %get-tuple-element.255), channel_id=1, source_target_pairs={{0,0},{4,1},{1,2},{5,3},{2,4},{6,5},{3,6},{7,7},{8,8},{12,9},{9,10... | collective-permute-start | bytes 786440 | tf_op jit(solution)/shard_map/ppermute | solution.py:1146
  121.5 7.0 %collective-permute-start.22 = (bf16[168,512]{1,0:T(8,128)(2,1)S(1)}, bf16[168,512]{1,0:T(8,128)(2,1)S(1)}, u32[]{:S(2)}, u32[]{:S(2)}) collective-permute-start(bf16[168,512]{1,0:T(8,128)(2,1)S(1)} %get-tuple-element.249), channel_id=1, source_target_pairs={{0,1},{1,0},{2,3},{3,2},{4,5},{5,4},{6,7},{7,6},{8,9},{9,8},{10,11... | collective-permute-start | bytes 516104 | tf_op jit(solution)/shard_map/ppermute | solution.py:561
  121.7 20.3 %collective-permute-start.30 = (bf16[256,512]{1,0:T(8,128)(2,1)S(1)}, bf16[256,512]{1,0:T(8,128)(2,1)S(1)}, u32[]{:S(2)}, u32[]{:S(2)}) collective-permute-start(bf16[256,512]{1,0:T(8,128)(2,1)S(1)} %get-tuple-element.260), channel_id=1, source_target_pairs={{1,0},{5,1},{0,2},{4,3},{3,4},{7,5},{2,6},{6,7},{9,8},{13,9},{8,10... | collective-permute-start | bytes 786440 | tf_op jit(solution)/shard_map/ppermute | solution.py:1146
  128.6 11.8 %collective-permute-start.27 = (bf16[168,512]{1,0:T(8,128)(2,1)S(1)}, bf16[168,512]{1,0:T(8,128)(2,1)S(1)}, u32[]{:S(2)}, u32[]{:S(2)}) collective-permute-start(bf16[168,512]{1,0:T(8,128)(2,1)S(1)} %add_convert_fusion.4), channel_id=1, source_target_pairs={{0,2},{1,3},{2,0},{3,1},{4,6},{5,7},{6,4},{7,5},{8,10},{9,11},{10,... | collective-permute-start | bytes 516104 | tf_op jit(solution)/shard_map/ppermute | solution.py:561
  130.1 13.6 %collective-permute-start.31 = (bf16[264,512]{1,0:T(8,128)(2,1)S(1)}, bf16[264,512]{1,0:T(8,128)(2,1)S(1)}, u32[]{:S(2)}, u32[]{:S(2)}) collective-permute-start(bf16[264,512]{1,0:T(8,128)(2,1)S(1)} %add_convert_fusion.1.mine), channel_id=1, source_target_pairs={{0,1},{1,0},{2,3},{3,2},{4,5},{5,4},{6,7},{7,6},{8,9},{9,8},{10,11... | collective-permute-start | bytes 811016 | tf_op jit(solution)/shard_map/ppermute | solution.py:561
  140.5 1.3 collective-permute-start.28
  141.9 6.7 %collective-permute-start.29 = (bf16[176,512]{1,0:T(8,128)(2,1)S(1)}, bf16[176,512]{1,0:T(8,128)(2,1)S(1)}, u32[]{:S(2)}, u32[]{:S(2)}) collective-permute-start(bf16[176,512]{1,0:T(8,128)(2,1)S(1)} %pad_maximum_fusion.3.mine), channel_id=1, source_target_pairs={{0,1},{1,0},{2,3},{3,2},{4,5},{5,4},{6,7},{7,6},{8,9},{9,8},{10,11... | collective-permute-start | bytes 540680 | tf_op jit(solution)/shard_map/ppermute | solution.py:561
  143.7 1.9 %collective-permute-start.32 = (bf16[2,72,512]{2,1,0:T(8,128)(2,1)S(1)}, bf16[2,72,512]{2,1,0:T(8,128)(2,1)S(1)}, u32[]{:S(2)}, u32[]{:S(2)}) collective-permute-start(bf16[2,72,512]{2,1,0:T(8,128)(2,1)S(1)} %pad_maximum_fusion.4), channel_id=1, source_target_pairs={{0,4},{4,0},{8,12},{12,8},{16,20},{20,16},{24,28},{28,24},{1,5},{5... | collective-permute-start | bytes 442376 | tf_op jit(solution)/shard_map/ppermute | solution.py:546
